TPU v7x, 32 devices: a whole 2x2x4 slice. The times are simulated.
32 devices in a mesh: depth: 8 (over y, x, core), inline: 4 (over z).
Axes of the slice: x: 2, y: 2, z: 4, core: 2. Of those that a mesh axis runs over, the one named last changes fastest.
Arguments:
- control: float32 [32, 32, 16, 128], P(None, 'depth', 'inline'), may hold values from -6 to 6
- filter_coeffs: float32 [4, 32, 32], P(None, None, 'depth'), may hold values from 0 to 1, as said below
- conv_kernels: float32 [8, 4, 4, 5, 5], replicated, may hold values from -0.625 to 0.625
- channel_order: int32 [32], replicated, may hold values from 0 to 31, each once
- point_cells: int32 [3, 8, 4, 256], P(None, 'depth', 'inline'), may hold values from 0 to 127, as said below
- point_values: float32 [32, 8, 4, 256], P(None, 'depth', 'inline'), may hold values from -6 to 6
- point_weights: float32 [8, 4, 256], P('depth', 'inline'), may hold values from 1 to 10
- orient_cells: int32 [3, 8, 4, 128], P(None, 'depth', 'inline'), may hold values from 0 to 126, as said below
- orient_normals: float32 [3, 32, 8, 4, 128], P(None, None, 'depth', 'inline'), may hold values from -6 to 6
- orient_weights: float32 [8, 4, 128], P('depth', 'inline'), may hold values from 1 to 10
Outputs:
- potential: float32 [32, 32, 16, 128], P(None, 'depth', 'inline')
- gradient: float32 [32, 32, 16, 128], P(None, 'depth', 'inline')
Inputs may be any that keep to these rules, and one draw needn't show every extreme that they name: `filter_coeffs`: positive; the four lags of one channel and depth cell sum to less than one. `channel_order`: each channel appears once. `point_cells`: the points of row (d, i) lie in depth cells d * 4 to d * 4 + 3 and inline cells i * 4 to i * 4 + 3; the first point of each row is the last cell of that block along all three dimensions. `orient_cells`: the points of row (d, i) lie in depth cells d * 4 to d * 4 + 2, inline cells i * 4 to i * 4 + 2 and crossline cells 0 to 126; the first point of each row is the last such cell along all three dimensions.
All inputs are finite; a program needn't handle non-finite values.
Results may differ from a plain program's by a relative error of at most 0.0003.
Values sent between devices are 32-bit elements; how exact they have to be, the bound alone decides.
No kernel may reach another device: no remote copies, remote signals or barrier semaphores. Data moves between devices by JAX's collectives and lax.ppermute only.
A program may use at most 128 MiB of HBM per device.

v0:
```python
import jax
import jax.numpy as jnp
from jax import lax
from jax.experimental import pallas as pl
from jax.experimental.pallas import tpu as pltpu
from jax.sharding import PartitionSpec as P

HIGHEST = lax.Precision.HIGHEST


def entering(value, axis, join, neutral, backward):
    count, mine = (lax.axis_size(axis), lax.axis_index(axis))
    pieces = jax.tree.map(lambda part: lax.all_gather(part, axis), value)
    if backward:
        pieces = jax.tree.map(lambda part: part[::-1], pieces)
        mine = count - 1 - mine
    so_far = jax.tree.map(
        lambda part, zero: jnp.full_like(part, 0) + jnp.asarray(zero, part.dtype), value, neutral
    )

    def hop(position, so_far):
        longer = join(so_far, jax.tree.map(lambda part: part[position], pieces))
        return jax.tree.map(lambda new, old: jnp.where(position < mine, new, old), longer, so_far)

    return lax.fori_loop(0, count - 1, hop, so_far)


def extended_2(cells, sides, width):
    for axis, dim in sides:
        count = lax.axis_size(axis)
        ends = count - 1
        head = lax.slice_in_dim(cells, 0, width, axis=dim)
        tail = lax.slice_in_dim(cells, cells.shape[dim] - width, cells.shape[dim], axis=dim)
        cells = jnp.concatenate(
            [
                lax.ppermute(tail, axis, [(i, (i + 1) % count) for i in range(ends)]),
                cells,
                lax.ppermute(head, axis, [((i + 1) % count, i) for i in range(ends)]),
            ],
            axis=dim,
        )
    return cells


def mixing(kernels, channel_order):
    groups = kernels.shape[0]
    group_size = kernels.shape[1]
    channels = groups * group_size
    slots = jnp.arange(channels, dtype=jnp.int32)
    chooser = (channel_order[:, None] == slots[None, :]).astype(jnp.float32)
    in_group = (
        slots[:, None] // group_size == jnp.arange(groups, dtype=jnp.int32)[None, :]
    ).astype(jnp.float32)
    in_place = (
        slots[:, None] % group_size == jnp.arange(group_size, dtype=jnp.int32)[None, :]
    ).astype(jnp.float32)
    block_mix = jnp.einsum(
        "sg,sa,tg,tb,gabhw->sthw",
        in_group,
        in_place,
        in_group,
        in_place,
        kernels,
        precision=HIGHEST,
    )
    return jnp.einsum("sc,td,sthw->cdhw", chooser, chooser, block_mix, precision=HIGHEST)


def padded_conv(padded, weights):
    return lax.conv_general_dilated(
        padded,
        weights,
        (1, 1),
        ((0, 0), (2, 2)),
        dimension_numbers=("CNHW", "OIHW", "CNHW"),
        precision=HIGHEST,
    )


def compose(earlier, later):
    first_map, first_shift = earlier
    second_map, second_shift = later
    joined_map = jnp.einsum("cnij,cnjk->cnik", second_map, first_map, precision=HIGHEST)
    joined_shift = (
        jnp.einsum("cnij,cnjk->cnik", second_map, first_shift, precision=HIGHEST) + second_shift
    )
    return (joined_map, joined_shift)


def build_tiles(coeffs, by_column, block_len):
    lead = coeffs.shape[1:3]
    lag_steps = jnp.arange(1, 5, dtype=jnp.int32)[:, None, None]
    if by_column:
        row_ids = jnp.arange(block_len + 4, dtype=jnp.int32)[None, :, None]
        col_ids = jnp.arange(block_len, dtype=jnp.int32)[None, None, :]
        picker = (row_ids == col_ids + lag_steps).astype(jnp.float32)
        extended = jnp.einsum("lcnk,lzk->cnzk", coeffs, picker, precision=HIGHEST)
        lower_tile = extended[:, :, :block_len, :]
        exit_map = extended[:, :, block_len:, :]
        entry_base = (
            jnp.arange(block_len, dtype=jnp.int32)[:, None]
            == jnp.arange(4, dtype=jnp.int32)[None, :]
        ).astype(jnp.float32)
        entry_map = jnp.broadcast_to(entry_base, lead + (block_len, 4))
    else:
        row_ids = jnp.arange(block_len, dtype=jnp.int32)[None, :, None]
        col_ids = jnp.arange(block_len + 4, dtype=jnp.int32)[None, None, :]
        picker = (col_ids == row_ids - lag_steps + 4).astype(jnp.float32)
        extended = jnp.einsum("lcnz,lzk->cnzk", coeffs, picker, precision=HIGHEST)
        lower_tile = extended[:, :, :, 4:]
        entry_map = extended[:, :, :, :4]
        exit_base = (
            jnp.arange(block_len, dtype=jnp.int32)[None, :]
            == jnp.arange(4, dtype=jnp.int32)[:, None] + block_len - 4
        ).astype(jnp.float32)
        exit_map = jnp.broadcast_to(exit_base, lead + (4, block_len))
    return (lower_tile, entry_map, exit_map)


def sweep_blocks(field, coeffs, by_column, upward, prefix):
    if upward:
        field = field[:, ::-1, ::-1]
        coeffs = coeffs[:, :, ::-1, ::-1]
    block_len = coeffs.shape[3]
    lower_tile, entry_map, exit_map = build_tiles(coeffs, by_column, block_len)
    identity_tile = jnp.eye(block_len, dtype=jnp.float32)
    inverse = identity_tile + lower_tile
    power = lower_tile
    power = jnp.einsum("cnij,cnjk->cnik", power, power, precision=HIGHEST)
    inverse = inverse + jnp.einsum("cnij,cnjk->cnik", inverse, power, precision=HIGHEST)
    reach_map = jnp.einsum("cnzk,cnkj->cnzj", inverse, entry_map, precision=HIGHEST)
    carry_map = jnp.einsum("cniz,cnzj->cnij", exit_map, reach_map, precision=HIGHEST)
    local_part = jnp.einsum("cnzk,cnkm->cnzm", inverse, field, precision=HIGHEST)
    carry_out = jnp.einsum("cniz,cnzm->cnim", exit_map, local_part, precision=HIGHEST)
    incoming = prefix((carry_map, carry_out), upward)
    result = local_part + jnp.einsum("cnzj,cnjm->cnzm", reach_map, incoming, precision=HIGHEST)
    if upward:
        result = result[:, ::-1, ::-1]
    return result


def shards(
    control,
    filter_coeffs,
    conv_kernels,
    channel_order,
    point_cells,
    point_values,
    point_weights,
    orient_cells,
    orient_normals,
    orient_weights,
):
    channels, block_len, inline_rows, cross_cols = control.shape
    plane_cells = inline_rows * cross_cols
    source = control.reshape(channels, block_len, plane_cells)
    coeffs = filter_coeffs[:, :, None, :]

    def to_blocks(field):
        return field[:, None]

    def from_blocks(field):
        return field[:, 0]

    def scaled(field, factor):
        return factor[..., None] * field

    def prefix(maps, upward):
        start = (
            jnp.broadcast_to(jnp.eye(4, dtype=jnp.float32), maps[0].shape),
            jnp.zeros_like(maps[1]),
        )
        return entering(maps, "depth", compose, start, upward)[1]

    scaling = 1.0 - jnp.sum(coeffs, axis=0)
    root_scale = jnp.sqrt(scaling)
    filtered = sweep_blocks(scaled(to_blocks(source), root_scale), coeffs, False, False, prefix)
    smoothed = sweep_blocks(scaled(filtered, scaling), coeffs, False, True, prefix)
    smoothed_field = from_blocks(smoothed).reshape(control.shape)
    weights = mixing(conv_kernels, channel_order)
    smoothed_padded = extended_2(smoothed_field, (("inline", 2),), 2)
    potential = padded_conv(smoothed_padded, weights)
    flat_field = potential.reshape(channels, -1)
    depth_base = lax.axis_index("depth") * block_len
    inline_base = lax.axis_index("inline") * inline_rows
    cells = point_cells.reshape(3, -1)
    flat_index = (
        (cells[0] - depth_base) * inline_rows + cells[1] - inline_base
    ) * cross_cols + cells[2]
    misfit = (
        flat_field[:, flat_index] - point_values.reshape(channels, -1)
    ) * point_weights.reshape(-1)[None, :]
    ocells = orient_cells.reshape(3, -1)
    base_cell = (
        (ocells[0] - depth_base) * inline_rows + ocells[1] - inline_base
    ) * cross_cols + ocells[2]
    normals = orient_normals.reshape(3, channels, -1)
    oweight = orient_weights.reshape(-1)[None, :]
    update_values = [misfit]
    update_cells = [flat_index]
    for component, stride in enumerate((plane_cells, cross_cols, 1)):
        mismatch = flat_field[:, base_cell + stride] - flat_field[:, base_cell] - normals[component]
        weighted = mismatch * oweight
        update_values.append(weighted)
        update_cells.append(base_cell + stride)
        update_values.append(-weighted)
        update_cells.append(base_cell)
    all_values = jnp.concatenate(update_values, axis=1)
    all_cells = jnp.concatenate(update_cells, axis=0)
    adjoint_weights = jnp.transpose(weights, (1, 0, 2, 3))[:, :, ::-1, ::-1]
    forcing = jnp.zeros_like(flat_field).at[:, all_cells].add(all_values)
    forcing_padded = extended_2(forcing.reshape(control.shape), (("inline", 2),), 2)
    spread = padded_conv(forcing_padded, adjoint_weights).reshape(channels, block_len, plane_cells)
    adjoint_back = scaled(sweep_blocks(to_blocks(spread), coeffs, True, False, prefix), scaling)
    adjoint_fore = scaled(sweep_blocks(adjoint_back, coeffs, True, True, prefix), root_scale)
    gradient = control + from_blocks(adjoint_fore).reshape(control.shape)
    return (potential, gradient)


CHUNK = 96
AT_VALUES, AT_NORMALS, AT_COEFFS, AT_MISC = 64, 72, 84, 88


def f32(*shape):
    return jax.ShapeDtypeStruct(shape, jnp.float32)


def in_vmem(count):
    return [pl.BlockSpec(memory_space=pltpu.VMEM) for _ in range(count)]


def lane_index(shape):
    return lax.broadcasted_iota(jnp.int32, shape, len(shape) - 1)


def pack_kernel(
    order, control, coeffs, values, normals, cells, weights, ocells, oweights, out, by_channel
):
    def flat_cell(ref):
        z, y, x = (ref[k, 0] for k in range(3))
        return (((y & 3) * 4 + (z & 3)) * 128 + x).astype(jnp.float32)

    flat, oflat = flat_cell(cells), flat_cell(ocells)
    weight = weights[0]
    misc = jnp.concatenate(
        [flat[:, :128], flat[:, 128:], oflat, weight[:, :128], weight[:, 128:], oweights[0]]
        + [jnp.zeros((2, 128), jnp.float32)],
        axis=0,
    )
    by_channel[...] = jnp.transpose(
        jnp.concatenate([coeffs[...], jnp.zeros((16, 96), jnp.float32)], axis=1)
    )
    for group in range(8):
        out[group, AT_MISC:CHUNK, :] = misc
    for slot in range(32):
        group, c = divmod(slot, 4)
        channel = order[slot]
        plane = control[channel]
        for z in range(4):
            row = z * 16 + c * 4
            out[group, row : row + 4, :] = plane[z * 4 : z * 4 + 4]
        row = AT_VALUES + 2 * c
        out[group, row : row + 2, :] = values[pl.ds(channel * 2, 2), :]
        for k in range(3):
            row = AT_NORMALS + 4 * k + c
            out[group, row : row + 1, :] = normals[pl.ds(k * 32 + channel, 1), :]
        row = AT_COEFFS + c
        out[group, row : row + 1, :16] = by_channel[pl.ds(channel, 1), :]


def coefficient(expanded, lag, z):
    block, local = divmod(z, 4)
    k = (lag - 1) * 4 + local
    return jnp.broadcast_to(expanded[block, :, k : k + 1], (16, 128))


def expand_coeffs(chunks, expanded, table, scale, root):
    for block in range(8):
        for c in range(4):
            row = AT_COEFFS + c
            expanded[block, 4 * c : 4 * c + 4, :] = jnp.broadcast_to(
                chunks[block, row : row + 1, :], (4, 128)
            )
    for z in range(32):
        lags = [coefficient(expanded, lag, z) for lag in range(1, 5)]
        for lag in range(4):
            table[z, lag] = lags[lag]
        scale[z] = 1.0 - ((lags[0] + lags[1]) + (lags[2] + lags[3]))
        root[z] = jnp.sqrt(scale[z])


def recurrence(source, factor, emit, order):
    history = []
    for t in order:
        total = source(t)
        for lag in range(len(history), 0, -1):
            before, value = history[lag - 1]
            total = total + factor(lag, t, before) * value
        history = [(t, total)] + history[:3]
        emit(t, total)


COEFF_SCRATCH = [
    pltpu.VMEM((8, 16, 128), jnp.float32),
    pltpu.VMEM((32, 4, 16, 128), jnp.float32),
    pltpu.VMEM((32, 16, 128), jnp.float32),
    pltpu.VMEM((32, 16, 128), jnp.float32),
]


def depth_rows(chunks, z):
    return chunks[z // 4, (z % 4) * 16 : (z % 4) * 16 + 16, :]


def smooth_kernel(chunks, smoothed, even, odd, expanded, table, scale, root, first, rows):
    expand_coeffs(chunks, expanded, table, scale, root)

    def keep_first(z, value):
        first[z] = scale[z] * value

    def keep_rows(z, value):
        rows[z * 16 : z * 16 + 16, :] = value

    recurrence(
        lambda z: root[z] * depth_rows(chunks, z),
        lambda lag, z, before: table[z, lag - 1],
        keep_first,
        range(32),
    )
    recurrence(
        lambda z: first[z],
        lambda lag, z, before: table[z, lag - 1],
        keep_rows,
        range(31, -1, -1),
    )
    parity = lax.axis_index("inline") % 2
    for y in range(4):
        for c in range(4):
            smoothed[y, c] = rows[pl.ds(c * 4 + y, 32, stride=16), :]
    for y in range(2):
        even[y] = smoothed[2 - 2 * parity + y]
        odd[y] = smoothed[2 * parity + y]


def tap(table, a, b, h, w):
    row = ((a * 5 + h) * 5 + w) * 4 + b
    return jnp.broadcast_to(table[row : row + 1, :], (8, 128))


def conv_rows(read, rows_in, start, table, adjoint, write):
    lane = lane_index((8, 128))

    def moved(value, shift):
        if shift == 0:
            return value
        inside = lane >= -shift if shift < 0 else lane < 128 - shift
        return jnp.where(inside, pltpu.roll(value, -shift % 128, 1), 0.0)

    def some_depths(k, carry):
        depths = pl.ds(pl.multiple_of(k * 8, 8), 8)
        total = [[start(y, o, depths) for o in range(4)] for y in range(4)]
        for i in range(4):
            lines = {row: read(row, i, depths) for row in rows_in}
            for w in range(5):
                if adjoint:
                    taps = [[tap(table, i, o, h, w) for h in range(5)] for o in range(4)]
                else:
                    taps = [[tap(table, o, i, h, w) for h in range(5)] for o in range(4)]
                for row in rows_in:
                    line = moved(lines[row], 2 - w if adjoint else w - 2)
                    for y in range(4):
                        h = y - row + 2 if adjoint else row - y + 2
                        if 0 <= h < 5:
                            for o in range(4):
                                total[y][o] = total[y][o] + taps[o][h] * line
        for y in range(4):
            for o in range(4):
                write(y, o, depths, total[y][o])
        return carry

    lax.fori_loop(0, 4, some_depths, 0)


OWN = (0, 1, 2, 3)
HALO = (-2, -1, 4, 5)


def halo_reader(even, odd):
    parity = lax.axis_index("inline") % 2

    def read(row, c, depths):
        y = row + 2 if row < 0 else row - 4
        through_even, through_odd = even[y, c, depths, :], odd[y, c, depths, :]
        below = parity == 1 if row < 0 else parity == 0
        return jnp.where(below, through_even, through_odd)

    return read


def split(value):
    high = value.astype(jnp.bfloat16)
    return high, (value - high.astype(jnp.float32)).astype(jnp.bfloat16)


def point_fields(chunks, constant, weight, oweight):
    row = lax.broadcasted_iota(jnp.int32, (16, 256), 0)
    orow = lax.broadcasted_iota(jnp.int32, (16, 128), 0)
    column = lax.broadcasted_iota(jnp.int32, (128, 384), 0)
    for block in range(8):

        def line(k, block=block):
            return chunks[block, k : k + 1, :]

        def double(k, line=line):
            return jnp.concatenate([line(k), line(k + 1)], axis=1)

        flat = double(AT_MISC).astype(jnp.int32)
        oflat = line(AT_MISC + 2).astype(jnp.int32)
        w, ow = double(AT_MISC + 3), line(AT_MISC + 5)
        cell, ocell = flat >> 7, oflat >> 7
        at_cross = jnp.concatenate([flat & 127, oflat & 127], axis=1)
        columns = (column == at_cross).astype(jnp.float32).astype(jnp.bfloat16)
        here, ohere = row == cell, orow == ocell
        below, beside = orow == ocell + 1, orow == ocell + 4
        main, along = [], []
        for c in range(4):
            value = w * double(AT_VALUES + 2 * c)
            n0, n1, n2 = (ow * line(AT_NORMALS + 4 * k + c) for k in range(3))
            placed = (
                jnp.where(below, n0, 0.0)
                + jnp.where(beside, n1, 0.0)
                - jnp.where(ohere, n0 + n1 + n2, 0.0)
            )
            main.append(jnp.concatenate([jnp.where(here, value, 0.0), placed], axis=1))
            along.append(
                jnp.concatenate([jnp.zeros((16, 256), jnp.float32), jnp.where(ohere, n2, 0.0)], axis=1)
            )
        both = [
            jnp.concatenate([jnp.where(here, w, 0.0), jnp.zeros((16, 128), jnp.float32)], axis=1),
            jnp.concatenate([jnp.zeros((16, 256), jnp.float32), jnp.where(ohere, ow, 0.0)], axis=1),
        ]
        high, low = split(jnp.concatenate(main + both + along, axis=0))
        sums = lax.dot_general(
            jnp.concatenate([high, low], axis=0),
            columns,
            (((1,), (1,)), ((), ())),
            preferred_element_type=jnp.float32,
        )
        sums = sums[:160] + sums[160:]
        moved = pltpu.roll(sums[96:160], 1, 1)
        z = 4 * block
        for y in range(4):
            for c in range(4):
                k = 16 * c + 4 * y
                constant[y, c, z : z + 4, :] = sums[k : k + 4] + moved[k : k + 4]
            weight[y, z : z + 4, :] = sums[64 + 4 * y : 68 + 4 * y]
            oweight[y, z : z + 4, :] = sums[80 + 4 * y : 84 + 4 * y]


def own_kernel(chunks, smoothed, kernels, partial, constant, weight, oweight, table):
    group = lax.axis_index("depth")
    picked = jnp.where(lane_index((400, 8)) == group, kernels[...], 0.0)
    table[...] = jnp.broadcast_to(jnp.sum(picked, axis=1, keepdims=True), (400, 128))
    point_fields(chunks, constant, weight, oweight)

    def write(y, o, depths, value):
        partial[y, o, depths, :] = value

    conv_rows(
        lambda row, c, depths: smoothed[row, c, depths, :],
        OWN,
        lambda y, o, depths: jnp.zeros((8, 128), jnp.float32),
        table,
        False,
        write,
    )


def forcing_kernel(
    partial, even_in, odd_in, table, constant, weight, oweight, potential, forcing, even, odd
):
    def write(y, o, depths, value):
        potential[y, o, depths, :] = value

    conv_rows(
        halo_reader(even_in, odd_in),
        HALO,
        lambda y, o, depths: partial[y, o, depths, :],
        table,
        False,
        write,
    )

    def one_channel(c, carry):
        lines = [potential[y, c] for y in range(4)]
        sums = [weight[y] * lines[y] - constant[y, c] for y in range(4)]
        for y in range(4):
            share = oweight[y]
            deeper = share * (pltpu.roll(lines[y], 31, 0) - lines[y])
            across = share * (pltpu.roll(lines[y], 127, 1) - lines[y])
            sums[y] = sums[y] - deeper + pltpu.roll(deeper, 1, 0)
            sums[y] = sums[y] - across + pltpu.roll(across, 1, 1)
            if y < 3:
                beside = share * (lines[y + 1] - lines[y])
                sums[y] = sums[y] - beside
                sums[y + 1] = sums[y + 1] + beside
        for y in range(4):
            forcing[y, c] = sums[y]
        return carry

    lax.fori_loop(0, 4, one_channel, 0)
    parity = lax.axis_index("inline") % 2
    for y in range(2):
        even[y] = forcing[2 - 2 * parity + y]
        odd[y] = forcing[2 * parity + y]


def spread_kernel(forcing, table, partial):
    def write(y, o, depths, value):
        partial[y, o, depths, :] = value

    conv_rows(
        lambda row, c, depths: forcing[row, c, depths, :],
        OWN,
        lambda y, o, depths: jnp.zeros((8, 128), jnp.float32),
        table,
        True,
        write,
    )


def gradient_kernel(
    chunks, partial, even_in, odd_in, taps, potential, out, expanded, table, scale, root, first, rows
):
    expand_coeffs(chunks, expanded, table, scale, root)
    for y in range(4):
        for c in range(4):
            rows[pl.ds((c * 4 + y) * 32, 32), :] = potential[y, c]
    for z in range(32):
        out[z // 4, (z % 4) * 16 : (z % 4) * 16 + 16, :] = rows[pl.ds(z, 16, stride=32), :]

    def write(y, o, depths, value):
        rows[pl.ds(pl.multiple_of((o * 4 + y) * 32 + depths.start, 8), 8), :] = value

    conv_rows(
        halo_reader(even_in, odd_in),
        HALO,
        lambda y, o, depths: partial[y, o, depths, :],
        taps,
        True,
        write,
    )

    def keep_first(z, value):
        first[z] = scale[z] * value

    def keep_out(z, value):
        row = 64 + (z % 4) * 16
        out[z // 4, row : row + 16, :] = depth_rows(chunks, z) + root[z] * value

    recurrence(
        lambda z: rows[pl.ds(z, 16, stride=32), :],
        lambda lag, z, before: table[before, lag - 1],
        keep_first,
        range(32),
    )
    recurrence(
        lambda z: first[z],
        lambda lag, z, before: table[before, lag - 1],
        keep_out,
        range(31, -1, -1),
    )


def unpack_kernel(order, chunks, potential, gradient):
    for slot in range(32):
        group, c = divmod(slot, 4)
        channel = order[slot]
        for out, base in ((potential, 0), (gradient, 64)):
            pieces = [
                chunks[group, base + z * 16 + c * 4 : base + z * 16 + c * 4 + 4, :] for z in range(4)
            ]
            out[channel] = jnp.concatenate(pieces, axis=0)


def swapped(even, odd):
    count = lax.axis_size("inline")

    def pairs(first):
        below = [(i, i + 1) for i in range(first, count - 1, 2)]
        return below + [(j, i) for i, j in below]

    return lax.ppermute(even, "inline", pairs(0)), lax.ppermute(odd, "inline", pairs(1))


def by_group(
    control,
    filter_coeffs,
    conv_kernels,
    channel_order,
    point_cells,
    point_values,
    point_weights,
    orient_cells,
    orient_normals,
    orient_weights,
):
    params = pltpu.CompilerParams(vmem_limit_bytes=48 << 20)
    in_smem = pl.BlockSpec(memory_space=pltpu.SMEM)

    def call(kernel, outs, operands, scratch=(), first=None):
        specs = in_vmem(len(operands))
        if first is not None:
            specs[0] = first
        return pl.pallas_call(
            kernel,
            out_shape=outs,
            in_specs=specs,
            out_specs=jax.tree.map(lambda _: pl.BlockSpec(memory_space=pltpu.VMEM), outs),
            scratch_shapes=list(scratch),
            compiler_params=params,
        )(*operands)

    chunks = call(
        pack_kernel,
        f32(8, CHUNK, 128),
        (
            channel_order,
            control.reshape(32, 16, 128),
            jnp.transpose(filter_coeffs, (0, 2, 1)).reshape(16, 32),
            point_values.reshape(64, 128),
            orient_normals.reshape(96, 128),
            point_cells,
            point_weights,
            orient_cells,
            orient_weights,
        ),
        (pltpu.VMEM((128, 16), jnp.float32),),
        in_smem,
    )
    chunks = lax.all_to_all(chunks, "depth", 0, 0)
    field, edge, plane = f32(4, 4, 32, 128), f32(2, 4, 32, 128), f32(4, 32, 128)
    rows = pltpu.VMEM((512, 128), jnp.float32)
    first = pltpu.VMEM((32, 16, 128), jnp.float32)
    smoothed, even, odd = call(
        smooth_kernel, (field, edge, edge), (chunks,), COEFF_SCRATCH + [first, rows]
    )
    even, odd = swapped(even, odd)
    kernels = jnp.transpose(conv_kernels, (1, 3, 4, 2, 0)).reshape(400, 8)
    partial, constant, weight, oweight, taps = call(
        own_kernel, (field, field, plane, plane, f32(400, 128)), (chunks, smoothed, kernels)
    )
    potential, forcing, even, odd = call(
        forcing_kernel,
        (field, field, edge, edge),
        (partial, even, odd, taps, constant, weight, oweight),
    )
    even, odd = swapped(even, odd)
    partial = call(spread_kernel, field, (forcing, taps))
    results = call(
        gradient_kernel,
        f32(8, 128, 128),
        (chunks, partial, even, odd, taps, potential),
        COEFF_SCRATCH + [first, rows],
    )
    results = lax.all_to_all(results, "depth", 0, 0)
    block = f32(32, 16, 128)
    potential, gradient = call(
        unpack_kernel, (block, block), (channel_order, results), (), in_smem
    )
    return potential.reshape(control.shape), gradient.reshape(control.shape)


def solution(mesh):
    placed = (
        P(None, "depth", "inline", None),
        P(None, None, "depth"),
        P(),
        P(),
        P(None, "depth", "inline", None),
        P(None, "depth", "inline", None),
        P("depth", "inline", None),
        P(None, "depth", "inline", None),
        P(None, None, "depth", "inline", None),
        P("depth", "inline", None),
    )

    def body(control, filter_coeffs, conv_kernels, *rest):
        groups, block = conv_kernels.shape, control.shape
        fits = groups[:3] == (mesh.shape["depth"], 4, 4) and groups[0] == 8
        if fits and block == (32, 4, 4, 128):
            return by_group(control, filter_coeffs, conv_kernels, *rest)
        return shards(control, filter_coeffs, conv_kernels, *rest)

    return jax.shard_map(
        body,
        mesh=mesh,
        in_specs=placed,
        out_specs=(P(None, "depth", "inline", None), P(None, "depth", "inline", None)),
        check_vma=False,
    )
```

profile of v0, /device:TPU:16, one launch (start us, length us, event | category | flops | bytes accessed | tf_op | source)
XLA Modules:
  0.0 50.0 jit_solution(17973876375951416858)
XLA Ops:
  0.6 0.0 copy-start.8
  0.6 0.0 copy-start.5
  0.7 0.0 copy-start.7
  0.7 0.0 copy-start.6
  0.7 0.0 copy-start.9
  0.7 0.6 %copy-done.8 = f32[1,1,256]{2,1,0:T(1,128)S(1)} copy-done((f32[1,1,256]{2,1,0:T(1,128)S(1)}, f32[1,1,256]{2,1,0:T(1,128)}, u32[]{:S(2)}) %copy-start.8) | copy-done | bytes 1048
  1.3 0.0 copy-done.5
  1.3 0.0 copy-done.7
  1.3 0.0 copy-done.6
  1.3 0.0 copy-done.9
  1.4 0.0 copy-start
  1.4 0.9 %copy-done = f32[32,4,4,128]{3,2,1,0:T(4,128)S(1)} copy-done((f32[32,4,4,128]{3,2,1,0:T(4,128)S(1)}, f32[32,4,4,128]{3,2,1,0:T(4,128)}, u32[]{:S(2)}) %copy-start) | copy-done | bytes 262168
  2.3 0.0 copy-start.2
  2.3 0.8 %copy-done.2 = f32[3,32,1,1,128]{4,3,2,1,0:T(1,128)S(1)} copy-done((f32[3,32,1,1,128]{4,3,2,1,0:T(1,128)S(1)}, f32[3,32,1,1,128]{4,3,2,1,0:T(1,128)}, u32[]{:S(2)}) %copy-start.2) | copy-done | bytes 49176
  3.1 0.0 copy-start.3
  3.1 0.8 %copy-done.3 = f32[32,1,1,256]{3,2,1,0:T(1,128)S(1)} copy-done((f32[32,1,1,256]{3,2,1,0:T(1,128)S(1)}, f32[32,1,1,256]{3,2,1,0:T(1,128)}, u32[]{:S(2)}) %copy-start.3) | copy-done | bytes 32792
  3.9 0.0 copy-start.4
  3.9 0.7 %copy-done.4 = f32[4,32,4]{1,2,0:T(4,128)S(1)} copy-done((f32[4,32,4]{1,2,0:T(4,128)S(1)}, f32[4,32,4]{1,2,0:T(4,128)}, u32[]{:S(2)}) %copy-start.4) | copy-done | bytes 2072
  4.6 0.7 %shard_map.113 = f32[8,96,128]{2,1,0:T(8,128)S(1)} custom-call(s32[32]{0:T(128)S(1)} %copy-done.6, f32[32,16,128]{2,1,0:T(8,128)S(1)} %bitcast.11, f32[16,32]{1,0:T(8,128)S(1)} %bitcast.15, f32[64,128]{1,0:T(8,128)S(1)} %bitcast.14, f32[96,128]{1,0:T(8,128)S(1)} %bitcast.13, s32[3,1,1,256]{3,2,1,0:T(1,128)S(1)} %copy-done.5, f32[1,1,256]{2,1,0:T(1,128)S(1)} %copy-done.8, ...), custom_call_target="tpu_custom_call" | custom-call | tf_op jit(solution)/shard_map/pallas_call | solution.py:615
  5.2 11.9 %all_to_all.10.chunks = f32[8,96,128]{2,1,0:T(8,128)S(1)} all-to-all(f32[8,96,128]{2,1,0:T(8,128)S(1)} %shard_map.113), channel_id=1, replica_groups=mesh['depth'=8,'inline'=4] {'depth'}, dimensions={0} | all-to-all | bytes 786432 | tf_op jit(solution)/shard_map/all_to_all | solution.py:641
  17.1 0.0 copy-start.1
  17.1 0.7 %shard_map.114 = (f32[4,4,32,128]{3,2,1,0:T(8,128)S(1)}, f32[2,4,32,128]{3,2,1,0:T(8,128)S(1)}, f32[2,4,32,128]{3,2,1,0:T(8,128)S(1)}) custom-call(f32[8,96,128]{2,1,0:T(8,128)S(1)} %all_to_all.10.chunks), custom_call_target="tpu_custom_call" | custom-call | tf_op jit(solution)/shard_map/pallas_call | solution.py:615
  17.8 1.6 %collective-permute-start = (f32[2,4,32,128]{3,2,1,0:T(8,128)S(1)}, f32[2,4,32,128]{3,2,1,0:T(8,128)S(1)}, u32[]{:S(2)}, u32[]{:S(2)}) collective-permute-start(f32[2,4,32,128]{3,2,1,0:T(8,128)S(1)} %get-tuple-element.18), channel_id=1, source_target_pairs={{0,1},{2,3},{1,0},{3,2},{4,5},{6,7},{5,4},{7,6},{8,9},{10,11},{9,8... | collective-permute-start | bytes 393224 | tf_op jit(solution)/shard_map/ppermute | solution.py:593
  19.4 1.9 %collective-permute-start.1 = (f32[2,4,32,128]{3,2,1,0:T(8,128)S(1)}, f32[2,4,32,128]{3,2,1,0:T(8,128)S(1)}, u32[]{:S(2)}, u32[]{:S(2)}) collective-permute-start(f32[2,4,32,128]{3,2,1,0:T(8,128)S(1)} %get-tuple-element.19), channel_id=1, source_target_pairs={{1,2},{2,1},{5,6},{6,5},{9,10},{10,9},{13,14},{14,13},{17,18},{18,... | collective-permute-start | bytes 393224 | tf_op jit(solution)/shard_map/ppermute | solution.py:593
  21.3 0.0 copy-done.1
  21.3 2.4 %shard_map.115 = (f32[4,4,32,128]{3,2,1,0:T(8,128)S(1)}, f32[4,4,32,128]{3,2,1,0:T(8,128)S(1)}, f32[4,32,128]{2,1,0:T(8,128)S(1)}, f32[4,32,128]{2,1,0:T(8,128)S(1)}, f32[400,128]{1,0:T(8,128)S(1)}) custom-call(f32[8,96,128]{2,1,0:T(8,128)S(1)} %all_to_all.10.chunks, f32[4,4,32,128]{3,2,1,0:T(8,128)S(1)} %get-tuple-element.16.smoothed, f32[400,8]{1,0:T(8,128)S(1)} %bitcast.12), custom_call_target="tpu_custom_call" | custom-call | tf_op jit(solution)/shard_map/pallas_call | solution.py:615
  23.8 0.0 collective-permute-done.even_in
  23.8 2.5 %collective-permute-done.1.odd_in = f32[2,4,32,128]{3,2,1,0:T(8,128)S(1)} collective-permute-done((f32[2,4,32,128]{3,2,1,0:T(8,128)S(1)}, f32[2,4,32,128]{3,2,1,0:T(8,128)S(1)}, u32[]{:S(2)}, u32[]{:S(2)}) %collective-permute-start.1) | collective-permute-done | bytes 131104 | tf_op jit(solution)/shard_map/ppermute | solution.py:593
  26.3 1.5 %shard_map.116 = (f32[4,4,32,128]{3,2,1,0:T(8,128)S(1)}, f32[4,4,32,128]{3,2,1,0:T(8,128)S(1)}, f32[2,4,32,128]{3,2,1,0:T(8,128)S(1)}, f32[2,4,32,128]{3,2,1,0:T(8,128)S(1)}) custom-call(f32[4,4,32,128]{3,2,1,0:T(8,128)S(1)} %get-tuple-element.17.partial, f32[2,4,32,128]{3,2,1,0:T(8,128)S(1)} %collective-permute-done.even_in, ...), custom_call_target="tpu_custom_call" | custom-call | tf_op jit(solution)/shard_map/pallas_call | solution.py:615
  27.8 0.1 collective-permute-start.2
  27.9 2.0 %collective-permute-start.3 = (f32[2,4,32,128]{3,2,1,0:T(8,128)S(1)}, f32[2,4,32,128]{3,2,1,0:T(8,128)S(1)}, u32[]{:S(2)}, u32[]{:S(2)}) collective-permute-start(f32[2,4,32,128]{3,2,1,0:T(8,128)S(1)} %get-tuple-element.26), channel_id=1, source_target_pairs={{1,2},{2,1},{5,6},{6,5},{9,10},{10,9},{13,14},{14,13},{17,18},{18,... | collective-permute-start | bytes 393224 | tf_op jit(solution)/shard_map/ppermute | solution.py:593
  29.9 1.6 %shard_map.117.partial = f32[4,4,32,128]{3,2,1,0:T(8,128)S(1)} custom-call(f32[4,4,32,128]{3,2,1,0:T(8,128)S(1)} %get-tuple-element.24.forcing, f32[400,128]{1,0:T(8,128)S(1)} %get-tuple-element.20.table.taps), custom_call_target="tpu_custom_call" | custom-call | tf_op jit(solution)/shard_map/pallas_call | solution.py:615
  31.5 1.3 %collective-permute-done.2.even_in = f32[2,4,32,128]{3,2,1,0:T(8,128)S(1)} collective-permute-done((f32[2,4,32,128]{3,2,1,0:T(8,128)S(1)}, f32[2,4,32,128]{3,2,1,0:T(8,128)S(1)}, u32[]{:S(2)}, u32[]{:S(2)}) %collective-permute-start.2) | collective-permute-done | bytes 131104 | tf_op jit(solution)/shard_map/ppermute | solution.py:593
  32.8 1.9 %collective-permute-done.3.odd_in = f32[2,4,32,128]{3,2,1,0:T(8,128)S(1)} collective-permute-done((f32[2,4,32,128]{3,2,1,0:T(8,128)S(1)}, f32[2,4,32,128]{3,2,1,0:T(8,128)S(1)}, u32[]{:S(2)}, u32[]{:S(2)}) %collective-permute-start.3) | collective-permute-done | bytes 131104 | tf_op jit(solution)/shard_map/ppermute | solution.py:593
  34.7 1.8 %shard_map.118 = f32[8,128,128]{2,1,0:T(8,128)S(1)} custom-call(f32[8,96,128]{2,1,0:T(8,128)S(1)} %all_to_all.10.chunks, f32[4,4,32,128]{3,2,1,0:T(8,128)S(1)} %shard_map.117.partial, f32[2,4,32,128]{3,2,1,0:T(8,128)S(1)} %collective-permute-done.2.even_in, f32[2,4,32,128]{3,2,1,0:T(8,128)S(1)} %collective-permute-done.3.odd_in, ...), custom_call_target="tpu_custom_call" | custom-call | tf_op jit(solution)/shard_map/pallas_call | solution.py:615
  36.5 12.2 %all_to_all.11.chunks = f32[8,128,128]{2,1,0:T(8,128)S(1)} all-to-all(f32[8,128,128]{2,1,0:T(8,128)S(1)} %shard_map.118), channel_id=1, replica_groups=mesh['depth'=8,'inline'=4] {'depth'}, dimensions={0} | all-to-all | bytes 1048576 | tf_op jit(solution)/shard_map/all_to_all | solution.py:666
  48.6 1.4 %shard_map.119 = (f32[32,16,128]{2,1,0:T(8,128)}, f32[32,16,128]{2,1,0:T(8,128)}) custom-call(s32[32]{0:T(128)S(1)} %copy-done.6, f32[8,128,128]{2,1,0:T(8,128)S(1)} %all_to_all.11.chunks), custom_call_target="tpu_custom_call" | custom-call | tf_op jit(solution)/shard_map/pallas_call | solution.py:615
Async XLA Ops:
  0.6 0.7 %copy-start.8 = (f32[1,1,256]{2,1,0:T(1,128)S(1)}, f32[1,1,256]{2,1,0:T(1,128)}, u32[]{:S(2)}) copy-start(f32[1,1,256]{2,1,0:T(1,128)} %weights.1) | copy-start | bytes 3076
  0.6 0.7 %copy-start.5 = (s32[3,1,1,256]{3,2,1,0:T(1,128)S(1)}, s32[3,1,1,256]{3,2,1,0:T(1,128)}, u32[]{:S(2)}) copy-start(s32[3,1,1,256]{3,2,1,0:T(1,128)} %cells.1) | copy-start | bytes 9220
  0.7 0.7 %copy-start.7 = (s32[3,1,1,128]{3,2,1,0:T(1,128)S(1)}, s32[3,1,1,128]{3,2,1,0:T(1,128)}, u32[]{:S(2)}) copy-start(s32[3,1,1,128]{3,2,1,0:T(1,128)} %ocells.1) | copy-start | bytes 4612
  0.7 0.7 %copy-start.6 = (s32[32]{0:T(128)S(1)}, s32[32]{0:T(128)}, u32[]{:S(2)}) copy-start(s32[32]{0:T(128)} %order.3) | copy-start | bytes 388
  0.7 0.7 %copy-start.9 = (f32[1,1,128]{2,1,0:T(1,128)S(1)}, f32[1,1,128]{2,1,0:T(1,128)}, u32[]{:S(2)}) copy-start(f32[1,1,128]{2,1,0:T(1,128)} %oweights.1) | copy-start | bytes 1540
  1.4 0.9 %copy-start = (f32[32,4,4,128]{3,2,1,0:T(4,128)S(1)}, f32[32,4,4,128]{3,2,1,0:T(4,128)}, u32[]{:S(2)}) copy-start(f32[32,4,4,128]{3,2,1,0:T(4,128)} %param.10) | copy-start | bytes 786436
  2.3 0.8 %copy-start.2 = (f32[3,32,1,1,128]{4,3,2,1,0:T(1,128)S(1)}, f32[3,32,1,1,128]{4,3,2,1,0:T(1,128)}, u32[]{:S(2)}) copy-start(f32[3,32,1,1,128]{4,3,2,1,0:T(1,128)} %param.18) | copy-start | bytes 147460
  3.1 0.8 %copy-start.3 = (f32[32,1,1,256]{3,2,1,0:T(1,128)S(1)}, f32[32,1,1,256]{3,2,1,0:T(1,128)}, u32[]{:S(2)}) copy-start(f32[32,1,1,256]{3,2,1,0:T(1,128)} %param.15) | copy-start | bytes 98308
  3.9 0.7 %copy-start.4 = (f32[4,32,4]{1,2,0:T(4,128)S(1)}, f32[4,32,4]{1,2,0:T(4,128)}, u32[]{:S(2)}) copy-start(f32[4,32,4]{1,2,0:T(4,128)} %param.11) | copy-start | bytes 6148
  17.1 4.2 %copy-start.1 = (f32[8,4,4,5,5]{0,2,4,3,1:T(4,128)S(1)}, f32[8,4,4,5,5]{0,2,4,3,1:T(4,128)}, u32[]{:S(2)}) copy-start(f32[8,4,4,5,5]{0,2,4,3,1:T(4,128)} %param.12) | copy-start | bytes 38404
  17.8 6.0 %collective-permute-start = (f32[2,4,32,128]{3,2,1,0:T(8,128)S(1)}, f32[2,4,32,128]{3,2,1,0:T(8,128)S(1)}, u32[]{:S(2)}, u32[]{:S(2)}) collective-permute-start(f32[2,4,32,128]{3,2,1,0:T(8,128)S(1)} %get-tuple-element.18), channel_id=1, source_target_pairs={{0,1},{2,3},{1,0},{3,2},{4,5},{6,7},{5,4},{7,6},{8,9},{10,11},{9,8... | collective-permute-start | bytes 393224 | tf_op jit(solution)/shard_map/ppermute | solution.py:593
  19.4 6.8 %collective-permute-start.1 = (f32[2,4,32,128]{3,2,1,0:T(8,128)S(1)}, f32[2,4,32,128]{3,2,1,0:T(8,128)S(1)}, u32[]{:S(2)}, u32[]{:S(2)}) collective-permute-start(f32[2,4,32,128]{3,2,1,0:T(8,128)S(1)} %get-tuple-element.19), channel_id=1, source_target_pairs={{1,2},{2,1},{5,6},{6,5},{9,10},{10,9},{13,14},{14,13},{17,18},{18,... | collective-permute-start | bytes 393224 | tf_op jit(solution)/shard_map/ppermute | solution.py:593
  27.8 5.0 %collective-permute-start.2 = (f32[2,4,32,128]{3,2,1,0:T(8,128)S(1)}, f32[2,4,32,128]{3,2,1,0:T(8,128)S(1)}, u32[]{:S(2)}, u32[]{:S(2)}) collective-permute-start(f32[2,4,32,128]{3,2,1,0:T(8,128)S(1)} %get-tuple-element.25), channel_id=1, source_target_pairs={{0,1},{2,3},{1,0},{3,2},{4,5},{6,7},{5,4},{7,6},{8,9},{10,11},{9,8... | collective-permute-start | bytes 393224 | tf_op jit(solution)/shard_map/ppermute | solution.py:593
  27.9 6.9 %collective-permute-start.3 = (f32[2,4,32,128]{3,2,1,0:T(8,128)S(1)}, f32[2,4,32,128]{3,2,1,0:T(8,128)S(1)}, u32[]{:S(2)}, u32[]{:S(2)}) collective-permute-start(f32[2,4,32,128]{3,2,1,0:T(8,128)S(1)} %get-tuple-element.26), channel_id=1, source_target_pairs={{1,2},{2,1},{5,6},{6,5},{9,10},{10,9},{13,14},{14,13},{17,18},{18,... | collective-permute-start | bytes 393224 | tf_op jit(solution)/shard_map/ppermute | solution.py:593
where the time goes:
time: 50.5 us; the launch traced here: 50 us
  blocking collectives  24 us (48%)
  Pallas kernels  10.1 us (20%)
  waiting for transfers between devices  5.68 us (11%)
  starting transfers between devices  5.61 us (11%)
  local copies, waits for them, and re-layouts  3.88 us (8%)
  between operations  0.76 us (2%)
    all_to_all x1, blocking collectives, by_group(): results = lax.all_to_all(results, 'depth', 0, 0)  12.2 us
    all_to_all x1, blocking collectives, by_group(): chunks = lax.all_to_all(chunks, 'depth', 0, 0)  11.9 us
    pallas_call x7, Pallas kernels, call(): pl.pallas_call(kernel, out_shape=outs, in_specs=specs, out_specs=jax.tree...  10.1 us
    ppermute x2, waiting for transfers between devices, swapped(): lax.ppermute(odd, 'inline', pairs(1))  4.38 us
    ppermute x2, starting transfers between devices, swapped(): lax.ppermute(odd, 'inline', pairs(1))  3.9 us
    unnamed x20, local copies, waits for them, and re-layouts  3.88 us
    ppermute x2, starting transfers between devices, swapped(): lax.ppermute(even, 'inline', pairs(0))  1.71 us
    ppermute x2, waiting for transfers between devices, swapped(): lax.ppermute(even, 'inline', pairs(0))  1.3 us
  transfers between devices with their start and end apart: 4, of which 3 were waited for; matrix products, arithmetic and copies ran while one was open for 0% of the time, Pallas kernels for 8%

commit v1 on v0

--- a/solution.py
+++ b/solution.py
@@ -225,21 +225,26 @@
     return jax.ShapeDtypeStruct(shape, jnp.float32)
 
 
-def in_vmem(count):
-    return [pl.BlockSpec(memory_space=pltpu.VMEM) for _ in range(count)]
-
-
 def lane_index(shape):
     return lax.broadcasted_iota(jnp.int32, shape, len(shape) - 1)
 
 
-def pack_kernel(
-    order, control, coeffs, values, normals, cells, weights, ocells, oweights, out, by_channel
-):
+def pack_kernel(*refs):
+    sources, out, by_channel, arrived, held = refs[:9], refs[9], refs[10], refs[11], refs[12:]
+    copies = [
+        pltpu.make_async_copy(source, target, arrived.at[k])
+        for k, (source, target) in enumerate(zip(sources, held))
+    ]
+    for copy in copies:
+        copy.start()
+    order, coeffs, values, normals, cells, weights, ocells, oweights, control = held
+
     def flat_cell(ref):
         z, y, x = (ref[k, 0] for k in range(3))
         return (((y & 3) * 4 + (z & 3)) * 128 + x).astype(jnp.float32)
 
+    for copy in copies[:-1]:
+        copy.wait()
     flat, oflat = flat_cell(cells), flat_cell(ocells)
     weight = weights[0]
     misc = jnp.concatenate(
@@ -255,10 +260,6 @@
     for slot in range(32):
         group, c = divmod(slot, 4)
         channel = order[slot]
-        plane = control[channel]
-        for z in range(4):
-            row = z * 16 + c * 4
-            out[group, row : row + 4, :] = plane[z * 4 : z * 4 + 4]
         row = AT_VALUES + 2 * c
         out[group, row : row + 2, :] = values[pl.ds(channel * 2, 2), :]
         for k in range(3):
@@ -266,6 +267,13 @@
             out[group, row : row + 1, :] = normals[pl.ds(k * 32 + channel, 1), :]
         row = AT_COEFFS + c
         out[group, row : row + 1, :16] = by_channel[pl.ds(channel, 1), :]
+    copies[-1].wait()
+    for slot in range(32):
+        group, c = divmod(slot, 4)
+        plane = control[order[slot]]
+        for z in range(4):
+            row = z * 16 + c * 4
+            out[group, row : row + 4, :] = plane[z * 4 : z * 4 + 4]
 
 
 def coefficient(expanded, lag, z):
@@ -300,19 +308,11 @@
         emit(t, total)
 
 
-COEFF_SCRATCH = [
-    pltpu.VMEM((8, 16, 128), jnp.float32),
-    pltpu.VMEM((32, 4, 16, 128), jnp.float32),
-    pltpu.VMEM((32, 16, 128), jnp.float32),
-    pltpu.VMEM((32, 16, 128), jnp.float32),
-]
-
-
 def depth_rows(chunks, z):
     return chunks[z // 4, (z % 4) * 16 : (z % 4) * 16 + 16, :]
 
 
-def smooth_kernel(chunks, smoothed, even, odd, expanded, table, scale, root, first, rows):
+def smooth_kernel(chunks, smoothed, even, odd, table, scale, root, expanded, first, rows):
     expand_coeffs(chunks, expanded, table, scale, root)
 
     def keep_first(z, value):
@@ -515,7 +515,7 @@
         odd[y] = forcing[2 * parity + y]
 
 
-def spread_kernel(forcing, table, partial):
+def spread_kernel(forcing, table, potential, partial, out, rows):
     def write(y, o, depths, value):
         partial[y, o, depths, :] = value
 
@@ -527,18 +527,16 @@
         True,
         write,
     )
-
-
-def gradient_kernel(
-    chunks, partial, even_in, odd_in, taps, potential, out, expanded, table, scale, root, first, rows
-):
-    expand_coeffs(chunks, expanded, table, scale, root)
     for y in range(4):
         for c in range(4):
             rows[pl.ds((c * 4 + y) * 32, 32), :] = potential[y, c]
     for z in range(32):
         out[z // 4, (z % 4) * 16 : (z % 4) * 16 + 16, :] = rows[pl.ds(z, 16, stride=32), :]
 
+
+def gradient_kernel(
+    results, chunks, partial, even_in, odd_in, taps, table, scale, root, out, first, rows
+):
     def write(y, o, depths, value):
         rows[pl.ds(pl.multiple_of((o * 4 + y) * 32 + depths.start, 8), 8), :] = value
 
@@ -572,15 +570,16 @@
     )
 
 
-def unpack_kernel(order, chunks, potential, gradient):
-    for slot in range(32):
-        group, c = divmod(slot, 4)
-        channel = order[slot]
-        for out, base in ((potential, 0), (gradient, 64)):
-            pieces = [
-                chunks[group, base + z * 16 + c * 4 : base + z * 16 + c * 4 + 4, :] for z in range(4)
-            ]
-            out[channel] = jnp.concatenate(pieces, axis=0)
+def unpack_kernel(order, chunks, potential, gradient, planes, sent):
+    for half, out in enumerate((potential, gradient)):
+        for slot in range(32):
+            group, c = divmod(slot, 4)
+            rows = [64 * half + z * 16 + c * 4 for z in range(4)]
+            pieces = [chunks[group, row : row + 4, :] for row in rows]
+            planes[half, slot] = jnp.concatenate(pieces, axis=0)
+            pltpu.make_async_copy(planes.at[half, slot], out.at[order[slot]], sent.at[half]).start()
+    for half, out in enumerate((potential, gradient)):
+        pltpu.make_async_copy(planes.at[half], out, sent.at[half]).wait()
 
 
 def swapped(even, odd):
@@ -606,44 +605,52 @@
     orient_weights,
 ):
     params = pltpu.CompilerParams(vmem_limit_bytes=48 << 20)
-    in_smem = pl.BlockSpec(memory_space=pltpu.SMEM)
-
-    def call(kernel, outs, operands, scratch=(), first=None):
-        specs = in_vmem(len(operands))
-        if first is not None:
-            specs[0] = first
+    in_vmem, in_smem, in_hbm = (
+        pl.BlockSpec(memory_space=space) for space in (pltpu.VMEM, pltpu.SMEM, pltpu.HBM)
+    )
+
+    def call(kernel, outs, operands, scratch=(), ins=None, to=in_vmem, aliases=None):
         return pl.pallas_call(
             kernel,
             out_shape=outs,
-            in_specs=specs,
-            out_specs=jax.tree.map(lambda _: pl.BlockSpec(memory_space=pltpu.VMEM), outs),
+            in_specs=ins or [in_vmem] * len(operands),
+            out_specs=jax.tree.map(lambda _: to, outs),
             scratch_shapes=list(scratch),
+            input_output_aliases=aliases or {},
             compiler_params=params,
         )(*operands)
 
+    sources = (
+        channel_order,
+        jnp.transpose(filter_coeffs, (0, 2, 1)).reshape(16, 32),
+        point_values.reshape(64, 128),
+        orient_normals.reshape(96, 128),
+        point_cells,
+        point_weights,
+        orient_cells,
+        orient_weights,
+        control.reshape(32, 16, 128),
+    )
+    sources = tuple(pltpu.with_memory_space_constraint(x, pltpu.HBM) for x in sources)
+    held = [pltpu.VMEM(source.shape, source.dtype) for source in sources]
+    held[0] = pltpu.SMEM((32,), jnp.int32)
     chunks = call(
         pack_kernel,
         f32(8, CHUNK, 128),
-        (
-            channel_order,
-            control.reshape(32, 16, 128),
-            jnp.transpose(filter_coeffs, (0, 2, 1)).reshape(16, 32),
-            point_values.reshape(64, 128),
-            orient_normals.reshape(96, 128),
-            point_cells,
-            point_weights,
-            orient_cells,
-            orient_weights,
-        ),
-        (pltpu.VMEM((128, 16), jnp.float32),),
-        in_smem,
+        sources,
+        [pltpu.VMEM((128, 16), jnp.float32), pltpu.SemaphoreType.DMA((9,))] + held,
+        [in_hbm] * 9,
     )
     chunks = lax.all_to_all(chunks, "depth", 0, 0)
     field, edge, plane = f32(4, 4, 32, 128), f32(2, 4, 32, 128), f32(4, 32, 128)
+    by_depth = f32(32, 16, 128)
     rows = pltpu.VMEM((512, 128), jnp.float32)
     first = pltpu.VMEM((32, 16, 128), jnp.float32)
-    smoothed, even, odd = call(
-        smooth_kernel, (field, edge, edge), (chunks,), COEFF_SCRATCH + [first, rows]
+    smoothed, even, odd, table, scale, root = call(
+        smooth_kernel,
+        (field, edge, edge, f32(32, 4, 16, 128), by_depth, by_depth),
+        (chunks,),
+        [pltpu.VMEM((8, 16, 128), jnp.float32), first, rows],
     )
     even, odd = swapped(even, odd)
     kernels = jnp.transpose(conv_kernels, (1, 3, 4, 2, 0)).reshape(400, 8)
@@ -656,17 +663,24 @@
         (partial, even, odd, taps, constant, weight, oweight),
     )
     even, odd = swapped(even, odd)
-    partial = call(spread_kernel, field, (forcing, taps))
+    partial, results = call(
+        spread_kernel, (field, f32(8, 128, 128)), (forcing, taps, potential), [rows]
+    )
     results = call(
         gradient_kernel,
         f32(8, 128, 128),
-        (chunks, partial, even, odd, taps, potential),
-        COEFF_SCRATCH + [first, rows],
+        (results, chunks, partial, even, odd, taps, table, scale, root),
+        [first, rows],
+        aliases={0: 0},
     )
     results = lax.all_to_all(results, "depth", 0, 0)
-    block = f32(32, 16, 128)
     potential, gradient = call(
-        unpack_kernel, (block, block), (channel_order, results), (), in_smem
+        unpack_kernel,
+        (by_depth, by_depth),
+        (channel_order, results),
+        [pltpu.VMEM((2, 32, 16, 128), jnp.float32), pltpu.SemaphoreType.DMA((2,))],
+        [in_smem, in_vmem],
+        in_hbm,
     )
     return potential.reshape(control.shape), gradient.reshape(control.shape)
 

time: 50.5 us -> 46.3 us (0.917)
  local copies, waits for them, and re-layouts: 3.88 us -> 0.01 us
    unnamed x20 -> x4, local copies, waits for them, and re-layouts: 3.88 us -> 0.01 us
  transfers between devices with their start and end apart: 4 -> 4, of which waited for: 3 -> 3; matrix products, arithmetic and copies ran while one was open for 0% -> 0% of each run, Pallas kernels for 8% -> 9%
where the time goes in v1:
time: 46.3 us; the launch traced here: 46.1 us
  blocking collectives  24 us (52%)
  Pallas kernels  10.2 us (22%)
  starting transfers between devices  5.61 us (12%)
  waiting for transfers between devices  5.5 us (12%)
  between operations  0.73 us (2%)
    all_to_all x1, blocking collectives, by_group(): results = lax.all_to_all(results, 'depth', 0, 0)  12.2 us
    all_to_all x1, blocking collectives, by_group(): chunks = lax.all_to_all(chunks, 'depth', 0, 0)  11.9 us
    pallas_call x7, Pallas kernels, call(): pl.pallas_call(kernel, out_shape=outs, in_specs=ins or [in_vmem] * len(op...  10.2 us
    ppermute x2, waiting for transfers between devices, swapped(): lax.ppermute(odd, 'inline', pairs(1))  4.38 us
    ppermute x2, starting transfers between devices, swapped(): lax.ppermute(odd, 'inline', pairs(1))  3.9 us
    ppermute x2, starting transfers between devices, swapped(): lax.ppermute(even, 'inline', pairs(0))  1.71 us
    ppermute x2, waiting for transfers between devices, swapped(): lax.ppermute(even, 'inline', pairs(0))  1.13 us
  transfers between devices with their start and end apart: 4, of which 3 were waited for; matrix products, arithmetic and copies ran while one was open for 0% of the time, Pallas kernels for 9%

profile of v1, /device:TPU:16, one launch (start us, length us, event | category | flops | bytes accessed | tf_op | source)
XLA Modules:
  0.0 46.1 jit_solution(2666414947614983192)
XLA Ops:
  0.6 1.2 %shard_map.113 = f32[8,96,128]{2,1,0:T(8,128)S(1)} custom-call(s32[32]{0:T(128)} %order.1, f32[16,32]{1,0:T(8,128)} %bitcast.15, f32[64,128]{1,0:T(8,128)} %bitcast.14, f32[96,128]{1,0:T(8,128)} %bitcast.13, s32[3,1,1,256]{3,2,1,0:T(1,128)} %refs_4_.1, f32[1,1,256]{2,1,0:T(1,128)} %refs_5_.1, s32[3,1,1,128]{3,2,1,0:T(1,128)} %refs_6_.1, ...), custom_call_target="tpu_custom_call" | custom-call | tf_op jit(solution)/shard_map/pallas_call | solution.py:613
  1.8 11.9 %all_to_all.10.chunks = f32[8,96,128]{2,1,0:T(8,128)S(1)} all-to-all(f32[8,96,128]{2,1,0:T(8,128)S(1)} %shard_map.113), channel_id=1, replica_groups=mesh['depth'=8,'inline'=4] {'depth'}, dimensions={0} | all-to-all | bytes 786432 | tf_op jit(solution)/shard_map/all_to_all | solution.py:644
  13.7 0.0 copy-start
  13.7 0.7 %shard_map.114 = (f32[4,4,32,128]{3,2,1,0:T(8,128)S(1)}, f32[2,4,32,128]{3,2,1,0:T(8,128)S(1)}, f32[2,4,32,128]{3,2,1,0:T(8,128)S(1)}, f32[32,4,16,128]{3,2,1,0:...) custom-call(f32[8,96,128]{2,1,0:T(8,128)S(1)} %all_to_all.10.chunks), custom_call_target="tpu_custom_call" | custom-call | tf_op jit(solution)/shard_map/pallas_call | solution.py:613
  14.4 1.6 %collective-permute-start = (f32[2,4,32,128]{3,2,1,0:T(8,128)S(1)}, f32[2,4,32,128]{3,2,1,0:T(8,128)S(1)}, u32[]{:S(2)}, u32[]{:S(2)}) collective-permute-start(f32[2,4,32,128]{3,2,1,0:T(8,128)S(1)} %get-tuple-element.23), channel_id=1, source_target_pairs={{0,1},{2,3},{1,0},{3,2},{4,5},{6,7},{5,4},{7,6},{8,9},{10,11},{9,8... | collective-permute-start | bytes 393224 | tf_op jit(solution)/shard_map/ppermute | solution.py:592
  16.0 1.9 %collective-permute-start.1 = (f32[2,4,32,128]{3,2,1,0:T(8,128)S(1)}, f32[2,4,32,128]{3,2,1,0:T(8,128)S(1)}, u32[]{:S(2)}, u32[]{:S(2)}) collective-permute-start(f32[2,4,32,128]{3,2,1,0:T(8,128)S(1)} %get-tuple-element.24), channel_id=1, source_target_pairs={{1,2},{2,1},{5,6},{6,5},{9,10},{10,9},{13,14},{14,13},{17,18},{18,... | collective-permute-start | bytes 393224 | tf_op jit(solution)/shard_map/ppermute | solution.py:592
  17.9 0.0 copy-done
  18.0 2.4 %shard_map.115 = (f32[4,4,32,128]{3,2,1,0:T(8,128)S(1)}, f32[4,4,32,128]{3,2,1,0:T(8,128)S(1)}, f32[4,32,128]{2,1,0:T(8,128)S(1)}, f32[4,32,128]{2,1,0:T(8,128)S(1)}, f32[400,128]{1,0:T(8,128)S(1)}) custom-call(f32[8,96,128]{2,1,0:T(8,128)S(1)} %all_to_all.10.chunks, f32[4,4,32,128]{3,2,1,0:T(8,128)S(1)} %get-tuple-element.21.smoothed, f32[400,8]{1,0:T(8,128)S(1)} %bitcast.11), custom_call_target="tpu_custom_call" | custom-call | tf_op jit(solution)/shard_map/pallas_call | solution.py:613
  20.4 0.0 collective-permute-done.even_in
  20.4 2.5 %collective-permute-done.1.odd_in = f32[2,4,32,128]{3,2,1,0:T(8,128)S(1)} collective-permute-done((f32[2,4,32,128]{3,2,1,0:T(8,128)S(1)}, f32[2,4,32,128]{3,2,1,0:T(8,128)S(1)}, u32[]{:S(2)}, u32[]{:S(2)}) %collective-permute-start.1) | collective-permute-done | bytes 131104 | tf_op jit(solution)/shard_map/ppermute | solution.py:592
  22.9 1.5 %shard_map.116 = (f32[4,4,32,128]{3,2,1,0:T(8,128)S(1)}, f32[4,4,32,128]{3,2,1,0:T(8,128)S(1)}, f32[2,4,32,128]{3,2,1,0:T(8,128)S(1)}, f32[2,4,32,128]{3,2,1,0:T(8,128)S(1)}) custom-call(f32[4,4,32,128]{3,2,1,0:T(8,128)S(1)} %get-tuple-element.22.partial, f32[2,4,32,128]{3,2,1,0:T(8,128)S(1)} %collective-permute-done.even_in, ...), custom_call_target="tpu_custom_call" | custom-call | tf_op jit(solution)/shard_map/pallas_call | solution.py:613
  24.4 0.1 collective-permute-start.2
  24.5 2.0 %collective-permute-start.3 = (f32[2,4,32,128]{3,2,1,0:T(8,128)S(1)}, f32[2,4,32,128]{3,2,1,0:T(8,128)S(1)}, u32[]{:S(2)}, u32[]{:S(2)}) collective-permute-start(f32[2,4,32,128]{3,2,1,0:T(8,128)S(1)} %get-tuple-element.34), channel_id=1, source_target_pairs={{1,2},{2,1},{5,6},{6,5},{9,10},{10,9},{13,14},{14,13},{17,18},{18,... | collective-permute-start | bytes 393224 | tf_op jit(solution)/shard_map/ppermute | solution.py:592
  26.5 1.8 %shard_map.117 = (f32[4,4,32,128]{3,2,1,0:T(8,128)S(1)}, f32[8,128,128]{2,1,0:T(8,128)S(1)}) custom-call(f32[4,4,32,128]{3,2,1,0:T(8,128)S(1)} %get-tuple-element.29.forcing, f32[400,128]{1,0:T(8,128)S(1)} %get-tuple-element.25.table.taps, f32[4,4,32,128]{3,2,1,0:T(8,128)S(1)} %get-tuple-element.30.potential), custom_call_target="tpu_custom_call" | custom-call | tf_op jit(solution)/shard_map/pallas_call | solution.py:613
  28.3 1.1 %collective-permute-done.2.even_in = f32[2,4,32,128]{3,2,1,0:T(8,128)S(1)} collective-permute-done((f32[2,4,32,128]{3,2,1,0:T(8,128)S(1)}, f32[2,4,32,128]{3,2,1,0:T(8,128)S(1)}, u32[]{:S(2)}, u32[]{:S(2)}) %collective-permute-start.2) | collective-permute-done | bytes 131104 | tf_op jit(solution)/shard_map/ppermute | solution.py:592
  29.4 1.9 %collective-permute-done.3.odd_in = f32[2,4,32,128]{3,2,1,0:T(8,128)S(1)} collective-permute-done((f32[2,4,32,128]{3,2,1,0:T(8,128)S(1)}, f32[2,4,32,128]{3,2,1,0:T(8,128)S(1)}, u32[]{:S(2)}, u32[]{:S(2)}) %collective-permute-start.3) | collective-permute-done | bytes 131104 | tf_op jit(solution)/shard_map/ppermute | solution.py:592
  31.3 1.2 %shard_map.118 = f32[8,128,128]{2,1,0:T(8,128)S(1)} custom-call(f32[8,128,128]{2,1,0:T(8,128)S(1)} %get-tuple-element.31.results, f32[8,96,128]{2,1,0:T(8,128)S(1)} %all_to_all.10.chunks, f32[4,4,32,128]{3,2,1,0:T(8,128)S(1)} %get-tuple-element.32.partial, f32[2,4,32,128]{3,2,1,0:T(8,128)S(1)} %collective-permute-done.2.even_in, ...), custom_call_target="tpu_custom_call", output_to_operand_aliasing={{}: (0, {})} | custom-call | tf_op jit(solution)/shard_map/pallas_call | solution.py:613
  32.5 0.0 copy-start.1
  32.5 12.2 %all_to_all.11.chunks = f32[8,128,128]{2,1,0:T(8,128)S(1)} all-to-all(f32[8,128,128]{2,1,0:T(8,128)S(1)} %shard_map.118), channel_id=1, replica_groups=mesh['depth'=8,'inline'=4] {'depth'}, dimensions={0} | all-to-all | bytes 1048576 | tf_op jit(solution)/shard_map/all_to_all | solution.py:676
  44.7 0.0 copy-done.1
  44.7 1.4 %shard_map.119 = (f32[32,16,128]{2,1,0:T(8,128)}, f32[32,16,128]{2,1,0:T(8,128)}) custom-call(s32[32]{0:T(128)S(1)} %copy-done.1, f32[8,128,128]{2,1,0:T(8,128)S(1)} %all_to_all.11.chunks), custom_call_target="tpu_custom_call" | custom-call | tf_op jit(solution)/shard_map/pallas_call | solution.py:613
Async XLA Ops:
  13.7 4.2 %copy-start = (f32[8,4,4,5,5]{0,2,4,3,1:T(4,128)S(1)}, f32[8,4,4,5,5]{0,2,4,3,1:T(4,128)}, u32[]{:S(2)}) copy-start(f32[8,4,4,5,5]{0,2,4,3,1:T(4,128)} %param.12) | copy-start | bytes 38404
  14.4 6.0 %collective-permute-start = (f32[2,4,32,128]{3,2,1,0:T(8,128)S(1)}, f32[2,4,32,128]{3,2,1,0:T(8,128)S(1)}, u32[]{:S(2)}, u32[]{:S(2)}) collective-permute-start(f32[2,4,32,128]{3,2,1,0:T(8,128)S(1)} %get-tuple-element.23), channel_id=1, source_target_pairs={{0,1},{2,3},{1,0},{3,2},{4,5},{6,7},{5,4},{7,6},{8,9},{10,11},{9,8... | collective-permute-start | bytes 393224 | tf_op jit(solution)/shard_map/ppermute | solution.py:592
  16.0 6.8 %collective-permute-start.1 = (f32[2,4,32,128]{3,2,1,0:T(8,128)S(1)}, f32[2,4,32,128]{3,2,1,0:T(8,128)S(1)}, u32[]{:S(2)}, u32[]{:S(2)}) collective-permute-start(f32[2,4,32,128]{3,2,1,0:T(8,128)S(1)} %get-tuple-element.24), channel_id=1, source_target_pairs={{1,2},{2,1},{5,6},{6,5},{9,10},{10,9},{13,14},{14,13},{17,18},{18,... | collective-permute-start | bytes 393224 | tf_op jit(solution)/shard_map/ppermute | solution.py:592
  24.4 5.0 %collective-permute-start.2 = (f32[2,4,32,128]{3,2,1,0:T(8,128)S(1)}, f32[2,4,32,128]{3,2,1,0:T(8,128)S(1)}, u32[]{:S(2)}, u32[]{:S(2)}) collective-permute-start(f32[2,4,32,128]{3,2,1,0:T(8,128)S(1)} %get-tuple-element.33), channel_id=1, source_target_pairs={{0,1},{2,3},{1,0},{3,2},{4,5},{6,7},{5,4},{7,6},{8,9},{10,11},{9,8... | collective-permute-start | bytes 393224 | tf_op jit(solution)/shard_map/ppermute | solution.py:592
  24.5 6.9 %collective-permute-start.3 = (f32[2,4,32,128]{3,2,1,0:T(8,128)S(1)}, f32[2,4,32,128]{3,2,1,0:T(8,128)S(1)}, u32[]{:S(2)}, u32[]{:S(2)}) collective-permute-start(f32[2,4,32,128]{3,2,1,0:T(8,128)S(1)} %get-tuple-element.34), channel_id=1, source_target_pairs={{1,2},{2,1},{5,6},{6,5},{9,10},{10,9},{13,14},{14,13},{17,18},{18,... | collective-permute-start | bytes 393224 | tf_op jit(solution)/shard_map/ppermute | solution.py:592
  32.5 12.2 %copy-start.1 = (s32[32]{0:T(128)S(1)}, s32[32]{0:T(128)}, u32[]{:S(2)}) copy-start(s32[32]{0:T(128)} %order.1) | copy-start | bytes 388

commit v2 on v1

--- a/solution.py
+++ b/solution.py
@@ -386,13 +386,15 @@
 
 
 def halo_reader(even, odd):
-    parity = lax.axis_index("inline") % 2
+    slab, last = lax.axis_index("inline"), lax.axis_size("inline") - 1
+    parity = slab % 2
 
     def read(row, c, depths):
         y = row + 2 if row < 0 else row - 4
         through_even, through_odd = even[y, c, depths, :], odd[y, c, depths, :]
         below = parity == 1 if row < 0 else parity == 0
-        return jnp.where(below, through_even, through_odd)
+        outside = slab == 0 if row < 0 else slab == last
+        return jnp.where(outside, 0.0, jnp.where(below, through_even, through_odd))
 
     return read
 
@@ -583,13 +585,18 @@
 
 
 def swapped(even, odd):
-    count = lax.axis_size("inline")
-
-    def pairs(first):
-        below = [(i, i + 1) for i in range(first, count - 1, 2)]
-        return below + [(j, i) for i, j in below]
-
-    return lax.ppermute(even, "inline", pairs(0)), lax.ppermute(odd, "inline", pairs(1))
+    depths, slabs = lax.axis_size("depth"), lax.axis_size("inline")
+
+    def swap(value, first):
+        pairs = []
+        for d in range(depths):
+            for i in range(slabs):
+                other = i + 1 if (i - first) % 2 == 0 else i - 1
+                to = (d, other) if 0 <= other < slabs else (d ^ 1, i)
+                pairs.append((d * slabs + i, to[0] * slabs + to[1]))
+        return lax.ppermute(value, ("depth", "inline"), pairs)
+
+    return swap(even, 0), swap(odd, 1)
 
 
 def by_group(

time: 46.3 us -> 43.1 us (0.931)
  the two profiles are of different devices: /device:TPU:16 before, /device:TPU:0 now
where the time goes in v2:
time: 43.1 us; the launch traced here: 42.9 us
  blocking collectives  25.5 us (59%)
  Pallas kernels  10.2 us (24%)
  starting transfers between devices  4.41 us (10%)
  waiting for transfers between devices  2.14 us (5%)
  between operations  0.69 us (2%)
    all_to_all x1, blocking collectives, by_group(): chunks = lax.all_to_all(chunks, 'depth', 0, 0)  13.3 us
    all_to_all x1, blocking collectives, by_group(): results = lax.all_to_all(results, 'depth', 0, 0)  12.2 us
    pallas_call x7, Pallas kernels, call(): pl.pallas_call(kernel, out_shape=outs, in_specs=ins or [in_vmem] * len(op...  10.2 us
    ppermute x4, starting transfers between devices, swap(): return lax.ppermute(value, ('depth', 'inline'), pairs)  4.41 us
    ppermute x4, waiting for transfers between devices, swap(): return lax.ppermute(value, ('depth', 'inline'), pairs)  2.14 us
  transfers between devices with their start and end apart: 4, of which 2 were waited for; matrix products, arithmetic and copies ran while one was open for 0% of the time, Pallas kernels for 10%

profile of v2, /device:TPU:0, one launch (start us, length us, event | category | flops | bytes accessed | tf_op | source)
XLA Modules:
  0.0 42.9 jit_solution(6014944913093351655)
XLA Ops:
  0.6 1.2 %shard_map.113 = f32[8,96,128]{2,1,0:T(8,128)S(1)} custom-call(s32[32]{0:T(128)} %order.1, f32[16,32]{1,0:T(8,128)} %bitcast.15, f32[64,128]{1,0:T(8,128)} %bitcast.14, f32[96,128]{1,0:T(8,128)} %bitcast.13, s32[3,1,1,256]{3,2,1,0:T(1,128)} %refs_4_.1, f32[1,1,256]{2,1,0:T(1,128)} %refs_5_.1, s32[3,1,1,128]{3,2,1,0:T(1,128)} %refs_6_.1, ...), custom_call_target="tpu_custom_call" | custom-call | tf_op jit(solution)/shard_map/pallas_call | solution.py:620
  1.8 13.3 %all_to_all.10.chunks = f32[8,96,128]{2,1,0:T(8,128)S(1)} all-to-all(f32[8,96,128]{2,1,0:T(8,128)S(1)} %shard_map.113), channel_id=1, replica_groups=mesh['depth'=8,'inline'=4] {'depth'}, dimensions={0} | all-to-all | bytes 786432 | tf_op jit(solution)/shard_map/all_to_all | solution.py:651
  15.1 0.0 copy-start
  15.1 0.7 %shard_map.114 = (f32[4,4,32,128]{3,2,1,0:T(8,128)S(1)}, f32[2,4,32,128]{3,2,1,0:T(8,128)S(1)}, f32[2,4,32,128]{3,2,1,0:T(8,128)S(1)}, f32[32,4,16,128]{3,2,1,0:...) custom-call(f32[8,96,128]{2,1,0:T(8,128)S(1)} %all_to_all.10.chunks), custom_call_target="tpu_custom_call" | custom-call | tf_op jit(solution)/shard_map/pallas_call | solution.py:620
  15.8 1.6 %collective-permute-start = (f32[2,4,32,128]{3,2,1,0:T(8,128)S(1)}, f32[2,4,32,128]{3,2,1,0:T(8,128)S(1)}, u32[]{:S(2)}, u32[]{:S(2)}) collective-permute-start(f32[2,4,32,128]{3,2,1,0:T(8,128)S(1)} %get-tuple-element.23), channel_id=1, source_target_pairs={{0,1},{1,0},{2,3},{3,2},{4,5},{5,4},{6,7},{7,6},{8,9},{9,8},{10,11... | collective-permute-start | bytes 393224 | tf_op jit(solution)/shard_map/ppermute | solution.py:597
  17.5 0.0 collective-permute-start.1
  17.5 0.0 copy-done
  17.5 2.4 %shard_map.115 = (f32[4,4,32,128]{3,2,1,0:T(8,128)S(1)}, f32[4,4,32,128]{3,2,1,0:T(8,128)S(1)}, f32[4,32,128]{2,1,0:T(8,128)S(1)}, f32[4,32,128]{2,1,0:T(8,128)S(1)}, f32[400,128]{1,0:T(8,128)S(1)}) custom-call(f32[8,96,128]{2,1,0:T(8,128)S(1)} %all_to_all.10.chunks, f32[4,4,32,128]{3,2,1,0:T(8,128)S(1)} %get-tuple-element.21.smoothed, f32[400,8]{1,0:T(8,128)S(1)} %bitcast.11), custom_call_target="tpu_custom_call" | custom-call | tf_op jit(solution)/shard_map/pallas_call | solution.py:620
  19.9 1.0 %collective-permute-done.even_in = f32[2,4,32,128]{3,2,1,0:T(8,128)S(1)} collective-permute-done((f32[2,4,32,128]{3,2,1,0:T(8,128)S(1)}, f32[2,4,32,128]{3,2,1,0:T(8,128)S(1)}, u32[]{:S(2)}, u32[]{:S(2)}) %collective-permute-start) | collective-permute-done | bytes 131104 | tf_op jit(solution)/shard_map/ppermute | solution.py:597
  20.9 0.0 collective-permute-done.1.odd_in
  20.9 1.5 %shard_map.116 = (f32[4,4,32,128]{3,2,1,0:T(8,128)S(1)}, f32[4,4,32,128]{3,2,1,0:T(8,128)S(1)}, f32[2,4,32,128]{3,2,1,0:T(8,128)S(1)}, f32[2,4,32,128]{3,2,1,0:T(8,128)S(1)}) custom-call(f32[4,4,32,128]{3,2,1,0:T(8,128)S(1)} %get-tuple-element.22.partial, f32[2,4,32,128]{3,2,1,0:T(8,128)S(1)} %collective-permute-done.even_in, ...), custom_call_target="tpu_custom_call" | custom-call | tf_op jit(solution)/shard_map/pallas_call | solution.py:620
  22.5 2.8 %collective-permute-start.2 = (f32[2,4,32,128]{3,2,1,0:T(8,128)S(1)}, f32[2,4,32,128]{3,2,1,0:T(8,128)S(1)}, u32[]{:S(2)}, u32[]{:S(2)}) collective-permute-start(f32[2,4,32,128]{3,2,1,0:T(8,128)S(1)} %get-tuple-element.33), channel_id=1, source_target_pairs={{0,1},{1,0},{2,3},{3,2},{4,5},{5,4},{6,7},{7,6},{8,9},{9,8},{10,11... | collective-permute-start | bytes 393224 | tf_op jit(solution)/shard_map/ppermute | solution.py:597
  25.2 0.0 collective-permute-start.3
  25.2 1.8 %shard_map.117 = (f32[4,4,32,128]{3,2,1,0:T(8,128)S(1)}, f32[8,128,128]{2,1,0:T(8,128)S(1)}) custom-call(f32[4,4,32,128]{3,2,1,0:T(8,128)S(1)} %get-tuple-element.29.forcing, f32[400,128]{1,0:T(8,128)S(1)} %get-tuple-element.25.table.taps, f32[4,4,32,128]{3,2,1,0:T(8,128)S(1)} %get-tuple-element.30.potential), custom_call_target="tpu_custom_call" | custom-call | tf_op jit(solution)/shard_map/pallas_call | solution.py:620
  27.1 1.1 %collective-permute-done.2.even_in = f32[2,4,32,128]{3,2,1,0:T(8,128)S(1)} collective-permute-done((f32[2,4,32,128]{3,2,1,0:T(8,128)S(1)}, f32[2,4,32,128]{3,2,1,0:T(8,128)S(1)}, u32[]{:S(2)}, u32[]{:S(2)}) %collective-permute-start.2) | collective-permute-done | bytes 131104 | tf_op jit(solution)/shard_map/ppermute | solution.py:597
  28.2 0.0 collective-permute-done.3.odd_in
  28.2 1.1 %shard_map.118 = f32[8,128,128]{2,1,0:T(8,128)S(1)} custom-call(f32[8,128,128]{2,1,0:T(8,128)S(1)} %get-tuple-element.31.results, f32[8,96,128]{2,1,0:T(8,128)S(1)} %all_to_all.10.chunks, f32[4,4,32,128]{3,2,1,0:T(8,128)S(1)} %get-tuple-element.32.partial, f32[2,4,32,128]{3,2,1,0:T(8,128)S(1)} %collective-permute-done.2.even_in, ...), custom_call_target="tpu_custom_call", output_to_operand_aliasing={{}: (0, {})} | custom-call | tf_op jit(solution)/shard_map/pallas_call | solution.py:620
  29.3 0.0 copy-start.1
  29.3 12.2 %all_to_all.11.chunks = f32[8,128,128]{2,1,0:T(8,128)S(1)} all-to-all(f32[8,128,128]{2,1,0:T(8,128)S(1)} %shard_map.118), channel_id=1, replica_groups=mesh['depth'=8,'inline'=4] {'depth'}, dimensions={0} | all-to-all | bytes 1048576 | tf_op jit(solution)/shard_map/all_to_all | solution.py:683
  41.5 0.0 copy-done.1
  41.5 1.4 %shard_map.119 = (f32[32,16,128]{2,1,0:T(8,128)}, f32[32,16,128]{2,1,0:T(8,128)}) custom-call(s32[32]{0:T(128)S(1)} %copy-done.1, f32[8,128,128]{2,1,0:T(8,128)S(1)} %all_to_all.11.chunks), custom_call_target="tpu_custom_call" | custom-call | tf_op jit(solution)/shard_map/pallas_call | solution.py:620
Async XLA Ops:
  15.1 2.3 %copy-start = (f32[8,4,4,5,5]{0,2,4,3,1:T(4,128)S(1)}, f32[8,4,4,5,5]{0,2,4,3,1:T(4,128)}, u32[]{:S(2)}) copy-start(f32[8,4,4,5,5]{0,2,4,3,1:T(4,128)} %param.12) | copy-start | bytes 38404
  15.8 5.1 %collective-permute-start = (f32[2,4,32,128]{3,2,1,0:T(8,128)S(1)}, f32[2,4,32,128]{3,2,1,0:T(8,128)S(1)}, u32[]{:S(2)}, u32[]{:S(2)}) collective-permute-start(f32[2,4,32,128]{3,2,1,0:T(8,128)S(1)} %get-tuple-element.23), channel_id=1, source_target_pairs={{0,1},{1,0},{2,3},{3,2},{4,5},{5,4},{6,7},{7,6},{8,9},{9,8},{10,11... | collective-permute-start | bytes 393224 | tf_op jit(solution)/shard_map/ppermute | solution.py:597
  17.5 3.5 %collective-permute-start.1 = (f32[2,4,32,128]{3,2,1,0:T(8,128)S(1)}, f32[2,4,32,128]{3,2,1,0:T(8,128)S(1)}, u32[]{:S(2)}, u32[]{:S(2)}) collective-permute-start(f32[2,4,32,128]{3,2,1,0:T(8,128)S(1)} %get-tuple-element.24), channel_id=1, source_target_pairs={{0,4},{1,2},{2,1},{3,7},{4,0},{5,6},{6,5},{7,3},{8,12},{9,10},{10,... | collective-permute-start | bytes 393224 | tf_op jit(solution)/shard_map/ppermute | solution.py:597
  22.5 5.7 %collective-permute-start.2 = (f32[2,4,32,128]{3,2,1,0:T(8,128)S(1)}, f32[2,4,32,128]{3,2,1,0:T(8,128)S(1)}, u32[]{:S(2)}, u32[]{:S(2)}) collective-permute-start(f32[2,4,32,128]{3,2,1,0:T(8,128)S(1)} %get-tuple-element.33), channel_id=1, source_target_pairs={{0,1},{1,0},{2,3},{3,2},{4,5},{5,4},{6,7},{7,6},{8,9},{9,8},{10,11... | collective-permute-start | bytes 393224 | tf_op jit(solution)/shard_map/ppermute | solution.py:597
  25.2 3.0 %collective-permute-start.3 = (f32[2,4,32,128]{3,2,1,0:T(8,128)S(1)}, f32[2,4,32,128]{3,2,1,0:T(8,128)S(1)}, u32[]{:S(2)}, u32[]{:S(2)}) collective-permute-start(f32[2,4,32,128]{3,2,1,0:T(8,128)S(1)} %get-tuple-element.34), channel_id=1, source_target_pairs={{0,4},{1,2},{2,1},{3,7},{4,0},{5,6},{6,5},{7,3},{8,12},{9,10},{10,... | collective-permute-start | bytes 393224 | tf_op jit(solution)/shard_map/ppermute | solution.py:597
  29.3 12.2 %copy-start.1 = (s32[32]{0:T(128)S(1)}, s32[32]{0:T(128)}, u32[]{:S(2)}) copy-start(s32[32]{0:T(128)} %order.1) | copy-start | bytes 388

commit v3 on v2

--- a/solution.py
+++ b/solution.py
@@ -1,3 +1,5 @@
+import functools
+
 import jax
 import jax.numpy as jnp
 from jax import lax
@@ -230,7 +232,8 @@
 
 
 def pack_kernel(*refs):
-    sources, out, by_channel, arrived, held = refs[:9], refs[9], refs[10], refs[11], refs[12:]
+    sources, give, keep, by_channel = refs[:9], refs[9], refs[10:14], refs[14]
+    arrived, held = refs[15], refs[16:]
     copies = [
         pltpu.make_async_copy(source, target, arrived.at[k])
         for k, (source, target) in enumerate(zip(sources, held))
@@ -255,25 +258,35 @@
     by_channel[...] = jnp.transpose(
         jnp.concatenate([coeffs[...], jnp.zeros((16, 96), jnp.float32)], axis=1)
     )
-    for group in range(8):
-        out[group, AT_MISC:CHUNK, :] = misc
-    for slot in range(32):
-        group, c = divmod(slot, 4)
-        channel = order[slot]
-        row = AT_VALUES + 2 * c
-        out[group, row : row + 2, :] = values[pl.ds(channel * 2, 2), :]
-        for k in range(3):
-            row = AT_NORMALS + 4 * k + c
-            out[group, row : row + 1, :] = normals[pl.ds(k * 32 + channel, 1), :]
-        row = AT_COEFFS + c
-        out[group, row : row + 1, :16] = by_channel[pl.ds(channel, 1), :]
+    me = lax.axis_index("depth")
+    places = []
+    for place in range(8):
+        target = give.at[place // 2] if place % 2 else keep[place // 2].at[0]
+        places.append((target, [order[(me ^ place) * 4 + c] for c in range(4)]))
+    for target, channels in places:
+        target[AT_MISC:CHUNK, :] = misc
+        for c, channel in enumerate(channels):
+            row = AT_VALUES + 2 * c
+            target[row : row + 2, :] = values[pl.ds(channel * 2, 2), :]
+            for k in range(3):
+                row = AT_NORMALS + 4 * k + c
+                target[row : row + 1, :] = normals[pl.ds(k * 32 + channel, 1), :]
+            row = AT_COEFFS + c
+            target[row : row + 1, :16] = by_channel[pl.ds(channel, 1), :]
     copies[-1].wait()
-    for slot in range(32):
-        group, c = divmod(slot, 4)
-        plane = control[order[slot]]
-        for z in range(4):
-            row = z * 16 + c * 4
-            out[group, row : row + 4, :] = plane[z * 4 : z * 4 + 4]
+    for target, channels in places:
+        for c, channel in enumerate(channels):
+            plane = control[channel]
+            for z in range(4):
+                row = z * 16 + c * 4
+                target[row : row + 4, :] = plane[z * 4 : z * 4 + 4]
+
+
+def join_kernel(got, *refs):
+    keep, joined = refs[:4], refs[4:]
+    for k in range(4):
+        joined[k][0] = keep[k][0]
+        joined[k][1] = got[k]
 
 
 def coefficient(expanded, lag, z):
@@ -312,7 +325,13 @@
     return chunks[z // 4, (z % 4) * 16 : (z % 4) * 16 + 16, :]
 
 
-def smooth_kernel(chunks, smoothed, even, odd, table, scale, root, expanded, first, rows):
+def smooth_kernel(*refs):
+    parts, refs = refs[:4], refs[4:]
+    chunks, smoothed, even, odd, table, scale, root, expanded, first, rows = refs
+    me = lax.axis_index("depth")
+    for k in range(4):
+        for half in range(2):
+            chunks[me ^ (2 * k + half)] = parts[k][half]
     expand_coeffs(chunks, expanded, table, scale, root)
 
     def keep_first(z, value):
@@ -536,9 +555,16 @@
         out[z // 4, (z % 4) * 16 : (z % 4) * 16 + 16, :] = rows[pl.ds(z, 16, stride=32), :]
 
 
-def gradient_kernel(
-    results, chunks, partial, even_in, odd_in, taps, table, scale, root, out, first, rows
-):
+def gradient_kernel(*refs):
+    chunks, partial, even_in, odd_in, taps, table, scale, root, potential = refs[:9]
+    give, keep, (first, rows, out) = refs[9], refs[10:14], refs[14:]
+    me = lax.axis_index("depth")
+    targets = [
+        give.at[place // 2] if place % 2 else keep[place // 2].at[0] for place in range(8)
+    ]
+    for place, target in enumerate(targets):
+        target[:64, :] = potential[me ^ place]
+
     def write(y, o, depths, value):
         rows[pl.ds(pl.multiple_of((o * 4 + y) * 32 + depths.start, 8), 8), :] = value
 
@@ -555,7 +581,7 @@
         first[z] = scale[z] * value
 
     def keep_out(z, value):
-        row = 64 + (z % 4) * 16
+        row = (z % 4) * 16
         out[z // 4, row : row + 16, :] = depth_rows(chunks, z) + root[z] * value
 
     recurrence(
@@ -570,18 +596,29 @@
         keep_out,
         range(31, -1, -1),
     )
-
-
-def unpack_kernel(order, chunks, potential, gradient, planes, sent):
+    for place, target in enumerate(targets):
+        target[64:, :] = out[me ^ place]
+
+
+def unpack_kernel(first, count, order, *refs):
+    parts, (potential, gradient, planes, sent) = refs[:count], refs[-4:]
+    me = lax.axis_index("depth")
     for half, out in enumerate((potential, gradient)):
-        for slot in range(32):
-            group, c = divmod(slot, 4)
-            rows = [64 * half + z * 16 + c * 4 for z in range(4)]
-            pieces = [chunks[group, row : row + 4, :] for row in rows]
-            planes[half, slot] = jnp.concatenate(pieces, axis=0)
-            pltpu.make_async_copy(planes.at[half, slot], out.at[order[slot]], sent.at[half]).start()
+        slot = 0
+        for k in range(count):
+            for source in range(2):
+                group = me ^ (2 * (first + k) + source)
+                for c in range(4):
+                    rows = [64 * half + z * 16 + c * 4 for z in range(4)]
+                    pieces = [parts[k][source, row : row + 4, :] for row in rows]
+                    planes[half, slot] = jnp.concatenate(pieces, axis=0)
+                    channel = order[group * 4 + c]
+                    pltpu.make_async_copy(
+                        planes.at[half, slot], out.at[channel], sent.at[half]
+                    ).start()
+                    slot += 1
     for half, out in enumerate((potential, gradient)):
-        pltpu.make_async_copy(planes.at[half], out, sent.at[half]).wait()
+        pltpu.make_async_copy(planes.at[half], out.at[: 8 * count], sent.at[half]).wait()
 
 
 def swapped(even, odd):
@@ -641,22 +678,34 @@
     sources = tuple(pltpu.with_memory_space_constraint(x, pltpu.HBM) for x in sources)
     held = [pltpu.VMEM(source.shape, source.dtype) for source in sources]
     held[0] = pltpu.SMEM((32,), jnp.int32)
-    chunks = call(
+
+    def exchange(rows, give, *keep):
+        def swap(value, flip):
+            return lax.ppermute(value, "depth", [(i, i ^ flip) for i in range(8)])
+
+        both = f32(2, rows, 128)
+        joined = call(join_kernel, (both,) * 4, (swap(give, 1), *keep))
+        return [joined[0]] + [swap(joined[k], 2 * k) for k in range(1, 4)]
+
+    def staged(rows):
+        return (f32(4, rows, 128),) + (f32(2, rows, 128),) * 4
+
+    packed = call(
         pack_kernel,
-        f32(8, CHUNK, 128),
+        staged(CHUNK),
         sources,
         [pltpu.VMEM((128, 16), jnp.float32), pltpu.SemaphoreType.DMA((9,))] + held,
         [in_hbm] * 9,
     )
-    chunks = lax.all_to_all(chunks, "depth", 0, 0)
+    parts = exchange(CHUNK, *packed)
     field, edge, plane = f32(4, 4, 32, 128), f32(2, 4, 32, 128), f32(4, 32, 128)
     by_depth = f32(32, 16, 128)
     rows = pltpu.VMEM((512, 128), jnp.float32)
     first = pltpu.VMEM((32, 16, 128), jnp.float32)
-    smoothed, even, odd, table, scale, root = call(
+    chunks, smoothed, even, odd, table, scale, root = call(
         smooth_kernel,
-        (field, edge, edge, f32(32, 4, 16, 128), by_depth, by_depth),
-        (chunks,),
+        (f32(8, CHUNK, 128), field, edge, edge, f32(32, 4, 16, 128), by_depth, by_depth),
+        parts,
         [pltpu.VMEM((8, 16, 128), jnp.float32), first, rows],
     )
     even, odd = swapped(even, odd)
@@ -670,25 +719,28 @@
         (partial, even, odd, taps, constant, weight, oweight),
     )
     even, odd = swapped(even, odd)
-    partial, results = call(
-        spread_kernel, (field, f32(8, 128, 128)), (forcing, taps, potential), [rows]
+    partial, potential = call(
+        spread_kernel, (field, f32(8, 64, 128)), (forcing, taps, potential), [rows]
     )
     results = call(
         gradient_kernel,
-        f32(8, 128, 128),
-        (results, chunks, partial, even, odd, taps, table, scale, root),
-        [first, rows],
-        aliases={0: 0},
-    )
-    results = lax.all_to_all(results, "depth", 0, 0)
-    potential, gradient = call(
-        unpack_kernel,
-        (by_depth, by_depth),
-        (channel_order, results),
-        [pltpu.VMEM((2, 32, 16, 128), jnp.float32), pltpu.SemaphoreType.DMA((2,))],
-        [in_smem, in_vmem],
-        in_hbm,
-    )
+        staged(128),
+        (chunks, partial, even, odd, taps, table, scale, root, potential),
+        [first, rows, pltpu.VMEM((8, 64, 128), jnp.float32)],
+    )
+    parts = exchange(128, *results)
+    outs = ()
+    for k, count in ((0, 1), (1, 1), (2, 2)):
+        outs = call(
+            functools.partial(unpack_kernel, k, count),
+            (by_depth, by_depth),
+            (channel_order, *parts[k : k + count], *outs),
+            [pltpu.VMEM((2, 8 * count, 16, 128), jnp.float32), pltpu.SemaphoreType.DMA((2,))],
+            [in_smem] + [in_vmem] * count + [in_hbm] * len(outs),
+            in_hbm,
+            {count + 1: 0, count + 2: 1} if outs else None,
+        )
+    potential, gradient = outs
     return potential.reshape(control.shape), gradient.reshape(control.shape)
 
 

time: 43.1 us -> 39.8 us (0.923)
  blocking collectives: 25.5 us -> 0 us
  waiting for transfers between devices: 2.14 us -> 13.1 us
  starting transfers between devices: 4.41 us -> 13 us
  Pallas kernels: 10.2 us -> 12.7 us
    all_to_all x2 -> x0, blocking collectives: 25.5 us -> none  [the longest x1 13.3 us: by_group(): chunks = lax.all_to_all(chunks, 'depth', 0, 0)]
    ppermute x0 -> x8, waiting for transfers between devices: none -> 11.1 us  [swap(): return lax.ppermute(value, 'depth', [(i, i ^ flip) for i in range(8)])]
    ppermute x0 -> x8, starting transfers between devices: none -> 8.61 us  [swap(): return lax.ppermute(value, 'depth', [(i, i ^ flip) for i in range(8)])]
    pallas_call x7 -> x11, Pallas kernels: 10.2 us -> 12.7 us  [call(): pl.pallas_call(kernel, out_shape=outs, in_specs=ins or [in_vmem] * len(op...]
  transfers between devices with their start and end apart: 4 -> 12, of which waited for: 2 -> 9; matrix products, arithmetic and copies ran while one was open for 0% -> 0% of each run, Pallas kernels for 10% -> 17%
where the time goes in v3:
time: 39.8 us; the launch traced here: 39.6 us
  waiting for transfers between devices  13.1 us (33%)
  starting transfers between devices  13 us (33%)
  Pallas kernels  12.7 us (32%)
  between operations  0.74 us (2%)
    pallas_call x11, Pallas kernels, call(): pl.pallas_call(kernel, out_shape=outs, in_specs=ins or [in_vmem] * len(op...  12.7 us
    ppermute x8, waiting for transfers between devices, swap(): return lax.ppermute(value, 'depth', [(i, i ^ flip) for i in range(8)])  11.1 us
    ppermute x8, starting transfers between devices, swap(): return lax.ppermute(value, 'depth', [(i, i ^ flip) for i in range(8)])  8.61 us
    ppermute x4, starting transfers between devices, swap(): return lax.ppermute(value, ('depth', 'inline'), pairs)  4.41 us
    ppermute x4, waiting for transfers between devices, swap(): return lax.ppermute(value, ('depth', 'inline'), pairs)  2.06 us
  transfers between devices with their start and end apart: 12, of which 9 were waited for; matrix products, arithmetic and copies ran while one was open for 0% of the time, Pallas kernels for 17%

profile of v3, /device:TPU:0, one launch (start us, length us, event | category | flops | bytes accessed | tf_op | source)
XLA Modules:
  0.0 39.6 jit_solution(2986650244509188379)
XLA Ops:
  0.6 1.2 %shard_map.113 = (f32[4,96,128]{2,1,0:T(8,128)S(1)}, f32[2,96,128]{2,1,0:T(8,128)S(1)}, f32[2,96,128]{2,1,0:T(8,128)S(1)}, f32[2,96,128]{2,1,0:T(8,128)S(1)}, f32[2,96,128]{2,1,0:T(8,128)S(1)}) custom-call(s32[32]{0:T(128)} %order.5, f32[16,32]{1,0:T(8,128)} %bitcast.17, f32[64,128]{1,0:T(8,128)} %bitcast.16, f32[96,128]{1,0:T(8,128)} %bitcast.15, ...), custom_call_target="tpu_custom_call" | custom-call | tf_op jit(solution)/shard_map/pallas_call | solution.py:657
  1.8 0.5 %collective-permute-start = (f32[4,96,128]{2,1,0:T(8,128)S(1)}, f32[4,96,128]{2,1,0:T(8,128)S(1)}, u32[]{:S(2)}, u32[]{:S(2)}) collective-permute-start(f32[4,96,128]{2,1,0:T(8,128)S(1)} %get-tuple-element.44), channel_id=1, source_target_pairs={{0,4},{4,0},{8,12},{12,8},{16,20},{20,16},{24,28},{28,24},{1,5},{5... | collective-permute-start | bytes 589832 | tf_op jit(solution)/shard_map/ppermute | solution.py:684
  2.4 1.1 %collective-permute-done.got = f32[4,96,128]{2,1,0:T(8,128)S(1)} collective-permute-done((f32[4,96,128]{2,1,0:T(8,128)S(1)}, f32[4,96,128]{2,1,0:T(8,128)S(1)}, u32[]{:S(2)}, u32[]{:S(2)}) %collective-permute-start) | collective-permute-done | bytes 196640 | tf_op jit(solution)/shard_map/ppermute | solution.py:684
  3.5 0.0 copy-start
  3.5 2.9 %collective-permute-start.1 = (f32[2,96,128]{2,1,0:T(8,128)S(1)}, f32[2,96,128]{2,1,0:T(8,128)S(1)}, u32[]{:S(2)}, u32[]{:S(2)}) collective-permute-start(f32[2,96,128]{2,1,0:T(8,128)S(1)} %get-tuple-element.50), channel_id=1, source_target_pairs={{0,8},{4,12},{8,0},{12,4},{16,24},{20,28},{24,16},{28,20},{1,9},{5... | collective-permute-start | bytes 294920 | tf_op jit(solution)/shard_map/ppermute | solution.py:684
  6.4 1.5 %collective-permute-start.2 = (f32[2,96,128]{2,1,0:T(8,128)S(1)}, f32[2,96,128]{2,1,0:T(8,128)S(1)}, u32[]{:S(2)}, u32[]{:S(2)}) collective-permute-start(f32[2,96,128]{2,1,0:T(8,128)S(1)} %get-tuple-element.51), channel_id=1, source_target_pairs={{0,16},{4,20},{8,24},{12,28},{16,0},{20,4},{24,8},{28,12},{1,17},{... | collective-permute-start | bytes 294920 | tf_op jit(solution)/shard_map/ppermute | solution.py:684
  7.9 0.0 collective-permute-start.3
  7.9 1.6 %collective-permute-done.1.refs_1_ = f32[2,96,128]{2,1,0:T(8,128)S(1)} collective-permute-done((f32[2,96,128]{2,1,0:T(8,128)S(1)}, f32[2,96,128]{2,1,0:T(8,128)S(1)}, u32[]{:S(2)}, u32[]{:S(2)}) %collective-permute-start.1) | collective-permute-done | bytes 98336 | tf_op jit(solution)/shard_map/ppermute | solution.py:684
  9.6 2.6 %collective-permute-done.2.refs_2_ = f32[2,96,128]{2,1,0:T(8,128)S(1)} collective-permute-done((f32[2,96,128]{2,1,0:T(8,128)S(1)}, f32[2,96,128]{2,1,0:T(8,128)S(1)}, u32[]{:S(2)}, u32[]{:S(2)}) %collective-permute-start.2) | collective-permute-done | bytes 98336 | tf_op jit(solution)/shard_map/ppermute | solution.py:684
  12.2 1.3 %collective-permute-done.3.refs_3_ = f32[2,96,128]{2,1,0:T(8,128)S(1)} collective-permute-done((f32[2,96,128]{2,1,0:T(8,128)S(1)}, f32[2,96,128]{2,1,0:T(8,128)S(1)}, u32[]{:S(2)}, u32[]{:S(2)}) %collective-permute-start.3) | collective-permute-done | bytes 98336 | tf_op jit(solution)/shard_map/ppermute | solution.py:684
  13.4 0.7 %shard_map.115 = (f32[8,96,128]{2,1,0:T(8,128)S(1)}, f32[4,4,32,128]{3,2,1,0:T(8,128)S(1)}, f32[2,4,32,128]{3,2,1,0:T(8,128)S(1)}, f32[2,4,32,128]{3,2,1,0:T(8,1...) custom-call(f32[2,96,128]{2,1,0:T(8,128)S(1)} %get-tuple-element.49.refs_0_, ...), custom_call_target="tpu_custom_call" | custom-call | tf_op jit(solution)/shard_map/pallas_call | solution.py:657
  14.1 1.6 %collective-permute-start.4 = (f32[2,4,32,128]{3,2,1,0:T(8,128)S(1)}, f32[2,4,32,128]{3,2,1,0:T(8,128)S(1)}, u32[]{:S(2)}, u32[]{:S(2)}) collective-permute-start(f32[2,4,32,128]{3,2,1,0:T(8,128)S(1)} %get-tuple-element.56), channel_id=1, source_target_pairs={{0,1},{1,0},{2,3},{3,2},{4,5},{5,4},{6,7},{7,6},{8,9},{9,8},{10,11... | collective-permute-start | bytes 393224 | tf_op jit(solution)/shard_map/ppermute | solution.py:634
  15.8 0.0 collective-permute-start.5
  15.8 0.0 copy-done
  15.8 2.4 %shard_map.116 = (f32[4,4,32,128]{3,2,1,0:T(8,128)S(1)}, f32[4,4,32,128]{3,2,1,0:T(8,128)S(1)}, f32[4,32,128]{2,1,0:T(8,128)S(1)}, f32[4,32,128]{2,1,0:T(8,128)S(1)}, f32[400,128]{1,0:T(8,128)S(1)}) custom-call(f32[8,96,128]{2,1,0:T(8,128)S(1)} %get-tuple-element.53.chunks.refs_0_, f32[4,4,32,128]{3,2,1,0:T(8,128)S(1)} %get-tuple-element.54.smoothed, ...), custom_call_target="tpu_custom_call" | custom-call | tf_op jit(solution)/shard_map/pallas_call | solution.py:657
  18.2 0.9 %collective-permute-done.4.even_in = f32[2,4,32,128]{3,2,1,0:T(8,128)S(1)} collective-permute-done((f32[2,4,32,128]{3,2,1,0:T(8,128)S(1)}, f32[2,4,32,128]{3,2,1,0:T(8,128)S(1)}, u32[]{:S(2)}, u32[]{:S(2)}) %collective-permute-start.4) | collective-permute-done | bytes 131104 | tf_op jit(solution)/shard_map/ppermute | solution.py:634
  19.2 0.0 collective-permute-done.5.odd_in
  19.2 1.5 %shard_map.117 = (f32[4,4,32,128]{3,2,1,0:T(8,128)S(1)}, f32[4,4,32,128]{3,2,1,0:T(8,128)S(1)}, f32[2,4,32,128]{3,2,1,0:T(8,128)S(1)}, f32[2,4,32,128]{3,2,1,0:T(8,128)S(1)}) custom-call(f32[4,4,32,128]{3,2,1,0:T(8,128)S(1)} %get-tuple-element.55.partial, f32[2,4,32,128]{3,2,1,0:T(8,128)S(1)} %collective-permute-done.4.even_in, ...), custom_call_target="tpu_custom_call" | custom-call | tf_op jit(solution)/shard_map/pallas_call | solution.py:657
  20.7 2.8 %collective-permute-start.6 = (f32[2,4,32,128]{3,2,1,0:T(8,128)S(1)}, f32[2,4,32,128]{3,2,1,0:T(8,128)S(1)}, u32[]{:S(2)}, u32[]{:S(2)}) collective-permute-start(f32[2,4,32,128]{3,2,1,0:T(8,128)S(1)} %get-tuple-element.65), channel_id=1, source_target_pairs={{0,1},{1,0},{2,3},{3,2},{4,5},{5,4},{6,7},{7,6},{8,9},{9,8},{10,11... | collective-permute-start | bytes 393224 | tf_op jit(solution)/shard_map/ppermute | solution.py:634
  23.5 0.0 collective-permute-start.7
  23.5 1.8 %shard_map.118 = (f32[4,4,32,128]{3,2,1,0:T(8,128)S(1)}, f32[8,64,128]{2,1,0:T(8,128)S(1)}) custom-call(f32[4,4,32,128]{3,2,1,0:T(8,128)S(1)} %get-tuple-element.62.forcing, f32[400,128]{1,0:T(8,128)S(1)} %get-tuple-element.58.table.refs_4_, f32[4,4,32,128]{3,2,1,0:T(8,128)S(1)} %get-tuple-element.63.potential), custom_call_target="tpu_custom_call" | custom-call | tf_op jit(solution)/shard_map/pallas_call | solution.py:657
  25.3 1.1 %collective-permute-done.6.refs_2_ = f32[2,4,32,128]{3,2,1,0:T(8,128)S(1)} collective-permute-done((f32[2,4,32,128]{3,2,1,0:T(8,128)S(1)}, f32[2,4,32,128]{3,2,1,0:T(8,128)S(1)}, u32[]{:S(2)}, u32[]{:S(2)}) %collective-permute-start.6) | collective-permute-done | bytes 131104 | tf_op jit(solution)/shard_map/ppermute | solution.py:634
  26.4 0.0 collective-permute-done.7.refs_3_
  26.4 1.2 %shard_map.119 = (f32[4,128,128]{2,1,0:T(8,128)S(1)}, f32[2,128,128]{2,1,0:T(8,128)S(1)}, f32[2,128,128]{2,1,0:T(8,128)S(1)}, f32[2,128,128]{2,1,0:T(8,128)S(1)}, f32[2,128,128]{2,1,0:T(8,128)S(1)}) custom-call(f32[8,96,128]{2,1,0:T(8,128)S(1)} %get-tuple-element.53.chunks.refs_0_, f32[4,4,32,128]{3,2,1,0:T(8,128)S(1)} %get-tuple-element.64.refs_1_, ...), custom_call_target="tpu_custom_call" | custom-call | tf_op jit(solution)/shard_map/pallas_call | solution.py:657
  27.6 0.1 collective-permute-start.8
  27.7 1.5 %collective-permute-done.8.got = f32[4,128,128]{2,1,0:T(8,128)S(1)} collective-permute-done((f32[4,128,128]{2,1,0:T(8,128)S(1)}, f32[4,128,128]{2,1,0:T(8,128)S(1)}, u32[]{:S(2)}, u32[]{:S(2)}) %collective-permute-start.8) | collective-permute-done | bytes 262176 | tf_op jit(solution)/shard_map/ppermute | solution.py:684
  29.3 0.9 %collective-permute-start.11 = (f32[2,128,128]{2,1,0:T(8,128)S(1)}, f32[2,128,128]{2,1,0:T(8,128)S(1)}, u32[]{:S(2)}, u32[]{:S(2)}) collective-permute-start(f32[2,128,128]{2,1,0:T(8,128)S(1)} %get-tuple-element.78), channel_id=1, source_target_pairs={{0,8},{4,12},{8,0},{12,4},{16,24},{20,28},{24,16},{28,20},{1,9},{5... | collective-permute-start | bytes 393224 | tf_op jit(solution)/shard_map/ppermute | solution.py:684
  30.2 0.9 %collective-permute-start.9 = (f32[2,128,128]{2,1,0:T(8,128)S(1)}, f32[2,128,128]{2,1,0:T(8,128)S(1)}, u32[]{:S(2)}, u32[]{:S(2)}) collective-permute-start(f32[2,128,128]{2,1,0:T(8,128)S(1)} %get-tuple-element.76), channel_id=1, source_target_pairs={{0,16},{4,20},{8,24},{12,28},{16,0},{20,4},{24,8},{28,12},{1,17},{... | collective-permute-start | bytes 393224 | tf_op jit(solution)/shard_map/ppermute | solution.py:684
  31.1 0.0 copy-start.1
  31.1 1.7 %collective-permute-start.10 = (f32[2,128,128]{2,1,0:T(8,128)S(1)}, f32[2,128,128]{2,1,0:T(8,128)S(1)}, u32[]{:S(2)}, u32[]{:S(2)}) collective-permute-start(f32[2,128,128]{2,1,0:T(8,128)S(1)} %get-tuple-element.77), channel_id=1, source_target_pairs={{0,24},{4,28},{8,16},{12,20},{16,8},{20,12},{24,0},{28,4},{1,25},{... | collective-permute-start | bytes 393224 | tf_op jit(solution)/shard_map/ppermute | solution.py:684
  32.8 0.0 copy-done.1
  32.8 1.2 %shard_map.121 = (f32[32,16,128]{2,1,0:T(8,128)}, f32[32,16,128]{2,1,0:T(8,128)}) custom-call(s32[32]{0:T(128)S(1)} %copy-done.1, f32[2,128,128]{2,1,0:T(8,128)S(1)} %get-tuple-element.79.refs_0_), custom_call_target="tpu_custom_call" | custom-call | tf_op jit(solution)/shard_map/pallas_call | solution.py:657
  34.1 1.6 %collective-permute-done.11.refs_0_ = f32[2,128,128]{2,1,0:T(8,128)S(1)} collective-permute-done((f32[2,128,128]{2,1,0:T(8,128)S(1)}, f32[2,128,128]{2,1,0:T(8,128)S(1)}, u32[]{:S(2)}, u32[]{:S(2)}) %collective-permute-start.11) | collective-permute-done | bytes 131104 | tf_op jit(solution)/shard_map/ppermute | solution.py:684
  35.7 1.2 %shard_map.122 = (f32[32,16,128]{2,1,0:T(8,128)}, f32[32,16,128]{2,1,0:T(8,128)}) custom-call(s32[32]{0:T(128)S(1)} %copy-done.1, f32[2,128,128]{2,1,0:T(8,128)S(1)} %collective-permute-done.11.refs_0_, f32[32,16,128]{2,1,0:T(8,128)} %get-tuple-element.80.refs_1_, f32[32,16,128]{2,1,0:T(8,128)} %get-tuple-element.81.refs_2_), custom_call_target="tpu_custom_call", output_to_operand_aliasing={{0}: (2, {}), {1}: (3, {})} | custom-call | tf_op jit(solution)/shard_map/pallas_call | solution.py:657
  36.9 0.0 collective-permute-done.9.refs_0_
  36.9 1.4 %collective-permute-done.10.refs_1_ = f32[2,128,128]{2,1,0:T(8,128)S(1)} collective-permute-done((f32[2,128,128]{2,1,0:T(8,128)S(1)}, f32[2,128,128]{2,1,0:T(8,128)S(1)}, u32[]{:S(2)}, u32[]{:S(2)}) %collective-permute-start.10) | collective-permute-done | bytes 131104 | tf_op jit(solution)/shard_map/ppermute | solution.py:684
  38.3 1.3 %shard_map.123 = (f32[32,16,128]{2,1,0:T(8,128)}, f32[32,16,128]{2,1,0:T(8,128)}) custom-call(s32[32]{0:T(128)S(1)} %copy-done.1, f32[2,128,128]{2,1,0:T(8,128)S(1)} %collective-permute-done.9.refs_0_, f32[2,128,128]{2,1,0:T(8,128)S(1)} %collective-permute-done.10.refs_1_, ...), custom_call_target="tpu_custom_call", output_to_operand_aliasing={{0}: (3, {}), {1}: (4, {})} | custom-call | tf_op jit(solution)/shard_map/pallas_call | solution.py:657
  (2 shorter events, 0.1 us)
Async XLA Ops:
  1.8 1.6 %collective-permute-start = (f32[4,96,128]{2,1,0:T(8,128)S(1)}, f32[4,96,128]{2,1,0:T(8,128)S(1)}, u32[]{:S(2)}, u32[]{:S(2)}) collective-permute-start(f32[4,96,128]{2,1,0:T(8,128)S(1)} %get-tuple-element.44), channel_id=1, source_target_pairs={{0,4},{4,0},{8,12},{12,8},{16,20},{20,16},{24,28},{28,24},{1,5},{5... | collective-permute-start | bytes 589832 | tf_op jit(solution)/shard_map/ppermute | solution.py:684
  3.5 12.3 %copy-start = (f32[8,4,4,5,5]{0,2,4,3,1:T(4,128)S(1)}, f32[8,4,4,5,5]{0,2,4,3,1:T(4,128)}, u32[]{:S(2)}) copy-start(f32[8,4,4,5,5]{0,2,4,3,1:T(4,128)} %param.12) | copy-start | bytes 38404
  3.5 6.1 %collective-permute-start.1 = (f32[2,96,128]{2,1,0:T(8,128)S(1)}, f32[2,96,128]{2,1,0:T(8,128)S(1)}, u32[]{:S(2)}, u32[]{:S(2)}) collective-permute-start(f32[2,96,128]{2,1,0:T(8,128)S(1)} %get-tuple-element.50), channel_id=1, source_target_pairs={{0,8},{4,12},{8,0},{12,4},{16,24},{20,28},{24,16},{28,20},{1,9},{5... | collective-permute-start | bytes 294920 | tf_op jit(solution)/shard_map/ppermute | solution.py:684
  6.4 5.8 %collective-permute-start.2 = (f32[2,96,128]{2,1,0:T(8,128)S(1)}, f32[2,96,128]{2,1,0:T(8,128)S(1)}, u32[]{:S(2)}, u32[]{:S(2)}) collective-permute-start(f32[2,96,128]{2,1,0:T(8,128)S(1)} %get-tuple-element.51), channel_id=1, source_target_pairs={{0,16},{4,20},{8,24},{12,28},{16,0},{20,4},{24,8},{28,12},{1,17},{... | collective-permute-start | bytes 294920 | tf_op jit(solution)/shard_map/ppermute | solution.py:684
  7.9 5.5 %collective-permute-start.3 = (f32[2,96,128]{2,1,0:T(8,128)S(1)}, f32[2,96,128]{2,1,0:T(8,128)S(1)}, u32[]{:S(2)}, u32[]{:S(2)}) collective-permute-start(f32[2,96,128]{2,1,0:T(8,128)S(1)} %get-tuple-element.52), channel_id=1, source_target_pairs={{0,24},{4,28},{8,16},{12,20},{16,8},{20,12},{24,0},{28,4},{1,25},{... | collective-permute-start | bytes 294920 | tf_op jit(solution)/shard_map/ppermute | solution.py:684
  14.1 5.0 %collective-permute-start.4 = (f32[2,4,32,128]{3,2,1,0:T(8,128)S(1)}, f32[2,4,32,128]{3,2,1,0:T(8,128)S(1)}, u32[]{:S(2)}, u32[]{:S(2)}) collective-permute-start(f32[2,4,32,128]{3,2,1,0:T(8,128)S(1)} %get-tuple-element.56), channel_id=1, source_target_pairs={{0,1},{1,0},{2,3},{3,2},{4,5},{5,4},{6,7},{7,6},{8,9},{9,8},{10,11... | collective-permute-start | bytes 393224 | tf_op jit(solution)/shard_map/ppermute | solution.py:634
  15.8 3.4 %collective-permute-start.5 = (f32[2,4,32,128]{3,2,1,0:T(8,128)S(1)}, f32[2,4,32,128]{3,2,1,0:T(8,128)S(1)}, u32[]{:S(2)}, u32[]{:S(2)}) collective-permute-start(f32[2,4,32,128]{3,2,1,0:T(8,128)S(1)} %get-tuple-element.57), channel_id=1, source_target_pairs={{0,4},{1,2},{2,1},{3,7},{4,0},{5,6},{6,5},{7,3},{8,12},{9,10},{10,... | collective-permute-start | bytes 393224 | tf_op jit(solution)/shard_map/ppermute | solution.py:634
  20.7 5.7 %collective-permute-start.6 = (f32[2,4,32,128]{3,2,1,0:T(8,128)S(1)}, f32[2,4,32,128]{3,2,1,0:T(8,128)S(1)}, u32[]{:S(2)}, u32[]{:S(2)}) collective-permute-start(f32[2,4,32,128]{3,2,1,0:T(8,128)S(1)} %get-tuple-element.65), channel_id=1, source_target_pairs={{0,1},{1,0},{2,3},{3,2},{4,5},{5,4},{6,7},{7,6},{8,9},{9,8},{10,11... | collective-permute-start | bytes 393224 | tf_op jit(solution)/shard_map/ppermute | solution.py:634
  23.5 3.0 %collective-permute-start.7 = (f32[2,4,32,128]{3,2,1,0:T(8,128)S(1)}, f32[2,4,32,128]{3,2,1,0:T(8,128)S(1)}, u32[]{:S(2)}, u32[]{:S(2)}) collective-permute-start(f32[2,4,32,128]{3,2,1,0:T(8,128)S(1)} %get-tuple-element.66), channel_id=1, source_target_pairs={{0,4},{1,2},{2,1},{3,7},{4,0},{5,6},{6,5},{7,3},{8,12},{9,10},{10,... | collective-permute-start | bytes 393224 | tf_op jit(solution)/shard_map/ppermute | solution.py:634
  27.6 1.6 %collective-permute-start.8 = (f32[4,128,128]{2,1,0:T(8,128)S(1)}, f32[4,128,128]{2,1,0:T(8,128)S(1)}, u32[]{:S(2)}, u32[]{:S(2)}) collective-permute-start(f32[4,128,128]{2,1,0:T(8,128)S(1)} %get-tuple-element.71), channel_id=1, source_target_pairs={{0,4},{4,0},{8,12},{12,8},{16,20},{20,16},{24,28},{28,24},{1,5},{5... | collective-permute-start | bytes 786440 | tf_op jit(solution)/shard_map/ppermute | solution.py:684
  29.3 6.4 %collective-permute-start.11 = (f32[2,128,128]{2,1,0:T(8,128)S(1)}, f32[2,128,128]{2,1,0:T(8,128)S(1)}, u32[]{:S(2)}, u32[]{:S(2)}) collective-permute-start(f32[2,128,128]{2,1,0:T(8,128)S(1)} %get-tuple-element.78), channel_id=1, source_target_pairs={{0,8},{4,12},{8,0},{12,4},{16,24},{20,28},{24,16},{28,20},{1,9},{5... | collective-permute-start | bytes 393224 | tf_op jit(solution)/shard_map/ppermute | solution.py:684
  30.2 6.7 %collective-permute-start.9 = (f32[2,128,128]{2,1,0:T(8,128)S(1)}, f32[2,128,128]{2,1,0:T(8,128)S(1)}, u32[]{:S(2)}, u32[]{:S(2)}) collective-permute-start(f32[2,128,128]{2,1,0:T(8,128)S(1)} %get-tuple-element.76), channel_id=1, source_target_pairs={{0,16},{4,20},{8,24},{12,28},{16,0},{20,4},{24,8},{28,12},{1,17},{... | collective-permute-start | bytes 393224 | tf_op jit(solution)/shard_map/ppermute | solution.py:684
  31.1 1.7 %copy-start.1 = (s32[32]{0:T(128)S(1)}, s32[32]{0:T(128)}, u32[]{:S(2)}) copy-start(s32[32]{0:T(128)} %order.5) | copy-start | bytes 388
  31.1 7.2 %collective-permute-start.10 = (f32[2,128,128]{2,1,0:T(8,128)S(1)}, f32[2,128,128]{2,1,0:T(8,128)S(1)}, u32[]{:S(2)}, u32[]{:S(2)}) collective-permute-start(f32[2,128,128]{2,1,0:T(8,128)S(1)} %get-tuple-element.77), channel_id=1, source_target_pairs={{0,24},{4,28},{8,16},{12,20},{16,8},{20,12},{24,0},{28,4},{1,25},{... | collective-permute-start | bytes 393224 | tf_op jit(solution)/shard_map/ppermute | solution.py:684

commit v4 on v3

--- a/solution.py
+++ b/solution.py
@@ -295,19 +295,13 @@
     return jnp.broadcast_to(expanded[block, :, k : k + 1], (16, 128))
 
 
-def expand_coeffs(chunks, expanded, table, scale, root):
+def repeat_coeffs(chunks, expanded):
     for block in range(8):
         for c in range(4):
             row = AT_COEFFS + c
             expanded[block, 4 * c : 4 * c + 4, :] = jnp.broadcast_to(
                 chunks[block, row : row + 1, :], (4, 128)
             )
-    for z in range(32):
-        lags = [coefficient(expanded, lag, z) for lag in range(1, 5)]
-        for lag in range(4):
-            table[z, lag] = lags[lag]
-        scale[z] = 1.0 - ((lags[0] + lags[1]) + (lags[2] + lags[3]))
-        root[z] = jnp.sqrt(scale[z])
 
 
 def recurrence(source, factor, emit, order):
@@ -332,20 +326,27 @@
     for k in range(4):
         for half in range(2):
             chunks[me ^ (2 * k + half)] = parts[k][half]
-    expand_coeffs(chunks, expanded, table, scale, root)
+    repeat_coeffs(chunks, expanded)
+    lags = {}
+
+    def start(z):
+        lags.clear()
+        lags.update({lag: coefficient(expanded, lag, z) for lag in range(1, 5)})
+        for lag in range(1, 5):
+            table[z, lag - 1] = lags[lag]
+        lags[0] = 1.0 - ((lags[1] + lags[2]) + (lags[3] + lags[4]))
+        scale[z] = lags[0]
+        lags[-1] = jnp.sqrt(lags[0])
+        root[z] = lags[-1]
+        return lags[-1] * depth_rows(chunks, z)
 
     def keep_first(z, value):
-        first[z] = scale[z] * value
+        first[z] = lags[0] * value
 
     def keep_rows(z, value):
         rows[z * 16 : z * 16 + 16, :] = value
 
-    recurrence(
-        lambda z: root[z] * depth_rows(chunks, z),
-        lambda lag, z, before: table[z, lag - 1],
-        keep_first,
-        range(32),
-    )
+    recurrence(start, lambda lag, z, before: lags[lag], keep_first, range(32))
     recurrence(
         lambda z: first[z],
         lambda lag, z, before: table[z, lag - 1],
@@ -512,28 +513,32 @@
         write,
     )
 
-    def one_channel(c, carry):
-        lines = [potential[y, c] for y in range(4)]
-        sums = [weight[y] * lines[y] - constant[y, c] for y in range(4)]
-        for y in range(4):
-            share = oweight[y]
-            deeper = share * (pltpu.roll(lines[y], 31, 0) - lines[y])
-            across = share * (pltpu.roll(lines[y], 127, 1) - lines[y])
-            sums[y] = sums[y] - deeper + pltpu.roll(deeper, 1, 0)
-            sums[y] = sums[y] - across + pltpu.roll(across, 1, 1)
-            if y < 3:
-                beside = share * (lines[y + 1] - lines[y])
-                sums[y] = sums[y] - beside
-                sums[y + 1] = sums[y + 1] + beside
-        for y in range(4):
-            forcing[y, c] = sums[y]
+    parity = lax.axis_index("inline") % 2
+
+    def some_depths(k, carry):
+        depths = pl.ds(pl.multiple_of(k * 8, 8), 8)
+        shares = [oweight[y, depths, :] for y in range(4)]
+        weights = [weight[y, depths, :] for y in range(4)]
+        for c in range(4):
+            lines = [potential[y, c, depths, :] for y in range(4)]
+            sums = [weights[y] * lines[y] - constant[y, c, depths, :] for y in range(4)]
+            for y in range(4):
+                deeper = shares[y] * (pltpu.roll(lines[y], 7, 0) - lines[y])
+                across = shares[y] * (pltpu.roll(lines[y], 127, 1) - lines[y])
+                sums[y] = sums[y] - deeper + pltpu.roll(deeper, 1, 0)
+                sums[y] = sums[y] - across + pltpu.roll(across, 1, 1)
+                if y < 3:
+                    beside = shares[y] * (lines[y + 1] - lines[y])
+                    sums[y] = sums[y] - beside
+                    sums[y + 1] = sums[y + 1] + beside
+            for y in range(4):
+                forcing[y, c, depths, :] = sums[y]
+            for y in range(2):
+                even[y, c, depths, :] = jnp.where(parity == 0, sums[2 + y], sums[y])
+                odd[y, c, depths, :] = jnp.where(parity == 0, sums[y], sums[2 + y])
         return carry
 
-    lax.fori_loop(0, 4, one_channel, 0)
-    parity = lax.axis_index("inline") % 2
-    for y in range(2):
-        even[y] = forcing[2 - 2 * parity + y]
-        odd[y] = forcing[2 * parity + y]
+    lax.fori_loop(0, 4, some_depths, 0)
 
 
 def spread_kernel(forcing, table, potential, partial, out, rows):
@@ -600,23 +605,22 @@
         target[64:, :] = out[me ^ place]
 
 
-def unpack_kernel(first, count, order, *refs):
-    parts, (potential, gradient, planes, sent) = refs[:count], refs[-4:]
+def unpack_kernel(first, count, order_in, *refs):
+    parts, (potential, gradient, planes, order, sent) = refs[:count], refs[-5:]
+    numbers = pltpu.make_async_copy(order_in, order, sent.at[2])
+    numbers.start()
+    for half in range(2):
+        for slot in range(8 * count):
+            k, source, c = slot // 8, slot // 4 % 2, slot % 4
+            rows = [64 * half + z * 16 + c * 4 for z in range(4)]
+            pieces = [parts[k][source, row : row + 4, :] for row in rows]
+            planes[half, slot] = jnp.concatenate(pieces, axis=0)
+    numbers.wait()
     me = lax.axis_index("depth")
-    for half, out in enumerate((potential, gradient)):
-        slot = 0
-        for k in range(count):
-            for source in range(2):
-                group = me ^ (2 * (first + k) + source)
-                for c in range(4):
-                    rows = [64 * half + z * 16 + c * 4 for z in range(4)]
-                    pieces = [parts[k][source, row : row + 4, :] for row in rows]
-                    planes[half, slot] = jnp.concatenate(pieces, axis=0)
-                    channel = order[group * 4 + c]
-                    pltpu.make_async_copy(
-                        planes.at[half, slot], out.at[channel], sent.at[half]
-                    ).start()
-                    slot += 1
+    for slot in range(8 * count):
+        channel = order[(me ^ (2 * first + slot // 4)) * 4 + slot % 4]
+        for half, out in enumerate((potential, gradient)):
+            pltpu.make_async_copy(planes.at[half, slot], out.at[channel], sent.at[half]).start()
     for half, out in enumerate((potential, gradient)):
         pltpu.make_async_copy(planes.at[half], out.at[: 8 * count], sent.at[half]).wait()
 
@@ -649,9 +653,7 @@
     orient_weights,
 ):
     params = pltpu.CompilerParams(vmem_limit_bytes=48 << 20)
-    in_vmem, in_smem, in_hbm = (
-        pl.BlockSpec(memory_space=space) for space in (pltpu.VMEM, pltpu.SMEM, pltpu.HBM)
-    )
+    in_vmem, in_hbm = (pl.BlockSpec(memory_space=space) for space in (pltpu.VMEM, pltpu.HBM))
 
     def call(kernel, outs, operands, scratch=(), ins=None, to=in_vmem, aliases=None):
         return pl.pallas_call(
@@ -735,8 +737,12 @@
             functools.partial(unpack_kernel, k, count),
             (by_depth, by_depth),
             (channel_order, *parts[k : k + count], *outs),
-            [pltpu.VMEM((2, 8 * count, 16, 128), jnp.float32), pltpu.SemaphoreType.DMA((2,))],
-            [in_smem] + [in_vmem] * count + [in_hbm] * len(outs),
+            [
+                pltpu.VMEM((2, 8 * count, 16, 128), jnp.float32),
+                pltpu.SMEM((32,), jnp.int32),
+                pltpu.SemaphoreType.DMA((3,)),
+            ],
+            [in_vmem] * (count + 1) + [in_hbm] * len(outs),
             in_hbm,
             {count + 1: 0, count + 2: 1} if outs else None,
         )

time: 39.8 us -> 39.8 us (level)
  no operation moved by 1% of the time
where the time goes in v4:
time: 39.8 us; the launch traced here: 39.6 us
  waiting for transfers between devices  13.2 us (33%)
  starting transfers between devices  13 us (33%)
  Pallas kernels  12.7 us (32%)
  between operations  0.74 us (2%)
    pallas_call x11, Pallas kernels, call(): pl.pallas_call(kernel, out_shape=outs, in_specs=ins or [in_vmem] * len(op...  12.7 us
    ppermute x8, waiting for transfers between devices, swap(): return lax.ppermute(value, 'depth', [(i, i ^ flip) for i in range(8)])  11.1 us
    ppermute x8, starting transfers between devices, swap(): return lax.ppermute(value, 'depth', [(i, i ^ flip) for i in range(8)])  8.61 us
    ppermute x4, starting transfers between devices, swap(): return lax.ppermute(value, ('depth', 'inline'), pairs)  4.41 us
    ppermute x4, waiting for transfers between devices, swap(): return lax.ppermute(value, ('depth', 'inline'), pairs)  2.08 us
  transfers between devices with their start and end apart: 12, of which 9 were waited for; matrix products, arithmetic and copies ran while one was open for 0% of the time, Pallas kernels for 17%

profile of v4, /device:TPU:0, one launch (start us, length us, event | category | flops | bytes accessed | tf_op | source)
XLA Modules:
  0.0 39.6 jit_solution(7708596403042668109)
XLA Ops:
  0.6 1.2 %shard_map.113 = (f32[4,96,128]{2,1,0:T(8,128)S(1)}, f32[2,96,128]{2,1,0:T(8,128)S(1)}, f32[2,96,128]{2,1,0:T(8,128)S(1)}, f32[2,96,128]{2,1,0:T(8,128)S(1)}, f32[2,96,128]{2,1,0:T(8,128)S(1)}) custom-call(s32[32]{0:T(128)} %order_in.5, f32[16,32]{1,0:T(8,128)} %bitcast.17, f32[64,128]{1,0:T(8,128)} %bitcast.16, f32[96,128]{1,0:T(8,128)} %bitcast.15, ...), custom_call_target="tpu_custom_call" | custom-call | tf_op jit(solution)/shard_map/pallas_call | solution.py:659
  1.8 0.5 %collective-permute-start = (f32[4,96,128]{2,1,0:T(8,128)S(1)}, f32[4,96,128]{2,1,0:T(8,128)S(1)}, u32[]{:S(2)}, u32[]{:S(2)}) collective-permute-start(f32[4,96,128]{2,1,0:T(8,128)S(1)} %get-tuple-element.44), channel_id=1, source_target_pairs={{0,4},{4,0},{8,12},{12,8},{16,20},{20,16},{24,28},{28,24},{1,5},{5... | collective-permute-start | bytes 589832 | tf_op jit(solution)/shard_map/ppermute | solution.py:686
  2.4 1.1 %collective-permute-done.got = f32[4,96,128]{2,1,0:T(8,128)S(1)} collective-permute-done((f32[4,96,128]{2,1,0:T(8,128)S(1)}, f32[4,96,128]{2,1,0:T(8,128)S(1)}, u32[]{:S(2)}, u32[]{:S(2)}) %collective-permute-start) | collective-permute-done | bytes 196640 | tf_op jit(solution)/shard_map/ppermute | solution.py:686
  3.5 0.0 copy-start
  3.5 2.9 %collective-permute-start.1 = (f32[2,96,128]{2,1,0:T(8,128)S(1)}, f32[2,96,128]{2,1,0:T(8,128)S(1)}, u32[]{:S(2)}, u32[]{:S(2)}) collective-permute-start(f32[2,96,128]{2,1,0:T(8,128)S(1)} %get-tuple-element.50), channel_id=1, source_target_pairs={{0,8},{4,12},{8,0},{12,4},{16,24},{20,28},{24,16},{28,20},{1,9},{5... | collective-permute-start | bytes 294920 | tf_op jit(solution)/shard_map/ppermute | solution.py:686
  6.4 1.5 %collective-permute-start.2 = (f32[2,96,128]{2,1,0:T(8,128)S(1)}, f32[2,96,128]{2,1,0:T(8,128)S(1)}, u32[]{:S(2)}, u32[]{:S(2)}) collective-permute-start(f32[2,96,128]{2,1,0:T(8,128)S(1)} %get-tuple-element.51), channel_id=1, source_target_pairs={{0,16},{4,20},{8,24},{12,28},{16,0},{20,4},{24,8},{28,12},{1,17},{... | collective-permute-start | bytes 294920 | tf_op jit(solution)/shard_map/ppermute | solution.py:686
  7.9 0.0 collective-permute-start.3
  7.9 1.6 %collective-permute-done.1.refs_1_ = f32[2,96,128]{2,1,0:T(8,128)S(1)} collective-permute-done((f32[2,96,128]{2,1,0:T(8,128)S(1)}, f32[2,96,128]{2,1,0:T(8,128)S(1)}, u32[]{:S(2)}, u32[]{:S(2)}) %collective-permute-start.1) | collective-permute-done | bytes 98336 | tf_op jit(solution)/shard_map/ppermute | solution.py:686
  9.6 2.6 %collective-permute-done.2.refs_2_ = f32[2,96,128]{2,1,0:T(8,128)S(1)} collective-permute-done((f32[2,96,128]{2,1,0:T(8,128)S(1)}, f32[2,96,128]{2,1,0:T(8,128)S(1)}, u32[]{:S(2)}, u32[]{:S(2)}) %collective-permute-start.2) | collective-permute-done | bytes 98336 | tf_op jit(solution)/shard_map/ppermute | solution.py:686
  12.2 1.3 %collective-permute-done.3.refs_3_ = f32[2,96,128]{2,1,0:T(8,128)S(1)} collective-permute-done((f32[2,96,128]{2,1,0:T(8,128)S(1)}, f32[2,96,128]{2,1,0:T(8,128)S(1)}, u32[]{:S(2)}, u32[]{:S(2)}) %collective-permute-start.3) | collective-permute-done | bytes 98336 | tf_op jit(solution)/shard_map/ppermute | solution.py:686
  13.4 0.7 %shard_map.115 = (f32[8,96,128]{2,1,0:T(8,128)S(1)}, f32[4,4,32,128]{3,2,1,0:T(8,128)S(1)}, f32[2,4,32,128]{3,2,1,0:T(8,128)S(1)}, f32[2,4,32,128]{3,2,1,0:T(8,1...) custom-call(f32[2,96,128]{2,1,0:T(8,128)S(1)} %get-tuple-element.49.refs_0_, ...), custom_call_target="tpu_custom_call" | custom-call | tf_op jit(solution)/shard_map/pallas_call | solution.py:659
  14.1 1.6 %collective-permute-start.4 = (f32[2,4,32,128]{3,2,1,0:T(8,128)S(1)}, f32[2,4,32,128]{3,2,1,0:T(8,128)S(1)}, u32[]{:S(2)}, u32[]{:S(2)}) collective-permute-start(f32[2,4,32,128]{3,2,1,0:T(8,128)S(1)} %get-tuple-element.56), channel_id=1, source_target_pairs={{0,1},{1,0},{2,3},{3,2},{4,5},{5,4},{6,7},{7,6},{8,9},{9,8},{10,11... | collective-permute-start | bytes 393224 | tf_op jit(solution)/shard_map/ppermute | solution.py:638
  15.8 0.0 collective-permute-start.5
  15.8 0.0 copy-done
  15.8 2.4 %shard_map.116 = (f32[4,4,32,128]{3,2,1,0:T(8,128)S(1)}, f32[4,4,32,128]{3,2,1,0:T(8,128)S(1)}, f32[4,32,128]{2,1,0:T(8,128)S(1)}, f32[4,32,128]{2,1,0:T(8,128)S(1)}, f32[400,128]{1,0:T(8,128)S(1)}) custom-call(f32[8,96,128]{2,1,0:T(8,128)S(1)} %get-tuple-element.53.chunks.refs_0_, f32[4,4,32,128]{3,2,1,0:T(8,128)S(1)} %get-tuple-element.54.smoothed, ...), custom_call_target="tpu_custom_call" | custom-call | tf_op jit(solution)/shard_map/pallas_call | solution.py:659
  18.2 1.0 %collective-permute-done.4.even_in = f32[2,4,32,128]{3,2,1,0:T(8,128)S(1)} collective-permute-done((f32[2,4,32,128]{3,2,1,0:T(8,128)S(1)}, f32[2,4,32,128]{3,2,1,0:T(8,128)S(1)}, u32[]{:S(2)}, u32[]{:S(2)}) %collective-permute-start.4) | collective-permute-done | bytes 131104 | tf_op jit(solution)/shard_map/ppermute | solution.py:638
  19.2 0.0 collective-permute-done.5.odd_in
  19.2 1.5 %shard_map.117 = (f32[4,4,32,128]{3,2,1,0:T(8,128)S(1)}, f32[4,4,32,128]{3,2,1,0:T(8,128)S(1)}, f32[2,4,32,128]{3,2,1,0:T(8,128)S(1)}, f32[2,4,32,128]{3,2,1,0:T(8,128)S(1)}) custom-call(f32[4,4,32,128]{3,2,1,0:T(8,128)S(1)} %get-tuple-element.55.partial, f32[2,4,32,128]{3,2,1,0:T(8,128)S(1)} %collective-permute-done.4.even_in, ...), custom_call_target="tpu_custom_call" | custom-call | tf_op jit(solution)/shard_map/pallas_call | solution.py:659
  20.7 2.8 %collective-permute-start.6 = (f32[2,4,32,128]{3,2,1,0:T(8,128)S(1)}, f32[2,4,32,128]{3,2,1,0:T(8,128)S(1)}, u32[]{:S(2)}, u32[]{:S(2)}) collective-permute-start(f32[2,4,32,128]{3,2,1,0:T(8,128)S(1)} %get-tuple-element.65), channel_id=1, source_target_pairs={{0,1},{1,0},{2,3},{3,2},{4,5},{5,4},{6,7},{7,6},{8,9},{9,8},{10,11... | collective-permute-start | bytes 393224 | tf_op jit(solution)/shard_map/ppermute | solution.py:638
  23.4 0.0 collective-permute-start.7
  23.4 1.8 %shard_map.118 = (f32[4,4,32,128]{3,2,1,0:T(8,128)S(1)}, f32[8,64,128]{2,1,0:T(8,128)S(1)}) custom-call(f32[4,4,32,128]{3,2,1,0:T(8,128)S(1)} %get-tuple-element.62.forcing, f32[400,128]{1,0:T(8,128)S(1)} %get-tuple-element.58.table.refs_4_, f32[4,4,32,128]{3,2,1,0:T(8,128)S(1)} %get-tuple-element.63.potential), custom_call_target="tpu_custom_call" | custom-call | tf_op jit(solution)/shard_map/pallas_call | solution.py:659
  25.3 1.1 %collective-permute-done.6.refs_2_ = f32[2,4,32,128]{3,2,1,0:T(8,128)S(1)} collective-permute-done((f32[2,4,32,128]{3,2,1,0:T(8,128)S(1)}, f32[2,4,32,128]{3,2,1,0:T(8,128)S(1)}, u32[]{:S(2)}, u32[]{:S(2)}) %collective-permute-start.6) | collective-permute-done | bytes 131104 | tf_op jit(solution)/shard_map/ppermute | solution.py:638
  26.4 0.0 collective-permute-done.7.refs_3_
  26.4 1.2 %shard_map.119 = (f32[4,128,128]{2,1,0:T(8,128)S(1)}, f32[2,128,128]{2,1,0:T(8,128)S(1)}, f32[2,128,128]{2,1,0:T(8,128)S(1)}, f32[2,128,128]{2,1,0:T(8,128)S(1)}, f32[2,128,128]{2,1,0:T(8,128)S(1)}) custom-call(f32[8,96,128]{2,1,0:T(8,128)S(1)} %get-tuple-element.53.chunks.refs_0_, f32[4,4,32,128]{3,2,1,0:T(8,128)S(1)} %get-tuple-element.64.refs_1_, ...), custom_call_target="tpu_custom_call" | custom-call | tf_op jit(solution)/shard_map/pallas_call | solution.py:659
  27.6 0.1 collective-permute-start.8
  27.7 1.5 %collective-permute-done.8.got = f32[4,128,128]{2,1,0:T(8,128)S(1)} collective-permute-done((f32[4,128,128]{2,1,0:T(8,128)S(1)}, f32[4,128,128]{2,1,0:T(8,128)S(1)}, u32[]{:S(2)}, u32[]{:S(2)}) %collective-permute-start.8) | collective-permute-done | bytes 262176 | tf_op jit(solution)/shard_map/ppermute | solution.py:686
  29.2 0.9 %collective-permute-start.11 = (f32[2,128,128]{2,1,0:T(8,128)S(1)}, f32[2,128,128]{2,1,0:T(8,128)S(1)}, u32[]{:S(2)}, u32[]{:S(2)}) collective-permute-start(f32[2,128,128]{2,1,0:T(8,128)S(1)} %get-tuple-element.78), channel_id=1, source_target_pairs={{0,8},{4,12},{8,0},{12,4},{16,24},{20,28},{24,16},{28,20},{1,9},{5... | collective-permute-start | bytes 393224 | tf_op jit(solution)/shard_map/ppermute | solution.py:686
  30.2 0.9 %collective-permute-start.9 = (f32[2,128,128]{2,1,0:T(8,128)S(1)}, f32[2,128,128]{2,1,0:T(8,128)S(1)}, u32[]{:S(2)}, u32[]{:S(2)}) collective-permute-start(f32[2,128,128]{2,1,0:T(8,128)S(1)} %get-tuple-element.76), channel_id=1, source_target_pairs={{0,16},{4,20},{8,24},{12,28},{16,0},{20,4},{24,8},{28,12},{1,17},{... | collective-permute-start | bytes 393224 | tf_op jit(solution)/shard_map/ppermute | solution.py:686
  31.1 0.0 copy-start.1
  31.1 1.7 %collective-permute-start.10 = (f32[2,128,128]{2,1,0:T(8,128)S(1)}, f32[2,128,128]{2,1,0:T(8,128)S(1)}, u32[]{:S(2)}, u32[]{:S(2)}) collective-permute-start(f32[2,128,128]{2,1,0:T(8,128)S(1)} %get-tuple-element.77), channel_id=1, source_target_pairs={{0,24},{4,28},{8,16},{12,20},{16,8},{20,12},{24,0},{28,4},{1,25},{... | collective-permute-start | bytes 393224 | tf_op jit(solution)/shard_map/ppermute | solution.py:686
  32.8 0.0 copy-done.1
  32.8 1.2 %shard_map.121 = (f32[32,16,128]{2,1,0:T(8,128)}, f32[32,16,128]{2,1,0:T(8,128)}) custom-call(s32[32]{0:T(128)S(1)} %copy-done.1, f32[2,128,128]{2,1,0:T(8,128)S(1)} %get-tuple-element.79.refs_0_), custom_call_target="tpu_custom_call" | custom-call | tf_op jit(solution)/shard_map/pallas_call | solution.py:659
  34.1 1.6 %collective-permute-done.11.refs_0_ = f32[2,128,128]{2,1,0:T(8,128)S(1)} collective-permute-done((f32[2,128,128]{2,1,0:T(8,128)S(1)}, f32[2,128,128]{2,1,0:T(8,128)S(1)}, u32[]{:S(2)}, u32[]{:S(2)}) %collective-permute-start.11) | collective-permute-done | bytes 131104 | tf_op jit(solution)/shard_map/ppermute | solution.py:686
  35.7 1.2 %shard_map.122 = (f32[32,16,128]{2,1,0:T(8,128)}, f32[32,16,128]{2,1,0:T(8,128)}) custom-call(s32[32]{0:T(128)S(1)} %copy-done.1, f32[2,128,128]{2,1,0:T(8,128)S(1)} %collective-permute-done.11.refs_0_, f32[32,16,128]{2,1,0:T(8,128)} %get-tuple-element.80.refs_1_, f32[32,16,128]{2,1,0:T(8,128)} %get-tuple-element.81.refs_2_), custom_call_target="tpu_custom_call", output_to_operand_aliasing={{0}: (2, {}), {1}: (3, {})} | custom-call | tf_op jit(solution)/shard_map/pallas_call | solution.py:659
  36.9 0.0 collective-permute-done.9.refs_0_
  36.9 1.4 %collective-permute-done.10.refs_1_ = f32[2,128,128]{2,1,0:T(8,128)S(1)} collective-permute-done((f32[2,128,128]{2,1,0:T(8,128)S(1)}, f32[2,128,128]{2,1,0:T(8,128)S(1)}, u32[]{:S(2)}, u32[]{:S(2)}) %collective-permute-start.10) | collective-permute-done | bytes 131104 | tf_op jit(solution)/shard_map/ppermute | solution.py:686
  38.3 1.3 %shard_map.123 = (f32[32,16,128]{2,1,0:T(8,128)}, f32[32,16,128]{2,1,0:T(8,128)}) custom-call(s32[32]{0:T(128)S(1)} %copy-done.1, f32[2,128,128]{2,1,0:T(8,128)S(1)} %collective-permute-done.9.refs_0_, f32[2,128,128]{2,1,0:T(8,128)S(1)} %collective-permute-done.10.refs_1_, ...), custom_call_target="tpu_custom_call", output_to_operand_aliasing={{0}: (3, {}), {1}: (4, {})} | custom-call | tf_op jit(solution)/shard_map/pallas_call | solution.py:659
  (2 shorter events, 0.1 us)
Async XLA Ops:
  1.8 1.6 %collective-permute-start = (f32[4,96,128]{2,1,0:T(8,128)S(1)}, f32[4,96,128]{2,1,0:T(8,128)S(1)}, u32[]{:S(2)}, u32[]{:S(2)}) collective-permute-start(f32[4,96,128]{2,1,0:T(8,128)S(1)} %get-tuple-element.44), channel_id=1, source_target_pairs={{0,4},{4,0},{8,12},{12,8},{16,20},{20,16},{24,28},{28,24},{1,5},{5... | collective-permute-start | bytes 589832 | tf_op jit(solution)/shard_map/ppermute | solution.py:686
  3.5 12.3 %copy-start = (f32[8,4,4,5,5]{0,2,4,3,1:T(4,128)S(1)}, f32[8,4,4,5,5]{0,2,4,3,1:T(4,128)}, u32[]{:S(2)}) copy-start(f32[8,4,4,5,5]{0,2,4,3,1:T(4,128)} %param.12) | copy-start | bytes 38404
  3.5 6.1 %collective-permute-start.1 = (f32[2,96,128]{2,1,0:T(8,128)S(1)}, f32[2,96,128]{2,1,0:T(8,128)S(1)}, u32[]{:S(2)}, u32[]{:S(2)}) collective-permute-start(f32[2,96,128]{2,1,0:T(8,128)S(1)} %get-tuple-element.50), channel_id=1, source_target_pairs={{0,8},{4,12},{8,0},{12,4},{16,24},{20,28},{24,16},{28,20},{1,9},{5... | collective-permute-start | bytes 294920 | tf_op jit(solution)/shard_map/ppermute | solution.py:686
  6.4 5.8 %collective-permute-start.2 = (f32[2,96,128]{2,1,0:T(8,128)S(1)}, f32[2,96,128]{2,1,0:T(8,128)S(1)}, u32[]{:S(2)}, u32[]{:S(2)}) collective-permute-start(f32[2,96,128]{2,1,0:T(8,128)S(1)} %get-tuple-element.51), channel_id=1, source_target_pairs={{0,16},{4,20},{8,24},{12,28},{16,0},{20,4},{24,8},{28,12},{1,17},{... | collective-permute-start | bytes 294920 | tf_op jit(solution)/shard_map/ppermute | solution.py:686
  7.9 5.5 %collective-permute-start.3 = (f32[2,96,128]{2,1,0:T(8,128)S(1)}, f32[2,96,128]{2,1,0:T(8,128)S(1)}, u32[]{:S(2)}, u32[]{:S(2)}) collective-permute-start(f32[2,96,128]{2,1,0:T(8,128)S(1)} %get-tuple-element.52), channel_id=1, source_target_pairs={{0,24},{4,28},{8,16},{12,20},{16,8},{20,12},{24,0},{28,4},{1,25},{... | collective-permute-start | bytes 294920 | tf_op jit(solution)/shard_map/ppermute | solution.py:686
  14.1 5.0 %collective-permute-start.4 = (f32[2,4,32,128]{3,2,1,0:T(8,128)S(1)}, f32[2,4,32,128]{3,2,1,0:T(8,128)S(1)}, u32[]{:S(2)}, u32[]{:S(2)}) collective-permute-start(f32[2,4,32,128]{3,2,1,0:T(8,128)S(1)} %get-tuple-element.56), channel_id=1, source_target_pairs={{0,1},{1,0},{2,3},{3,2},{4,5},{5,4},{6,7},{7,6},{8,9},{9,8},{10,11... | collective-permute-start | bytes 393224 | tf_op jit(solution)/shard_map/ppermute | solution.py:638
  15.8 3.4 %collective-permute-start.5 = (f32[2,4,32,128]{3,2,1,0:T(8,128)S(1)}, f32[2,4,32,128]{3,2,1,0:T(8,128)S(1)}, u32[]{:S(2)}, u32[]{:S(2)}) collective-permute-start(f32[2,4,32,128]{3,2,1,0:T(8,128)S(1)} %get-tuple-element.57), channel_id=1, source_target_pairs={{0,4},{1,2},{2,1},{3,7},{4,0},{5,6},{6,5},{7,3},{8,12},{9,10},{10,... | collective-permute-start | bytes 393224 | tf_op jit(solution)/shard_map/ppermute | solution.py:638
  20.7 5.7 %collective-permute-start.6 = (f32[2,4,32,128]{3,2,1,0:T(8,128)S(1)}, f32[2,4,32,128]{3,2,1,0:T(8,128)S(1)}, u32[]{:S(2)}, u32[]{:S(2)}) collective-permute-start(f32[2,4,32,128]{3,2,1,0:T(8,128)S(1)} %get-tuple-element.65), channel_id=1, source_target_pairs={{0,1},{1,0},{2,3},{3,2},{4,5},{5,4},{6,7},{7,6},{8,9},{9,8},{10,11... | collective-permute-start | bytes 393224 | tf_op jit(solution)/shard_map/ppermute | solution.py:638
  23.4 3.0 %collective-permute-start.7 = (f32[2,4,32,128]{3,2,1,0:T(8,128)S(1)}, f32[2,4,32,128]{3,2,1,0:T(8,128)S(1)}, u32[]{:S(2)}, u32[]{:S(2)}) collective-permute-start(f32[2,4,32,128]{3,2,1,0:T(8,128)S(1)} %get-tuple-element.66), channel_id=1, source_target_pairs={{0,4},{1,2},{2,1},{3,7},{4,0},{5,6},{6,5},{7,3},{8,12},{9,10},{10,... | collective-permute-start | bytes 393224 | tf_op jit(solution)/shard_map/ppermute | solution.py:638
  27.6 1.6 %collective-permute-start.8 = (f32[4,128,128]{2,1,0:T(8,128)S(1)}, f32[4,128,128]{2,1,0:T(8,128)S(1)}, u32[]{:S(2)}, u32[]{:S(2)}) collective-permute-start(f32[4,128,128]{2,1,0:T(8,128)S(1)} %get-tuple-element.71), channel_id=1, source_target_pairs={{0,4},{4,0},{8,12},{12,8},{16,20},{20,16},{24,28},{28,24},{1,5},{5... | collective-permute-start | bytes 786440 | tf_op jit(solution)/shard_map/ppermute | solution.py:686
  29.2 6.4 %collective-permute-start.11 = (f32[2,128,128]{2,1,0:T(8,128)S(1)}, f32[2,128,128]{2,1,0:T(8,128)S(1)}, u32[]{:S(2)}, u32[]{:S(2)}) collective-permute-start(f32[2,128,128]{2,1,0:T(8,128)S(1)} %get-tuple-element.78), channel_id=1, source_target_pairs={{0,8},{4,12},{8,0},{12,4},{16,24},{20,28},{24,16},{28,20},{1,9},{5... | collective-permute-start | bytes 393224 | tf_op jit(solution)/shard_map/ppermute | solution.py:686
  30.2 6.7 %collective-permute-start.9 = (f32[2,128,128]{2,1,0:T(8,128)S(1)}, f32[2,128,128]{2,1,0:T(8,128)S(1)}, u32[]{:S(2)}, u32[]{:S(2)}) collective-permute-start(f32[2,128,128]{2,1,0:T(8,128)S(1)} %get-tuple-element.76), channel_id=1, source_target_pairs={{0,16},{4,20},{8,24},{12,28},{16,0},{20,4},{24,8},{28,12},{1,17},{... | collective-permute-start | bytes 393224 | tf_op jit(solution)/shard_map/ppermute | solution.py:686
  31.1 1.7 %copy-start.1 = (s32[32]{0:T(128)S(1)}, s32[32]{0:T(128)}, u32[]{:S(2)}) copy-start(s32[32]{0:T(128)} %order_in.5) | copy-start | bytes 388
  31.1 7.2 %collective-permute-start.10 = (f32[2,128,128]{2,1,0:T(8,128)S(1)}, f32[2,128,128]{2,1,0:T(8,128)S(1)}, u32[]{:S(2)}, u32[]{:S(2)}) collective-permute-start(f32[2,128,128]{2,1,0:T(8,128)S(1)} %get-tuple-element.77), channel_id=1, source_target_pairs={{0,24},{4,28},{8,16},{12,20},{16,8},{20,12},{24,0},{28,4},{1,25},{... | collective-permute-start | bytes 393224 | tf_op jit(solution)/shard_map/ppermute | solution.py:686

commit v5 on v4

--- a/solution.py
+++ b/solution.py
@@ -220,6 +220,7 @@
 
 
 CHUNK = 96
+CHIPS = (0, 3, 1, 2)
 AT_VALUES, AT_NORMALS, AT_COEFFS, AT_MISC = 64, 72, 84, 88
 
 
@@ -323,9 +324,9 @@
     parts, refs = refs[:4], refs[4:]
     chunks, smoothed, even, odd, table, scale, root, expanded, first, rows = refs
     me = lax.axis_index("depth")
-    for k in range(4):
+    for k, part in zip(CHIPS, parts):
         for half in range(2):
-            chunks[me ^ (2 * k + half)] = parts[k][half]
+            chunks[me ^ (2 * k + half)] = part[half]
     repeat_coeffs(chunks, expanded)
     lags = {}
 
@@ -377,28 +378,31 @@
         return jnp.where(inside, pltpu.roll(value, -shift % 128, 1), 0.0)
 
     def some_depths(k, carry):
-        depths = pl.ds(pl.multiple_of(k * 8, 8), 8)
-        total = [[start(y, o, depths) for o in range(4)] for y in range(4)]
+        pieces = [pl.ds(pl.multiple_of(k * 16 + 8 * n, 8), 8) for n in range(2)]
+        total = [[[start(y, o, at) for at in pieces] for o in range(4)] for y in range(4)]
         for i in range(4):
-            lines = {row: read(row, i, depths) for row in rows_in}
+            lines = {row: [read(row, i, at) for at in pieces] for row in rows_in}
             for w in range(5):
-                if adjoint:
-                    taps = [[tap(table, i, o, h, w) for h in range(5)] for o in range(4)]
-                else:
-                    taps = [[tap(table, o, i, h, w) for h in range(5)] for o in range(4)]
-                for row in rows_in:
-                    line = moved(lines[row], 2 - w if adjoint else w - 2)
-                    for y in range(4):
-                        h = y - row + 2 if adjoint else row - y + 2
-                        if 0 <= h < 5:
-                            for o in range(4):
-                                total[y][o] = total[y][o] + taps[o][h] * line
+                shift = 2 - w if adjoint else w - 2
+                shifted_lines = {
+                    row: [moved(value, shift) for value in lines[row]] for row in rows_in
+                }
+                for h in range(5):
+                    rows = [y - h + 2 if adjoint else y + h - 2 for y in range(4)]
+                    for o in range(4):
+                        weight = tap(table, i, o, h, w) if adjoint else tap(table, o, i, h, w)
+                        for y, row in enumerate(rows):
+                            if row in rows_in:
+                                for n in range(2):
+                                    line = shifted_lines[row][n]
+                                    total[y][o][n] = total[y][o][n] + weight * line
         for y in range(4):
             for o in range(4):
-                write(y, o, depths, total[y][o])
+                for n in range(2):
+                    write(y, o, pieces[n], total[y][o][n])
         return carry
 
-    lax.fori_loop(0, 4, some_depths, 0)
+    lax.fori_loop(0, 2, some_depths, 0)
 
 
 OWN = (0, 1, 2, 3)
@@ -605,7 +609,8 @@
         target[64:, :] = out[me ^ place]
 
 
-def unpack_kernel(first, count, order_in, *refs):
+def unpack_kernel(chips, order_in, *refs):
+    count = len(chips)
     parts, (potential, gradient, planes, order, sent) = refs[:count], refs[-5:]
     numbers = pltpu.make_async_copy(order_in, order, sent.at[2])
     numbers.start()
@@ -618,7 +623,8 @@
     numbers.wait()
     me = lax.axis_index("depth")
     for slot in range(8 * count):
-        channel = order[(me ^ (2 * first + slot // 4)) * 4 + slot % 4]
+        place = 2 * chips[slot // 8] + slot // 4 % 2
+        channel = order[(me ^ place) * 4 + slot % 4]
         for half, out in enumerate((potential, gradient)):
             pltpu.make_async_copy(planes.at[half, slot], out.at[channel], sent.at[half]).start()
     for half, out in enumerate((potential, gradient)):
@@ -687,7 +693,7 @@
 
         both = f32(2, rows, 128)
         joined = call(join_kernel, (both,) * 4, (swap(give, 1), *keep))
-        return [joined[0]] + [swap(joined[k], 2 * k) for k in range(1, 4)]
+        return [joined[k] if k == 0 else swap(joined[k], 2 * k) for k in CHIPS]
 
     def staged(rows):
         return (f32(4, rows, 128),) + (f32(2, rows, 128),) * 4
@@ -732,11 +738,12 @@
     )
     parts = exchange(128, *results)
     outs = ()
-    for k, count in ((0, 1), (1, 1), (2, 2)):
+    for some in (slice(0, 1), slice(1, 2), slice(2, 4)):
+        count = len(CHIPS[some])
         outs = call(
-            functools.partial(unpack_kernel, k, count),
+            functools.partial(unpack_kernel, CHIPS[some]),
             (by_depth, by_depth),
-            (channel_order, *parts[k : k + count], *outs),
+            (channel_order, *parts[some], *outs),
             [
                 pltpu.VMEM((2, 8 * count, 16, 128), jnp.float32),
                 pltpu.SMEM((32,), jnp.int32),

time: 39.8 us -> 39.4 us (0.990)
  Pallas kernels: 12.7 us -> 12 us
    pallas_call x11, Pallas kernels: 12.7 us -> 12 us  [call(): pl.pallas_call(kernel, out_shape=outs, in_specs=ins or [in_vmem] * len(op...]
    ppermute x8, waiting for transfers between devices: 11.1 us -> 10.6 us  [swap(): return lax.ppermute(value, 'depth', [(i, i ^ flip) for i in range(8)])]
  transfers between devices with their start and end apart: 12 -> 12, of which waited for: 9 -> 8; matrix products, arithmetic and copies ran while one was open for 0% -> 0% of each run, Pallas kernels for 17% -> 16%
where the time goes in v5:
time: 39.4 us; the launch traced here: 39.2 us
  starting transfers between devices  13.2 us (34%)
  waiting for transfers between devices  13 us (33%)
  Pallas kernels  12 us (30%)
  between operations  0.73 us (2%)
    pallas_call x11, Pallas kernels, call(): pl.pallas_call(kernel, out_shape=outs, in_specs=ins or [in_vmem] * len(op...  12 us
    ppermute x8, waiting for transfers between devices, swap(): return lax.ppermute(value, 'depth', [(i, i ^ flip) for i in range(8)])  10.6 us
    ppermute x8, starting transfers between devices, swap(): return lax.ppermute(value, 'depth', [(i, i ^ flip) for i in range(8)])  8.66 us
    ppermute x4, starting transfers between devices, swap(): return lax.ppermute(value, ('depth', 'inline'), pairs)  4.5 us
    ppermute x4, waiting for transfers between devices, swap(): return lax.ppermute(value, ('depth', 'inline'), pairs)  2.38 us
  transfers between devices with their start and end apart: 12, of which 8 were waited for; matrix products, arithmetic and copies ran while one was open for 0% of the time, Pallas kernels for 16%

profile of v5, /device:TPU:0, one launch (start us, length us, event | category | flops | bytes accessed | tf_op | source)
XLA Modules:
  0.0 39.2 jit_solution(15506845126668304385)
XLA Ops:
  0.6 1.2 %shard_map.113 = (f32[4,96,128]{2,1,0:T(8,128)S(1)}, f32[2,96,128]{2,1,0:T(8,128)S(1)}, f32[2,96,128]{2,1,0:T(8,128)S(1)}, f32[2,96,128]{2,1,0:T(8,128)S(1)}, f32[2,96,128]{2,1,0:T(8,128)S(1)}) custom-call(s32[32]{0:T(128)} %order_in.5, f32[16,32]{1,0:T(8,128)} %bitcast.17, f32[64,128]{1,0:T(8,128)} %bitcast.16, f32[96,128]{1,0:T(8,128)} %bitcast.15, ...), custom_call_target="tpu_custom_call" | custom-call | tf_op jit(solution)/shard_map/pallas_call | solution.py:665
  1.8 0.5 %collective-permute-start = (f32[4,96,128]{2,1,0:T(8,128)S(1)}, f32[4,96,128]{2,1,0:T(8,128)S(1)}, u32[]{:S(2)}, u32[]{:S(2)}) collective-permute-start(f32[4,96,128]{2,1,0:T(8,128)S(1)} %get-tuple-element.44), channel_id=1, source_target_pairs={{0,4},{4,0},{8,12},{12,8},{16,20},{20,16},{24,28},{28,24},{1,5},{5... | collective-permute-start | bytes 589832 | tf_op jit(solution)/shard_map/ppermute | solution.py:692
  2.4 1.1 %collective-permute-done.got = f32[4,96,128]{2,1,0:T(8,128)S(1)} collective-permute-done((f32[4,96,128]{2,1,0:T(8,128)S(1)}, f32[4,96,128]{2,1,0:T(8,128)S(1)}, u32[]{:S(2)}, u32[]{:S(2)}) %collective-permute-start) | collective-permute-done | bytes 196640 | tf_op jit(solution)/shard_map/ppermute | solution.py:692
  3.5 0.0 copy-start
  3.5 3.9 %collective-permute-start.1 = (f32[2,96,128]{2,1,0:T(8,128)S(1)}, f32[2,96,128]{2,1,0:T(8,128)S(1)}, u32[]{:S(2)}, u32[]{:S(2)}) collective-permute-start(f32[2,96,128]{2,1,0:T(8,128)S(1)} %get-tuple-element.50), channel_id=1, source_target_pairs={{0,24},{4,28},{8,16},{12,20},{16,8},{20,12},{24,0},{28,4},{1,25},{... | collective-permute-start | bytes 294920 | tf_op jit(solution)/shard_map/ppermute | solution.py:692
  7.3 0.5 %collective-permute-start.2 = (f32[2,96,128]{2,1,0:T(8,128)S(1)}, f32[2,96,128]{2,1,0:T(8,128)S(1)}, u32[]{:S(2)}, u32[]{:S(2)}) collective-permute-start(f32[2,96,128]{2,1,0:T(8,128)S(1)} %get-tuple-element.51), channel_id=1, source_target_pairs={{0,8},{4,12},{8,0},{12,4},{16,24},{20,28},{24,16},{28,20},{1,9},{5... | collective-permute-start | bytes 294920 | tf_op jit(solution)/shard_map/ppermute | solution.py:692
  7.9 0.1 collective-permute-start.3
  8.0 2.9 %collective-permute-done.1.refs_1_ = f32[2,96,128]{2,1,0:T(8,128)S(1)} collective-permute-done((f32[2,96,128]{2,1,0:T(8,128)S(1)}, f32[2,96,128]{2,1,0:T(8,128)S(1)}, u32[]{:S(2)}, u32[]{:S(2)}) %collective-permute-start.1) | collective-permute-done | bytes 98336 | tf_op jit(solution)/shard_map/ppermute | solution.py:692
  10.9 1.9 %collective-permute-done.2.refs_2_ = f32[2,96,128]{2,1,0:T(8,128)S(1)} collective-permute-done((f32[2,96,128]{2,1,0:T(8,128)S(1)}, f32[2,96,128]{2,1,0:T(8,128)S(1)}, u32[]{:S(2)}, u32[]{:S(2)}) %collective-permute-start.2) | collective-permute-done | bytes 98336 | tf_op jit(solution)/shard_map/ppermute | solution.py:692
  12.8 0.0 collective-permute-done.3.refs_3_
  12.8 0.7 %shard_map.115 = (f32[8,96,128]{2,1,0:T(8,128)S(1)}, f32[4,4,32,128]{3,2,1,0:T(8,128)S(1)}, f32[2,4,32,128]{3,2,1,0:T(8,128)S(1)}, f32[2,4,32,128]{3,2,1,0:T(8,1...) custom-call(f32[2,96,128]{2,1,0:T(8,128)S(1)} %get-tuple-element.49.refs_0_, ...), custom_call_target="tpu_custom_call" | custom-call | tf_op jit(solution)/shard_map/pallas_call | solution.py:665
  13.5 1.7 %collective-permute-start.4 = (f32[2,4,32,128]{3,2,1,0:T(8,128)S(1)}, f32[2,4,32,128]{3,2,1,0:T(8,128)S(1)}, u32[]{:S(2)}, u32[]{:S(2)}) collective-permute-start(f32[2,4,32,128]{3,2,1,0:T(8,128)S(1)} %get-tuple-element.56), channel_id=1, source_target_pairs={{0,1},{1,0},{2,3},{3,2},{4,5},{5,4},{6,7},{7,6},{8,9},{9,8},{10,11... | collective-permute-start | bytes 393224 | tf_op jit(solution)/shard_map/ppermute | solution.py:644
  15.2 0.0 collective-permute-start.5
  15.2 0.0 copy-done
  15.2 2.2 %shard_map.116 = (f32[4,4,32,128]{3,2,1,0:T(8,128)S(1)}, f32[4,4,32,128]{3,2,1,0:T(8,128)S(1)}, f32[4,32,128]{2,1,0:T(8,128)S(1)}, f32[4,32,128]{2,1,0:T(8,128)S(1)}, f32[400,128]{1,0:T(8,128)S(1)}) custom-call(f32[8,96,128]{2,1,0:T(8,128)S(1)} %get-tuple-element.53.chunks.refs_0_, f32[4,4,32,128]{3,2,1,0:T(8,128)S(1)} %get-tuple-element.54.smoothed, ...), custom_call_target="tpu_custom_call" | custom-call | tf_op jit(solution)/shard_map/pallas_call | solution.py:665
  17.4 1.1 %collective-permute-done.4.even_in = f32[2,4,32,128]{3,2,1,0:T(8,128)S(1)} collective-permute-done((f32[2,4,32,128]{3,2,1,0:T(8,128)S(1)}, f32[2,4,32,128]{3,2,1,0:T(8,128)S(1)}, u32[]{:S(2)}, u32[]{:S(2)}) %collective-permute-start.4) | collective-permute-done | bytes 131104 | tf_op jit(solution)/shard_map/ppermute | solution.py:644
  18.6 0.0 collective-permute-done.5.odd_in
  18.6 1.3 %shard_map.117 = (f32[4,4,32,128]{3,2,1,0:T(8,128)S(1)}, f32[4,4,32,128]{3,2,1,0:T(8,128)S(1)}, f32[2,4,32,128]{3,2,1,0:T(8,128)S(1)}, f32[2,4,32,128]{3,2,1,0:T(8,128)S(1)}) custom-call(f32[4,4,32,128]{3,2,1,0:T(8,128)S(1)} %get-tuple-element.55.partial, f32[2,4,32,128]{3,2,1,0:T(8,128)S(1)} %collective-permute-done.4.even_in, ...), custom_call_target="tpu_custom_call" | custom-call | tf_op jit(solution)/shard_map/pallas_call | solution.py:665
  19.9 2.8 %collective-permute-start.6 = (f32[2,4,32,128]{3,2,1,0:T(8,128)S(1)}, f32[2,4,32,128]{3,2,1,0:T(8,128)S(1)}, u32[]{:S(2)}, u32[]{:S(2)}) collective-permute-start(f32[2,4,32,128]{3,2,1,0:T(8,128)S(1)} %get-tuple-element.65), channel_id=1, source_target_pairs={{0,1},{1,0},{2,3},{3,2},{4,5},{5,4},{6,7},{7,6},{8,9},{9,8},{10,11... | collective-permute-start | bytes 393224 | tf_op jit(solution)/shard_map/ppermute | solution.py:644
  22.7 0.0 collective-permute-start.7
  22.7 1.7 %shard_map.118 = (f32[4,4,32,128]{3,2,1,0:T(8,128)S(1)}, f32[8,64,128]{2,1,0:T(8,128)S(1)}) custom-call(f32[4,4,32,128]{3,2,1,0:T(8,128)S(1)} %get-tuple-element.62.forcing, f32[400,128]{1,0:T(8,128)S(1)} %get-tuple-element.58.table.refs_4_, f32[4,4,32,128]{3,2,1,0:T(8,128)S(1)} %get-tuple-element.63.potential), custom_call_target="tpu_custom_call" | custom-call | tf_op jit(solution)/shard_map/pallas_call | solution.py:665
  24.4 1.2 %collective-permute-done.6.refs_2_ = f32[2,4,32,128]{3,2,1,0:T(8,128)S(1)} collective-permute-done((f32[2,4,32,128]{3,2,1,0:T(8,128)S(1)}, f32[2,4,32,128]{3,2,1,0:T(8,128)S(1)}, u32[]{:S(2)}, u32[]{:S(2)}) %collective-permute-start.6) | collective-permute-done | bytes 131104 | tf_op jit(solution)/shard_map/ppermute | solution.py:644
  25.7 0.0 collective-permute-done.7.refs_3_
  25.7 1.1 %shard_map.119 = (f32[4,128,128]{2,1,0:T(8,128)S(1)}, f32[2,128,128]{2,1,0:T(8,128)S(1)}, f32[2,128,128]{2,1,0:T(8,128)S(1)}, f32[2,128,128]{2,1,0:T(8,128)S(1)}, f32[2,128,128]{2,1,0:T(8,128)S(1)}) custom-call(f32[8,96,128]{2,1,0:T(8,128)S(1)} %get-tuple-element.53.chunks.refs_0_, f32[4,4,32,128]{3,2,1,0:T(8,128)S(1)} %get-tuple-element.64.refs_1_, ...), custom_call_target="tpu_custom_call" | custom-call | tf_op jit(solution)/shard_map/pallas_call | solution.py:665
  26.7 0.1 collective-permute-start.8
  26.8 1.5 %collective-permute-done.8.got = f32[4,128,128]{2,1,0:T(8,128)S(1)} collective-permute-done((f32[4,128,128]{2,1,0:T(8,128)S(1)}, f32[4,128,128]{2,1,0:T(8,128)S(1)}, u32[]{:S(2)}, u32[]{:S(2)}) %collective-permute-start.8) | collective-permute-done | bytes 262176 | tf_op jit(solution)/shard_map/ppermute | solution.py:692
  28.4 2.6 %collective-permute-start.11 = (f32[2,128,128]{2,1,0:T(8,128)S(1)}, f32[2,128,128]{2,1,0:T(8,128)S(1)}, u32[]{:S(2)}, u32[]{:S(2)}) collective-permute-start(f32[2,128,128]{2,1,0:T(8,128)S(1)} %get-tuple-element.78), channel_id=1, source_target_pairs={{0,24},{4,28},{8,16},{12,20},{16,8},{20,12},{24,0},{28,4},{1,25},{... | collective-permute-start | bytes 393224 | tf_op jit(solution)/shard_map/ppermute | solution.py:692
  31.0 0.5 %collective-permute-start.9 = (f32[2,128,128]{2,1,0:T(8,128)S(1)}, f32[2,128,128]{2,1,0:T(8,128)S(1)}, u32[]{:S(2)}, u32[]{:S(2)}) collective-permute-start(f32[2,128,128]{2,1,0:T(8,128)S(1)} %get-tuple-element.76), channel_id=1, source_target_pairs={{0,8},{4,12},{8,0},{12,4},{16,24},{20,28},{24,16},{28,20},{1,9},{5... | collective-permute-start | bytes 393224 | tf_op jit(solution)/shard_map/ppermute | solution.py:692
  31.6 0.0 copy-start.1
  31.6 0.4 collective-permute-start.10
  31.9 0.3 copy-done.1
  32.2 1.2 %shard_map.121 = (f32[32,16,128]{2,1,0:T(8,128)}, f32[32,16,128]{2,1,0:T(8,128)}) custom-call(s32[32]{0:T(128)S(1)} %copy-done.1, f32[2,128,128]{2,1,0:T(8,128)S(1)} %get-tuple-element.79.refs_0_), custom_call_target="tpu_custom_call" | custom-call | tf_op jit(solution)/shard_map/pallas_call | solution.py:665
  33.5 2.2 %collective-permute-done.11.refs_0_ = f32[2,128,128]{2,1,0:T(8,128)S(1)} collective-permute-done((f32[2,128,128]{2,1,0:T(8,128)S(1)}, f32[2,128,128]{2,1,0:T(8,128)S(1)}, u32[]{:S(2)}, u32[]{:S(2)}) %collective-permute-start.11) | collective-permute-done | bytes 131104 | tf_op jit(solution)/shard_map/ppermute | solution.py:692
  35.7 1.2 %shard_map.122 = (f32[32,16,128]{2,1,0:T(8,128)}, f32[32,16,128]{2,1,0:T(8,128)}) custom-call(s32[32]{0:T(128)S(1)} %copy-done.1, f32[2,128,128]{2,1,0:T(8,128)S(1)} %collective-permute-done.11.refs_0_, f32[32,16,128]{2,1,0:T(8,128)} %get-tuple-element.80.refs_1_, f32[32,16,128]{2,1,0:T(8,128)} %get-tuple-element.81.refs_2_), custom_call_target="tpu_custom_call", output_to_operand_aliasing={{0}: (2, {}), {1}: (3, {})} | custom-call | tf_op jit(solution)/shard_map/pallas_call | solution.py:665
  36.9 1.0 %collective-permute-done.9.refs_0_ = f32[2,128,128]{2,1,0:T(8,128)S(1)} collective-permute-done((f32[2,128,128]{2,1,0:T(8,128)S(1)}, f32[2,128,128]{2,1,0:T(8,128)S(1)}, u32[]{:S(2)}, u32[]{:S(2)}) %collective-permute-start.9) | collective-permute-done | bytes 131104 | tf_op jit(solution)/shard_map/ppermute | solution.py:692
  37.9 0.0 collective-permute-done.10.refs_1_
  37.9 1.3 %shard_map.123 = (f32[32,16,128]{2,1,0:T(8,128)}, f32[32,16,128]{2,1,0:T(8,128)}) custom-call(s32[32]{0:T(128)S(1)} %copy-done.1, f32[2,128,128]{2,1,0:T(8,128)S(1)} %collective-permute-done.9.refs_0_, f32[2,128,128]{2,1,0:T(8,128)S(1)} %collective-permute-done.10.refs_1_, ...), custom_call_target="tpu_custom_call", output_to_operand_aliasing={{0}: (3, {}), {1}: (4, {})} | custom-call | tf_op jit(solution)/shard_map/pallas_call | solution.py:665
  (2 shorter events, 0.1 us)
Async XLA Ops:
  1.8 1.6 %collective-permute-start = (f32[4,96,128]{2,1,0:T(8,128)S(1)}, f32[4,96,128]{2,1,0:T(8,128)S(1)}, u32[]{:S(2)}, u32[]{:S(2)}) collective-permute-start(f32[4,96,128]{2,1,0:T(8,128)S(1)} %get-tuple-element.44), channel_id=1, source_target_pairs={{0,4},{4,0},{8,12},{12,8},{16,20},{20,16},{24,28},{28,24},{1,5},{5... | collective-permute-start | bytes 589832 | tf_op jit(solution)/shard_map/ppermute | solution.py:692
  3.5 11.8 %copy-start = (f32[8,4,4,5,5]{0,2,4,3,1:T(4,128)S(1)}, f32[8,4,4,5,5]{0,2,4,3,1:T(4,128)}, u32[]{:S(2)}) copy-start(f32[8,4,4,5,5]{0,2,4,3,1:T(4,128)} %param.12) | copy-start | bytes 38404
  3.5 7.5 %collective-permute-start.1 = (f32[2,96,128]{2,1,0:T(8,128)S(1)}, f32[2,96,128]{2,1,0:T(8,128)S(1)}, u32[]{:S(2)}, u32[]{:S(2)}) collective-permute-start(f32[2,96,128]{2,1,0:T(8,128)S(1)} %get-tuple-element.50), channel_id=1, source_target_pairs={{0,24},{4,28},{8,16},{12,20},{16,8},{20,12},{24,0},{28,4},{1,25},{... | collective-permute-start | bytes 294920 | tf_op jit(solution)/shard_map/ppermute | solution.py:692
  7.3 5.5 %collective-permute-start.2 = (f32[2,96,128]{2,1,0:T(8,128)S(1)}, f32[2,96,128]{2,1,0:T(8,128)S(1)}, u32[]{:S(2)}, u32[]{:S(2)}) collective-permute-start(f32[2,96,128]{2,1,0:T(8,128)S(1)} %get-tuple-element.51), channel_id=1, source_target_pairs={{0,8},{4,12},{8,0},{12,4},{16,24},{20,28},{24,16},{28,20},{1,9},{5... | collective-permute-start | bytes 294920 | tf_op jit(solution)/shard_map/ppermute | solution.py:692
  7.9 4.9 %collective-permute-start.3 = (f32[2,96,128]{2,1,0:T(8,128)S(1)}, f32[2,96,128]{2,1,0:T(8,128)S(1)}, u32[]{:S(2)}, u32[]{:S(2)}) collective-permute-start(f32[2,96,128]{2,1,0:T(8,128)S(1)} %get-tuple-element.52), channel_id=1, source_target_pairs={{0,16},{4,20},{8,24},{12,28},{16,0},{20,4},{24,8},{28,12},{1,17},{... | collective-permute-start | bytes 294920 | tf_op jit(solution)/shard_map/ppermute | solution.py:692
  13.5 5.0 %collective-permute-start.4 = (f32[2,4,32,128]{3,2,1,0:T(8,128)S(1)}, f32[2,4,32,128]{3,2,1,0:T(8,128)S(1)}, u32[]{:S(2)}, u32[]{:S(2)}) collective-permute-start(f32[2,4,32,128]{3,2,1,0:T(8,128)S(1)} %get-tuple-element.56), channel_id=1, source_target_pairs={{0,1},{1,0},{2,3},{3,2},{4,5},{5,4},{6,7},{7,6},{8,9},{9,8},{10,11... | collective-permute-start | bytes 393224 | tf_op jit(solution)/shard_map/ppermute | solution.py:644
  15.2 3.4 %collective-permute-start.5 = (f32[2,4,32,128]{3,2,1,0:T(8,128)S(1)}, f32[2,4,32,128]{3,2,1,0:T(8,128)S(1)}, u32[]{:S(2)}, u32[]{:S(2)}) collective-permute-start(f32[2,4,32,128]{3,2,1,0:T(8,128)S(1)} %get-tuple-element.57), channel_id=1, source_target_pairs={{0,4},{1,2},{2,1},{3,7},{4,0},{5,6},{6,5},{7,3},{8,12},{9,10},{10,... | collective-permute-start | bytes 393224 | tf_op jit(solution)/shard_map/ppermute | solution.py:644
  19.9 5.8 %collective-permute-start.6 = (f32[2,4,32,128]{3,2,1,0:T(8,128)S(1)}, f32[2,4,32,128]{3,2,1,0:T(8,128)S(1)}, u32[]{:S(2)}, u32[]{:S(2)}) collective-permute-start(f32[2,4,32,128]{3,2,1,0:T(8,128)S(1)} %get-tuple-element.65), channel_id=1, source_target_pairs={{0,1},{1,0},{2,3},{3,2},{4,5},{5,4},{6,7},{7,6},{8,9},{9,8},{10,11... | collective-permute-start | bytes 393224 | tf_op jit(solution)/shard_map/ppermute | solution.py:644
  22.7 3.0 %collective-permute-start.7 = (f32[2,4,32,128]{3,2,1,0:T(8,128)S(1)}, f32[2,4,32,128]{3,2,1,0:T(8,128)S(1)}, u32[]{:S(2)}, u32[]{:S(2)}) collective-permute-start(f32[2,4,32,128]{3,2,1,0:T(8,128)S(1)} %get-tuple-element.66), channel_id=1, source_target_pairs={{0,4},{1,2},{2,1},{3,7},{4,0},{5,6},{6,5},{7,3},{8,12},{9,10},{10,... | collective-permute-start | bytes 393224 | tf_op jit(solution)/shard_map/ppermute | solution.py:644
  26.7 1.6 %collective-permute-start.8 = (f32[4,128,128]{2,1,0:T(8,128)S(1)}, f32[4,128,128]{2,1,0:T(8,128)S(1)}, u32[]{:S(2)}, u32[]{:S(2)}) collective-permute-start(f32[4,128,128]{2,1,0:T(8,128)S(1)} %get-tuple-element.71), channel_id=1, source_target_pairs={{0,4},{4,0},{8,12},{12,8},{16,20},{20,16},{24,28},{28,24},{1,5},{5... | collective-permute-start | bytes 786440 | tf_op jit(solution)/shard_map/ppermute | solution.py:692
  28.4 7.3 %collective-permute-start.11 = (f32[2,128,128]{2,1,0:T(8,128)S(1)}, f32[2,128,128]{2,1,0:T(8,128)S(1)}, u32[]{:S(2)}, u32[]{:S(2)}) collective-permute-start(f32[2,128,128]{2,1,0:T(8,128)S(1)} %get-tuple-element.78), channel_id=1, source_target_pairs={{0,24},{4,28},{8,16},{12,20},{16,8},{20,12},{24,0},{28,4},{1,25},{... | collective-permute-start | bytes 393224 | tf_op jit(solution)/shard_map/ppermute | solution.py:692
  31.0 6.9 %collective-permute-start.9 = (f32[2,128,128]{2,1,0:T(8,128)S(1)}, f32[2,128,128]{2,1,0:T(8,128)S(1)}, u32[]{:S(2)}, u32[]{:S(2)}) collective-permute-start(f32[2,128,128]{2,1,0:T(8,128)S(1)} %get-tuple-element.76), channel_id=1, source_target_pairs={{0,8},{4,12},{8,0},{12,4},{16,24},{20,28},{24,16},{28,20},{1,9},{5... | collective-permute-start | bytes 393224 | tf_op jit(solution)/shard_map/ppermute | solution.py:692
  31.6 0.7 %copy-start.1 = (s32[32]{0:T(128)S(1)}, s32[32]{0:T(128)}, u32[]{:S(2)}) copy-start(s32[32]{0:T(128)} %order_in.5) | copy-start | bytes 388
  31.6 6.3 %collective-permute-start.10 = (f32[2,128,128]{2,1,0:T(8,128)S(1)}, f32[2,128,128]{2,1,0:T(8,128)S(1)}, u32[]{:S(2)}, u32[]{:S(2)}) collective-permute-start(f32[2,128,128]{2,1,0:T(8,128)S(1)} %get-tuple-element.77), channel_id=1, source_target_pairs={{0,16},{4,20},{8,24},{12,28},{16,0},{20,4},{24,8},{28,12},{1,17},{... | collective-permute-start | bytes 393224 | tf_op jit(solution)/shard_map/ppermute | solution.py:692

commit v6 on v5

--- a/solution.py
+++ b/solution.py
@@ -220,7 +220,7 @@
 
 
 CHUNK = 96
-CHIPS = (0, 3, 1, 2)
+CHIPS = (0, 3, 2, 1)
 AT_VALUES, AT_NORMALS, AT_COEFFS, AT_MISC = 64, 72, 84, 88
 
 
@@ -232,16 +232,36 @@
     return lax.broadcasted_iota(jnp.int32, shape, len(shape) - 1)
 
 
+def place_points(target, channels, values, normals, misc, by_channel):
+    target[AT_MISC:CHUNK, :] = misc
+    for c, channel in enumerate(channels):
+        row = AT_VALUES + 2 * c
+        target[row : row + 2, :] = values[pl.ds(channel * 2, 2), :]
+        for k in range(3):
+            row = AT_NORMALS + 4 * k + c
+            target[row : row + 1, :] = normals[pl.ds(k * 32 + channel, 1), :]
+        row = AT_COEFFS + c
+        target[row : row + 1, :] = by_channel[pl.ds(channel, 1), :]
+
+
+def place_control(target, channels, control):
+    for c, channel in enumerate(channels):
+        plane = control[channel]
+        for z in range(4):
+            row = z * 16 + c * 4
+            target[row : row + 4, :] = plane[z * 4 : z * 4 + 4]
+
+
 def pack_kernel(*refs):
-    sources, give, keep, by_channel = refs[:9], refs[9], refs[10:14], refs[14]
-    arrived, held = refs[15], refs[16:]
+    sources, give, misc, by_channel, number = refs[:9], refs[9], refs[10], refs[11], refs[12]
+    control, values, normals, order, coeffs, cells, weights, ocells, oweights, arrived = refs[13:]
+    held = (order, number, coeffs, cells, weights, ocells, oweights, values, normals, control)
     copies = [
         pltpu.make_async_copy(source, target, arrived.at[k])
-        for k, (source, target) in enumerate(zip(sources, held))
+        for k, (source, target) in enumerate(zip(sources[:1] + sources, held))
     ]
     for copy in copies:
         copy.start()
-    order, coeffs, values, normals, cells, weights, ocells, oweights, control = held
 
     def flat_cell(ref):
         z, y, x = (ref[k, 0] for k in range(3))
@@ -251,42 +271,42 @@
         copy.wait()
     flat, oflat = flat_cell(cells), flat_cell(ocells)
     weight = weights[0]
-    misc = jnp.concatenate(
+    misc[...] = jnp.concatenate(
         [flat[:, :128], flat[:, 128:], oflat, weight[:, :128], weight[:, 128:], oweights[0]]
         + [jnp.zeros((2, 128), jnp.float32)],
         axis=0,
     )
-    by_channel[...] = jnp.transpose(
+    by_channel[:, :16] = jnp.transpose(
         jnp.concatenate([coeffs[...], jnp.zeros((16, 96), jnp.float32)], axis=1)
     )
+    by_channel[:, 16:] = jnp.zeros((128, 112), jnp.float32)
     me = lax.axis_index("depth")
-    places = []
-    for place in range(8):
-        target = give.at[place // 2] if place % 2 else keep[place // 2].at[0]
-        places.append((target, [order[(me ^ place) * 4 + c] for c in range(4)]))
+    places = [
+        (give.at[k], [order[(me ^ (2 * k + 1)) * 4 + c] for c in range(4)]) for k in range(4)
+    ]
     for target, channels in places:
-        target[AT_MISC:CHUNK, :] = misc
-        for c, channel in enumerate(channels):
-            row = AT_VALUES + 2 * c
-            target[row : row + 2, :] = values[pl.ds(channel * 2, 2), :]
-            for k in range(3):
-                row = AT_NORMALS + 4 * k + c
-                target[row : row + 1, :] = normals[pl.ds(k * 32 + channel, 1), :]
-            row = AT_COEFFS + c
-            target[row : row + 1, :16] = by_channel[pl.ds(channel, 1), :]
+        place_points(target, channels, values, normals, misc[...], by_channel)
     copies[-1].wait()
     for target, channels in places:
-        for c, channel in enumerate(channels):
-            plane = control[channel]
-            for z in range(4):
-                row = z * 16 + c * 4
-                target[row : row + 4, :] = plane[z * 4 : z * 4 + 4]
+        place_control(target, channels, control)
+
+
+def keep_kernel(misc, by_channel, number, control, values, normals, *refs):
+    keep, order, arrived = refs[:4], refs[4], refs[5]
+    numbers = pltpu.make_async_copy(number, order, arrived)
+    numbers.start()
+    numbers.wait()
+    me = lax.axis_index("depth")
+    for k in range(4):
+        channels = [order[(me ^ (2 * k)) * 4 + c] for c in range(4)]
+        place_points(keep[k], channels, values, normals, misc[...], by_channel)
+        place_control(keep[k], channels, control)
 
 
 def join_kernel(got, *refs):
     keep, joined = refs[:4], refs[4:]
     for k in range(4):
-        joined[k][0] = keep[k][0]
+        joined[k][0] = keep[k][...]
         joined[k][1] = got[k]
 
 
@@ -569,7 +589,7 @@
     give, keep, (first, rows, out) = refs[9], refs[10:14], refs[14:]
     me = lax.axis_index("depth")
     targets = [
-        give.at[place // 2] if place % 2 else keep[place // 2].at[0] for place in range(8)
+        give.at[place // 2] if place % 2 else keep[place // 2] for place in range(8)
     ]
     for place, target in enumerate(targets):
         target[:64, :] = potential[me ^ place]
@@ -609,24 +629,28 @@
         target[64:, :] = out[me ^ place]
 
 
-def unpack_kernel(chips, order_in, *refs):
+def unpack_kernel(chips, number, *refs):
     count = len(chips)
-    parts, (potential, gradient, planes, order, sent) = refs[:count], refs[-5:]
-    numbers = pltpu.make_async_copy(order_in, order, sent.at[2])
-    numbers.start()
+    parts, (potential, gradient, planes, sent) = refs[:count], refs[-4:]
+    me = lax.axis_index("depth")
+    order = number[...].reshape(1, 32)
+    lane = lane_index((1, 32))
+    channels = []
+    for slot in range(8 * count):
+        place = 2 * chips[slot // 8] + slot // 4 % 2
+        here = lane == (me ^ place) * 4 + slot % 4
+        channels.append(jnp.sum(jnp.where(here, order, 0)))
     for half in range(2):
         for slot in range(8 * count):
             k, source, c = slot // 8, slot // 4 % 2, slot % 4
             rows = [64 * half + z * 16 + c * 4 for z in range(4)]
             pieces = [parts[k][source, row : row + 4, :] for row in rows]
             planes[half, slot] = jnp.concatenate(pieces, axis=0)
-    numbers.wait()
-    me = lax.axis_index("depth")
     for slot in range(8 * count):
-        place = 2 * chips[slot // 8] + slot // 4 % 2
-        channel = order[(me ^ place) * 4 + slot % 4]
         for half, out in enumerate((potential, gradient)):
-            pltpu.make_async_copy(planes.at[half, slot], out.at[channel], sent.at[half]).start()
+            pltpu.make_async_copy(
+                planes.at[half, slot], out.at[channels[slot]], sent.at[half]
+            ).start()
     for half, out in enumerate((potential, gradient)):
         pltpu.make_async_copy(planes.at[half], out.at[: 8 * count], sent.at[half]).wait()
 
@@ -675,37 +699,48 @@
     sources = (
         channel_order,
         jnp.transpose(filter_coeffs, (0, 2, 1)).reshape(16, 32),
-        point_values.reshape(64, 128),
-        orient_normals.reshape(96, 128),
         point_cells,
         point_weights,
         orient_cells,
         orient_weights,
+        point_values.reshape(64, 128),
+        orient_normals.reshape(96, 128),
         control.reshape(32, 16, 128),
     )
     sources = tuple(pltpu.with_memory_space_constraint(x, pltpu.HBM) for x in sources)
-    held = [pltpu.VMEM(source.shape, source.dtype) for source in sources]
-    held[0] = pltpu.SMEM((32,), jnp.int32)
-
-    def exchange(rows, give, *keep):
+    held = [pltpu.VMEM(source.shape, source.dtype) for source in sources[1:6]]
+
+    def exchange(rows, give, keep, chips):
         def swap(value, flip):
             return lax.ppermute(value, "depth", [(i, i ^ flip) for i in range(8)])
 
         both = f32(2, rows, 128)
         joined = call(join_kernel, (both,) * 4, (swap(give, 1), *keep))
-        return [joined[k] if k == 0 else swap(joined[k], 2 * k) for k in CHIPS]
-
-    def staged(rows):
-        return (f32(4, rows, 128),) + (f32(2, rows, 128),) * 4
-
-    packed = call(
+        return [joined[k] if k == 0 else swap(joined[k], 2 * k) for k in chips]
+
+    give, *held = call(
         pack_kernel,
-        staged(CHUNK),
+        (
+            f32(4, CHUNK, 128),
+            f32(8, 128),
+            f32(128, 128),
+            jax.ShapeDtypeStruct((32,), jnp.int32),
+            f32(32, 16, 128),
+            f32(64, 128),
+            f32(96, 128),
+        ),
         sources,
-        [pltpu.VMEM((128, 16), jnp.float32), pltpu.SemaphoreType.DMA((9,))] + held,
+        [pltpu.SMEM((32,), jnp.int32), *held, pltpu.SemaphoreType.DMA((10,))],
         [in_hbm] * 9,
     )
-    parts = exchange(CHUNK, *packed)
+    keep = call(
+        keep_kernel,
+        (f32(CHUNK, 128),) * 4,
+        held,
+        [pltpu.SMEM((32,), jnp.int32), pltpu.SemaphoreType.DMA],
+    )
+    number = held[2]
+    parts = exchange(CHUNK, give, keep, CHIPS)
     field, edge, plane = f32(4, 4, 32, 128), f32(2, 4, 32, 128), f32(4, 32, 128)
     by_depth = f32(32, 16, 128)
     rows = pltpu.VMEM((512, 128), jnp.float32)
@@ -730,24 +765,23 @@
     partial, potential = call(
         spread_kernel, (field, f32(8, 64, 128)), (forcing, taps, potential), [rows]
     )
-    results = call(
+    give, *keep = call(
         gradient_kernel,
-        staged(128),
+        (f32(4, 128, 128),) + (f32(128, 128),) * 4,
         (chunks, partial, even, odd, taps, table, scale, root, potential),
         [first, rows, pltpu.VMEM((8, 64, 128), jnp.float32)],
     )
-    parts = exchange(128, *results)
+    parts = exchange(128, give, keep, range(4))
     outs = ()
-    for some in (slice(0, 1), slice(1, 2), slice(2, 4)):
-        count = len(CHIPS[some])
+    for some in (range(1), range(1, 2), range(2, 4)):
+        count = len(some)
         outs = call(
-            functools.partial(unpack_kernel, CHIPS[some]),
+            functools.partial(unpack_kernel, some),
             (by_depth, by_depth),
-            (channel_order, *parts[some], *outs),
+            (number, *parts[some.start : some.stop], *outs),
             [
                 pltpu.VMEM((2, 8 * count, 16, 128), jnp.float32),
-                pltpu.SMEM((32,), jnp.int32),
-                pltpu.SemaphoreType.DMA((3,)),
+                pltpu.SemaphoreType.DMA((2,)),
             ],
             [in_vmem] * (count + 1) + [in_hbm] * len(outs),
             in_hbm,

time: 39.4 us -> 39.4 us (level)
  waiting for transfers between devices: 13 us -> 13.9 us
  Pallas kernels: 12 us -> 11.3 us
    ppermute x8, waiting for transfers between devices: 10.6 us -> 11.4 us  [swap(): return lax.ppermute(value, 'depth', [(i, i ^ flip) for i in range(8)])]
    pallas_call x11 -> x12, Pallas kernels: 12 us -> 11.3 us  [call(): pl.pallas_call(kernel, out_shape=outs, in_specs=ins or [in_vmem] * len(op...]
  transfers between devices with their start and end apart: 12 -> 12, of which waited for: 8 -> 9; matrix products, arithmetic and copies ran while one was open for 0% -> 0% of each run, Pallas kernels for 16% -> 16%
where the time goes in v6:
time: 39.4 us; the launch traced here: 39.2 us
  waiting for transfers between devices  13.9 us (35%)
  starting transfers between devices  13.2 us (34%)
  Pallas kernels  11.3 us (29%)
  between operations  0.74 us (2%)
    ppermute x8, waiting for transfers between devices, swap(): return lax.ppermute(value, 'depth', [(i, i ^ flip) for i in range(8)])  11.4 us
    pallas_call x12, Pallas kernels, call(): pl.pallas_call(kernel, out_shape=outs, in_specs=ins or [in_vmem] * len(op...  11.3 us
    ppermute x8, starting transfers between devices, swap(): return lax.ppermute(value, 'depth', [(i, i ^ flip) for i in range(8)])  8.66 us
    ppermute x4, starting transfers between devices, swap(): return lax.ppermute(value, ('depth', 'inline'), pairs)  4.57 us
    ppermute x4, waiting for transfers between devices, swap(): return lax.ppermute(value, ('depth', 'inline'), pairs)  2.47 us
  transfers between devices with their start and end apart: 12, of which 9 were waited for; matrix products, arithmetic and copies ran while one was open for 0% of the time, Pallas kernels for 16%

profile of v6, /device:TPU:0, one launch (start us, length us, event | category | flops | bytes accessed | tf_op | source)
XLA Modules:
  0.0 39.2 jit_solution(10511769025625631696)
XLA Ops:
  0.6 1.2 %shard_map.113 = (f32[4,96,128]{2,1,0:T(8,128)S(1)}, f32[8,128]{1,0:T(8,128)S(1)}, f32[128,128]{1,0:T(8,128)S(1)}, s32[32]{0:T(128)S(1)}, f32[32,16,128]{2,1,0:T...) custom-call(s32[32]{0:T(128)} %refs_0_.1, f32[16,32]{1,0:T(8,128)} %bitcast.17, s32[3,1,1,256]{3,2,1,0:T(1,128)} %refs_2_.1, ...), custom_call_target="tpu_custom_call" | custom-call | tf_op jit(solution)/shard_map/pallas_call | solution.py:689
  1.8 0.5 %collective-permute-start = (f32[4,96,128]{2,1,0:T(8,128)S(1)}, f32[4,96,128]{2,1,0:T(8,128)S(1)}, u32[]{:S(2)}, u32[]{:S(2)}) collective-permute-start(f32[4,96,128]{2,1,0:T(8,128)S(1)} %get-tuple-element.51), channel_id=1, source_target_pairs={{0,4},{4,0},{8,12},{12,8},{16,20},{20,16},{24,28},{28,24},{1,5},{5... | collective-permute-start | bytes 589832 | tf_op jit(solution)/shard_map/ppermute | solution.py:715
  2.4 0.6 %shard_map.114 = (f32[96,128]{1,0:T(8,128)S(1)}, f32[96,128]{1,0:T(8,128)S(1)}, f32[96,128]{1,0:T(8,128)S(1)}, f32[96,128]{1,0:T(8,128)S(1)}) custom-call(f32[8,128]{1,0:T(8,128)S(1)} %get-tuple-element.52.misc, f32[128,128]{1,0:T(8,128)S(1)} %get-tuple-element.53.by_channel, s32[32]{0:T(128)S(1)} %get-tuple-element.50.number, ...), custom_call_target="tpu_custom_call" | custom-call | tf_op jit(solution)/shard_map/pallas_call | solution.py:689
  3.0 0.4 %collective-permute-done.got = f32[4,96,128]{2,1,0:T(8,128)S(1)} collective-permute-done((f32[4,96,128]{2,1,0:T(8,128)S(1)}, f32[4,96,128]{2,1,0:T(8,128)S(1)}, u32[]{:S(2)}, u32[]{:S(2)}) %collective-permute-start) | collective-permute-done | bytes 196640 | tf_op jit(solution)/shard_map/ppermute | solution.py:715
  3.5 0.0 copy-start
  3.5 3.9 %collective-permute-start.1 = (f32[2,96,128]{2,1,0:T(8,128)S(1)}, f32[2,96,128]{2,1,0:T(8,128)S(1)}, u32[]{:S(2)}, u32[]{:S(2)}) collective-permute-start(f32[2,96,128]{2,1,0:T(8,128)S(1)} %get-tuple-element.62), channel_id=1, source_target_pairs={{0,24},{4,28},{8,16},{12,20},{16,8},{20,12},{24,0},{28,4},{1,25},{... | collective-permute-start | bytes 294920 | tf_op jit(solution)/shard_map/ppermute | solution.py:715
  7.3 0.5 %collective-permute-start.2 = (f32[2,96,128]{2,1,0:T(8,128)S(1)}, f32[2,96,128]{2,1,0:T(8,128)S(1)}, u32[]{:S(2)}, u32[]{:S(2)}) collective-permute-start(f32[2,96,128]{2,1,0:T(8,128)S(1)} %get-tuple-element.63), channel_id=1, source_target_pairs={{0,16},{4,20},{8,24},{12,28},{16,0},{20,4},{24,8},{28,12},{1,17},{... | collective-permute-start | bytes 294920 | tf_op jit(solution)/shard_map/ppermute | solution.py:715
  7.9 0.1 collective-permute-start.3
  8.0 2.6 %collective-permute-done.1.refs_1_ = f32[2,96,128]{2,1,0:T(8,128)S(1)} collective-permute-done((f32[2,96,128]{2,1,0:T(8,128)S(1)}, f32[2,96,128]{2,1,0:T(8,128)S(1)}, u32[]{:S(2)}, u32[]{:S(2)}) %collective-permute-start.1) | collective-permute-done | bytes 98336 | tf_op jit(solution)/shard_map/ppermute | solution.py:715
  10.6 2.0 %collective-permute-done.2.refs_2_ = f32[2,96,128]{2,1,0:T(8,128)S(1)} collective-permute-done((f32[2,96,128]{2,1,0:T(8,128)S(1)}, f32[2,96,128]{2,1,0:T(8,128)S(1)}, u32[]{:S(2)}, u32[]{:S(2)}) %collective-permute-start.2) | collective-permute-done | bytes 98336 | tf_op jit(solution)/shard_map/ppermute | solution.py:715
  12.6 0.2 collective-permute-done.3.refs_3_
  12.8 0.7 %shard_map.116 = (f32[8,96,128]{2,1,0:T(8,128)S(1)}, f32[4,4,32,128]{3,2,1,0:T(8,128)S(1)}, f32[2,4,32,128]{3,2,1,0:T(8,128)S(1)}, f32[2,4,32,128]{3,2,1,0:T(8,1...) custom-call(f32[2,96,128]{2,1,0:T(8,128)S(1)} %get-tuple-element.61.refs_0_, ...), custom_call_target="tpu_custom_call" | custom-call | tf_op jit(solution)/shard_map/pallas_call | solution.py:689
  13.5 1.6 %collective-permute-start.4 = (f32[2,4,32,128]{3,2,1,0:T(8,128)S(1)}, f32[2,4,32,128]{3,2,1,0:T(8,128)S(1)}, u32[]{:S(2)}, u32[]{:S(2)}) collective-permute-start(f32[2,4,32,128]{3,2,1,0:T(8,128)S(1)} %get-tuple-element.68), channel_id=1, source_target_pairs={{0,1},{1,0},{2,3},{3,2},{4,5},{5,4},{6,7},{7,6},{8,9},{9,8},{10,11... | collective-permute-start | bytes 393224 | tf_op jit(solution)/shard_map/ppermute | solution.py:668
  15.2 0.0 collective-permute-start.5
  15.2 0.0 copy-done
  15.2 2.2 %shard_map.117 = (f32[4,4,32,128]{3,2,1,0:T(8,128)S(1)}, f32[4,4,32,128]{3,2,1,0:T(8,128)S(1)}, f32[4,32,128]{2,1,0:T(8,128)S(1)}, f32[4,32,128]{2,1,0:T(8,128)S(1)}, f32[400,128]{1,0:T(8,128)S(1)}) custom-call(f32[8,96,128]{2,1,0:T(8,128)S(1)} %get-tuple-element.65.chunks.refs_0_, f32[4,4,32,128]{3,2,1,0:T(8,128)S(1)} %get-tuple-element.66.smoothed, ...), custom_call_target="tpu_custom_call" | custom-call | tf_op jit(solution)/shard_map/pallas_call | solution.py:689
  17.4 1.2 %collective-permute-done.4.even_in = f32[2,4,32,128]{3,2,1,0:T(8,128)S(1)} collective-permute-done((f32[2,4,32,128]{3,2,1,0:T(8,128)S(1)}, f32[2,4,32,128]{3,2,1,0:T(8,128)S(1)}, u32[]{:S(2)}, u32[]{:S(2)}) %collective-permute-start.4) | collective-permute-done | bytes 131104 | tf_op jit(solution)/shard_map/ppermute | solution.py:668
  18.6 0.0 collective-permute-done.5.odd_in
  18.6 1.3 %shard_map.118 = (f32[4,4,32,128]{3,2,1,0:T(8,128)S(1)}, f32[4,4,32,128]{3,2,1,0:T(8,128)S(1)}, f32[2,4,32,128]{3,2,1,0:T(8,128)S(1)}, f32[2,4,32,128]{3,2,1,0:T(8,128)S(1)}) custom-call(f32[4,4,32,128]{3,2,1,0:T(8,128)S(1)} %get-tuple-element.67.partial, f32[2,4,32,128]{3,2,1,0:T(8,128)S(1)} %collective-permute-done.4.even_in, ...), custom_call_target="tpu_custom_call" | custom-call | tf_op jit(solution)/shard_map/pallas_call | solution.py:689
  20.0 2.9 %collective-permute-start.6 = (f32[2,4,32,128]{3,2,1,0:T(8,128)S(1)}, f32[2,4,32,128]{3,2,1,0:T(8,128)S(1)}, u32[]{:S(2)}, u32[]{:S(2)}) collective-permute-start(f32[2,4,32,128]{3,2,1,0:T(8,128)S(1)} %get-tuple-element.77), channel_id=1, source_target_pairs={{0,1},{1,0},{2,3},{3,2},{4,5},{5,4},{6,7},{7,6},{8,9},{9,8},{10,11... | collective-permute-start | bytes 393224 | tf_op jit(solution)/shard_map/ppermute | solution.py:668
  22.9 0.0 collective-permute-start.7
  22.9 1.7 %shard_map.119 = (f32[4,4,32,128]{3,2,1,0:T(8,128)S(1)}, f32[8,64,128]{2,1,0:T(8,128)S(1)}) custom-call(f32[4,4,32,128]{3,2,1,0:T(8,128)S(1)} %get-tuple-element.74.forcing, f32[400,128]{1,0:T(8,128)S(1)} %get-tuple-element.70.table.refs_4_, f32[4,4,32,128]{3,2,1,0:T(8,128)S(1)} %get-tuple-element.75.potential), custom_call_target="tpu_custom_call" | custom-call | tf_op jit(solution)/shard_map/pallas_call | solution.py:689
  24.6 1.2 %collective-permute-done.6.refs_2_ = f32[2,4,32,128]{3,2,1,0:T(8,128)S(1)} collective-permute-done((f32[2,4,32,128]{3,2,1,0:T(8,128)S(1)}, f32[2,4,32,128]{3,2,1,0:T(8,128)S(1)}, u32[]{:S(2)}, u32[]{:S(2)}) %collective-permute-start.6) | collective-permute-done | bytes 131104 | tf_op jit(solution)/shard_map/ppermute | solution.py:668
  25.8 0.0 collective-permute-done.7.refs_3_
  25.8 1.1 %shard_map.120 = (f32[4,128,128]{2,1,0:T(8,128)S(1)}, f32[128,128]{1,0:T(8,128)S(1)}, f32[128,128]{1,0:T(8,128)S(1)}, f32[128,128]{1,0:T(8,128)S(1)}, f32[128,128]{1,0:T(8,128)S(1)}) custom-call(f32[8,96,128]{2,1,0:T(8,128)S(1)} %get-tuple-element.65.chunks.refs_0_, f32[4,4,32,128]{3,2,1,0:T(8,128)S(1)} %get-tuple-element.76.refs_1_, ...), custom_call_target="tpu_custom_call" | custom-call | tf_op jit(solution)/shard_map/pallas_call | solution.py:689
  26.9 0.1 collective-permute-start.8
  27.0 1.5 %collective-permute-done.8.got = f32[4,128,128]{2,1,0:T(8,128)S(1)} collective-permute-done((f32[4,128,128]{2,1,0:T(8,128)S(1)}, f32[4,128,128]{2,1,0:T(8,128)S(1)}, u32[]{:S(2)}, u32[]{:S(2)}) %collective-permute-start.8) | collective-permute-done | bytes 262176 | tf_op jit(solution)/shard_map/ppermute | solution.py:715
  28.5 1.7 %collective-permute-start.11 = (f32[2,128,128]{2,1,0:T(8,128)S(1)}, f32[2,128,128]{2,1,0:T(8,128)S(1)}, u32[]{:S(2)}, u32[]{:S(2)}) collective-permute-start(f32[2,128,128]{2,1,0:T(8,128)S(1)} %get-tuple-element.90), channel_id=1, source_target_pairs={{0,8},{4,12},{8,0},{12,4},{16,24},{20,28},{24,16},{28,20},{1,9},{5... | collective-permute-start | bytes 393224 | tf_op jit(solution)/shard_map/ppermute | solution.py:715
  30.3 0.4 collective-permute-start.9
  30.6 1.5 %collective-permute-start.10 = (f32[2,128,128]{2,1,0:T(8,128)S(1)}, f32[2,128,128]{2,1,0:T(8,128)S(1)}, u32[]{:S(2)}, u32[]{:S(2)}) collective-permute-start(f32[2,128,128]{2,1,0:T(8,128)S(1)} %get-tuple-element.89), channel_id=1, source_target_pairs={{0,24},{4,28},{8,16},{12,20},{16,8},{20,12},{24,0},{28,4},{1,25},{... | collective-permute-start | bytes 393224 | tf_op jit(solution)/shard_map/ppermute | solution.py:715
  32.1 0.8 %shard_map.122 = (f32[32,16,128]{2,1,0:T(8,128)}, f32[32,16,128]{2,1,0:T(8,128)}) custom-call(s32[32]{0:T(128)S(1)} %get-tuple-element.50.number, f32[2,128,128]{2,1,0:T(8,128)S(1)} %get-tuple-element.91.refs_0_), custom_call_target="tpu_custom_call" | custom-call | tf_op jit(solution)/shard_map/pallas_call | solution.py:689
  32.9 1.4 %collective-permute-done.11.refs_0_ = f32[2,128,128]{2,1,0:T(8,128)S(1)} collective-permute-done((f32[2,128,128]{2,1,0:T(8,128)S(1)}, f32[2,128,128]{2,1,0:T(8,128)S(1)}, u32[]{:S(2)}, u32[]{:S(2)}) %collective-permute-start.11) | collective-permute-done | bytes 131104 | tf_op jit(solution)/shard_map/ppermute | solution.py:715
  34.3 0.8 %shard_map.123 = (f32[32,16,128]{2,1,0:T(8,128)}, f32[32,16,128]{2,1,0:T(8,128)}) custom-call(s32[32]{0:T(128)S(1)} %get-tuple-element.50.number, f32[2,128,128]{2,1,0:T(8,128)S(1)} %collective-permute-done.11.refs_0_, f32[32,16,128]{2,1,0:T(8,128)} %get-tuple-element.92.refs_1_, ...), custom_call_target="tpu_custom_call", output_to_operand_aliasing={{0}: (2, {}), {1}: (3, {})} | custom-call | tf_op jit(solution)/shard_map/pallas_call | solution.py:689
  35.1 3.2 %collective-permute-done.9.refs_0_ = f32[2,128,128]{2,1,0:T(8,128)S(1)} collective-permute-done((f32[2,128,128]{2,1,0:T(8,128)S(1)}, f32[2,128,128]{2,1,0:T(8,128)S(1)}, u32[]{:S(2)}, u32[]{:S(2)}) %collective-permute-start.9) | collective-permute-done | bytes 131104 | tf_op jit(solution)/shard_map/ppermute | solution.py:715
  38.3 0.0 collective-permute-done.10.refs_1_
  38.4 0.9 %shard_map.124 = (f32[32,16,128]{2,1,0:T(8,128)}, f32[32,16,128]{2,1,0:T(8,128)}) custom-call(s32[32]{0:T(128)S(1)} %get-tuple-element.50.number, f32[2,128,128]{2,1,0:T(8,128)S(1)} %collective-permute-done.9.refs_0_, f32[2,128,128]{2,1,0:T(8,128)S(1)} %collective-permute-done.10.refs_1_, ...), custom_call_target="tpu_custom_call", output_to_operand_aliasing={{0}: (3, {}), {1}: (4, {})} | custom-call | tf_op jit(solution)/shard_map/pallas_call | solution.py:689
  (2 shorter events, 0.1 us)
Async XLA Ops:
  1.8 1.6 %collective-permute-start = (f32[4,96,128]{2,1,0:T(8,128)S(1)}, f32[4,96,128]{2,1,0:T(8,128)S(1)}, u32[]{:S(2)}, u32[]{:S(2)}) collective-permute-start(f32[4,96,128]{2,1,0:T(8,128)S(1)} %get-tuple-element.51), channel_id=1, source_target_pairs={{0,4},{4,0},{8,12},{12,8},{16,20},{20,16},{24,28},{28,24},{1,5},{5... | collective-permute-start | bytes 589832 | tf_op jit(solution)/shard_map/ppermute | solution.py:715
  3.5 11.7 %copy-start = (f32[8,4,4,5,5]{0,2,4,3,1:T(4,128)S(1)}, f32[8,4,4,5,5]{0,2,4,3,1:T(4,128)}, u32[]{:S(2)}) copy-start(f32[8,4,4,5,5]{0,2,4,3,1:T(4,128)} %param.12) | copy-start | bytes 38404
  3.5 7.1 %collective-permute-start.1 = (f32[2,96,128]{2,1,0:T(8,128)S(1)}, f32[2,96,128]{2,1,0:T(8,128)S(1)}, u32[]{:S(2)}, u32[]{:S(2)}) collective-permute-start(f32[2,96,128]{2,1,0:T(8,128)S(1)} %get-tuple-element.62), channel_id=1, source_target_pairs={{0,24},{4,28},{8,16},{12,20},{16,8},{20,12},{24,0},{28,4},{1,25},{... | collective-permute-start | bytes 294920 | tf_op jit(solution)/shard_map/ppermute | solution.py:715
  7.3 5.2 %collective-permute-start.2 = (f32[2,96,128]{2,1,0:T(8,128)S(1)}, f32[2,96,128]{2,1,0:T(8,128)S(1)}, u32[]{:S(2)}, u32[]{:S(2)}) collective-permute-start(f32[2,96,128]{2,1,0:T(8,128)S(1)} %get-tuple-element.63), channel_id=1, source_target_pairs={{0,16},{4,20},{8,24},{12,28},{16,0},{20,4},{24,8},{28,12},{1,17},{... | collective-permute-start | bytes 294920 | tf_op jit(solution)/shard_map/ppermute | solution.py:715
  7.9 4.9 %collective-permute-start.3 = (f32[2,96,128]{2,1,0:T(8,128)S(1)}, f32[2,96,128]{2,1,0:T(8,128)S(1)}, u32[]{:S(2)}, u32[]{:S(2)}) collective-permute-start(f32[2,96,128]{2,1,0:T(8,128)S(1)} %get-tuple-element.64), channel_id=1, source_target_pairs={{0,8},{4,12},{8,0},{12,4},{16,24},{20,28},{24,16},{28,20},{1,9},{5... | collective-permute-start | bytes 294920 | tf_op jit(solution)/shard_map/ppermute | solution.py:715
  13.5 5.1 %collective-permute-start.4 = (f32[2,4,32,128]{3,2,1,0:T(8,128)S(1)}, f32[2,4,32,128]{3,2,1,0:T(8,128)S(1)}, u32[]{:S(2)}, u32[]{:S(2)}) collective-permute-start(f32[2,4,32,128]{3,2,1,0:T(8,128)S(1)} %get-tuple-element.68), channel_id=1, source_target_pairs={{0,1},{1,0},{2,3},{3,2},{4,5},{5,4},{6,7},{7,6},{8,9},{9,8},{10,11... | collective-permute-start | bytes 393224 | tf_op jit(solution)/shard_map/ppermute | solution.py:668
  15.2 3.5 %collective-permute-start.5 = (f32[2,4,32,128]{3,2,1,0:T(8,128)S(1)}, f32[2,4,32,128]{3,2,1,0:T(8,128)S(1)}, u32[]{:S(2)}, u32[]{:S(2)}) collective-permute-start(f32[2,4,32,128]{3,2,1,0:T(8,128)S(1)} %get-tuple-element.69), channel_id=1, source_target_pairs={{0,4},{1,2},{2,1},{3,7},{4,0},{5,6},{6,5},{7,3},{8,12},{9,10},{10,... | collective-permute-start | bytes 393224 | tf_op jit(solution)/shard_map/ppermute | solution.py:668
  20.0 5.9 %collective-permute-start.6 = (f32[2,4,32,128]{3,2,1,0:T(8,128)S(1)}, f32[2,4,32,128]{3,2,1,0:T(8,128)S(1)}, u32[]{:S(2)}, u32[]{:S(2)}) collective-permute-start(f32[2,4,32,128]{3,2,1,0:T(8,128)S(1)} %get-tuple-element.77), channel_id=1, source_target_pairs={{0,1},{1,0},{2,3},{3,2},{4,5},{5,4},{6,7},{7,6},{8,9},{9,8},{10,11... | collective-permute-start | bytes 393224 | tf_op jit(solution)/shard_map/ppermute | solution.py:668
  22.9 3.0 %collective-permute-start.7 = (f32[2,4,32,128]{3,2,1,0:T(8,128)S(1)}, f32[2,4,32,128]{3,2,1,0:T(8,128)S(1)}, u32[]{:S(2)}, u32[]{:S(2)}) collective-permute-start(f32[2,4,32,128]{3,2,1,0:T(8,128)S(1)} %get-tuple-element.78), channel_id=1, source_target_pairs={{0,4},{1,2},{2,1},{3,7},{4,0},{5,6},{6,5},{7,3},{8,12},{9,10},{10,... | collective-permute-start | bytes 393224 | tf_op jit(solution)/shard_map/ppermute | solution.py:668
  26.9 1.6 %collective-permute-start.8 = (f32[4,128,128]{2,1,0:T(8,128)S(1)}, f32[4,128,128]{2,1,0:T(8,128)S(1)}, u32[]{:S(2)}, u32[]{:S(2)}) collective-permute-start(f32[4,128,128]{2,1,0:T(8,128)S(1)} %get-tuple-element.83), channel_id=1, source_target_pairs={{0,4},{4,0},{8,12},{12,8},{16,20},{20,16},{24,28},{28,24},{1,5},{5... | collective-permute-start | bytes 786440 | tf_op jit(solution)/shard_map/ppermute | solution.py:715
  28.5 5.8 %collective-permute-start.11 = (f32[2,128,128]{2,1,0:T(8,128)S(1)}, f32[2,128,128]{2,1,0:T(8,128)S(1)}, u32[]{:S(2)}, u32[]{:S(2)}) collective-permute-start(f32[2,128,128]{2,1,0:T(8,128)S(1)} %get-tuple-element.90), channel_id=1, source_target_pairs={{0,8},{4,12},{8,0},{12,4},{16,24},{20,28},{24,16},{28,20},{1,9},{5... | collective-permute-start | bytes 393224 | tf_op jit(solution)/shard_map/ppermute | solution.py:715
  30.3 8.1 %collective-permute-start.9 = (f32[2,128,128]{2,1,0:T(8,128)S(1)}, f32[2,128,128]{2,1,0:T(8,128)S(1)}, u32[]{:S(2)}, u32[]{:S(2)}) collective-permute-start(f32[2,128,128]{2,1,0:T(8,128)S(1)} %get-tuple-element.88), channel_id=1, source_target_pairs={{0,16},{4,20},{8,24},{12,28},{16,0},{20,4},{24,8},{28,12},{1,17},{... | collective-permute-start | bytes 393224 | tf_op jit(solution)/shard_map/ppermute | solution.py:715
  30.6 7.7 %collective-permute-start.10 = (f32[2,128,128]{2,1,0:T(8,128)S(1)}, f32[2,128,128]{2,1,0:T(8,128)S(1)}, u32[]{:S(2)}, u32[]{:S(2)}) collective-permute-start(f32[2,128,128]{2,1,0:T(8,128)S(1)} %get-tuple-element.89), channel_id=1, source_target_pairs={{0,24},{4,28},{8,16},{12,20},{16,8},{20,12},{24,0},{28,4},{1,25},{... | collective-permute-start | bytes 393224 | tf_op jit(solution)/shard_map/ppermute | solution.py:715

commit v7 on v6

--- a/solution.py
+++ b/solution.py
@@ -255,10 +255,12 @@
 def pack_kernel(*refs):
     sources, give, misc, by_channel, number = refs[:9], refs[9], refs[10], refs[11], refs[12]
     control, values, normals, order, coeffs, cells, weights, ocells, oweights, arrived = refs[13:]
-    held = (order, number, coeffs, cells, weights, ocells, oweights, values, normals, control)
+    held = (order, number, coeffs, cells, weights, ocells, oweights, values, normals)
+    pairs = [(sources[8].at[8 * k : 8 * k + 8], control.at[8 * k : 8 * k + 8]) for k in range(4)]
+    pairs += zip(sources[:1] + sources[:8], held)
     copies = [
         pltpu.make_async_copy(source, target, arrived.at[k])
-        for k, (source, target) in enumerate(zip(sources[:1] + sources, held))
+        for k, (source, target) in enumerate(pairs)
     ]
     for copy in copies:
         copy.start()
@@ -267,7 +269,7 @@
         z, y, x = (ref[k, 0] for k in range(3))
         return (((y & 3) * 4 + (z & 3)) * 128 + x).astype(jnp.float32)
 
-    for copy in copies[:-1]:
+    for copy in copies[4:]:
         copy.wait()
     flat, oflat = flat_cell(cells), flat_cell(ocells)
     weight = weights[0]
@@ -286,7 +288,8 @@
     ]
     for target, channels in places:
         place_points(target, channels, values, normals, misc[...], by_channel)
-    copies[-1].wait()
+    for copy in copies[:4]:
+        copy.wait()
     for target, channels in places:
         place_control(target, channels, control)
 
@@ -730,7 +733,7 @@
             f32(96, 128),
         ),
         sources,
-        [pltpu.SMEM((32,), jnp.int32), *held, pltpu.SemaphoreType.DMA((10,))],
+        [pltpu.SMEM((32,), jnp.int32), *held, pltpu.SemaphoreType.DMA((13,))],
         [in_hbm] * 9,
     )
     keep = call(
@@ -771,14 +774,14 @@
         (chunks, partial, even, odd, taps, table, scale, root, potential),
         [first, rows, pltpu.VMEM((8, 64, 128), jnp.float32)],
     )
-    parts = exchange(128, give, keep, range(4))
+    parts = exchange(128, give, keep, CHIPS)
     outs = ()
-    for some in (range(1), range(1, 2), range(2, 4)):
-        count = len(some)
+    for some in (slice(0, 1), slice(1, 2), slice(2, 4)):
+        count = len(CHIPS[some])
         outs = call(
-            functools.partial(unpack_kernel, some),
+            functools.partial(unpack_kernel, CHIPS[some]),
             (by_depth, by_depth),
-            (number, *parts[some.start : some.stop], *outs),
+            (number, *parts[some], *outs),
             [
                 pltpu.VMEM((2, 8 * count, 16, 128), jnp.float32),
                 pltpu.SemaphoreType.DMA((2,)),

time: 39.4 us -> 39.2 us (level)
  transfers between devices with their start and end apart: 12 -> 12, of which waited for: 9 -> 10; matrix products, arithmetic and copies ran while one was open for 0% -> 0% of each run, Pallas kernels for 16% -> 16%
where the time goes in v7:
time: 39.2 us; the launch traced here: 39 us
  waiting for transfers between devices  13.7 us (35%)
  starting transfers between devices  13.2 us (34%)
  Pallas kernels  11.4 us (29%)
  between operations  0.74 us (2%)
    pallas_call x12, Pallas kernels, call(): pl.pallas_call(kernel, out_shape=outs, in_specs=ins or [in_vmem] * len(op...  11.4 us
    ppermute x8, waiting for transfers between devices, swap(): return lax.ppermute(value, 'depth', [(i, i ^ flip) for i in range(8)])  11.2 us
    ppermute x8, starting transfers between devices, swap(): return lax.ppermute(value, 'depth', [(i, i ^ flip) for i in range(8)])  8.66 us
    ppermute x4, starting transfers between devices, swap(): return lax.ppermute(value, ('depth', 'inline'), pairs)  4.57 us
    ppermute x4, waiting for transfers between devices, swap(): return lax.ppermute(value, ('depth', 'inline'), pairs)  2.49 us
  transfers between devices with their start and end apart: 12, of which 10 were waited for; matrix products, arithmetic and copies ran while one was open for 0% of the time, Pallas kernels for 16%

profile of v7, /device:TPU:0, one launch (start us, length us, event | category | flops | bytes accessed | tf_op | source)
XLA Modules:
  0.0 39.0 jit_solution(4972779391372898680)
XLA Ops:
  0.6 1.3 %shard_map.113 = (f32[4,96,128]{2,1,0:T(8,128)S(1)}, f32[8,128]{1,0:T(8,128)S(1)}, f32[128,128]{1,0:T(8,128)S(1)}, s32[32]{0:T(128)S(1)}, f32[32,16,128]{2,1,0:T...) custom-call(s32[32]{0:T(128)} %refs_0_.1, f32[16,32]{1,0:T(8,128)} %bitcast.17, s32[3,1,1,256]{3,2,1,0:T(1,128)} %refs_2_.1, ...), custom_call_target="tpu_custom_call" | custom-call | tf_op jit(solution)/shard_map/pallas_call | solution.py:692
  1.9 0.5 %collective-permute-start = (f32[4,96,128]{2,1,0:T(8,128)S(1)}, f32[4,96,128]{2,1,0:T(8,128)S(1)}, u32[]{:S(2)}, u32[]{:S(2)}) collective-permute-start(f32[4,96,128]{2,1,0:T(8,128)S(1)} %get-tuple-element.51), channel_id=1, source_target_pairs={{0,4},{4,0},{8,12},{12,8},{16,20},{20,16},{24,28},{28,24},{1,5},{5... | collective-permute-start | bytes 589832 | tf_op jit(solution)/shard_map/ppermute | solution.py:718
  2.4 0.6 %shard_map.114 = (f32[96,128]{1,0:T(8,128)S(1)}, f32[96,128]{1,0:T(8,128)S(1)}, f32[96,128]{1,0:T(8,128)S(1)}, f32[96,128]{1,0:T(8,128)S(1)}) custom-call(f32[8,128]{1,0:T(8,128)S(1)} %get-tuple-element.52.misc, f32[128,128]{1,0:T(8,128)S(1)} %get-tuple-element.53.by_channel, s32[32]{0:T(128)S(1)} %get-tuple-element.50.number, ...), custom_call_target="tpu_custom_call" | custom-call | tf_op jit(solution)/shard_map/pallas_call | solution.py:692
  3.0 0.4 %collective-permute-done.got = f32[4,96,128]{2,1,0:T(8,128)S(1)} collective-permute-done((f32[4,96,128]{2,1,0:T(8,128)S(1)}, f32[4,96,128]{2,1,0:T(8,128)S(1)}, u32[]{:S(2)}, u32[]{:S(2)}) %collective-permute-start) | collective-permute-done | bytes 196640 | tf_op jit(solution)/shard_map/ppermute | solution.py:718
  3.5 0.0 copy-start
  3.5 3.9 %collective-permute-start.1 = (f32[2,96,128]{2,1,0:T(8,128)S(1)}, f32[2,96,128]{2,1,0:T(8,128)S(1)}, u32[]{:S(2)}, u32[]{:S(2)}) collective-permute-start(f32[2,96,128]{2,1,0:T(8,128)S(1)} %get-tuple-element.62), channel_id=1, source_target_pairs={{0,24},{4,28},{8,16},{12,20},{16,8},{20,12},{24,0},{28,4},{1,25},{... | collective-permute-start | bytes 294920 | tf_op jit(solution)/shard_map/ppermute | solution.py:718
  7.4 0.5 %collective-permute-start.2 = (f32[2,96,128]{2,1,0:T(8,128)S(1)}, f32[2,96,128]{2,1,0:T(8,128)S(1)}, u32[]{:S(2)}, u32[]{:S(2)}) collective-permute-start(f32[2,96,128]{2,1,0:T(8,128)S(1)} %get-tuple-element.63), channel_id=1, source_target_pairs={{0,16},{4,20},{8,24},{12,28},{16,0},{20,4},{24,8},{28,12},{1,17},{... | collective-permute-start | bytes 294920 | tf_op jit(solution)/shard_map/ppermute | solution.py:718
  7.9 0.1 collective-permute-start.3
  8.1 2.6 %collective-permute-done.1.refs_1_ = f32[2,96,128]{2,1,0:T(8,128)S(1)} collective-permute-done((f32[2,96,128]{2,1,0:T(8,128)S(1)}, f32[2,96,128]{2,1,0:T(8,128)S(1)}, u32[]{:S(2)}, u32[]{:S(2)}) %collective-permute-start.1) | collective-permute-done | bytes 98336 | tf_op jit(solution)/shard_map/ppermute | solution.py:718
  10.6 2.0 %collective-permute-done.2.refs_2_ = f32[2,96,128]{2,1,0:T(8,128)S(1)} collective-permute-done((f32[2,96,128]{2,1,0:T(8,128)S(1)}, f32[2,96,128]{2,1,0:T(8,128)S(1)}, u32[]{:S(2)}, u32[]{:S(2)}) %collective-permute-start.2) | collective-permute-done | bytes 98336 | tf_op jit(solution)/shard_map/ppermute | solution.py:718
  12.6 0.2 collective-permute-done.3.refs_3_
  12.9 0.7 %shard_map.116 = (f32[8,96,128]{2,1,0:T(8,128)S(1)}, f32[4,4,32,128]{3,2,1,0:T(8,128)S(1)}, f32[2,4,32,128]{3,2,1,0:T(8,128)S(1)}, f32[2,4,32,128]{3,2,1,0:T(8,1...) custom-call(f32[2,96,128]{2,1,0:T(8,128)S(1)} %get-tuple-element.61.refs_0_, ...), custom_call_target="tpu_custom_call" | custom-call | tf_op jit(solution)/shard_map/pallas_call | solution.py:692
  13.6 1.6 %collective-permute-start.4 = (f32[2,4,32,128]{3,2,1,0:T(8,128)S(1)}, f32[2,4,32,128]{3,2,1,0:T(8,128)S(1)}, u32[]{:S(2)}, u32[]{:S(2)}) collective-permute-start(f32[2,4,32,128]{3,2,1,0:T(8,128)S(1)} %get-tuple-element.68), channel_id=1, source_target_pairs={{0,1},{1,0},{2,3},{3,2},{4,5},{5,4},{6,7},{7,6},{8,9},{9,8},{10,11... | collective-permute-start | bytes 393224 | tf_op jit(solution)/shard_map/ppermute | solution.py:671
  15.2 0.0 collective-permute-start.5
  15.2 0.0 copy-done
  15.2 2.2 %shard_map.117 = (f32[4,4,32,128]{3,2,1,0:T(8,128)S(1)}, f32[4,4,32,128]{3,2,1,0:T(8,128)S(1)}, f32[4,32,128]{2,1,0:T(8,128)S(1)}, f32[4,32,128]{2,1,0:T(8,128)S(1)}, f32[400,128]{1,0:T(8,128)S(1)}) custom-call(f32[8,96,128]{2,1,0:T(8,128)S(1)} %get-tuple-element.65.chunks.refs_0_, f32[4,4,32,128]{3,2,1,0:T(8,128)S(1)} %get-tuple-element.66.smoothed, ...), custom_call_target="tpu_custom_call" | custom-call | tf_op jit(solution)/shard_map/pallas_call | solution.py:692
  17.4 1.2 %collective-permute-done.4.even_in = f32[2,4,32,128]{3,2,1,0:T(8,128)S(1)} collective-permute-done((f32[2,4,32,128]{3,2,1,0:T(8,128)S(1)}, f32[2,4,32,128]{3,2,1,0:T(8,128)S(1)}, u32[]{:S(2)}, u32[]{:S(2)}) %collective-permute-start.4) | collective-permute-done | bytes 131104 | tf_op jit(solution)/shard_map/ppermute | solution.py:671
  18.7 0.0 collective-permute-done.5.odd_in
  18.7 1.3 %shard_map.118 = (f32[4,4,32,128]{3,2,1,0:T(8,128)S(1)}, f32[4,4,32,128]{3,2,1,0:T(8,128)S(1)}, f32[2,4,32,128]{3,2,1,0:T(8,128)S(1)}, f32[2,4,32,128]{3,2,1,0:T(8,128)S(1)}) custom-call(f32[4,4,32,128]{3,2,1,0:T(8,128)S(1)} %get-tuple-element.67.partial, f32[2,4,32,128]{3,2,1,0:T(8,128)S(1)} %collective-permute-done.4.even_in, ...), custom_call_target="tpu_custom_call" | custom-call | tf_op jit(solution)/shard_map/pallas_call | solution.py:692
  20.0 2.9 %collective-permute-start.6 = (f32[2,4,32,128]{3,2,1,0:T(8,128)S(1)}, f32[2,4,32,128]{3,2,1,0:T(8,128)S(1)}, u32[]{:S(2)}, u32[]{:S(2)}) collective-permute-start(f32[2,4,32,128]{3,2,1,0:T(8,128)S(1)} %get-tuple-element.77), channel_id=1, source_target_pairs={{0,1},{1,0},{2,3},{3,2},{4,5},{5,4},{6,7},{7,6},{8,9},{9,8},{10,11... | collective-permute-start | bytes 393224 | tf_op jit(solution)/shard_map/ppermute | solution.py:671
  23.0 0.0 collective-permute-start.7
  23.0 1.7 %shard_map.119 = (f32[4,4,32,128]{3,2,1,0:T(8,128)S(1)}, f32[8,64,128]{2,1,0:T(8,128)S(1)}) custom-call(f32[4,4,32,128]{3,2,1,0:T(8,128)S(1)} %get-tuple-element.74.forcing, f32[400,128]{1,0:T(8,128)S(1)} %get-tuple-element.70.table.refs_4_, f32[4,4,32,128]{3,2,1,0:T(8,128)S(1)} %get-tuple-element.75.potential), custom_call_target="tpu_custom_call" | custom-call | tf_op jit(solution)/shard_map/pallas_call | solution.py:692
  24.7 1.2 %collective-permute-done.6.refs_2_ = f32[2,4,32,128]{3,2,1,0:T(8,128)S(1)} collective-permute-done((f32[2,4,32,128]{3,2,1,0:T(8,128)S(1)}, f32[2,4,32,128]{3,2,1,0:T(8,128)S(1)}, u32[]{:S(2)}, u32[]{:S(2)}) %collective-permute-start.6) | collective-permute-done | bytes 131104 | tf_op jit(solution)/shard_map/ppermute | solution.py:671
  25.9 0.0 collective-permute-done.7.refs_3_
  25.9 1.1 %shard_map.120 = (f32[4,128,128]{2,1,0:T(8,128)S(1)}, f32[128,128]{1,0:T(8,128)S(1)}, f32[128,128]{1,0:T(8,128)S(1)}, f32[128,128]{1,0:T(8,128)S(1)}, f32[128,128]{1,0:T(8,128)S(1)}) custom-call(f32[8,96,128]{2,1,0:T(8,128)S(1)} %get-tuple-element.65.chunks.refs_0_, f32[4,4,32,128]{3,2,1,0:T(8,128)S(1)} %get-tuple-element.76.refs_1_, ...), custom_call_target="tpu_custom_call" | custom-call | tf_op jit(solution)/shard_map/pallas_call | solution.py:692
  27.0 0.1 collective-permute-start.8
  27.1 1.5 %collective-permute-done.8.got = f32[4,128,128]{2,1,0:T(8,128)S(1)} collective-permute-done((f32[4,128,128]{2,1,0:T(8,128)S(1)}, f32[4,128,128]{2,1,0:T(8,128)S(1)}, u32[]{:S(2)}, u32[]{:S(2)}) %collective-permute-start.8) | collective-permute-done | bytes 262176 | tf_op jit(solution)/shard_map/ppermute | solution.py:718
  28.6 1.5 %collective-permute-start.11 = (f32[2,128,128]{2,1,0:T(8,128)S(1)}, f32[2,128,128]{2,1,0:T(8,128)S(1)}, u32[]{:S(2)}, u32[]{:S(2)}) collective-permute-start(f32[2,128,128]{2,1,0:T(8,128)S(1)} %get-tuple-element.90), channel_id=1, source_target_pairs={{0,24},{4,28},{8,16},{12,20},{16,8},{20,12},{24,0},{28,4},{1,25},{... | collective-permute-start | bytes 393224 | tf_op jit(solution)/shard_map/ppermute | solution.py:718
  30.1 1.7 %collective-permute-start.9 = (f32[2,128,128]{2,1,0:T(8,128)S(1)}, f32[2,128,128]{2,1,0:T(8,128)S(1)}, u32[]{:S(2)}, u32[]{:S(2)}) collective-permute-start(f32[2,128,128]{2,1,0:T(8,128)S(1)} %get-tuple-element.88), channel_id=1, source_target_pairs={{0,16},{4,20},{8,24},{12,28},{16,0},{20,4},{24,8},{28,12},{1,17},{... | collective-permute-start | bytes 393224 | tf_op jit(solution)/shard_map/ppermute | solution.py:718
  31.8 0.4 collective-permute-start.10
  32.2 0.8 %shard_map.122 = (f32[32,16,128]{2,1,0:T(8,128)}, f32[32,16,128]{2,1,0:T(8,128)}) custom-call(s32[32]{0:T(128)S(1)} %get-tuple-element.50.number, f32[2,128,128]{2,1,0:T(8,128)S(1)} %get-tuple-element.91.refs_0_), custom_call_target="tpu_custom_call" | custom-call | tf_op jit(solution)/shard_map/pallas_call | solution.py:692
  33.0 3.0 %collective-permute-done.11.refs_0_ = f32[2,128,128]{2,1,0:T(8,128)S(1)} collective-permute-done((f32[2,128,128]{2,1,0:T(8,128)S(1)}, f32[2,128,128]{2,1,0:T(8,128)S(1)}, u32[]{:S(2)}, u32[]{:S(2)}) %collective-permute-start.11) | collective-permute-done | bytes 131104 | tf_op jit(solution)/shard_map/ppermute | solution.py:718
  35.9 0.8 %shard_map.123 = (f32[32,16,128]{2,1,0:T(8,128)}, f32[32,16,128]{2,1,0:T(8,128)}) custom-call(s32[32]{0:T(128)S(1)} %get-tuple-element.50.number, f32[2,128,128]{2,1,0:T(8,128)S(1)} %collective-permute-done.11.refs_0_, f32[32,16,128]{2,1,0:T(8,128)} %get-tuple-element.92.refs_1_, ...), custom_call_target="tpu_custom_call", output_to_operand_aliasing={{0}: (2, {}), {1}: (3, {})} | custom-call | tf_op jit(solution)/shard_map/pallas_call | solution.py:692
  36.7 1.2 %collective-permute-done.9.refs_0_ = f32[2,128,128]{2,1,0:T(8,128)S(1)} collective-permute-done((f32[2,128,128]{2,1,0:T(8,128)S(1)}, f32[2,128,128]{2,1,0:T(8,128)S(1)}, u32[]{:S(2)}, u32[]{:S(2)}) %collective-permute-start.9) | collective-permute-done | bytes 131104 | tf_op jit(solution)/shard_map/ppermute | solution.py:718
  37.9 0.3 collective-permute-done.10.refs_1_
  38.2 0.9 %shard_map.124 = (f32[32,16,128]{2,1,0:T(8,128)}, f32[32,16,128]{2,1,0:T(8,128)}) custom-call(s32[32]{0:T(128)S(1)} %get-tuple-element.50.number, f32[2,128,128]{2,1,0:T(8,128)S(1)} %collective-permute-done.9.refs_0_, f32[2,128,128]{2,1,0:T(8,128)S(1)} %collective-permute-done.10.refs_1_, ...), custom_call_target="tpu_custom_call", output_to_operand_aliasing={{0}: (3, {}), {1}: (4, {})} | custom-call | tf_op jit(solution)/shard_map/pallas_call | solution.py:692
  (2 shorter events, 0.1 us)
Async XLA Ops:
  1.9 1.6 %collective-permute-start = (f32[4,96,128]{2,1,0:T(8,128)S(1)}, f32[4,96,128]{2,1,0:T(8,128)S(1)}, u32[]{:S(2)}, u32[]{:S(2)}) collective-permute-start(f32[4,96,128]{2,1,0:T(8,128)S(1)} %get-tuple-element.51), channel_id=1, source_target_pairs={{0,4},{4,0},{8,12},{12,8},{16,20},{20,16},{24,28},{28,24},{1,5},{5... | collective-permute-start | bytes 589832 | tf_op jit(solution)/shard_map/ppermute | solution.py:718
  3.5 11.7 %copy-start = (f32[8,4,4,5,5]{0,2,4,3,1:T(4,128)S(1)}, f32[8,4,4,5,5]{0,2,4,3,1:T(4,128)}, u32[]{:S(2)}) copy-start(f32[8,4,4,5,5]{0,2,4,3,1:T(4,128)} %param.12) | copy-start | bytes 38404
  3.5 7.1 %collective-permute-start.1 = (f32[2,96,128]{2,1,0:T(8,128)S(1)}, f32[2,96,128]{2,1,0:T(8,128)S(1)}, u32[]{:S(2)}, u32[]{:S(2)}) collective-permute-start(f32[2,96,128]{2,1,0:T(8,128)S(1)} %get-tuple-element.62), channel_id=1, source_target_pairs={{0,24},{4,28},{8,16},{12,20},{16,8},{20,12},{24,0},{28,4},{1,25},{... | collective-permute-start | bytes 294920 | tf_op jit(solution)/shard_map/ppermute | solution.py:718
  7.4 5.2 %collective-permute-start.2 = (f32[2,96,128]{2,1,0:T(8,128)S(1)}, f32[2,96,128]{2,1,0:T(8,128)S(1)}, u32[]{:S(2)}, u32[]{:S(2)}) collective-permute-start(f32[2,96,128]{2,1,0:T(8,128)S(1)} %get-tuple-element.63), channel_id=1, source_target_pairs={{0,16},{4,20},{8,24},{12,28},{16,0},{20,4},{24,8},{28,12},{1,17},{... | collective-permute-start | bytes 294920 | tf_op jit(solution)/shard_map/ppermute | solution.py:718
  7.9 4.9 %collective-permute-start.3 = (f32[2,96,128]{2,1,0:T(8,128)S(1)}, f32[2,96,128]{2,1,0:T(8,128)S(1)}, u32[]{:S(2)}, u32[]{:S(2)}) collective-permute-start(f32[2,96,128]{2,1,0:T(8,128)S(1)} %get-tuple-element.64), channel_id=1, source_target_pairs={{0,8},{4,12},{8,0},{12,4},{16,24},{20,28},{24,16},{28,20},{1,9},{5... | collective-permute-start | bytes 294920 | tf_op jit(solution)/shard_map/ppermute | solution.py:718
  13.6 5.1 %collective-permute-start.4 = (f32[2,4,32,128]{3,2,1,0:T(8,128)S(1)}, f32[2,4,32,128]{3,2,1,0:T(8,128)S(1)}, u32[]{:S(2)}, u32[]{:S(2)}) collective-permute-start(f32[2,4,32,128]{3,2,1,0:T(8,128)S(1)} %get-tuple-element.68), channel_id=1, source_target_pairs={{0,1},{1,0},{2,3},{3,2},{4,5},{5,4},{6,7},{7,6},{8,9},{9,8},{10,11... | collective-permute-start | bytes 393224 | tf_op jit(solution)/shard_map/ppermute | solution.py:671
  15.2 3.5 %collective-permute-start.5 = (f32[2,4,32,128]{3,2,1,0:T(8,128)S(1)}, f32[2,4,32,128]{3,2,1,0:T(8,128)S(1)}, u32[]{:S(2)}, u32[]{:S(2)}) collective-permute-start(f32[2,4,32,128]{3,2,1,0:T(8,128)S(1)} %get-tuple-element.69), channel_id=1, source_target_pairs={{0,4},{1,2},{2,1},{3,7},{4,0},{5,6},{6,5},{7,3},{8,12},{9,10},{10,... | collective-permute-start | bytes 393224 | tf_op jit(solution)/shard_map/ppermute | solution.py:671
  20.0 5.9 %collective-permute-start.6 = (f32[2,4,32,128]{3,2,1,0:T(8,128)S(1)}, f32[2,4,32,128]{3,2,1,0:T(8,128)S(1)}, u32[]{:S(2)}, u32[]{:S(2)}) collective-permute-start(f32[2,4,32,128]{3,2,1,0:T(8,128)S(1)} %get-tuple-element.77), channel_id=1, source_target_pairs={{0,1},{1,0},{2,3},{3,2},{4,5},{5,4},{6,7},{7,6},{8,9},{9,8},{10,11... | collective-permute-start | bytes 393224 | tf_op jit(solution)/shard_map/ppermute | solution.py:671
  23.0 3.0 %collective-permute-start.7 = (f32[2,4,32,128]{3,2,1,0:T(8,128)S(1)}, f32[2,4,32,128]{3,2,1,0:T(8,128)S(1)}, u32[]{:S(2)}, u32[]{:S(2)}) collective-permute-start(f32[2,4,32,128]{3,2,1,0:T(8,128)S(1)} %get-tuple-element.78), channel_id=1, source_target_pairs={{0,4},{1,2},{2,1},{3,7},{4,0},{5,6},{6,5},{7,3},{8,12},{9,10},{10,... | collective-permute-start | bytes 393224 | tf_op jit(solution)/shard_map/ppermute | solution.py:671
  27.0 1.6 %collective-permute-start.8 = (f32[4,128,128]{2,1,0:T(8,128)S(1)}, f32[4,128,128]{2,1,0:T(8,128)S(1)}, u32[]{:S(2)}, u32[]{:S(2)}) collective-permute-start(f32[4,128,128]{2,1,0:T(8,128)S(1)} %get-tuple-element.83), channel_id=1, source_target_pairs={{0,4},{4,0},{8,12},{12,8},{16,20},{20,16},{24,28},{28,24},{1,5},{5... | collective-permute-start | bytes 786440 | tf_op jit(solution)/shard_map/ppermute | solution.py:718
  28.6 7.3 %collective-permute-start.11 = (f32[2,128,128]{2,1,0:T(8,128)S(1)}, f32[2,128,128]{2,1,0:T(8,128)S(1)}, u32[]{:S(2)}, u32[]{:S(2)}) collective-permute-start(f32[2,128,128]{2,1,0:T(8,128)S(1)} %get-tuple-element.90), channel_id=1, source_target_pairs={{0,24},{4,28},{8,16},{12,20},{16,8},{20,12},{24,0},{28,4},{1,25},{... | collective-permute-start | bytes 393224 | tf_op jit(solution)/shard_map/ppermute | solution.py:718
  30.1 7.8 %collective-permute-start.9 = (f32[2,128,128]{2,1,0:T(8,128)S(1)}, f32[2,128,128]{2,1,0:T(8,128)S(1)}, u32[]{:S(2)}, u32[]{:S(2)}) collective-permute-start(f32[2,128,128]{2,1,0:T(8,128)S(1)} %get-tuple-element.88), channel_id=1, source_target_pairs={{0,16},{4,20},{8,24},{12,28},{16,0},{20,4},{24,8},{28,12},{1,17},{... | collective-permute-start | bytes 393224 | tf_op jit(solution)/shard_map/ppermute | solution.py:718
  31.8 6.4 %collective-permute-start.10 = (f32[2,128,128]{2,1,0:T(8,128)S(1)}, f32[2,128,128]{2,1,0:T(8,128)S(1)}, u32[]{:S(2)}, u32[]{:S(2)}) collective-permute-start(f32[2,128,128]{2,1,0:T(8,128)S(1)} %get-tuple-element.89), channel_id=1, source_target_pairs={{0,8},{4,12},{8,0},{12,4},{16,24},{20,28},{24,16},{28,20},{1,9},{5... | collective-permute-start | bytes 393224 | tf_op jit(solution)/shard_map/ppermute | solution.py:718

commit v8 on v7

--- a/solution.py
+++ b/solution.py
@@ -253,8 +253,8 @@
 
 
 def pack_kernel(*refs):
-    sources, give, misc, by_channel, number = refs[:9], refs[9], refs[10], refs[11], refs[12]
-    control, values, normals, order, coeffs, cells, weights, ocells, oweights, arrived = refs[13:]
+    sources, chips, number, by_channel, control = refs[:9], refs[9:13], refs[13], refs[14], refs[15]
+    order, coeffs, cells, weights, ocells, oweights, values, normals, arrived = refs[16:]
     held = (order, number, coeffs, cells, weights, ocells, oweights, values, normals)
     pairs = [(sources[8].at[8 * k : 8 * k + 8], control.at[8 * k : 8 * k + 8]) for k in range(4)]
     pairs += zip(sources[:1] + sources[:8], held)
@@ -273,7 +273,7 @@
         copy.wait()
     flat, oflat = flat_cell(cells), flat_cell(ocells)
     weight = weights[0]
-    misc[...] = jnp.concatenate(
+    misc = jnp.concatenate(
         [flat[:, :128], flat[:, 128:], oflat, weight[:, :128], weight[:, 128:], oweights[0]]
         + [jnp.zeros((2, 128), jnp.float32)],
         axis=0,
@@ -284,33 +284,15 @@
     by_channel[:, 16:] = jnp.zeros((128, 112), jnp.float32)
     me = lax.axis_index("depth")
     places = [
-        (give.at[k], [order[(me ^ (2 * k + 1)) * 4 + c] for c in range(4)]) for k in range(4)
+        (chips[place // 2].at[place % 2], [order[(me ^ place) * 4 + c] for c in range(4)])
+        for place in range(8)
     ]
     for target, channels in places:
-        place_points(target, channels, values, normals, misc[...], by_channel)
+        place_points(target, channels, values, normals, misc, by_channel)
     for copy in copies[:4]:
         copy.wait()
     for target, channels in places:
         place_control(target, channels, control)
-
-
-def keep_kernel(misc, by_channel, number, control, values, normals, *refs):
-    keep, order, arrived = refs[:4], refs[4], refs[5]
-    numbers = pltpu.make_async_copy(number, order, arrived)
-    numbers.start()
-    numbers.wait()
-    me = lax.axis_index("depth")
-    for k in range(4):
-        channels = [order[(me ^ (2 * k)) * 4 + c] for c in range(4)]
-        place_points(keep[k], channels, values, normals, misc[...], by_channel)
-        place_control(keep[k], channels, control)
-
-
-def join_kernel(got, *refs):
-    keep, joined = refs[:4], refs[4:]
-    for k in range(4):
-        joined[k][0] = keep[k][...]
-        joined[k][1] = got[k]
 
 
 def coefficient(expanded, lag, z):
@@ -344,12 +326,12 @@
 
 
 def smooth_kernel(*refs):
-    parts, refs = refs[:4], refs[4:]
+    direct, passed, refs = refs[:4], refs[4:8], refs[8:]
     chunks, smoothed, even, odd, table, scale, root, expanded, first, rows = refs
     me = lax.axis_index("depth")
-    for k, part in zip(CHIPS, parts):
-        for half in range(2):
-            chunks[me ^ (2 * k + half)] = part[half]
+    for n, k in enumerate(CHIPS):
+        chunks[me ^ (2 * k)] = direct[n][0]
+        chunks[me ^ (2 * k + 1)] = passed[n][...]
     repeat_coeffs(chunks, expanded)
     lags = {}
 
@@ -589,11 +571,9 @@
 
 def gradient_kernel(*refs):
     chunks, partial, even_in, odd_in, taps, table, scale, root, potential = refs[:9]
-    give, keep, (first, rows, out) = refs[9], refs[10:14], refs[14:]
+    chips, (first, rows, out) = refs[9:13], refs[13:]
     me = lax.axis_index("depth")
-    targets = [
-        give.at[place // 2] if place % 2 else keep[place // 2] for place in range(8)
-    ]
+    targets = [chips[place // 2].at[place % 2] for place in range(8)]
     for place, target in enumerate(targets):
         target[:64, :] = potential[me ^ place]
 
@@ -632,30 +612,29 @@
         target[64:, :] = out[me ^ place]
 
 
-def unpack_kernel(chips, number, *refs):
-    count = len(chips)
+def unpack_kernel(places, number, *refs):
+    count = len(places)
     parts, (potential, gradient, planes, sent) = refs[:count], refs[-4:]
     me = lax.axis_index("depth")
     order = number[...].reshape(1, 32)
     lane = lane_index((1, 32))
     channels = []
-    for slot in range(8 * count):
-        place = 2 * chips[slot // 8] + slot // 4 % 2
-        here = lane == (me ^ place) * 4 + slot % 4
+    for slot in range(4 * count):
+        here = lane == (me ^ places[slot // 4]) * 4 + slot % 4
         channels.append(jnp.sum(jnp.where(here, order, 0)))
     for half in range(2):
-        for slot in range(8 * count):
-            k, source, c = slot // 8, slot // 4 % 2, slot % 4
-            rows = [64 * half + z * 16 + c * 4 for z in range(4)]
-            pieces = [parts[k][source, row : row + 4, :] for row in rows]
-            planes[half, slot] = jnp.concatenate(pieces, axis=0)
-    for slot in range(8 * count):
+        for slot in range(4 * count):
+            place, part = places[slot // 4], parts[slot // 4]
+            part = part if place % 2 else part.at[0]
+            rows = [64 * half + z * 16 + slot % 4 * 4 for z in range(4)]
+            planes[half, slot] = jnp.concatenate([part[row : row + 4, :] for row in rows], axis=0)
+    for slot in range(4 * count):
         for half, out in enumerate((potential, gradient)):
             pltpu.make_async_copy(
                 planes.at[half, slot], out.at[channels[slot]], sent.at[half]
             ).start()
     for half, out in enumerate((potential, gradient)):
-        pltpu.make_async_copy(planes.at[half], out.at[: 8 * count], sent.at[half]).wait()
+        pltpu.make_async_copy(planes.at[half], out.at[: 4 * count], sent.at[half]).wait()
 
 
 def swapped(even, odd):
@@ -711,39 +690,29 @@
         control.reshape(32, 16, 128),
     )
     sources = tuple(pltpu.with_memory_space_constraint(x, pltpu.HBM) for x in sources)
-    held = [pltpu.VMEM(source.shape, source.dtype) for source in sources[1:6]]
-
-    def exchange(rows, give, keep, chips):
+    held = [pltpu.VMEM(source.shape, source.dtype) for source in sources[1:8]]
+
+    def exchange(*chips):
         def swap(value, flip):
             return lax.ppermute(value, "depth", [(i, i ^ flip) for i in range(8)])
 
-        both = f32(2, rows, 128)
-        joined = call(join_kernel, (both,) * 4, (swap(give, 1), *keep))
-        return [joined[k] if k == 0 else swap(joined[k], 2 * k) for k in chips]
-
-    give, *held = call(
+        direct = [chips[k] if k == 0 else swap(chips[k], 2 * k) for k in CHIPS]
+        return direct, [swap(part[1], 1) for part in direct]
+
+    *chips, number = call(
         pack_kernel,
-        (
-            f32(4, CHUNK, 128),
-            f32(8, 128),
-            f32(128, 128),
-            jax.ShapeDtypeStruct((32,), jnp.int32),
-            f32(32, 16, 128),
-            f32(64, 128),
-            f32(96, 128),
-        ),
+        (f32(2, CHUNK, 128),) * 4 + (jax.ShapeDtypeStruct((32,), jnp.int32),),
         sources,
-        [pltpu.SMEM((32,), jnp.int32), *held, pltpu.SemaphoreType.DMA((13,))],
+        [
+            pltpu.VMEM((128, 128), jnp.float32),
+            pltpu.VMEM((32, 16, 128), jnp.float32),
+            pltpu.SMEM((32,), jnp.int32),
+            *held,
+            pltpu.SemaphoreType.DMA((13,)),
+        ],
         [in_hbm] * 9,
     )
-    keep = call(
-        keep_kernel,
-        (f32(CHUNK, 128),) * 4,
-        held,
-        [pltpu.SMEM((32,), jnp.int32), pltpu.SemaphoreType.DMA],
-    )
-    number = held[2]
-    parts = exchange(CHUNK, give, keep, CHIPS)
+    direct, passed = exchange(*chips)
     field, edge, plane = f32(4, 4, 32, 128), f32(2, 4, 32, 128), f32(4, 32, 128)
     by_depth = f32(32, 16, 128)
     rows = pltpu.VMEM((512, 128), jnp.float32)
@@ -751,7 +720,7 @@
     chunks, smoothed, even, odd, table, scale, root = call(
         smooth_kernel,
         (f32(8, CHUNK, 128), field, edge, edge, f32(32, 4, 16, 128), by_depth, by_depth),
-        parts,
+        (*direct, *passed),
         [pltpu.VMEM((8, 16, 128), jnp.float32), first, rows],
     )
     even, odd = swapped(even, odd)
@@ -768,22 +737,24 @@
     partial, potential = call(
         spread_kernel, (field, f32(8, 64, 128)), (forcing, taps, potential), [rows]
     )
-    give, *keep = call(
+    chips = call(
         gradient_kernel,
-        (f32(4, 128, 128),) + (f32(128, 128),) * 4,
+        (f32(2, 128, 128),) * 4,
         (chunks, partial, even, odd, taps, table, scale, root, potential),
         [first, rows, pltpu.VMEM((8, 64, 128), jnp.float32)],
     )
-    parts = exchange(128, give, keep, CHIPS)
+    direct, passed = exchange(*chips)
+    came = {2 * k: part for k, part in zip(CHIPS, direct)}
+    came |= {2 * k + 1: part for k, part in zip(CHIPS, passed)}
     outs = ()
-    for some in (slice(0, 1), slice(1, 2), slice(2, 4)):
-        count = len(CHIPS[some])
+    for places in ((0, 1), (2 * CHIPS[1], 2 * CHIPS[2]), (2 * CHIPS[3], 7, 5, 3)):
+        count = len(places)
         outs = call(
-            functools.partial(unpack_kernel, CHIPS[some]),
+            functools.partial(unpack_kernel, places),
             (by_depth, by_depth),
-            (number, *parts[some], *outs),
+            (number, *(came[place] for place in places), *outs),
             [
-                pltpu.VMEM((2, 8 * count, 16, 128), jnp.float32),
+                pltpu.VMEM((2, 4 * count, 16, 128), jnp.float32),
                 pltpu.SemaphoreType.DMA((2,)),
             ],
             [in_vmem] * (count + 1) + [in_hbm] * len(outs),

time: 39.2 us -> 41.6 us (1.061)
  waiting for transfers between devices: 13.7 us -> 16.6 us
  Pallas kernels: 11.4 us -> 10.8 us
    ppermute x8 -> x14, waiting for transfers between devices: 11.2 us -> 13.2 us  [swap(): return lax.ppermute(value, 'depth', [(i, i ^ flip) for i in range(8)])]
    ppermute x4, waiting for transfers between devices: 2.49 us -> 3.4 us  [swap(): return lax.ppermute(value, ('depth', 'inline'), pairs)]
    pallas_call x12 -> x9, Pallas kernels: 11.4 us -> 10.8 us  [call(): pl.pallas_call(kernel, out_shape=outs, in_specs=ins or [in_vmem] * len(op...]
    ppermute x8 -> x14, starting transfers between devices: 8.66 us -> 8.68 us  [swap(): return lax.ppermute(value, 'depth', [(i, i ^ flip) for i in range(8)])]
  transfers between devices with their start and end apart: 12 -> 18, of which waited for: 10 -> 10; matrix products, arithmetic and copies ran while one was open for 0% -> 0% of each run, Pallas kernels for 16% -> 13%
where the time goes in v8:
time: 41.6 us; the launch traced here: 41.4 us
  waiting for transfers between devices  16.6 us (40%)
  starting transfers between devices  13.2 us (32%)
  Pallas kernels  10.8 us (26%)
  between operations  0.77 us (2%)
    ppermute x14, waiting for transfers between devices, swap(): return lax.ppermute(value, 'depth', [(i, i ^ flip) for i in range(8)])  13.2 us
    pallas_call x9, Pallas kernels, call(): pl.pallas_call(kernel, out_shape=outs, in_specs=ins or [in_vmem] * len(op...  10.8 us
    ppermute x14, starting transfers between devices, swap(): return lax.ppermute(value, 'depth', [(i, i ^ flip) for i in range(8)])  8.68 us
    ppermute x4, starting transfers between devices, swap(): return lax.ppermute(value, ('depth', 'inline'), pairs)  4.47 us
    ppermute x4, waiting for transfers between devices, swap(): return lax.ppermute(value, ('depth', 'inline'), pairs)  3.4 us
  transfers between devices with their start and end apart: 18, of which 10 were waited for; matrix products, arithmetic and copies ran while one was open for 0% of the time, Pallas kernels for 13%

profile of v8, /device:TPU:0, one launch (start us, length us, event | category | flops | bytes accessed | tf_op | source)
XLA Modules:
  0.0 41.4 jit_solution(7181254074298517574)
XLA Ops:
  0.6 1.3 %shard_map.113 = (f32[2,96,128]{2,1,0:T(8,128)S(1)}, f32[2,96,128]{2,1,0:T(8,128)S(1)}, f32[2,96,128]{2,1,0:T(8,128)S(1)}, f32[2,96,128]{2,1,0:T(8,128)S(1)}, s32[32]{0:T(128)S(1)}) custom-call(s32[32]{0:T(128)} %refs_0_.1, f32[16,32]{1,0:T(8,128)} %bitcast.33, s32[3,1,1,256]{3,2,1,0:T(1,128)} %refs_2_.1, f32[1,1,256]{2,1,0:T(1,128)} %refs_3_.1, ...), custom_call_target="tpu_custom_call" | custom-call | tf_op jit(solution)/shard_map/pallas_call | solution.py:671
  1.9 4.0 %collective-permute-start = (f32[2,96,128]{2,1,0:T(8,128)S(1)}, f32[2,96,128]{2,1,0:T(8,128)S(1)}, u32[]{:S(2)}, u32[]{:S(2)}) collective-permute-start(f32[2,96,128]{2,1,0:T(8,128)S(1)} %get-tuple-element.37), channel_id=1, source_target_pairs={{0,24},{4,28},{8,16},{12,20},{16,8},{20,12},{24,0},{28,4},{1,25},{... | collective-permute-start | bytes 294920 | tf_op jit(solution)/shard_map/ppermute | solution.py:697
  5.9 0.0 collective-permute-start.3
  5.9 0.6 %collective-permute-start.1 = (f32[2,96,128]{2,1,0:T(8,128)S(1)}, f32[2,96,128]{2,1,0:T(8,128)S(1)}, u32[]{:S(2)}, u32[]{:S(2)}) collective-permute-start(f32[2,96,128]{2,1,0:T(8,128)S(1)} %get-tuple-element.38), channel_id=1, source_target_pairs={{0,16},{4,20},{8,24},{12,28},{16,0},{20,4},{24,8},{28,12},{1,17},{... | collective-permute-start | bytes 294920 | tf_op jit(solution)/shard_map/ppermute | solution.py:697
  6.5 0.2 collective-permute-start.2
  6.6 2.4 %collective-permute-done.refs_1_ = f32[2,96,128]{2,1,0:T(8,128)S(1)} collective-permute-done((f32[2,96,128]{2,1,0:T(8,128)S(1)}, f32[2,96,128]{2,1,0:T(8,128)S(1)}, u32[]{:S(2)}, u32[]{:S(2)}) %collective-permute-start) | collective-permute-done | bytes 98336 | tf_op jit(solution)/shard_map/ppermute | solution.py:697
  9.0 0.0 collective-permute-start.4
  9.0 2.1 %collective-permute-done.1.refs_2_ = f32[2,96,128]{2,1,0:T(8,128)S(1)} collective-permute-done((f32[2,96,128]{2,1,0:T(8,128)S(1)}, f32[2,96,128]{2,1,0:T(8,128)S(1)}, u32[]{:S(2)}, u32[]{:S(2)}) %collective-permute-start.1) | collective-permute-done | bytes 98336 | tf_op jit(solution)/shard_map/ppermute | solution.py:697
  11.1 0.0 collective-permute-start.5
  11.1 0.2 collective-permute-done.2.refs_3_
  11.3 0.0 copy-start
  11.3 0.4 collective-permute-start.6
  11.7 0.0 collective-permute-done.3.refs_4_
  11.7 0.0 collective-permute-done.4.refs_5_
  11.7 0.6 %collective-permute-done.5.refs_6_ = f32[96,128]{1,0:T(8,128)S(1)} collective-permute-done((f32[96,128]{1,0:T(8,128)S(1)}, f32[96,128]{1,0:T(8,128)S(1)}, u32[]{:S(2)}, u32[]{:S(2)}) %collective-permute-start.5) | collective-permute-done | bytes 49184 | tf_op jit(solution)/shard_map/ppermute | solution.py:697
  12.3 0.2 collective-permute-done.6.refs_7_
  12.6 0.7 %shard_map.114 = (f32[8,96,128]{2,1,0:T(8,128)S(1)}, f32[4,4,32,128]{3,2,1,0:T(8,128)S(1)}, f32[2,4,32,128]{3,2,1,0:T(8,128)S(1)}, f32[2,4,32,128]{3,2,1,0:T(8,1...) custom-call(f32[2,96,128]{2,1,0:T(8,128)S(1)} %get-tuple-element.36.refs_0_, ...), custom_call_target="tpu_custom_call" | custom-call | tf_op jit(solution)/shard_map/pallas_call | solution.py:671
  13.3 1.6 %collective-permute-start.7 = (f32[2,4,32,128]{3,2,1,0:T(8,128)S(1)}, f32[2,4,32,128]{3,2,1,0:T(8,128)S(1)}, u32[]{:S(2)}, u32[]{:S(2)}) collective-permute-start(f32[2,4,32,128]{3,2,1,0:T(8,128)S(1)} %get-tuple-element.43), channel_id=1, source_target_pairs={{0,1},{1,0},{2,3},{3,2},{4,5},{5,4},{6,7},{7,6},{8,9},{9,8},{10,11... | collective-permute-start | bytes 393224 | tf_op jit(solution)/shard_map/ppermute | solution.py:650
  14.9 0.1 collective-permute-start.8
  15.0 0.0 copy-done
  15.0 2.2 %shard_map.115 = (f32[4,4,32,128]{3,2,1,0:T(8,128)S(1)}, f32[4,4,32,128]{3,2,1,0:T(8,128)S(1)}, f32[4,32,128]{2,1,0:T(8,128)S(1)}, f32[4,32,128]{2,1,0:T(8,128)S(1)}, f32[400,128]{1,0:T(8,128)S(1)}) custom-call(f32[8,96,128]{2,1,0:T(8,128)S(1)} %get-tuple-element.40.chunks.refs_0_, f32[4,4,32,128]{3,2,1,0:T(8,128)S(1)} %get-tuple-element.41.smoothed, ...), custom_call_target="tpu_custom_call" | custom-call | tf_op jit(solution)/shard_map/pallas_call | solution.py:671
  17.2 1.9 %collective-permute-done.7.even_in = f32[2,4,32,128]{3,2,1,0:T(8,128)S(1)} collective-permute-done((f32[2,4,32,128]{3,2,1,0:T(8,128)S(1)}, f32[2,4,32,128]{3,2,1,0:T(8,128)S(1)}, u32[]{:S(2)}, u32[]{:S(2)}) %collective-permute-start.7) | collective-permute-done | bytes 131104 | tf_op jit(solution)/shard_map/ppermute | solution.py:650
  19.1 0.0 collective-permute-done.8.odd_in
  19.1 1.3 %shard_map.116 = (f32[4,4,32,128]{3,2,1,0:T(8,128)S(1)}, f32[4,4,32,128]{3,2,1,0:T(8,128)S(1)}, f32[2,4,32,128]{3,2,1,0:T(8,128)S(1)}, f32[2,4,32,128]{3,2,1,0:T(8,128)S(1)}) custom-call(f32[4,4,32,128]{3,2,1,0:T(8,128)S(1)} %get-tuple-element.42.partial, f32[2,4,32,128]{3,2,1,0:T(8,128)S(1)} %collective-permute-done.7.even_in, ...), custom_call_target="tpu_custom_call" | custom-call | tf_op jit(solution)/shard_map/pallas_call | solution.py:671
  20.5 2.8 %collective-permute-start.9 = (f32[2,4,32,128]{3,2,1,0:T(8,128)S(1)}, f32[2,4,32,128]{3,2,1,0:T(8,128)S(1)}, u32[]{:S(2)}, u32[]{:S(2)}) collective-permute-start(f32[2,4,32,128]{3,2,1,0:T(8,128)S(1)} %get-tuple-element.52), channel_id=1, source_target_pairs={{0,1},{1,0},{2,3},{3,2},{4,5},{5,4},{6,7},{7,6},{8,9},{9,8},{10,11... | collective-permute-start | bytes 393224 | tf_op jit(solution)/shard_map/ppermute | solution.py:650
  23.2 0.0 collective-permute-start.10
  23.2 1.7 %shard_map.117 = (f32[4,4,32,128]{3,2,1,0:T(8,128)S(1)}, f32[8,64,128]{2,1,0:T(8,128)S(1)}) custom-call(f32[4,4,32,128]{3,2,1,0:T(8,128)S(1)} %get-tuple-element.49.forcing, f32[400,128]{1,0:T(8,128)S(1)} %get-tuple-element.45.table.refs_4_, f32[4,4,32,128]{3,2,1,0:T(8,128)S(1)} %get-tuple-element.50.potential), custom_call_target="tpu_custom_call" | custom-call | tf_op jit(solution)/shard_map/pallas_call | solution.py:671
  24.9 1.5 %collective-permute-done.9.refs_2_ = f32[2,4,32,128]{3,2,1,0:T(8,128)S(1)} collective-permute-done((f32[2,4,32,128]{3,2,1,0:T(8,128)S(1)}, f32[2,4,32,128]{3,2,1,0:T(8,128)S(1)}, u32[]{:S(2)}, u32[]{:S(2)}) %collective-permute-start.9) | collective-permute-done | bytes 131104 | tf_op jit(solution)/shard_map/ppermute | solution.py:650
  26.4 0.0 collective-permute-done.10.refs_3_
  26.4 1.1 %shard_map.118 = (f32[2,128,128]{2,1,0:T(8,128)S(1)}, f32[2,128,128]{2,1,0:T(8,128)S(1)}, f32[2,128,128]{2,1,0:T(8,128)S(1)}, f32[2,128,128]{2,1,0:T(8,128)S(1)}) custom-call(f32[8,96,128]{2,1,0:T(8,128)S(1)} %get-tuple-element.40.chunks.refs_0_, f32[4,4,32,128]{3,2,1,0:T(8,128)S(1)} %get-tuple-element.51.refs_1_, ...), custom_call_target="tpu_custom_call" | custom-call | tf_op jit(solution)/shard_map/pallas_call | solution.py:671
  27.5 1.5 %collective-permute-start.11 = (f32[2,128,128]{2,1,0:T(8,128)S(1)}, f32[2,128,128]{2,1,0:T(8,128)S(1)}, u32[]{:S(2)}, u32[]{:S(2)}) collective-permute-start(f32[2,128,128]{2,1,0:T(8,128)S(1)} %get-tuple-element.58), channel_id=1, source_target_pairs={{0,8},{4,12},{8,0},{12,4},{16,24},{20,28},{24,16},{28,20},{1,9},{5... | collective-permute-start | bytes 393224 | tf_op jit(solution)/shard_map/ppermute | solution.py:697
  29.0 0.0 collective-permute-start.17
  29.0 1.5 %collective-permute-start.12 = (f32[2,128,128]{2,1,0:T(8,128)S(1)}, f32[2,128,128]{2,1,0:T(8,128)S(1)}, u32[]{:S(2)}, u32[]{:S(2)}) collective-permute-start(f32[2,128,128]{2,1,0:T(8,128)S(1)} %get-tuple-element.59), channel_id=1, source_target_pairs={{0,24},{4,28},{8,16},{12,20},{16,8},{20,12},{24,0},{28,4},{1,25},{... | collective-permute-start | bytes 393224 | tf_op jit(solution)/shard_map/ppermute | solution.py:697
  30.5 0.6 %collective-permute-start.14 = (f32[2,128,128]{2,1,0:T(8,128)S(1)}, f32[2,128,128]{2,1,0:T(8,128)S(1)}, u32[]{:S(2)}, u32[]{:S(2)}) collective-permute-start(f32[2,128,128]{2,1,0:T(8,128)S(1)} %get-tuple-element.60), channel_id=1, source_target_pairs={{0,16},{4,20},{8,24},{12,28},{16,0},{20,4},{24,8},{28,12},{1,17},{... | collective-permute-start | bytes 393224 | tf_op jit(solution)/shard_map/ppermute | solution.py:697
  31.1 1.4 %collective-permute-done.11.refs_0_ = f32[2,128,128]{2,1,0:T(8,128)S(1)} collective-permute-done((f32[2,128,128]{2,1,0:T(8,128)S(1)}, f32[2,128,128]{2,1,0:T(8,128)S(1)}, u32[]{:S(2)}, u32[]{:S(2)}) %collective-permute-start.11) | collective-permute-done | bytes 131104 | tf_op jit(solution)/shard_map/ppermute | solution.py:697
  32.6 0.0 collective-permute-start.16
  32.6 3.8 %collective-permute-done.12.refs_0_ = f32[2,128,128]{2,1,0:T(8,128)S(1)} collective-permute-done((f32[2,128,128]{2,1,0:T(8,128)S(1)}, f32[2,128,128]{2,1,0:T(8,128)S(1)}, u32[]{:S(2)}, u32[]{:S(2)}) %collective-permute-start.12) | collective-permute-done | bytes 131104 | tf_op jit(solution)/shard_map/ppermute | solution.py:697
  36.3 0.0 collective-permute-start.13
  36.3 2.4 %collective-permute-done.14.refs_1_ = f32[2,128,128]{2,1,0:T(8,128)S(1)} collective-permute-done((f32[2,128,128]{2,1,0:T(8,128)S(1)}, f32[2,128,128]{2,1,0:T(8,128)S(1)}, u32[]{:S(2)}, u32[]{:S(2)}) %collective-permute-start.14) | collective-permute-done | bytes 131104 | tf_op jit(solution)/shard_map/ppermute | solution.py:697
  38.8 0.0 collective-permute-start.15
  38.8 0.0 collective-permute-done.17.refs_1_
  38.8 0.8 %shard_map.119 = (f32[32,16,128]{2,1,0:T(8,128)}, f32[32,16,128]{2,1,0:T(8,128)}) custom-call(s32[32]{0:T(128)S(1)} %get-tuple-element.35.number, f32[2,128,128]{2,1,0:T(8,128)S(1)} %get-tuple-element.61.refs_0_, f32[128,128]{1,0:T(8,128)S(1)} %collective-permute-done.17.refs_1_), custom_call_target="tpu_custom_call" | custom-call | tf_op jit(solution)/shard_map/pallas_call | solution.py:671
  39.6 0.8 %shard_map.120 = (f32[32,16,128]{2,1,0:T(8,128)}, f32[32,16,128]{2,1,0:T(8,128)}) custom-call(s32[32]{0:T(128)S(1)} %get-tuple-element.35.number, f32[2,128,128]{2,1,0:T(8,128)S(1)} %collective-permute-done.12.refs_0_, f32[2,128,128]{2,1,0:T(8,128)S(1)} %collective-permute-done.14.refs_1_, ...), custom_call_target="tpu_custom_call", output_to_operand_aliasing={{0}: (3, {}), {1}: (4, {})} | custom-call | tf_op jit(solution)/shard_map/pallas_call | solution.py:671
  40.4 0.0 collective-permute-done.16.refs_3_
  40.5 0.0 collective-permute-done.13.refs_1_
  40.5 0.0 collective-permute-done.15.refs_2_
  40.5 0.9 %shard_map.121 = (f32[32,16,128]{2,1,0:T(8,128)}, f32[32,16,128]{2,1,0:T(8,128)}) custom-call(s32[32]{0:T(128)S(1)} %get-tuple-element.35.number, f32[2,128,128]{2,1,0:T(8,128)S(1)} %collective-permute-done.11.refs_0_, f32[128,128]{1,0:T(8,128)S(1)} %collective-permute-done.13.refs_1_, ...), custom_call_target="tpu_custom_call", output_to_operand_aliasing={{0}: (5, {}), {1}: (6, {})} | custom-call | tf_op jit(solution)/shard_map/pallas_call | solution.py:671
  (8 shorter events, 0.0 us)
Async XLA Ops:
  1.9 7.1 %collective-permute-start = (f32[2,96,128]{2,1,0:T(8,128)S(1)}, f32[2,96,128]{2,1,0:T(8,128)S(1)}, u32[]{:S(2)}, u32[]{:S(2)}) collective-permute-start(f32[2,96,128]{2,1,0:T(8,128)S(1)} %get-tuple-element.37), channel_id=1, source_target_pairs={{0,24},{4,28},{8,16},{12,20},{16,8},{20,12},{24,0},{28,4},{1,25},{... | collective-permute-start | bytes 294920 | tf_op jit(solution)/shard_map/ppermute | solution.py:697
  5.9 5.8 %collective-permute-start.3 = (f32[96,128]{1,0:T(8,128)S(1)}, f32[96,128]{1,0:T(8,128)S(1)}, u32[]{:S(2)}, u32[]{:S(2)}) collective-permute-start(f32[96,128]{1,0:T(8,128)S(1)} %slice_bitcast_fusion.7), channel_id=1, source_target_pairs={{0,4},{4,0},{8,12},{12,8},{16,20},{20,16},{24,28},{28,24},{1,5},{5... | collective-permute-start | bytes 147464 | tf_op jit(solution)/shard_map/ppermute | solution.py:697
  5.9 5.2 %collective-permute-start.1 = (f32[2,96,128]{2,1,0:T(8,128)S(1)}, f32[2,96,128]{2,1,0:T(8,128)S(1)}, u32[]{:S(2)}, u32[]{:S(2)}) collective-permute-start(f32[2,96,128]{2,1,0:T(8,128)S(1)} %get-tuple-element.38), channel_id=1, source_target_pairs={{0,16},{4,20},{8,24},{12,28},{16,0},{20,4},{24,8},{28,12},{1,17},{... | collective-permute-start | bytes 294920 | tf_op jit(solution)/shard_map/ppermute | solution.py:697
  6.5 4.9 %collective-permute-start.2 = (f32[2,96,128]{2,1,0:T(8,128)S(1)}, f32[2,96,128]{2,1,0:T(8,128)S(1)}, u32[]{:S(2)}, u32[]{:S(2)}) collective-permute-start(f32[2,96,128]{2,1,0:T(8,128)S(1)} %get-tuple-element.39), channel_id=1, source_target_pairs={{0,8},{4,12},{8,0},{12,4},{16,24},{20,28},{24,16},{28,20},{1,9},{5... | collective-permute-start | bytes 294920 | tf_op jit(solution)/shard_map/ppermute | solution.py:697
  9.0 2.7 %collective-permute-start.4 = (f32[96,128]{1,0:T(8,128)S(1)}, f32[96,128]{1,0:T(8,128)S(1)}, u32[]{:S(2)}, u32[]{:S(2)}) collective-permute-start(f32[96,128]{1,0:T(8,128)S(1)} %slice_bitcast_fusion.6), channel_id=1, source_target_pairs={{0,4},{4,0},{8,12},{12,8},{16,20},{20,16},{24,28},{28,24},{1,5},{5... | collective-permute-start | bytes 147464 | tf_op jit(solution)/shard_map/ppermute | solution.py:697
  11.1 1.2 %collective-permute-start.5 = (f32[96,128]{1,0:T(8,128)S(1)}, f32[96,128]{1,0:T(8,128)S(1)}, u32[]{:S(2)}, u32[]{:S(2)}) collective-permute-start(f32[96,128]{1,0:T(8,128)S(1)} %slice_bitcast_fusion.5), channel_id=1, source_target_pairs={{0,4},{4,0},{8,12},{12,8},{16,20},{20,16},{24,28},{28,24},{1,5},{5... | collective-permute-start | bytes 147464 | tf_op jit(solution)/shard_map/ppermute | solution.py:697
  11.3 3.7 %copy-start = (f32[8,4,4,5,5]{0,2,4,3,1:T(4,128)S(1)}, f32[8,4,4,5,5]{0,2,4,3,1:T(4,128)}, u32[]{:S(2)}) copy-start(f32[8,4,4,5,5]{0,2,4,3,1:T(4,128)} %param.12) | copy-start | bytes 38404
  11.3 1.2 %collective-permute-start.6 = (f32[96,128]{1,0:T(8,128)S(1)}, f32[96,128]{1,0:T(8,128)S(1)}, u32[]{:S(2)}, u32[]{:S(2)}) collective-permute-start(f32[96,128]{1,0:T(8,128)S(1)} %slice_bitcast_fusion.4), channel_id=1, source_target_pairs={{0,4},{4,0},{8,12},{12,8},{16,20},{20,16},{24,28},{28,24},{1,5},{5... | collective-permute-start | bytes 147464 | tf_op jit(solution)/shard_map/ppermute | solution.py:697
  13.3 5.8 %collective-permute-start.7 = (f32[2,4,32,128]{3,2,1,0:T(8,128)S(1)}, f32[2,4,32,128]{3,2,1,0:T(8,128)S(1)}, u32[]{:S(2)}, u32[]{:S(2)}) collective-permute-start(f32[2,4,32,128]{3,2,1,0:T(8,128)S(1)} %get-tuple-element.43), channel_id=1, source_target_pairs={{0,1},{1,0},{2,3},{3,2},{4,5},{5,4},{6,7},{7,6},{8,9},{9,8},{10,11... | collective-permute-start | bytes 393224 | tf_op jit(solution)/shard_map/ppermute | solution.py:650
  14.9 4.2 %collective-permute-start.8 = (f32[2,4,32,128]{3,2,1,0:T(8,128)S(1)}, f32[2,4,32,128]{3,2,1,0:T(8,128)S(1)}, u32[]{:S(2)}, u32[]{:S(2)}) collective-permute-start(f32[2,4,32,128]{3,2,1,0:T(8,128)S(1)} %get-tuple-element.44), channel_id=1, source_target_pairs={{0,4},{1,2},{2,1},{3,7},{4,0},{5,6},{6,5},{7,3},{8,12},{9,10},{10,... | collective-permute-start | bytes 393224 | tf_op jit(solution)/shard_map/ppermute | solution.py:650
  20.5 6.0 %collective-permute-start.9 = (f32[2,4,32,128]{3,2,1,0:T(8,128)S(1)}, f32[2,4,32,128]{3,2,1,0:T(8,128)S(1)}, u32[]{:S(2)}, u32[]{:S(2)}) collective-permute-start(f32[2,4,32,128]{3,2,1,0:T(8,128)S(1)} %get-tuple-element.52), channel_id=1, source_target_pairs={{0,1},{1,0},{2,3},{3,2},{4,5},{5,4},{6,7},{7,6},{8,9},{9,8},{10,11... | collective-permute-start | bytes 393224 | tf_op jit(solution)/shard_map/ppermute | solution.py:650
  23.2 3.2 %collective-permute-start.10 = (f32[2,4,32,128]{3,2,1,0:T(8,128)S(1)}, f32[2,4,32,128]{3,2,1,0:T(8,128)S(1)}, u32[]{:S(2)}, u32[]{:S(2)}) collective-permute-start(f32[2,4,32,128]{3,2,1,0:T(8,128)S(1)} %get-tuple-element.53), channel_id=1, source_target_pairs={{0,4},{1,2},{2,1},{3,7},{4,0},{5,6},{6,5},{7,3},{8,12},{9,10},{10,... | collective-permute-start | bytes 393224 | tf_op jit(solution)/shard_map/ppermute | solution.py:650
  27.5 5.0 %collective-permute-start.11 = (f32[2,128,128]{2,1,0:T(8,128)S(1)}, f32[2,128,128]{2,1,0:T(8,128)S(1)}, u32[]{:S(2)}, u32[]{:S(2)}) collective-permute-start(f32[2,128,128]{2,1,0:T(8,128)S(1)} %get-tuple-element.58), channel_id=1, source_target_pairs={{0,8},{4,12},{8,0},{12,4},{16,24},{20,28},{24,16},{28,20},{1,9},{5... | collective-permute-start | bytes 393224 | tf_op jit(solution)/shard_map/ppermute | solution.py:697
  29.0 9.8 %collective-permute-start.17 = (f32[128,128]{1,0:T(8,128)S(1)}, f32[128,128]{1,0:T(8,128)S(1)}, u32[]{:S(2)}, u32[]{:S(2)}) collective-permute-start(f32[128,128]{1,0:T(8,128)S(1)} %slice_bitcast_fusion.3), channel_id=1, source_target_pairs={{0,4},{4,0},{8,12},{12,8},{16,20},{20,16},{24,28},{28,24},{1,5},{5... | collective-permute-start | bytes 196616 | tf_op jit(solution)/shard_map/ppermute | solution.py:697
  29.0 7.3 %collective-permute-start.12 = (f32[2,128,128]{2,1,0:T(8,128)S(1)}, f32[2,128,128]{2,1,0:T(8,128)S(1)}, u32[]{:S(2)}, u32[]{:S(2)}) collective-permute-start(f32[2,128,128]{2,1,0:T(8,128)S(1)} %get-tuple-element.59), channel_id=1, source_target_pairs={{0,24},{4,28},{8,16},{12,20},{16,8},{20,12},{24,0},{28,4},{1,25},{... | collective-permute-start | bytes 393224 | tf_op jit(solution)/shard_map/ppermute | solution.py:697
  30.5 8.2 %collective-permute-start.14 = (f32[2,128,128]{2,1,0:T(8,128)S(1)}, f32[2,128,128]{2,1,0:T(8,128)S(1)}, u32[]{:S(2)}, u32[]{:S(2)}) collective-permute-start(f32[2,128,128]{2,1,0:T(8,128)S(1)} %get-tuple-element.60), channel_id=1, source_target_pairs={{0,16},{4,20},{8,24},{12,28},{16,0},{20,4},{24,8},{28,12},{1,17},{... | collective-permute-start | bytes 393224 | tf_op jit(solution)/shard_map/ppermute | solution.py:697
  32.6 7.9 %collective-permute-start.16 = (f32[128,128]{1,0:T(8,128)S(1)}, f32[128,128]{1,0:T(8,128)S(1)}, u32[]{:S(2)}, u32[]{:S(2)}) collective-permute-start(f32[128,128]{1,0:T(8,128)S(1)} %slice_bitcast_fusion), channel_id=1, source_target_pairs={{0,4},{4,0},{8,12},{12,8},{16,20},{20,16},{24,28},{28,24},{1,5},{5... | collective-permute-start | bytes 196616 | tf_op jit(solution)/shard_map/ppermute | solution.py:697
  36.3 4.1 %collective-permute-start.13 = (f32[128,128]{1,0:T(8,128)S(1)}, f32[128,128]{1,0:T(8,128)S(1)}, u32[]{:S(2)}, u32[]{:S(2)}) collective-permute-start(f32[128,128]{1,0:T(8,128)S(1)} %slice_bitcast_fusion.2), channel_id=1, source_target_pairs={{0,4},{4,0},{8,12},{12,8},{16,20},{20,16},{24,28},{28,24},{1,5},{5... | collective-permute-start | bytes 196616 | tf_op jit(solution)/shard_map/ppermute | solution.py:697
  38.8 1.7 %collective-permute-start.15 = (f32[128,128]{1,0:T(8,128)S(1)}, f32[128,128]{1,0:T(8,128)S(1)}, u32[]{:S(2)}, u32[]{:S(2)}) collective-permute-start(f32[128,128]{1,0:T(8,128)S(1)} %slice_bitcast_fusion.1), channel_id=1, source_target_pairs={{0,4},{4,0},{8,12},{12,8},{16,20},{20,16},{24,28},{28,24},{1,5},{5... | collective-permute-start | bytes 196616 | tf_op jit(solution)/shard_map/ppermute | solution.py:697

commit v9 on v8

--- a/solution.py
+++ b/solution.py
@@ -295,6 +295,17 @@
         place_control(target, channels, control)
 
 
+def join_kernel(got, *refs):
+    keep, joined = refs[:4], refs[4:]
+    for k in range(4):
+        joined[k][0] = keep[k][...]
+        joined[k][1] = got[k]
+
+
+def second_kernel(both, out):
+    out[...] = both[1]
+
+
 def coefficient(expanded, lag, z):
     block, local = divmod(z, 4)
     k = (lag - 1) * 4 + local
@@ -571,9 +582,11 @@
 
 def gradient_kernel(*refs):
     chunks, partial, even_in, odd_in, taps, table, scale, root, potential = refs[:9]
-    chips, (first, rows, out) = refs[9:13], refs[13:]
+    give, keep, (first, rows, out) = refs[9], refs[10:14], refs[14:]
     me = lax.axis_index("depth")
-    targets = [chips[place // 2].at[place % 2] for place in range(8)]
+    targets = [
+        give.at[place // 2] if place % 2 else keep[place // 2] for place in range(8)
+    ]
     for place, target in enumerate(targets):
         target[:64, :] = potential[me ^ place]
 
@@ -612,29 +625,30 @@
         target[64:, :] = out[me ^ place]
 
 
-def unpack_kernel(places, number, *refs):
-    count = len(places)
+def unpack_kernel(chips, number, *refs):
+    count = len(chips)
     parts, (potential, gradient, planes, sent) = refs[:count], refs[-4:]
     me = lax.axis_index("depth")
     order = number[...].reshape(1, 32)
     lane = lane_index((1, 32))
     channels = []
-    for slot in range(4 * count):
-        here = lane == (me ^ places[slot // 4]) * 4 + slot % 4
+    for slot in range(8 * count):
+        place = 2 * chips[slot // 8] + slot // 4 % 2
+        here = lane == (me ^ place) * 4 + slot % 4
         channels.append(jnp.sum(jnp.where(here, order, 0)))
     for half in range(2):
-        for slot in range(4 * count):
-            place, part = places[slot // 4], parts[slot // 4]
-            part = part if place % 2 else part.at[0]
-            rows = [64 * half + z * 16 + slot % 4 * 4 for z in range(4)]
-            planes[half, slot] = jnp.concatenate([part[row : row + 4, :] for row in rows], axis=0)
-    for slot in range(4 * count):
+        for slot in range(8 * count):
+            k, source, c = slot // 8, slot // 4 % 2, slot % 4
+            rows = [64 * half + z * 16 + c * 4 for z in range(4)]
+            pieces = [parts[k][source, row : row + 4, :] for row in rows]
+            planes[half, slot] = jnp.concatenate(pieces, axis=0)
+    for slot in range(8 * count):
         for half, out in enumerate((potential, gradient)):
             pltpu.make_async_copy(
                 planes.at[half, slot], out.at[channels[slot]], sent.at[half]
             ).start()
     for half, out in enumerate((potential, gradient)):
-        pltpu.make_async_copy(planes.at[half], out.at[: 4 * count], sent.at[half]).wait()
+        pltpu.make_async_copy(planes.at[half], out.at[: 8 * count], sent.at[half]).wait()
 
 
 def swapped(even, odd):
@@ -692,12 +706,17 @@
     sources = tuple(pltpu.with_memory_space_constraint(x, pltpu.HBM) for x in sources)
     held = [pltpu.VMEM(source.shape, source.dtype) for source in sources[1:8]]
 
+    def swap(value, flip):
+        return lax.ppermute(value, "depth", [(i, i ^ flip) for i in range(8)])
+
     def exchange(*chips):
-        def swap(value, flip):
-            return lax.ppermute(value, "depth", [(i, i ^ flip) for i in range(8)])
-
         direct = [chips[k] if k == 0 else swap(chips[k], 2 * k) for k in CHIPS]
-        return direct, [swap(part[1], 1) for part in direct]
+        passed = [call(second_kernel, f32(*part.shape[1:]), (part,)) for part in direct]
+        return direct, [swap(part, 1) for part in passed]
+
+    def exchange_home(give, *keep):
+        joined = call(join_kernel, (f32(2, 128, 128),) * 4, (swap(give, 1), *keep))
+        return [joined[k] if k == 0 else swap(joined[k], 2 * k) for k in CHIPS]
 
     *chips, number = call(
         pack_kernel,
@@ -737,24 +756,22 @@
     partial, potential = call(
         spread_kernel, (field, f32(8, 64, 128)), (forcing, taps, potential), [rows]
     )
-    chips = call(
+    give, *keep = call(
         gradient_kernel,
-        (f32(2, 128, 128),) * 4,
+        (f32(4, 128, 128),) + (f32(128, 128),) * 4,
         (chunks, partial, even, odd, taps, table, scale, root, potential),
         [first, rows, pltpu.VMEM((8, 64, 128), jnp.float32)],
     )
-    direct, passed = exchange(*chips)
-    came = {2 * k: part for k, part in zip(CHIPS, direct)}
-    came |= {2 * k + 1: part for k, part in zip(CHIPS, passed)}
+    parts = exchange_home(give, *keep)
     outs = ()
-    for places in ((0, 1), (2 * CHIPS[1], 2 * CHIPS[2]), (2 * CHIPS[3], 7, 5, 3)):
-        count = len(places)
+    for some in (slice(0, 1), slice(1, 2), slice(2, 4)):
+        count = len(CHIPS[some])
         outs = call(
-            functools.partial(unpack_kernel, places),
+            functools.partial(unpack_kernel, CHIPS[some]),
             (by_depth, by_depth),
-            (number, *(came[place] for place in places), *outs),
+            (number, *parts[some], *outs),
             [
-                pltpu.VMEM((2, 4 * count, 16, 128), jnp.float32),
+                pltpu.VMEM((2, 8 * count, 16, 128), jnp.float32),
                 pltpu.SemaphoreType.DMA((2,)),
             ],
             [in_vmem] * (count + 1) + [in_hbm] * len(outs),

time: 41.6 us -> 39.5 us (0.950)
  waiting for transfers between devices: 16.6 us -> 14.5 us
    ppermute x14 -> x11, waiting for transfers between devices: 13.2 us -> 11.2 us  [swap(): return lax.ppermute(value, 'depth', [(i, i ^ flip) for i in range(8)])]
    ppermute x14 -> x11, starting transfers between devices: 8.68 us -> 8.49 us  [swap(): return lax.ppermute(value, 'depth', [(i, i ^ flip) for i in range(8)])]
    pallas_call x9 -> x14, Pallas kernels: 10.8 us -> 10.8 us  [call(): pl.pallas_call(kernel, out_shape=outs, in_specs=ins or [in_vmem] * len(op...]
  transfers between devices with their start and end apart: 18 -> 15, of which waited for: 10 -> 10; matrix products, arithmetic and copies ran while one was open for 0% -> 0% of each run, Pallas kernels for 13% -> 14%
where the time goes in v9:
time: 39.5 us; the launch traced here: 39.3 us
  waiting for transfers between devices  14.5 us (37%)
  starting transfers between devices  13.3 us (34%)
  Pallas kernels  10.8 us (27%)
  between operations  0.72 us (2%)
    ppermute x11, waiting for transfers between devices, swap(): return lax.ppermute(value, 'depth', [(i, i ^ flip) for i in range(8)])  11.2 us
    pallas_call x14, Pallas kernels, call(): pl.pallas_call(kernel, out_shape=outs, in_specs=ins or [in_vmem] * len(op...  10.8 us
    ppermute x11, starting transfers between devices, swap(): return lax.ppermute(value, 'depth', [(i, i ^ flip) for i in range(8)])  8.49 us
    ppermute x4, starting transfers between devices, swap(): return lax.ppermute(value, ('depth', 'inline'), pairs)  4.82 us
    ppermute x4, waiting for transfers between devices, swap(): return lax.ppermute(value, ('depth', 'inline'), pairs)  3.25 us
  transfers between devices with their start and end apart: 15, of which 10 were waited for; matrix products, arithmetic and copies ran while one was open for 0% of the time, Pallas kernels for 14%

profile of v9, /device:TPU:0, one launch (start us, length us, event | category | flops | bytes accessed | tf_op | source)
XLA Modules:
  0.0 39.3 jit_solution(17068506767201944616)
XLA Ops:
  0.6 1.3 %shard_map.113 = (f32[2,96,128]{2,1,0:T(8,128)S(1)}, f32[2,96,128]{2,1,0:T(8,128)S(1)}, f32[2,96,128]{2,1,0:T(8,128)S(1)}, f32[2,96,128]{2,1,0:T(8,128)S(1)}, s32[32]{0:T(128)S(1)}) custom-call(s32[32]{0:T(128)} %refs_0_.1, f32[16,32]{1,0:T(8,128)} %bitcast.17, s32[3,1,1,256]{3,2,1,0:T(1,128)} %refs_2_.1, f32[1,1,256]{2,1,0:T(1,128)} %refs_3_.1, ...), custom_call_target="tpu_custom_call" | custom-call | tf_op jit(solution)/shard_map/pallas_call | solution.py:685
  1.9 4.0 %collective-permute-start = (f32[2,96,128]{2,1,0:T(8,128)S(1)}, f32[2,96,128]{2,1,0:T(8,128)S(1)}, u32[]{:S(2)}, u32[]{:S(2)}) collective-permute-start(f32[2,96,128]{2,1,0:T(8,128)S(1)} %get-tuple-element.42), channel_id=1, source_target_pairs={{0,24},{4,28},{8,16},{12,20},{16,8},{20,12},{24,0},{28,4},{1,25},{... | collective-permute-start | bytes 294920 | tf_op jit(solution)/shard_map/ppermute | solution.py:710
  5.9 0.5 %collective-permute-start.1 = (f32[2,96,128]{2,1,0:T(8,128)S(1)}, f32[2,96,128]{2,1,0:T(8,128)S(1)}, u32[]{:S(2)}, u32[]{:S(2)}) collective-permute-start(f32[2,96,128]{2,1,0:T(8,128)S(1)} %get-tuple-element.43), channel_id=1, source_target_pairs={{0,16},{4,20},{8,24},{12,28},{16,0},{20,4},{24,8},{28,12},{1,17},{... | collective-permute-start | bytes 294920 | tf_op jit(solution)/shard_map/ppermute | solution.py:710
  6.4 0.1 collective-permute-start.2
  6.5 0.0 collective-permute-start.3
  6.5 2.5 %collective-permute-done.both.refs_1_ = f32[2,96,128]{2,1,0:T(8,128)S(1)} collective-permute-done((f32[2,96,128]{2,1,0:T(8,128)S(1)}, f32[2,96,128]{2,1,0:T(8,128)S(1)}, u32[]{:S(2)}, u32[]{:S(2)}) %collective-permute-start) | collective-permute-done | bytes 98336 | tf_op jit(solution)/shard_map/ppermute | solution.py:710
  9.1 0.0 collective-permute-start.4
  9.1 1.7 %collective-permute-done.1.both.refs_2_ = f32[2,96,128]{2,1,0:T(8,128)S(1)} collective-permute-done((f32[2,96,128]{2,1,0:T(8,128)S(1)}, f32[2,96,128]{2,1,0:T(8,128)S(1)}, u32[]{:S(2)}, u32[]{:S(2)}) %collective-permute-start.1) | collective-permute-done | bytes 98336 | tf_op jit(solution)/shard_map/ppermute | solution.py:710
  10.8 0.0 collective-permute-start.5
  10.8 0.3 collective-permute-done.2.both.refs_3_
  11.1 0.0 copy-start
  11.1 0.3 collective-permute-start.6
  11.4 0.0 collective-permute-done.3.refs_4_
  11.4 0.0 collective-permute-done.4.refs_5_
  11.4 0.6 %collective-permute-done.5.refs_6_ = f32[96,128]{1,0:T(8,128)S(1)} collective-permute-done((f32[96,128]{1,0:T(8,128)S(1)}, f32[96,128]{1,0:T(8,128)S(1)}, u32[]{:S(2)}, u32[]{:S(2)}) %collective-permute-start.5) | collective-permute-done | bytes 49184 | tf_op jit(solution)/shard_map/ppermute | solution.py:710
  12.0 0.3 collective-permute-done.6.refs_7_
  12.4 0.7 %shard_map.118 = (f32[8,96,128]{2,1,0:T(8,128)S(1)}, f32[4,4,32,128]{3,2,1,0:T(8,128)S(1)}, f32[2,4,32,128]{3,2,1,0:T(8,128)S(1)}, f32[2,4,32,128]{3,2,1,0:T(8,1...) custom-call(f32[2,96,128]{2,1,0:T(8,128)S(1)} %get-tuple-element.41.both.refs_0_, ...), custom_call_target="tpu_custom_call" | custom-call | tf_op jit(solution)/shard_map/pallas_call | solution.py:685
  13.1 1.8 %collective-permute-start.7 = (f32[2,4,32,128]{3,2,1,0:T(8,128)S(1)}, f32[2,4,32,128]{3,2,1,0:T(8,128)S(1)}, u32[]{:S(2)}, u32[]{:S(2)}) collective-permute-start(f32[2,4,32,128]{3,2,1,0:T(8,128)S(1)} %get-tuple-element.48), channel_id=1, source_target_pairs={{0,1},{1,0},{2,3},{3,2},{4,5},{5,4},{6,7},{7,6},{8,9},{9,8},{10,11... | collective-permute-start | bytes 393224 | tf_op jit(solution)/shard_map/ppermute | solution.py:664
  14.9 0.1 collective-permute-start.8
  15.0 0.0 copy-done
  15.0 2.2 %shard_map.119 = (f32[4,4,32,128]{3,2,1,0:T(8,128)S(1)}, f32[4,4,32,128]{3,2,1,0:T(8,128)S(1)}, f32[4,32,128]{2,1,0:T(8,128)S(1)}, f32[4,32,128]{2,1,0:T(8,128)S(1)}, f32[400,128]{1,0:T(8,128)S(1)}) custom-call(f32[8,96,128]{2,1,0:T(8,128)S(1)} %get-tuple-element.45.chunks.refs_0_, f32[4,4,32,128]{3,2,1,0:T(8,128)S(1)} %get-tuple-element.46.smoothed, ...), custom_call_target="tpu_custom_call" | custom-call | tf_op jit(solution)/shard_map/pallas_call | solution.py:685
  17.2 1.7 %collective-permute-done.7.even_in = f32[2,4,32,128]{3,2,1,0:T(8,128)S(1)} collective-permute-done((f32[2,4,32,128]{3,2,1,0:T(8,128)S(1)}, f32[2,4,32,128]{3,2,1,0:T(8,128)S(1)}, u32[]{:S(2)}, u32[]{:S(2)}) %collective-permute-start.7) | collective-permute-done | bytes 131104 | tf_op jit(solution)/shard_map/ppermute | solution.py:664
  18.9 0.0 collective-permute-done.8.odd_in
  18.9 1.3 %shard_map.120 = (f32[4,4,32,128]{3,2,1,0:T(8,128)S(1)}, f32[4,4,32,128]{3,2,1,0:T(8,128)S(1)}, f32[2,4,32,128]{3,2,1,0:T(8,128)S(1)}, f32[2,4,32,128]{3,2,1,0:T(8,128)S(1)}) custom-call(f32[4,4,32,128]{3,2,1,0:T(8,128)S(1)} %get-tuple-element.47.partial, f32[2,4,32,128]{3,2,1,0:T(8,128)S(1)} %collective-permute-done.7.even_in, ...), custom_call_target="tpu_custom_call" | custom-call | tf_op jit(solution)/shard_map/pallas_call | solution.py:685
  20.3 2.9 %collective-permute-start.9 = (f32[2,4,32,128]{3,2,1,0:T(8,128)S(1)}, f32[2,4,32,128]{3,2,1,0:T(8,128)S(1)}, u32[]{:S(2)}, u32[]{:S(2)}) collective-permute-start(f32[2,4,32,128]{3,2,1,0:T(8,128)S(1)} %get-tuple-element.57), channel_id=1, source_target_pairs={{0,1},{1,0},{2,3},{3,2},{4,5},{5,4},{6,7},{7,6},{8,9},{9,8},{10,11... | collective-permute-start | bytes 393224 | tf_op jit(solution)/shard_map/ppermute | solution.py:664
  23.2 0.0 collective-permute-start.10
  23.2 1.7 %shard_map.121 = (f32[4,4,32,128]{3,2,1,0:T(8,128)S(1)}, f32[8,64,128]{2,1,0:T(8,128)S(1)}) custom-call(f32[4,4,32,128]{3,2,1,0:T(8,128)S(1)} %get-tuple-element.54.forcing, f32[400,128]{1,0:T(8,128)S(1)} %get-tuple-element.50.table.refs_4_, f32[4,4,32,128]{3,2,1,0:T(8,128)S(1)} %get-tuple-element.55.potential), custom_call_target="tpu_custom_call" | custom-call | tf_op jit(solution)/shard_map/pallas_call | solution.py:685
  24.9 1.5 %collective-permute-done.9.refs_2_ = f32[2,4,32,128]{3,2,1,0:T(8,128)S(1)} collective-permute-done((f32[2,4,32,128]{3,2,1,0:T(8,128)S(1)}, f32[2,4,32,128]{3,2,1,0:T(8,128)S(1)}, u32[]{:S(2)}, u32[]{:S(2)}) %collective-permute-start.9) | collective-permute-done | bytes 131104 | tf_op jit(solution)/shard_map/ppermute | solution.py:664
  26.4 0.0 collective-permute-done.10.refs_3_
  26.4 1.1 %shard_map.122 = (f32[4,128,128]{2,1,0:T(8,128)S(1)}, f32[128,128]{1,0:T(8,128)S(1)}, f32[128,128]{1,0:T(8,128)S(1)}, f32[128,128]{1,0:T(8,128)S(1)}, f32[128,128]{1,0:T(8,128)S(1)}) custom-call(f32[8,96,128]{2,1,0:T(8,128)S(1)} %get-tuple-element.45.chunks.refs_0_, f32[4,4,32,128]{3,2,1,0:T(8,128)S(1)} %get-tuple-element.56.refs_1_, ...), custom_call_target="tpu_custom_call" | custom-call | tf_op jit(solution)/shard_map/pallas_call | solution.py:685
  27.5 0.1 collective-permute-start.11
  27.6 1.5 %collective-permute-done.11.got = f32[4,128,128]{2,1,0:T(8,128)S(1)} collective-permute-done((f32[4,128,128]{2,1,0:T(8,128)S(1)}, f32[4,128,128]{2,1,0:T(8,128)S(1)}, u32[]{:S(2)}, u32[]{:S(2)}) %collective-permute-start.11) | collective-permute-done | bytes 262176 | tf_op jit(solution)/shard_map/ppermute | solution.py:710
  29.1 1.6 %collective-permute-start.14 = (f32[2,128,128]{2,1,0:T(8,128)S(1)}, f32[2,128,128]{2,1,0:T(8,128)S(1)}, u32[]{:S(2)}, u32[]{:S(2)}) collective-permute-start(f32[2,128,128]{2,1,0:T(8,128)S(1)} %get-tuple-element.70), channel_id=1, source_target_pairs={{0,24},{4,28},{8,16},{12,20},{16,8},{20,12},{24,0},{28,4},{1,25},{... | collective-permute-start | bytes 393224 | tf_op jit(solution)/shard_map/ppermute | solution.py:710
  30.7 1.4 %collective-permute-start.12 = (f32[2,128,128]{2,1,0:T(8,128)S(1)}, f32[2,128,128]{2,1,0:T(8,128)S(1)}, u32[]{:S(2)}, u32[]{:S(2)}) collective-permute-start(f32[2,128,128]{2,1,0:T(8,128)S(1)} %get-tuple-element.68), channel_id=1, source_target_pairs={{0,16},{4,20},{8,24},{12,28},{16,0},{20,4},{24,8},{28,12},{1,17},{... | collective-permute-start | bytes 393224 | tf_op jit(solution)/shard_map/ppermute | solution.py:710
  32.1 0.6 %collective-permute-start.13 = (f32[2,128,128]{2,1,0:T(8,128)S(1)}, f32[2,128,128]{2,1,0:T(8,128)S(1)}, u32[]{:S(2)}, u32[]{:S(2)}) collective-permute-start(f32[2,128,128]{2,1,0:T(8,128)S(1)} %get-tuple-element.69), channel_id=1, source_target_pairs={{0,8},{4,12},{8,0},{12,4},{16,24},{20,28},{24,16},{28,20},{1,9},{5... | collective-permute-start | bytes 393224 | tf_op jit(solution)/shard_map/ppermute | solution.py:710
  32.7 0.8 %shard_map.124 = (f32[32,16,128]{2,1,0:T(8,128)}, f32[32,16,128]{2,1,0:T(8,128)}) custom-call(s32[32]{0:T(128)S(1)} %get-tuple-element.40.number, f32[2,128,128]{2,1,0:T(8,128)S(1)} %get-tuple-element.71.refs_0_), custom_call_target="tpu_custom_call" | custom-call | tf_op jit(solution)/shard_map/pallas_call | solution.py:685
  33.5 3.0 %collective-permute-done.14.refs_0_ = f32[2,128,128]{2,1,0:T(8,128)S(1)} collective-permute-done((f32[2,128,128]{2,1,0:T(8,128)S(1)}, f32[2,128,128]{2,1,0:T(8,128)S(1)}, u32[]{:S(2)}, u32[]{:S(2)}) %collective-permute-start.14) | collective-permute-done | bytes 131104 | tf_op jit(solution)/shard_map/ppermute | solution.py:710
  36.4 0.8 %shard_map.125 = (f32[32,16,128]{2,1,0:T(8,128)}, f32[32,16,128]{2,1,0:T(8,128)}) custom-call(s32[32]{0:T(128)S(1)} %get-tuple-element.40.number, f32[2,128,128]{2,1,0:T(8,128)S(1)} %collective-permute-done.14.refs_0_, f32[32,16,128]{2,1,0:T(8,128)} %get-tuple-element.72.refs_1_, ...), custom_call_target="tpu_custom_call", output_to_operand_aliasing={{0}: (2, {}), {1}: (3, {})} | custom-call | tf_op jit(solution)/shard_map/pallas_call | solution.py:685
  37.2 1.2 %collective-permute-done.12.refs_0_ = f32[2,128,128]{2,1,0:T(8,128)S(1)} collective-permute-done((f32[2,128,128]{2,1,0:T(8,128)S(1)}, f32[2,128,128]{2,1,0:T(8,128)S(1)}, u32[]{:S(2)}, u32[]{:S(2)}) %collective-permute-start.12) | collective-permute-done | bytes 131104 | tf_op jit(solution)/shard_map/ppermute | solution.py:710
  38.4 0.0 collective-permute-done.13.refs_1_
  38.4 0.9 %shard_map.126 = (f32[32,16,128]{2,1,0:T(8,128)}, f32[32,16,128]{2,1,0:T(8,128)}) custom-call(s32[32]{0:T(128)S(1)} %get-tuple-element.40.number, f32[2,128,128]{2,1,0:T(8,128)S(1)} %collective-permute-done.12.refs_0_, f32[2,128,128]{2,1,0:T(8,128)S(1)} %collective-permute-done.13.refs_1_, ...), custom_call_target="tpu_custom_call", output_to_operand_aliasing={{0}: (3, {}), {1}: (4, {})} | custom-call | tf_op jit(solution)/shard_map/pallas_call | solution.py:685
  (5 shorter events, 0.1 us)
Async XLA Ops:
  1.9 7.1 %collective-permute-start = (f32[2,96,128]{2,1,0:T(8,128)S(1)}, f32[2,96,128]{2,1,0:T(8,128)S(1)}, u32[]{:S(2)}, u32[]{:S(2)}) collective-permute-start(f32[2,96,128]{2,1,0:T(8,128)S(1)} %get-tuple-element.42), channel_id=1, source_target_pairs={{0,24},{4,28},{8,16},{12,20},{16,8},{20,12},{24,0},{28,4},{1,25},{... | collective-permute-start | bytes 294920 | tf_op jit(solution)/shard_map/ppermute | solution.py:710
  5.9 4.9 %collective-permute-start.1 = (f32[2,96,128]{2,1,0:T(8,128)S(1)}, f32[2,96,128]{2,1,0:T(8,128)S(1)}, u32[]{:S(2)}, u32[]{:S(2)}) collective-permute-start(f32[2,96,128]{2,1,0:T(8,128)S(1)} %get-tuple-element.43), channel_id=1, source_target_pairs={{0,16},{4,20},{8,24},{12,28},{16,0},{20,4},{24,8},{28,12},{1,17},{... | collective-permute-start | bytes 294920 | tf_op jit(solution)/shard_map/ppermute | solution.py:710
  6.4 4.7 %collective-permute-start.2 = (f32[2,96,128]{2,1,0:T(8,128)S(1)}, f32[2,96,128]{2,1,0:T(8,128)S(1)}, u32[]{:S(2)}, u32[]{:S(2)}) collective-permute-start(f32[2,96,128]{2,1,0:T(8,128)S(1)} %get-tuple-element.44), channel_id=1, source_target_pairs={{0,8},{4,12},{8,0},{12,4},{16,24},{20,28},{24,16},{28,20},{1,9},{5... | collective-permute-start | bytes 294920 | tf_op jit(solution)/shard_map/ppermute | solution.py:710
  6.5 4.9 %collective-permute-start.3 = (f32[96,128]{1,0:T(8,128)S(1)}, f32[96,128]{1,0:T(8,128)S(1)}, u32[]{:S(2)}, u32[]{:S(2)}) collective-permute-start(f32[96,128]{1,0:T(8,128)S(1)} %shard_map.114), channel_id=1, source_target_pairs={{0,4},{4,0},{8,12},{12,8},{16,20},{20,16},{24,28},{28,24},{1,5},{5... | collective-permute-start | bytes 147464 | tf_op jit(solution)/shard_map/ppermute | solution.py:710
  9.1 2.3 %collective-permute-start.4 = (f32[96,128]{1,0:T(8,128)S(1)}, f32[96,128]{1,0:T(8,128)S(1)}, u32[]{:S(2)}, u32[]{:S(2)}) collective-permute-start(f32[96,128]{1,0:T(8,128)S(1)} %shard_map.115), channel_id=1, source_target_pairs={{0,4},{4,0},{8,12},{12,8},{16,20},{20,16},{24,28},{28,24},{1,5},{5... | collective-permute-start | bytes 147464 | tf_op jit(solution)/shard_map/ppermute | solution.py:710
  10.8 1.2 %collective-permute-start.5 = (f32[96,128]{1,0:T(8,128)S(1)}, f32[96,128]{1,0:T(8,128)S(1)}, u32[]{:S(2)}, u32[]{:S(2)}) collective-permute-start(f32[96,128]{1,0:T(8,128)S(1)} %shard_map.116), channel_id=1, source_target_pairs={{0,4},{4,0},{8,12},{12,8},{16,20},{20,16},{24,28},{28,24},{1,5},{5... | collective-permute-start | bytes 147464 | tf_op jit(solution)/shard_map/ppermute | solution.py:710
  11.1 3.8 %copy-start = (f32[8,4,4,5,5]{0,2,4,3,1:T(4,128)S(1)}, f32[8,4,4,5,5]{0,2,4,3,1:T(4,128)}, u32[]{:S(2)}) copy-start(f32[8,4,4,5,5]{0,2,4,3,1:T(4,128)} %param.12) | copy-start | bytes 38404
  11.1 1.2 %collective-permute-start.6 = (f32[96,128]{1,0:T(8,128)S(1)}, f32[96,128]{1,0:T(8,128)S(1)}, u32[]{:S(2)}, u32[]{:S(2)}) collective-permute-start(f32[96,128]{1,0:T(8,128)S(1)} %shard_map.117), channel_id=1, source_target_pairs={{0,4},{4,0},{8,12},{12,8},{16,20},{20,16},{24,28},{28,24},{1,5},{5... | collective-permute-start | bytes 147464 | tf_op jit(solution)/shard_map/ppermute | solution.py:710
  13.1 5.8 %collective-permute-start.7 = (f32[2,4,32,128]{3,2,1,0:T(8,128)S(1)}, f32[2,4,32,128]{3,2,1,0:T(8,128)S(1)}, u32[]{:S(2)}, u32[]{:S(2)}) collective-permute-start(f32[2,4,32,128]{3,2,1,0:T(8,128)S(1)} %get-tuple-element.48), channel_id=1, source_target_pairs={{0,1},{1,0},{2,3},{3,2},{4,5},{5,4},{6,7},{7,6},{8,9},{9,8},{10,11... | collective-permute-start | bytes 393224 | tf_op jit(solution)/shard_map/ppermute | solution.py:664
  14.9 4.0 %collective-permute-start.8 = (f32[2,4,32,128]{3,2,1,0:T(8,128)S(1)}, f32[2,4,32,128]{3,2,1,0:T(8,128)S(1)}, u32[]{:S(2)}, u32[]{:S(2)}) collective-permute-start(f32[2,4,32,128]{3,2,1,0:T(8,128)S(1)} %get-tuple-element.49), channel_id=1, source_target_pairs={{0,4},{1,2},{2,1},{3,7},{4,0},{5,6},{6,5},{7,3},{8,12},{9,10},{10,... | collective-permute-start | bytes 393224 | tf_op jit(solution)/shard_map/ppermute | solution.py:664
  20.3 6.1 %collective-permute-start.9 = (f32[2,4,32,128]{3,2,1,0:T(8,128)S(1)}, f32[2,4,32,128]{3,2,1,0:T(8,128)S(1)}, u32[]{:S(2)}, u32[]{:S(2)}) collective-permute-start(f32[2,4,32,128]{3,2,1,0:T(8,128)S(1)} %get-tuple-element.57), channel_id=1, source_target_pairs={{0,1},{1,0},{2,3},{3,2},{4,5},{5,4},{6,7},{7,6},{8,9},{9,8},{10,11... | collective-permute-start | bytes 393224 | tf_op jit(solution)/shard_map/ppermute | solution.py:664
  23.2 3.2 %collective-permute-start.10 = (f32[2,4,32,128]{3,2,1,0:T(8,128)S(1)}, f32[2,4,32,128]{3,2,1,0:T(8,128)S(1)}, u32[]{:S(2)}, u32[]{:S(2)}) collective-permute-start(f32[2,4,32,128]{3,2,1,0:T(8,128)S(1)} %get-tuple-element.58), channel_id=1, source_target_pairs={{0,4},{1,2},{2,1},{3,7},{4,0},{5,6},{6,5},{7,3},{8,12},{9,10},{10,... | collective-permute-start | bytes 393224 | tf_op jit(solution)/shard_map/ppermute | solution.py:664
  27.5 1.6 %collective-permute-start.11 = (f32[4,128,128]{2,1,0:T(8,128)S(1)}, f32[4,128,128]{2,1,0:T(8,128)S(1)}, u32[]{:S(2)}, u32[]{:S(2)}) collective-permute-start(f32[4,128,128]{2,1,0:T(8,128)S(1)} %get-tuple-element.63), channel_id=1, source_target_pairs={{0,4},{4,0},{8,12},{12,8},{16,20},{20,16},{24,28},{28,24},{1,5},{5... | collective-permute-start | bytes 786440 | tf_op jit(solution)/shard_map/ppermute | solution.py:710
  29.1 7.3 %collective-permute-start.14 = (f32[2,128,128]{2,1,0:T(8,128)S(1)}, f32[2,128,128]{2,1,0:T(8,128)S(1)}, u32[]{:S(2)}, u32[]{:S(2)}) collective-permute-start(f32[2,128,128]{2,1,0:T(8,128)S(1)} %get-tuple-element.70), channel_id=1, source_target_pairs={{0,24},{4,28},{8,16},{12,20},{16,8},{20,12},{24,0},{28,4},{1,25},{... | collective-permute-start | bytes 393224 | tf_op jit(solution)/shard_map/ppermute | solution.py:710
  30.7 7.7 %collective-permute-start.12 = (f32[2,128,128]{2,1,0:T(8,128)S(1)}, f32[2,128,128]{2,1,0:T(8,128)S(1)}, u32[]{:S(2)}, u32[]{:S(2)}) collective-permute-start(f32[2,128,128]{2,1,0:T(8,128)S(1)} %get-tuple-element.68), channel_id=1, source_target_pairs={{0,16},{4,20},{8,24},{12,28},{16,0},{20,4},{24,8},{28,12},{1,17},{... | collective-permute-start | bytes 393224 | tf_op jit(solution)/shard_map/ppermute | solution.py:710
  32.1 6.4 %collective-permute-start.13 = (f32[2,128,128]{2,1,0:T(8,128)S(1)}, f32[2,128,128]{2,1,0:T(8,128)S(1)}, u32[]{:S(2)}, u32[]{:S(2)}) collective-permute-start(f32[2,128,128]{2,1,0:T(8,128)S(1)} %get-tuple-element.69), channel_id=1, source_target_pairs={{0,8},{4,12},{8,0},{12,4},{16,24},{20,28},{24,16},{28,20},{1,9},{5... | collective-permute-start | bytes 393224 | tf_op jit(solution)/shard_map/ppermute | solution.py:710

commit v10 on v7

--- a/solution.py
+++ b/solution.py
@@ -256,11 +256,9 @@
     sources, give, misc, by_channel, number = refs[:9], refs[9], refs[10], refs[11], refs[12]
     control, values, normals, order, coeffs, cells, weights, ocells, oweights, arrived = refs[13:]
     held = (order, number, coeffs, cells, weights, ocells, oweights, values, normals)
-    pairs = [(sources[8].at[8 * k : 8 * k + 8], control.at[8 * k : 8 * k + 8]) for k in range(4)]
-    pairs += zip(sources[:1] + sources[:8], held)
     copies = [
         pltpu.make_async_copy(source, target, arrived.at[k])
-        for k, (source, target) in enumerate(pairs)
+        for k, (source, target) in enumerate(zip(sources[:1] + sources, held + (control,)))
     ]
     for copy in copies:
         copy.start()
@@ -269,7 +267,7 @@
         z, y, x = (ref[k, 0] for k in range(3))
         return (((y & 3) * 4 + (z & 3)) * 128 + x).astype(jnp.float32)
 
-    for copy in copies[4:]:
+    for copy in copies[:-1]:
         copy.wait()
     flat, oflat = flat_cell(cells), flat_cell(ocells)
     weight = weights[0]
@@ -288,8 +286,7 @@
     ]
     for target, channels in places:
         place_points(target, channels, values, normals, misc[...], by_channel)
-    for copy in copies[:4]:
-        copy.wait()
+    copies[-1].wait()
     for target, channels in places:
         place_control(target, channels, control)
 
@@ -525,21 +522,38 @@
     )
 
 
+def fold_rows(came, through, partial, table, out):
+    slab, last = lax.axis_index("inline"), lax.axis_size("inline") - 1
+
+    def fold(rows, outside):
+        def read(row, c, depths):
+            line = came[row + 2 if row < 0 else row - 4, c, depths, :]
+            return jnp.where(outside, 0.0, line)
+
+        def write(y, o, depths, value):
+            out[y, o, depths, :] = value
+
+        conv_rows(
+            read, rows, lambda y, o, depths: partial[y, o, depths, :], table, False, write
+        )
+
+    @pl.when(slab % 2 == through)
+    def _():
+        fold(HALO[2:], slab == last)
+
+    @pl.when(slab % 2 != through)
+    def _():
+        fold(HALO[:2], slab == 0)
+
+
+def even_kernel(partial, even_in, table, out):
+    fold_rows(even_in, 0, partial, table, out)
+
+
 def forcing_kernel(
-    partial, even_in, odd_in, table, constant, weight, oweight, potential, forcing, even, odd
+    partial, odd_in, table, constant, weight, oweight, potential, forcing, even, odd
 ):
-    def write(y, o, depths, value):
-        potential[y, o, depths, :] = value
-
-    conv_rows(
-        halo_reader(even_in, odd_in),
-        HALO,
-        lambda y, o, depths: partial[y, o, depths, :],
-        table,
-        False,
-        write,
-    )
-
+    fold_rows(odd_in, 1, partial, table, potential)
     parity = lax.axis_index("inline") % 2
 
     def some_depths(k, carry):
@@ -733,7 +747,7 @@
             f32(96, 128),
         ),
         sources,
-        [pltpu.SMEM((32,), jnp.int32), *held, pltpu.SemaphoreType.DMA((13,))],
+        [pltpu.SMEM((32,), jnp.int32), *held, pltpu.SemaphoreType.DMA((10,))],
         [in_hbm] * 9,
     )
     keep = call(
@@ -759,10 +773,11 @@
     partial, constant, weight, oweight, taps = call(
         own_kernel, (field, field, plane, plane, f32(400, 128)), (chunks, smoothed, kernels)
     )
+    partial = call(even_kernel, field, (partial, even, taps))
     potential, forcing, even, odd = call(
         forcing_kernel,
         (field, field, edge, edge),
-        (partial, even, odd, taps, constant, weight, oweight),
+        (partial, odd, taps, constant, weight, oweight),
     )
     even, odd = swapped(even, odd)
     partial, potential = call(

time: 39.2 us -> 38.8 us (0.990)
  starting transfers between devices: 13.2 us -> 12.8 us
    ppermute x4, starting transfers between devices: 4.57 us -> 4.12 us  [swap(): return lax.ppermute(value, ('depth', 'inline'), pairs)]
    pallas_call x12 -> x13, Pallas kernels: 11.4 us -> 11.5 us  [call(): pl.pallas_call(kernel, out_shape=outs, in_specs=ins or [in_vmem] * len(op...]
  transfers between devices with their start and end apart: 12 -> 12, of which waited for: 10 -> 10; matrix products, arithmetic and copies ran while one was open for 0% -> 0% of each run, Pallas kernels for 16% -> 17%
where the time goes in v10:
time: 38.8 us; the launch traced here: 38.7 us
  waiting for transfers between devices  13.7 us (35%)
  starting transfers between devices  12.8 us (33%)
  Pallas kernels  11.5 us (30%)
  between operations  0.75 us (2%)
    pallas_call x13, Pallas kernels, call(): pl.pallas_call(kernel, out_shape=outs, in_specs=ins or [in_vmem] * len(op...  11.5 us
    ppermute x8, waiting for transfers between devices, swap(): return lax.ppermute(value, 'depth', [(i, i ^ flip) for i in range(8)])  11.2 us
    ppermute x8, starting transfers between devices, swap(): return lax.ppermute(value, 'depth', [(i, i ^ flip) for i in range(8)])  8.66 us
    ppermute x4, starting transfers between devices, swap(): return lax.ppermute(value, ('depth', 'inline'), pairs)  4.12 us
    ppermute x4, waiting for transfers between devices, swap(): return lax.ppermute(value, ('depth', 'inline'), pairs)  2.47 us
  transfers between devices with their start and end apart: 12, of which 10 were waited for; matrix products, arithmetic and copies ran while one was open for 0% of the time, Pallas kernels for 17%

profile of v10, /device:TPU:0, one launch (start us, length us, event | category | flops | bytes accessed | tf_op | source)
XLA Modules:
  0.0 38.7 jit_solution(16003861267861934260)
XLA Ops:
  0.6 1.2 %shard_map.113 = (f32[4,96,128]{2,1,0:T(8,128)S(1)}, f32[8,128]{1,0:T(8,128)S(1)}, f32[128,128]{1,0:T(8,128)S(1)}, s32[32]{0:T(128)S(1)}, f32[32,16,128]{2,1,0:T...) custom-call(s32[32]{0:T(128)} %refs_0_.1, f32[16,32]{1,0:T(8,128)} %bitcast.17, s32[3,1,1,256]{3,2,1,0:T(1,128)} %refs_2_.1, ...), custom_call_target="tpu_custom_call" | custom-call | tf_op jit(solution)/shard_map/pallas_call | solution.py:706
  1.8 0.5 %collective-permute-start = (f32[4,96,128]{2,1,0:T(8,128)S(1)}, f32[4,96,128]{2,1,0:T(8,128)S(1)}, u32[]{:S(2)}, u32[]{:S(2)}) collective-permute-start(f32[4,96,128]{2,1,0:T(8,128)S(1)} %get-tuple-element.51), channel_id=1, source_target_pairs={{0,4},{4,0},{8,12},{12,8},{16,20},{20,16},{24,28},{28,24},{1,5},{5... | collective-permute-start | bytes 589832 | tf_op jit(solution)/shard_map/ppermute | solution.py:732
  2.4 0.6 %shard_map.114 = (f32[96,128]{1,0:T(8,128)S(1)}, f32[96,128]{1,0:T(8,128)S(1)}, f32[96,128]{1,0:T(8,128)S(1)}, f32[96,128]{1,0:T(8,128)S(1)}) custom-call(f32[8,128]{1,0:T(8,128)S(1)} %get-tuple-element.52.misc, f32[128,128]{1,0:T(8,128)S(1)} %get-tuple-element.53.by_channel, s32[32]{0:T(128)S(1)} %get-tuple-element.50.number, ...), custom_call_target="tpu_custom_call" | custom-call | tf_op jit(solution)/shard_map/pallas_call | solution.py:706
  3.0 0.5 %collective-permute-done.got = f32[4,96,128]{2,1,0:T(8,128)S(1)} collective-permute-done((f32[4,96,128]{2,1,0:T(8,128)S(1)}, f32[4,96,128]{2,1,0:T(8,128)S(1)}, u32[]{:S(2)}, u32[]{:S(2)}) %collective-permute-start) | collective-permute-done | bytes 196640 | tf_op jit(solution)/shard_map/ppermute | solution.py:732
  3.5 0.0 copy-start
  3.5 3.9 %collective-permute-start.1 = (f32[2,96,128]{2,1,0:T(8,128)S(1)}, f32[2,96,128]{2,1,0:T(8,128)S(1)}, u32[]{:S(2)}, u32[]{:S(2)}) collective-permute-start(f32[2,96,128]{2,1,0:T(8,128)S(1)} %get-tuple-element.62), channel_id=1, source_target_pairs={{0,24},{4,28},{8,16},{12,20},{16,8},{20,12},{24,0},{28,4},{1,25},{... | collective-permute-start | bytes 294920 | tf_op jit(solution)/shard_map/ppermute | solution.py:732
  7.3 0.5 %collective-permute-start.2 = (f32[2,96,128]{2,1,0:T(8,128)S(1)}, f32[2,96,128]{2,1,0:T(8,128)S(1)}, u32[]{:S(2)}, u32[]{:S(2)}) collective-permute-start(f32[2,96,128]{2,1,0:T(8,128)S(1)} %get-tuple-element.63), channel_id=1, source_target_pairs={{0,16},{4,20},{8,24},{12,28},{16,0},{20,4},{24,8},{28,12},{1,17},{... | collective-permute-start | bytes 294920 | tf_op jit(solution)/shard_map/ppermute | solution.py:732
  7.9 0.1 collective-permute-start.3
  8.0 2.6 %collective-permute-done.1.refs_1_ = f32[2,96,128]{2,1,0:T(8,128)S(1)} collective-permute-done((f32[2,96,128]{2,1,0:T(8,128)S(1)}, f32[2,96,128]{2,1,0:T(8,128)S(1)}, u32[]{:S(2)}, u32[]{:S(2)}) %collective-permute-start.1) | collective-permute-done | bytes 98336 | tf_op jit(solution)/shard_map/ppermute | solution.py:732
  10.6 2.0 %collective-permute-done.2.refs_2_ = f32[2,96,128]{2,1,0:T(8,128)S(1)} collective-permute-done((f32[2,96,128]{2,1,0:T(8,128)S(1)}, f32[2,96,128]{2,1,0:T(8,128)S(1)}, u32[]{:S(2)}, u32[]{:S(2)}) %collective-permute-start.2) | collective-permute-done | bytes 98336 | tf_op jit(solution)/shard_map/ppermute | solution.py:732
  12.6 0.2 collective-permute-done.3.refs_3_
  12.8 0.7 %shard_map.116 = (f32[8,96,128]{2,1,0:T(8,128)S(1)}, f32[4,4,32,128]{3,2,1,0:T(8,128)S(1)}, f32[2,4,32,128]{3,2,1,0:T(8,128)S(1)}, f32[2,4,32,128]{3,2,1,0:T(8,1...) custom-call(f32[2,96,128]{2,1,0:T(8,128)S(1)} %get-tuple-element.61.refs_0_, ...), custom_call_target="tpu_custom_call" | custom-call | tf_op jit(solution)/shard_map/pallas_call | solution.py:706
  13.5 1.6 %collective-permute-start.4 = (f32[2,4,32,128]{3,2,1,0:T(8,128)S(1)}, f32[2,4,32,128]{3,2,1,0:T(8,128)S(1)}, u32[]{:S(2)}, u32[]{:S(2)}) collective-permute-start(f32[2,4,32,128]{3,2,1,0:T(8,128)S(1)} %get-tuple-element.68), channel_id=1, source_target_pairs={{0,1},{1,0},{2,3},{3,2},{4,5},{5,4},{6,7},{7,6},{8,9},{9,8},{10,11... | collective-permute-start | bytes 393224 | tf_op jit(solution)/shard_map/ppermute | solution.py:685
  15.2 0.0 collective-permute-start.5
  15.2 0.0 copy-done
  15.2 2.2 %shard_map.117 = (f32[4,4,32,128]{3,2,1,0:T(8,128)S(1)}, f32[4,4,32,128]{3,2,1,0:T(8,128)S(1)}, f32[4,32,128]{2,1,0:T(8,128)S(1)}, f32[4,32,128]{2,1,0:T(8,128)S(1)}, f32[400,128]{1,0:T(8,128)S(1)}) custom-call(f32[8,96,128]{2,1,0:T(8,128)S(1)} %get-tuple-element.65.chunks.refs_0_, f32[4,4,32,128]{3,2,1,0:T(8,128)S(1)} %get-tuple-element.66.smoothed, ...), custom_call_target="tpu_custom_call" | custom-call | tf_op jit(solution)/shard_map/pallas_call | solution.py:706
  17.4 1.2 %collective-permute-done.4.even_in = f32[2,4,32,128]{3,2,1,0:T(8,128)S(1)} collective-permute-done((f32[2,4,32,128]{3,2,1,0:T(8,128)S(1)}, f32[2,4,32,128]{3,2,1,0:T(8,128)S(1)}, u32[]{:S(2)}, u32[]{:S(2)}) %collective-permute-start.4) | collective-permute-done | bytes 131104 | tf_op jit(solution)/shard_map/ppermute | solution.py:685
  18.6 0.4 %shard_map.118.partial = f32[4,4,32,128]{3,2,1,0:T(8,128)S(1)} custom-call(f32[4,4,32,128]{3,2,1,0:T(8,128)S(1)} %get-tuple-element.67.partial, f32[2,4,32,128]{3,2,1,0:T(8,128)S(1)} %collective-permute-done.4.even_in, f32[400,128]{1,0:T(8,128)S(1)} %get-tuple-element.69.table.refs_4_), custom_call_target="tpu_custom_call" | custom-call | tf_op jit(solution)/shard_map/pallas_call | solution.py:706
  19.0 0.0 collective-permute-done.5.odd_in
  19.0 1.1 %shard_map.119 = (f32[4,4,32,128]{3,2,1,0:T(8,128)S(1)}, f32[4,4,32,128]{3,2,1,0:T(8,128)S(1)}, f32[2,4,32,128]{3,2,1,0:T(8,128)S(1)}, f32[2,4,32,128]{3,2,1,0:T(8,128)S(1)}) custom-call(f32[4,4,32,128]{3,2,1,0:T(8,128)S(1)} %shard_map.118.partial, f32[2,4,32,128]{3,2,1,0:T(8,128)S(1)} %collective-permute-done.5.odd_in, ...), custom_call_target="tpu_custom_call" | custom-call | tf_op jit(solution)/shard_map/pallas_call | solution.py:706
  20.1 2.5 %collective-permute-start.6 = (f32[2,4,32,128]{3,2,1,0:T(8,128)S(1)}, f32[2,4,32,128]{3,2,1,0:T(8,128)S(1)}, u32[]{:S(2)}, u32[]{:S(2)}) collective-permute-start(f32[2,4,32,128]{3,2,1,0:T(8,128)S(1)} %get-tuple-element.77), channel_id=1, source_target_pairs={{0,1},{1,0},{2,3},{3,2},{4,5},{5,4},{6,7},{7,6},{8,9},{9,8},{10,11... | collective-permute-start | bytes 393224 | tf_op jit(solution)/shard_map/ppermute | solution.py:685
  22.6 0.0 collective-permute-start.7
  22.6 1.7 %shard_map.120 = (f32[4,4,32,128]{3,2,1,0:T(8,128)S(1)}, f32[8,64,128]{2,1,0:T(8,128)S(1)}) custom-call(f32[4,4,32,128]{3,2,1,0:T(8,128)S(1)} %get-tuple-element.74.forcing, f32[400,128]{1,0:T(8,128)S(1)} %get-tuple-element.69.table.refs_4_, f32[4,4,32,128]{3,2,1,0:T(8,128)S(1)} %get-tuple-element.75.potential), custom_call_target="tpu_custom_call" | custom-call | tf_op jit(solution)/shard_map/pallas_call | solution.py:706
  24.3 1.2 %collective-permute-done.6.refs_2_ = f32[2,4,32,128]{3,2,1,0:T(8,128)S(1)} collective-permute-done((f32[2,4,32,128]{3,2,1,0:T(8,128)S(1)}, f32[2,4,32,128]{3,2,1,0:T(8,128)S(1)}, u32[]{:S(2)}, u32[]{:S(2)}) %collective-permute-start.6) | collective-permute-done | bytes 131104 | tf_op jit(solution)/shard_map/ppermute | solution.py:685
  25.5 0.0 collective-permute-done.7.refs_3_
  25.6 1.1 %shard_map.121 = (f32[4,128,128]{2,1,0:T(8,128)S(1)}, f32[128,128]{1,0:T(8,128)S(1)}, f32[128,128]{1,0:T(8,128)S(1)}, f32[128,128]{1,0:T(8,128)S(1)}, f32[128,128]{1,0:T(8,128)S(1)}) custom-call(f32[8,96,128]{2,1,0:T(8,128)S(1)} %get-tuple-element.65.chunks.refs_0_, f32[4,4,32,128]{3,2,1,0:T(8,128)S(1)} %get-tuple-element.76.refs_1_, ...), custom_call_target="tpu_custom_call" | custom-call | tf_op jit(solution)/shard_map/pallas_call | solution.py:706
  26.6 0.1 collective-permute-start.8
  26.7 1.5 %collective-permute-done.8.got = f32[4,128,128]{2,1,0:T(8,128)S(1)} collective-permute-done((f32[4,128,128]{2,1,0:T(8,128)S(1)}, f32[4,128,128]{2,1,0:T(8,128)S(1)}, u32[]{:S(2)}, u32[]{:S(2)}) %collective-permute-start.8) | collective-permute-done | bytes 262176 | tf_op jit(solution)/shard_map/ppermute | solution.py:732
  28.3 1.5 %collective-permute-start.11 = (f32[2,128,128]{2,1,0:T(8,128)S(1)}, f32[2,128,128]{2,1,0:T(8,128)S(1)}, u32[]{:S(2)}, u32[]{:S(2)}) collective-permute-start(f32[2,128,128]{2,1,0:T(8,128)S(1)} %get-tuple-element.90), channel_id=1, source_target_pairs={{0,24},{4,28},{8,16},{12,20},{16,8},{20,12},{24,0},{28,4},{1,25},{... | collective-permute-start | bytes 393224 | tf_op jit(solution)/shard_map/ppermute | solution.py:732
  29.8 1.7 %collective-permute-start.9 = (f32[2,128,128]{2,1,0:T(8,128)S(1)}, f32[2,128,128]{2,1,0:T(8,128)S(1)}, u32[]{:S(2)}, u32[]{:S(2)}) collective-permute-start(f32[2,128,128]{2,1,0:T(8,128)S(1)} %get-tuple-element.88), channel_id=1, source_target_pairs={{0,16},{4,20},{8,24},{12,28},{16,0},{20,4},{24,8},{28,12},{1,17},{... | collective-permute-start | bytes 393224 | tf_op jit(solution)/shard_map/ppermute | solution.py:732
  31.5 0.4 collective-permute-start.10
  31.8 0.8 %shard_map.123 = (f32[32,16,128]{2,1,0:T(8,128)}, f32[32,16,128]{2,1,0:T(8,128)}) custom-call(s32[32]{0:T(128)S(1)} %get-tuple-element.50.number, f32[2,128,128]{2,1,0:T(8,128)S(1)} %get-tuple-element.91.refs_0_), custom_call_target="tpu_custom_call" | custom-call | tf_op jit(solution)/shard_map/pallas_call | solution.py:706
  32.6 3.0 %collective-permute-done.11.refs_0_ = f32[2,128,128]{2,1,0:T(8,128)S(1)} collective-permute-done((f32[2,128,128]{2,1,0:T(8,128)S(1)}, f32[2,128,128]{2,1,0:T(8,128)S(1)}, u32[]{:S(2)}, u32[]{:S(2)}) %collective-permute-start.11) | collective-permute-done | bytes 131104 | tf_op jit(solution)/shard_map/ppermute | solution.py:732
  35.6 0.8 %shard_map.124 = (f32[32,16,128]{2,1,0:T(8,128)}, f32[32,16,128]{2,1,0:T(8,128)}) custom-call(s32[32]{0:T(128)S(1)} %get-tuple-element.50.number, f32[2,128,128]{2,1,0:T(8,128)S(1)} %collective-permute-done.11.refs_0_, f32[32,16,128]{2,1,0:T(8,128)} %get-tuple-element.92.refs_1_, ...), custom_call_target="tpu_custom_call", output_to_operand_aliasing={{0}: (2, {}), {1}: (3, {})} | custom-call | tf_op jit(solution)/shard_map/pallas_call | solution.py:706
  36.4 1.2 %collective-permute-done.9.refs_0_ = f32[2,128,128]{2,1,0:T(8,128)S(1)} collective-permute-done((f32[2,128,128]{2,1,0:T(8,128)S(1)}, f32[2,128,128]{2,1,0:T(8,128)S(1)}, u32[]{:S(2)}, u32[]{:S(2)}) %collective-permute-start.9) | collective-permute-done | bytes 131104 | tf_op jit(solution)/shard_map/ppermute | solution.py:732
  37.6 0.3 collective-permute-done.10.refs_1_
  37.8 0.9 %shard_map.125 = (f32[32,16,128]{2,1,0:T(8,128)}, f32[32,16,128]{2,1,0:T(8,128)}) custom-call(s32[32]{0:T(128)S(1)} %get-tuple-element.50.number, f32[2,128,128]{2,1,0:T(8,128)S(1)} %collective-permute-done.9.refs_0_, f32[2,128,128]{2,1,0:T(8,128)S(1)} %collective-permute-done.10.refs_1_, ...), custom_call_target="tpu_custom_call", output_to_operand_aliasing={{0}: (3, {}), {1}: (4, {})} | custom-call | tf_op jit(solution)/shard_map/pallas_call | solution.py:706
  (2 shorter events, 0.1 us)
Async XLA Ops:
  1.8 1.6 %collective-permute-start = (f32[4,96,128]{2,1,0:T(8,128)S(1)}, f32[4,96,128]{2,1,0:T(8,128)S(1)}, u32[]{:S(2)}, u32[]{:S(2)}) collective-permute-start(f32[4,96,128]{2,1,0:T(8,128)S(1)} %get-tuple-element.51), channel_id=1, source_target_pairs={{0,4},{4,0},{8,12},{12,8},{16,20},{20,16},{24,28},{28,24},{1,5},{5... | collective-permute-start | bytes 589832 | tf_op jit(solution)/shard_map/ppermute | solution.py:732
  3.5 11.7 %copy-start = (f32[8,4,4,5,5]{0,2,4,3,1:T(4,128)S(1)}, f32[8,4,4,5,5]{0,2,4,3,1:T(4,128)}, u32[]{:S(2)}) copy-start(f32[8,4,4,5,5]{0,2,4,3,1:T(4,128)} %param.12) | copy-start | bytes 38404
  3.5 7.1 %collective-permute-start.1 = (f32[2,96,128]{2,1,0:T(8,128)S(1)}, f32[2,96,128]{2,1,0:T(8,128)S(1)}, u32[]{:S(2)}, u32[]{:S(2)}) collective-permute-start(f32[2,96,128]{2,1,0:T(8,128)S(1)} %get-tuple-element.62), channel_id=1, source_target_pairs={{0,24},{4,28},{8,16},{12,20},{16,8},{20,12},{24,0},{28,4},{1,25},{... | collective-permute-start | bytes 294920 | tf_op jit(solution)/shard_map/ppermute | solution.py:732
  7.3 5.2 %collective-permute-start.2 = (f32[2,96,128]{2,1,0:T(8,128)S(1)}, f32[2,96,128]{2,1,0:T(8,128)S(1)}, u32[]{:S(2)}, u32[]{:S(2)}) collective-permute-start(f32[2,96,128]{2,1,0:T(8,128)S(1)} %get-tuple-element.63), channel_id=1, source_target_pairs={{0,16},{4,20},{8,24},{12,28},{16,0},{20,4},{24,8},{28,12},{1,17},{... | collective-permute-start | bytes 294920 | tf_op jit(solution)/shard_map/ppermute | solution.py:732
  7.9 4.9 %collective-permute-start.3 = (f32[2,96,128]{2,1,0:T(8,128)S(1)}, f32[2,96,128]{2,1,0:T(8,128)S(1)}, u32[]{:S(2)}, u32[]{:S(2)}) collective-permute-start(f32[2,96,128]{2,1,0:T(8,128)S(1)} %get-tuple-element.64), channel_id=1, source_target_pairs={{0,8},{4,12},{8,0},{12,4},{16,24},{20,28},{24,16},{28,20},{1,9},{5... | collective-permute-start | bytes 294920 | tf_op jit(solution)/shard_map/ppermute | solution.py:732
  13.5 5.1 %collective-permute-start.4 = (f32[2,4,32,128]{3,2,1,0:T(8,128)S(1)}, f32[2,4,32,128]{3,2,1,0:T(8,128)S(1)}, u32[]{:S(2)}, u32[]{:S(2)}) collective-permute-start(f32[2,4,32,128]{3,2,1,0:T(8,128)S(1)} %get-tuple-element.68), channel_id=1, source_target_pairs={{0,1},{1,0},{2,3},{3,2},{4,5},{5,4},{6,7},{7,6},{8,9},{9,8},{10,11... | collective-permute-start | bytes 393224 | tf_op jit(solution)/shard_map/ppermute | solution.py:685
  15.2 3.9 %collective-permute-start.5 = (f32[2,4,32,128]{3,2,1,0:T(8,128)S(1)}, f32[2,4,32,128]{3,2,1,0:T(8,128)S(1)}, u32[]{:S(2)}, u32[]{:S(2)}) collective-permute-start(f32[2,4,32,128]{3,2,1,0:T(8,128)S(1)} %get-tuple-element.70), channel_id=1, source_target_pairs={{0,4},{1,2},{2,1},{3,7},{4,0},{5,6},{6,5},{7,3},{8,12},{9,10},{10,... | collective-permute-start | bytes 393224 | tf_op jit(solution)/shard_map/ppermute | solution.py:685
  20.1 5.4 %collective-permute-start.6 = (f32[2,4,32,128]{3,2,1,0:T(8,128)S(1)}, f32[2,4,32,128]{3,2,1,0:T(8,128)S(1)}, u32[]{:S(2)}, u32[]{:S(2)}) collective-permute-start(f32[2,4,32,128]{3,2,1,0:T(8,128)S(1)} %get-tuple-element.77), channel_id=1, source_target_pairs={{0,1},{1,0},{2,3},{3,2},{4,5},{5,4},{6,7},{7,6},{8,9},{9,8},{10,11... | collective-permute-start | bytes 393224 | tf_op jit(solution)/shard_map/ppermute | solution.py:685
  22.6 3.0 %collective-permute-start.7 = (f32[2,4,32,128]{3,2,1,0:T(8,128)S(1)}, f32[2,4,32,128]{3,2,1,0:T(8,128)S(1)}, u32[]{:S(2)}, u32[]{:S(2)}) collective-permute-start(f32[2,4,32,128]{3,2,1,0:T(8,128)S(1)} %get-tuple-element.78), channel_id=1, source_target_pairs={{0,4},{1,2},{2,1},{3,7},{4,0},{5,6},{6,5},{7,3},{8,12},{9,10},{10,... | collective-permute-start | bytes 393224 | tf_op jit(solution)/shard_map/ppermute | solution.py:685
  26.6 1.6 %collective-permute-start.8 = (f32[4,128,128]{2,1,0:T(8,128)S(1)}, f32[4,128,128]{2,1,0:T(8,128)S(1)}, u32[]{:S(2)}, u32[]{:S(2)}) collective-permute-start(f32[4,128,128]{2,1,0:T(8,128)S(1)} %get-tuple-element.83), channel_id=1, source_target_pairs={{0,4},{4,0},{8,12},{12,8},{16,20},{20,16},{24,28},{28,24},{1,5},{5... | collective-permute-start | bytes 786440 | tf_op jit(solution)/shard_map/ppermute | solution.py:732
  28.3 7.3 %collective-permute-start.11 = (f32[2,128,128]{2,1,0:T(8,128)S(1)}, f32[2,128,128]{2,1,0:T(8,128)S(1)}, u32[]{:S(2)}, u32[]{:S(2)}) collective-permute-start(f32[2,128,128]{2,1,0:T(8,128)S(1)} %get-tuple-element.90), channel_id=1, source_target_pairs={{0,24},{4,28},{8,16},{12,20},{16,8},{20,12},{24,0},{28,4},{1,25},{... | collective-permute-start | bytes 393224 | tf_op jit(solution)/shard_map/ppermute | solution.py:732
  29.8 7.8 %collective-permute-start.9 = (f32[2,128,128]{2,1,0:T(8,128)S(1)}, f32[2,128,128]{2,1,0:T(8,128)S(1)}, u32[]{:S(2)}, u32[]{:S(2)}) collective-permute-start(f32[2,128,128]{2,1,0:T(8,128)S(1)} %get-tuple-element.88), channel_id=1, source_target_pairs={{0,16},{4,20},{8,24},{12,28},{16,0},{20,4},{24,8},{28,12},{1,17},{... | collective-permute-start | bytes 393224 | tf_op jit(solution)/shard_map/ppermute | solution.py:732
  31.5 6.4 %collective-permute-start.10 = (f32[2,128,128]{2,1,0:T(8,128)S(1)}, f32[2,128,128]{2,1,0:T(8,128)S(1)}, u32[]{:S(2)}, u32[]{:S(2)}) collective-permute-start(f32[2,128,128]{2,1,0:T(8,128)S(1)} %get-tuple-element.89), channel_id=1, source_target_pairs={{0,8},{4,12},{8,0},{12,4},{16,24},{20,28},{24,16},{28,20},{1,9},{5... | collective-permute-start | bytes 393224 | tf_op jit(solution)/shard_map/ppermute | solution.py:732

commit v11 on v10

--- a/solution.py
+++ b/solution.py
@@ -429,20 +429,6 @@
 HALO = (-2, -1, 4, 5)
 
 
-def halo_reader(even, odd):
-    slab, last = lax.axis_index("inline"), lax.axis_size("inline") - 1
-    parity = slab % 2
-
-    def read(row, c, depths):
-        y = row + 2 if row < 0 else row - 4
-        through_even, through_odd = even[y, c, depths, :], odd[y, c, depths, :]
-        below = parity == 1 if row < 0 else parity == 0
-        outside = slab == 0 if row < 0 else slab == last
-        return jnp.where(outside, 0.0, jnp.where(below, through_even, through_odd))
-
-    return read
-
-
 def split(value):
     high = value.astype(jnp.bfloat16)
     return high, (value - high.astype(jnp.float32)).astype(jnp.bfloat16)
@@ -522,7 +508,7 @@
     )
 
 
-def fold_rows(came, through, partial, table, out):
+def fold_rows(came, through, partial, table, adjoint, write):
     slab, last = lax.axis_index("inline"), lax.axis_size("inline") - 1
 
     def fold(rows, outside):
@@ -530,11 +516,8 @@
             line = came[row + 2 if row < 0 else row - 4, c, depths, :]
             return jnp.where(outside, 0.0, line)
 
-        def write(y, o, depths, value):
-            out[y, o, depths, :] = value
-
         conv_rows(
-            read, rows, lambda y, o, depths: partial[y, o, depths, :], table, False, write
+            read, rows, lambda y, o, depths: partial[y, o, depths, :], table, adjoint, write
         )
 
     @pl.when(slab % 2 == through)
@@ -546,14 +529,20 @@
         fold(HALO[:2], slab == 0)
 
 
-def even_kernel(partial, even_in, table, out):
-    fold_rows(even_in, 0, partial, table, out)
+def even_kernel(adjoint, partial, even_in, table, out):
+    def write(y, o, depths, value):
+        out[y, o, depths, :] = value
+
+    fold_rows(even_in, 0, partial, table, adjoint, write)
 
 
 def forcing_kernel(
     partial, odd_in, table, constant, weight, oweight, potential, forcing, even, odd
 ):
-    fold_rows(odd_in, 1, partial, table, potential)
+    def write(y, o, depths, value):
+        potential[y, o, depths, :] = value
+
+    fold_rows(odd_in, 1, partial, table, False, write)
     parity = lax.axis_index("inline") % 2
 
     def some_depths(k, carry):
@@ -602,8 +591,8 @@
 
 
 def gradient_kernel(*refs):
-    chunks, partial, even_in, odd_in, taps, table, scale, root, potential = refs[:9]
-    give, keep, (first, rows, out) = refs[9], refs[10:14], refs[14:]
+    chunks, partial, odd_in, taps, table, scale, root, potential = refs[:8]
+    give, keep, (first, rows, out) = refs[8], refs[9:13], refs[13:]
     me = lax.axis_index("depth")
     targets = [
         give.at[place // 2] if place % 2 else keep[place // 2] for place in range(8)
@@ -614,14 +603,7 @@
     def write(y, o, depths, value):
         rows[pl.ds(pl.multiple_of((o * 4 + y) * 32 + depths.start, 8), 8), :] = value
 
-    conv_rows(
-        halo_reader(even_in, odd_in),
-        HALO,
-        lambda y, o, depths: partial[y, o, depths, :],
-        taps,
-        True,
-        write,
-    )
+    fold_rows(odd_in, 1, partial, taps, True, write)
 
     def keep_first(z, value):
         first[z] = scale[z] * value
@@ -773,7 +755,7 @@
     partial, constant, weight, oweight, taps = call(
         own_kernel, (field, field, plane, plane, f32(400, 128)), (chunks, smoothed, kernels)
     )
-    partial = call(even_kernel, field, (partial, even, taps))
+    partial = call(functools.partial(even_kernel, False), field, (partial, even, taps))
     potential, forcing, even, odd = call(
         forcing_kernel,
         (field, field, edge, edge),
@@ -783,10 +765,11 @@
     partial, potential = call(
         spread_kernel, (field, f32(8, 64, 128)), (forcing, taps, potential), [rows]
     )
+    partial = call(functools.partial(even_kernel, True), field, (partial, even, taps))
     give, *keep = call(
         gradient_kernel,
         (f32(4, 128, 128),) + (f32(128, 128),) * 4,
-        (chunks, partial, even, odd, taps, table, scale, root, potential),
+        (chunks, partial, odd, taps, table, scale, root, potential),
         [first, rows, pltpu.VMEM((8, 64, 128), jnp.float32)],
     )
     parts = exchange(128, give, keep, CHIPS)

time: 38.8 us -> 39 us (level)
    pallas_call x13 -> x14, Pallas kernels: 11.5 us -> 11.6 us  [call(): pl.pallas_call(kernel, out_shape=outs, in_specs=ins or [in_vmem] * len(op...]
  transfers between devices with their start and end apart: 12 -> 12, of which waited for: 10 -> 10; matrix products, arithmetic and copies ran while one was open for 0% -> 0% of each run, Pallas kernels for 17% -> 18%
where the time goes in v11:
time: 39 us; the launch traced here: 38.8 us
  waiting for transfers between devices  13.7 us (35%)
  starting transfers between devices  12.8 us (33%)
  Pallas kernels  11.6 us (30%)
  between operations  0.76 us (2%)
    pallas_call x14, Pallas kernels, call(): pl.pallas_call(kernel, out_shape=outs, in_specs=ins or [in_vmem] * len(op...  11.6 us
    ppermute x8, waiting for transfers between devices, swap(): return lax.ppermute(value, 'depth', [(i, i ^ flip) for i in range(8)])  11.2 us
    ppermute x8, starting transfers between devices, swap(): return lax.ppermute(value, 'depth', [(i, i ^ flip) for i in range(8)])  8.66 us
    ppermute x4, starting transfers between devices, swap(): return lax.ppermute(value, ('depth', 'inline'), pairs)  4.12 us
    ppermute x4, waiting for transfers between devices, swap(): return lax.ppermute(value, ('depth', 'inline'), pairs)  2.49 us
  transfers between devices with their start and end apart: 12, of which 10 were waited for; matrix products, arithmetic and copies ran while one was open for 0% of the time, Pallas kernels for 18%

profile of v11, /device:TPU:0, one launch (start us, length us, event | category | flops | bytes accessed | tf_op | source)
XLA Modules:
  0.0 38.8 jit_solution(6627588818729972787)
XLA Ops:
  0.6 1.2 %shard_map.113 = (f32[4,96,128]{2,1,0:T(8,128)S(1)}, f32[8,128]{1,0:T(8,128)S(1)}, f32[128,128]{1,0:T(8,128)S(1)}, s32[32]{0:T(128)S(1)}, f32[32,16,128]{2,1,0:T...) custom-call(s32[32]{0:T(128)} %refs_0_.1, f32[16,32]{1,0:T(8,128)} %bitcast.17, s32[3,1,1,256]{3,2,1,0:T(1,128)} %refs_2_.1, ...), custom_call_target="tpu_custom_call" | custom-call | tf_op jit(solution)/shard_map/pallas_call | solution.py:688
  1.8 0.5 %collective-permute-start = (f32[4,96,128]{2,1,0:T(8,128)S(1)}, f32[4,96,128]{2,1,0:T(8,128)S(1)}, u32[]{:S(2)}, u32[]{:S(2)}) collective-permute-start(f32[4,96,128]{2,1,0:T(8,128)S(1)} %get-tuple-element.51), channel_id=1, source_target_pairs={{0,4},{4,0},{8,12},{12,8},{16,20},{20,16},{24,28},{28,24},{1,5},{5... | collective-permute-start | bytes 589832 | tf_op jit(solution)/shard_map/ppermute | solution.py:714
  2.4 0.6 %shard_map.114 = (f32[96,128]{1,0:T(8,128)S(1)}, f32[96,128]{1,0:T(8,128)S(1)}, f32[96,128]{1,0:T(8,128)S(1)}, f32[96,128]{1,0:T(8,128)S(1)}) custom-call(f32[8,128]{1,0:T(8,128)S(1)} %get-tuple-element.52.misc, f32[128,128]{1,0:T(8,128)S(1)} %get-tuple-element.53.by_channel, s32[32]{0:T(128)S(1)} %get-tuple-element.50.number, ...), custom_call_target="tpu_custom_call" | custom-call | tf_op jit(solution)/shard_map/pallas_call | solution.py:688
  3.0 0.4 %collective-permute-done.got = f32[4,96,128]{2,1,0:T(8,128)S(1)} collective-permute-done((f32[4,96,128]{2,1,0:T(8,128)S(1)}, f32[4,96,128]{2,1,0:T(8,128)S(1)}, u32[]{:S(2)}, u32[]{:S(2)}) %collective-permute-start) | collective-permute-done | bytes 196640 | tf_op jit(solution)/shard_map/ppermute | solution.py:714
  3.5 0.0 copy-start
  3.5 3.9 %collective-permute-start.1 = (f32[2,96,128]{2,1,0:T(8,128)S(1)}, f32[2,96,128]{2,1,0:T(8,128)S(1)}, u32[]{:S(2)}, u32[]{:S(2)}) collective-permute-start(f32[2,96,128]{2,1,0:T(8,128)S(1)} %get-tuple-element.62), channel_id=1, source_target_pairs={{0,24},{4,28},{8,16},{12,20},{16,8},{20,12},{24,0},{28,4},{1,25},{... | collective-permute-start | bytes 294920 | tf_op jit(solution)/shard_map/ppermute | solution.py:714
  7.3 0.5 %collective-permute-start.2 = (f32[2,96,128]{2,1,0:T(8,128)S(1)}, f32[2,96,128]{2,1,0:T(8,128)S(1)}, u32[]{:S(2)}, u32[]{:S(2)}) collective-permute-start(f32[2,96,128]{2,1,0:T(8,128)S(1)} %get-tuple-element.63), channel_id=1, source_target_pairs={{0,16},{4,20},{8,24},{12,28},{16,0},{20,4},{24,8},{28,12},{1,17},{... | collective-permute-start | bytes 294920 | tf_op jit(solution)/shard_map/ppermute | solution.py:714
  7.9 0.1 collective-permute-start.3
  8.0 2.6 %collective-permute-done.1.refs_1_ = f32[2,96,128]{2,1,0:T(8,128)S(1)} collective-permute-done((f32[2,96,128]{2,1,0:T(8,128)S(1)}, f32[2,96,128]{2,1,0:T(8,128)S(1)}, u32[]{:S(2)}, u32[]{:S(2)}) %collective-permute-start.1) | collective-permute-done | bytes 98336 | tf_op jit(solution)/shard_map/ppermute | solution.py:714
  10.6 2.0 %collective-permute-done.2.refs_2_ = f32[2,96,128]{2,1,0:T(8,128)S(1)} collective-permute-done((f32[2,96,128]{2,1,0:T(8,128)S(1)}, f32[2,96,128]{2,1,0:T(8,128)S(1)}, u32[]{:S(2)}, u32[]{:S(2)}) %collective-permute-start.2) | collective-permute-done | bytes 98336 | tf_op jit(solution)/shard_map/ppermute | solution.py:714
  12.6 0.2 collective-permute-done.3.refs_3_
  12.8 0.7 %shard_map.116 = (f32[8,96,128]{2,1,0:T(8,128)S(1)}, f32[4,4,32,128]{3,2,1,0:T(8,128)S(1)}, f32[2,4,32,128]{3,2,1,0:T(8,128)S(1)}, f32[2,4,32,128]{3,2,1,0:T(8,1...) custom-call(f32[2,96,128]{2,1,0:T(8,128)S(1)} %get-tuple-element.61.refs_0_, ...), custom_call_target="tpu_custom_call" | custom-call | tf_op jit(solution)/shard_map/pallas_call | solution.py:688
  13.5 1.6 %collective-permute-start.4 = (f32[2,4,32,128]{3,2,1,0:T(8,128)S(1)}, f32[2,4,32,128]{3,2,1,0:T(8,128)S(1)}, u32[]{:S(2)}, u32[]{:S(2)}) collective-permute-start(f32[2,4,32,128]{3,2,1,0:T(8,128)S(1)} %get-tuple-element.68), channel_id=1, source_target_pairs={{0,1},{1,0},{2,3},{3,2},{4,5},{5,4},{6,7},{7,6},{8,9},{9,8},{10,11... | collective-permute-start | bytes 393224 | tf_op jit(solution)/shard_map/ppermute | solution.py:667
  15.2 0.0 collective-permute-start.5
  15.2 0.0 copy-done
  15.2 2.2 %shard_map.117 = (f32[4,4,32,128]{3,2,1,0:T(8,128)S(1)}, f32[4,4,32,128]{3,2,1,0:T(8,128)S(1)}, f32[4,32,128]{2,1,0:T(8,128)S(1)}, f32[4,32,128]{2,1,0:T(8,128)S(1)}, f32[400,128]{1,0:T(8,128)S(1)}) custom-call(f32[8,96,128]{2,1,0:T(8,128)S(1)} %get-tuple-element.65.chunks.refs_0_, f32[4,4,32,128]{3,2,1,0:T(8,128)S(1)} %get-tuple-element.66.smoothed, ...), custom_call_target="tpu_custom_call" | custom-call | tf_op jit(solution)/shard_map/pallas_call | solution.py:688
  17.4 1.2 %collective-permute-done.4.even_in = f32[2,4,32,128]{3,2,1,0:T(8,128)S(1)} collective-permute-done((f32[2,4,32,128]{3,2,1,0:T(8,128)S(1)}, f32[2,4,32,128]{3,2,1,0:T(8,128)S(1)}, u32[]{:S(2)}, u32[]{:S(2)}) %collective-permute-start.4) | collective-permute-done | bytes 131104 | tf_op jit(solution)/shard_map/ppermute | solution.py:667
  18.6 0.4 %shard_map.118.partial = f32[4,4,32,128]{3,2,1,0:T(8,128)S(1)} custom-call(f32[4,4,32,128]{3,2,1,0:T(8,128)S(1)} %get-tuple-element.67.partial, f32[2,4,32,128]{3,2,1,0:T(8,128)S(1)} %collective-permute-done.4.even_in, f32[400,128]{1,0:T(8,128)S(1)} %get-tuple-element.69.table.refs_3_), custom_call_target="tpu_custom_call" | custom-call | tf_op jit(solution)/shard_map/pallas_call | solution.py:688
  19.0 0.0 collective-permute-done.5.odd_in
  19.0 1.1 %shard_map.119 = (f32[4,4,32,128]{3,2,1,0:T(8,128)S(1)}, f32[4,4,32,128]{3,2,1,0:T(8,128)S(1)}, f32[2,4,32,128]{3,2,1,0:T(8,128)S(1)}, f32[2,4,32,128]{3,2,1,0:T(8,128)S(1)}) custom-call(f32[4,4,32,128]{3,2,1,0:T(8,128)S(1)} %shard_map.118.partial, f32[2,4,32,128]{3,2,1,0:T(8,128)S(1)} %collective-permute-done.5.odd_in, ...), custom_call_target="tpu_custom_call" | custom-call | tf_op jit(solution)/shard_map/pallas_call | solution.py:688
  20.1 2.5 %collective-permute-start.6 = (f32[2,4,32,128]{3,2,1,0:T(8,128)S(1)}, f32[2,4,32,128]{3,2,1,0:T(8,128)S(1)}, u32[]{:S(2)}, u32[]{:S(2)}) collective-permute-start(f32[2,4,32,128]{3,2,1,0:T(8,128)S(1)} %get-tuple-element.77), channel_id=1, source_target_pairs={{0,1},{1,0},{2,3},{3,2},{4,5},{5,4},{6,7},{7,6},{8,9},{9,8},{10,11... | collective-permute-start | bytes 393224 | tf_op jit(solution)/shard_map/ppermute | solution.py:667
  22.6 0.0 collective-permute-start.7
  22.6 1.7 %shard_map.120 = (f32[4,4,32,128]{3,2,1,0:T(8,128)S(1)}, f32[8,64,128]{2,1,0:T(8,128)S(1)}) custom-call(f32[4,4,32,128]{3,2,1,0:T(8,128)S(1)} %get-tuple-element.74.forcing, f32[400,128]{1,0:T(8,128)S(1)} %get-tuple-element.69.table.refs_3_, f32[4,4,32,128]{3,2,1,0:T(8,128)S(1)} %get-tuple-element.75.potential), custom_call_target="tpu_custom_call" | custom-call | tf_op jit(solution)/shard_map/pallas_call | solution.py:688
  24.3 1.2 %collective-permute-done.6.even_in = f32[2,4,32,128]{3,2,1,0:T(8,128)S(1)} collective-permute-done((f32[2,4,32,128]{3,2,1,0:T(8,128)S(1)}, f32[2,4,32,128]{3,2,1,0:T(8,128)S(1)}, u32[]{:S(2)}, u32[]{:S(2)}) %collective-permute-start.6) | collective-permute-done | bytes 131104 | tf_op jit(solution)/shard_map/ppermute | solution.py:667
  25.6 0.4 %shard_map.121.refs_1_ = f32[4,4,32,128]{3,2,1,0:T(8,128)S(1)} custom-call(f32[4,4,32,128]{3,2,1,0:T(8,128)S(1)} %get-tuple-element.76.partial, f32[2,4,32,128]{3,2,1,0:T(8,128)S(1)} %collective-permute-done.6.even_in, f32[400,128]{1,0:T(8,128)S(1)} %get-tuple-element.69.table.refs_3_), custom_call_target="tpu_custom_call" | custom-call | tf_op jit(solution)/shard_map/pallas_call | solution.py:688
  26.0 0.0 collective-permute-done.7.refs_2_
  26.0 0.7 %shard_map.122 = (f32[4,128,128]{2,1,0:T(8,128)S(1)}, f32[128,128]{1,0:T(8,128)S(1)}, f32[128,128]{1,0:T(8,128)S(1)}, f32[128,128]{1,0:T(8,128)S(1)}, f32[128,128]{1,0:T(8,128)S(1)}) custom-call(f32[8,96,128]{2,1,0:T(8,128)S(1)} %get-tuple-element.65.chunks.refs_0_, f32[4,4,32,128]{3,2,1,0:T(8,128)S(1)} %shard_map.121.refs_1_, ...), custom_call_target="tpu_custom_call" | custom-call | tf_op jit(solution)/shard_map/pallas_call | solution.py:688
  26.7 0.1 collective-permute-start.8
  26.8 1.5 %collective-permute-done.8.got = f32[4,128,128]{2,1,0:T(8,128)S(1)} collective-permute-done((f32[4,128,128]{2,1,0:T(8,128)S(1)}, f32[4,128,128]{2,1,0:T(8,128)S(1)}, u32[]{:S(2)}, u32[]{:S(2)}) %collective-permute-start.8) | collective-permute-done | bytes 262176 | tf_op jit(solution)/shard_map/ppermute | solution.py:714
  28.4 1.5 %collective-permute-start.11 = (f32[2,128,128]{2,1,0:T(8,128)S(1)}, f32[2,128,128]{2,1,0:T(8,128)S(1)}, u32[]{:S(2)}, u32[]{:S(2)}) collective-permute-start(f32[2,128,128]{2,1,0:T(8,128)S(1)} %get-tuple-element.90), channel_id=1, source_target_pairs={{0,24},{4,28},{8,16},{12,20},{16,8},{20,12},{24,0},{28,4},{1,25},{... | collective-permute-start | bytes 393224 | tf_op jit(solution)/shard_map/ppermute | solution.py:714
  29.9 1.7 %collective-permute-start.9 = (f32[2,128,128]{2,1,0:T(8,128)S(1)}, f32[2,128,128]{2,1,0:T(8,128)S(1)}, u32[]{:S(2)}, u32[]{:S(2)}) collective-permute-start(f32[2,128,128]{2,1,0:T(8,128)S(1)} %get-tuple-element.88), channel_id=1, source_target_pairs={{0,16},{4,20},{8,24},{12,28},{16,0},{20,4},{24,8},{28,12},{1,17},{... | collective-permute-start | bytes 393224 | tf_op jit(solution)/shard_map/ppermute | solution.py:714
  31.6 0.4 collective-permute-start.10
  31.9 0.8 %shard_map.124 = (f32[32,16,128]{2,1,0:T(8,128)}, f32[32,16,128]{2,1,0:T(8,128)}) custom-call(s32[32]{0:T(128)S(1)} %get-tuple-element.50.number, f32[2,128,128]{2,1,0:T(8,128)S(1)} %get-tuple-element.91.refs_0_), custom_call_target="tpu_custom_call" | custom-call | tf_op jit(solution)/shard_map/pallas_call | solution.py:688
  32.7 3.0 %collective-permute-done.11.refs_0_ = f32[2,128,128]{2,1,0:T(8,128)S(1)} collective-permute-done((f32[2,128,128]{2,1,0:T(8,128)S(1)}, f32[2,128,128]{2,1,0:T(8,128)S(1)}, u32[]{:S(2)}, u32[]{:S(2)}) %collective-permute-start.11) | collective-permute-done | bytes 131104 | tf_op jit(solution)/shard_map/ppermute | solution.py:714
  35.7 0.8 %shard_map.125 = (f32[32,16,128]{2,1,0:T(8,128)}, f32[32,16,128]{2,1,0:T(8,128)}) custom-call(s32[32]{0:T(128)S(1)} %get-tuple-element.50.number, f32[2,128,128]{2,1,0:T(8,128)S(1)} %collective-permute-done.11.refs_0_, f32[32,16,128]{2,1,0:T(8,128)} %get-tuple-element.92.refs_1_, ...), custom_call_target="tpu_custom_call", output_to_operand_aliasing={{0}: (2, {}), {1}: (3, {})} | custom-call | tf_op jit(solution)/shard_map/pallas_call | solution.py:688
  36.5 1.2 %collective-permute-done.9.refs_0_ = f32[2,128,128]{2,1,0:T(8,128)S(1)} collective-permute-done((f32[2,128,128]{2,1,0:T(8,128)S(1)}, f32[2,128,128]{2,1,0:T(8,128)S(1)}, u32[]{:S(2)}, u32[]{:S(2)}) %collective-permute-start.9) | collective-permute-done | bytes 131104 | tf_op jit(solution)/shard_map/ppermute | solution.py:714
  37.7 0.3 collective-permute-done.10.refs_1_
  37.9 0.9 %shard_map.126 = (f32[32,16,128]{2,1,0:T(8,128)}, f32[32,16,128]{2,1,0:T(8,128)}) custom-call(s32[32]{0:T(128)S(1)} %get-tuple-element.50.number, f32[2,128,128]{2,1,0:T(8,128)S(1)} %collective-permute-done.9.refs_0_, f32[2,128,128]{2,1,0:T(8,128)S(1)} %collective-permute-done.10.refs_1_, ...), custom_call_target="tpu_custom_call", output_to_operand_aliasing={{0}: (3, {}), {1}: (4, {})} | custom-call | tf_op jit(solution)/shard_map/pallas_call | solution.py:688
  (2 shorter events, 0.1 us)
Async XLA Ops:
  1.8 1.6 %collective-permute-start = (f32[4,96,128]{2,1,0:T(8,128)S(1)}, f32[4,96,128]{2,1,0:T(8,128)S(1)}, u32[]{:S(2)}, u32[]{:S(2)}) collective-permute-start(f32[4,96,128]{2,1,0:T(8,128)S(1)} %get-tuple-element.51), channel_id=1, source_target_pairs={{0,4},{4,0},{8,12},{12,8},{16,20},{20,16},{24,28},{28,24},{1,5},{5... | collective-permute-start | bytes 589832 | tf_op jit(solution)/shard_map/ppermute | solution.py:714
  3.5 11.7 %copy-start = (f32[8,4,4,5,5]{0,2,4,3,1:T(4,128)S(1)}, f32[8,4,4,5,5]{0,2,4,3,1:T(4,128)}, u32[]{:S(2)}) copy-start(f32[8,4,4,5,5]{0,2,4,3,1:T(4,128)} %param.12) | copy-start | bytes 38404
  3.5 7.1 %collective-permute-start.1 = (f32[2,96,128]{2,1,0:T(8,128)S(1)}, f32[2,96,128]{2,1,0:T(8,128)S(1)}, u32[]{:S(2)}, u32[]{:S(2)}) collective-permute-start(f32[2,96,128]{2,1,0:T(8,128)S(1)} %get-tuple-element.62), channel_id=1, source_target_pairs={{0,24},{4,28},{8,16},{12,20},{16,8},{20,12},{24,0},{28,4},{1,25},{... | collective-permute-start | bytes 294920 | tf_op jit(solution)/shard_map/ppermute | solution.py:714
  7.3 5.2 %collective-permute-start.2 = (f32[2,96,128]{2,1,0:T(8,128)S(1)}, f32[2,96,128]{2,1,0:T(8,128)S(1)}, u32[]{:S(2)}, u32[]{:S(2)}) collective-permute-start(f32[2,96,128]{2,1,0:T(8,128)S(1)} %get-tuple-element.63), channel_id=1, source_target_pairs={{0,16},{4,20},{8,24},{12,28},{16,0},{20,4},{24,8},{28,12},{1,17},{... | collective-permute-start | bytes 294920 | tf_op jit(solution)/shard_map/ppermute | solution.py:714
  7.9 4.9 %collective-permute-start.3 = (f32[2,96,128]{2,1,0:T(8,128)S(1)}, f32[2,96,128]{2,1,0:T(8,128)S(1)}, u32[]{:S(2)}, u32[]{:S(2)}) collective-permute-start(f32[2,96,128]{2,1,0:T(8,128)S(1)} %get-tuple-element.64), channel_id=1, source_target_pairs={{0,8},{4,12},{8,0},{12,4},{16,24},{20,28},{24,16},{28,20},{1,9},{5... | collective-permute-start | bytes 294920 | tf_op jit(solution)/shard_map/ppermute | solution.py:714
  13.5 5.1 %collective-permute-start.4 = (f32[2,4,32,128]{3,2,1,0:T(8,128)S(1)}, f32[2,4,32,128]{3,2,1,0:T(8,128)S(1)}, u32[]{:S(2)}, u32[]{:S(2)}) collective-permute-start(f32[2,4,32,128]{3,2,1,0:T(8,128)S(1)} %get-tuple-element.68), channel_id=1, source_target_pairs={{0,1},{1,0},{2,3},{3,2},{4,5},{5,4},{6,7},{7,6},{8,9},{9,8},{10,11... | collective-permute-start | bytes 393224 | tf_op jit(solution)/shard_map/ppermute | solution.py:667
  15.2 3.9 %collective-permute-start.5 = (f32[2,4,32,128]{3,2,1,0:T(8,128)S(1)}, f32[2,4,32,128]{3,2,1,0:T(8,128)S(1)}, u32[]{:S(2)}, u32[]{:S(2)}) collective-permute-start(f32[2,4,32,128]{3,2,1,0:T(8,128)S(1)} %get-tuple-element.70), channel_id=1, source_target_pairs={{0,4},{1,2},{2,1},{3,7},{4,0},{5,6},{6,5},{7,3},{8,12},{9,10},{10,... | collective-permute-start | bytes 393224 | tf_op jit(solution)/shard_map/ppermute | solution.py:667
  20.1 5.4 %collective-permute-start.6 = (f32[2,4,32,128]{3,2,1,0:T(8,128)S(1)}, f32[2,4,32,128]{3,2,1,0:T(8,128)S(1)}, u32[]{:S(2)}, u32[]{:S(2)}) collective-permute-start(f32[2,4,32,128]{3,2,1,0:T(8,128)S(1)} %get-tuple-element.77), channel_id=1, source_target_pairs={{0,1},{1,0},{2,3},{3,2},{4,5},{5,4},{6,7},{7,6},{8,9},{9,8},{10,11... | collective-permute-start | bytes 393224 | tf_op jit(solution)/shard_map/ppermute | solution.py:667
  22.6 3.4 %collective-permute-start.7 = (f32[2,4,32,128]{3,2,1,0:T(8,128)S(1)}, f32[2,4,32,128]{3,2,1,0:T(8,128)S(1)}, u32[]{:S(2)}, u32[]{:S(2)}) collective-permute-start(f32[2,4,32,128]{3,2,1,0:T(8,128)S(1)} %get-tuple-element.78), channel_id=1, source_target_pairs={{0,4},{1,2},{2,1},{3,7},{4,0},{5,6},{6,5},{7,3},{8,12},{9,10},{10,... | collective-permute-start | bytes 393224 | tf_op jit(solution)/shard_map/ppermute | solution.py:667
  26.7 1.6 %collective-permute-start.8 = (f32[4,128,128]{2,1,0:T(8,128)S(1)}, f32[4,128,128]{2,1,0:T(8,128)S(1)}, u32[]{:S(2)}, u32[]{:S(2)}) collective-permute-start(f32[4,128,128]{2,1,0:T(8,128)S(1)} %get-tuple-element.83), channel_id=1, source_target_pairs={{0,4},{4,0},{8,12},{12,8},{16,20},{20,16},{24,28},{28,24},{1,5},{5... | collective-permute-start | bytes 786440 | tf_op jit(solution)/shard_map/ppermute | solution.py:714
  28.4 7.3 %collective-permute-start.11 = (f32[2,128,128]{2,1,0:T(8,128)S(1)}, f32[2,128,128]{2,1,0:T(8,128)S(1)}, u32[]{:S(2)}, u32[]{:S(2)}) collective-permute-start(f32[2,128,128]{2,1,0:T(8,128)S(1)} %get-tuple-element.90), channel_id=1, source_target_pairs={{0,24},{4,28},{8,16},{12,20},{16,8},{20,12},{24,0},{28,4},{1,25},{... | collective-permute-start | bytes 393224 | tf_op jit(solution)/shard_map/ppermute | solution.py:714
  29.9 7.8 %collective-permute-start.9 = (f32[2,128,128]{2,1,0:T(8,128)S(1)}, f32[2,128,128]{2,1,0:T(8,128)S(1)}, u32[]{:S(2)}, u32[]{:S(2)}) collective-permute-start(f32[2,128,128]{2,1,0:T(8,128)S(1)} %get-tuple-element.88), channel_id=1, source_target_pairs={{0,16},{4,20},{8,24},{12,28},{16,0},{20,4},{24,8},{28,12},{1,17},{... | collective-permute-start | bytes 393224 | tf_op jit(solution)/shard_map/ppermute | solution.py:714
  31.6 6.4 %collective-permute-start.10 = (f32[2,128,128]{2,1,0:T(8,128)S(1)}, f32[2,128,128]{2,1,0:T(8,128)S(1)}, u32[]{:S(2)}, u32[]{:S(2)}) collective-permute-start(f32[2,128,128]{2,1,0:T(8,128)S(1)} %get-tuple-element.89), channel_id=1, source_target_pairs={{0,8},{4,12},{8,0},{12,4},{16,24},{20,28},{24,16},{28,20},{1,9},{5... | collective-permute-start | bytes 393224 | tf_op jit(solution)/shard_map/ppermute | solution.py:714

commit v12 on v11

--- a/solution.py
+++ b/solution.py
@@ -511,22 +511,36 @@
 def fold_rows(came, through, partial, table, adjoint, write):
     slab, last = lax.axis_index("inline"), lax.axis_size("inline") - 1
 
-    def fold(rows, outside):
+    upper = slab % 2 == through
+    outside = slab == jnp.where(upper, last, 0)
+
+    def start(y, o, depths):
+        return partial[y, o, depths, :]
+
+    def fold(rows):
         def read(row, c, depths):
-            line = came[row + 2 if row < 0 else row - 4, c, depths, :]
-            return jnp.where(outside, 0.0, line)
-
-        conv_rows(
-            read, rows, lambda y, o, depths: partial[y, o, depths, :], table, adjoint, write
-        )
-
-    @pl.when(slab % 2 == through)
+            return came[row + 2 if row < 0 else row - 4, c, depths, :]
+
+        conv_rows(read, rows, start, table, adjoint, write)
+
+    @pl.when(upper & ~outside)
     def _():
-        fold(HALO[2:], slab == last)
-
-    @pl.when(slab % 2 != through)
+        fold(HALO[2:])
+
+    @pl.when(~upper & ~outside)
     def _():
-        fold(HALO[:2], slab == 0)
+        fold(HALO[:2])
+
+    @pl.when(outside)
+    def _():
+        def some_depths(k, carry):
+            depths = pl.ds(pl.multiple_of(k * 8, 8), 8)
+            for y in range(4):
+                for o in range(4):
+                    write(y, o, depths, start(y, o, depths))
+            return carry
+
+        lax.fori_loop(0, 4, some_depths, 0)
 
 
 def even_kernel(adjoint, partial, even_in, table, out):

time: 39 us -> 38.6 us (0.990)
  Pallas kernels: 11.6 us -> 10.8 us
  starting transfers between devices: 12.8 us -> 13.2 us
    pallas_call x14, Pallas kernels: 11.6 us -> 10.8 us  [call(): pl.pallas_call(kernel, out_shape=outs, in_specs=ins or [in_vmem] * len(op...]
where the time goes in v12:
time: 38.6 us; the launch traced here: 38.4 us
  waiting for transfers between devices  13.7 us (35%)
  starting transfers between devices  13.2 us (34%)
  Pallas kernels  10.8 us (28%)
  between operations  0.76 us (2%)
    ppermute x8, waiting for transfers between devices, swap(): return lax.ppermute(value, 'depth', [(i, i ^ flip) for i in range(8)])  11.2 us
    pallas_call x14, Pallas kernels, call(): pl.pallas_call(kernel, out_shape=outs, in_specs=ins or [in_vmem] * len(op...  10.8 us
    ppermute x8, starting transfers between devices, swap(): return lax.ppermute(value, 'depth', [(i, i ^ flip) for i in range(8)])  8.66 us
    ppermute x4, starting transfers between devices, swap(): return lax.ppermute(value, ('depth', 'inline'), pairs)  4.49 us
    ppermute x4, waiting for transfers between devices, swap(): return lax.ppermute(value, ('depth', 'inline'), pairs)  2.49 us
  transfers between devices with their start and end apart: 12, of which 10 were waited for; matrix products, arithmetic and copies ran while one was open for 0% of the time, Pallas kernels for 18%

profile of v12, /device:TPU:0, one launch (start us, length us, event | category | flops | bytes accessed | tf_op | source)
XLA Modules:
  0.0 38.4 jit_solution(8068354423849562139)
XLA Ops:
  0.6 1.2 %shard_map.113 = (f32[4,96,128]{2,1,0:T(8,128)S(1)}, f32[8,128]{1,0:T(8,128)S(1)}, f32[128,128]{1,0:T(8,128)S(1)}, s32[32]{0:T(128)S(1)}, f32[32,16,128]{2,1,0:T...) custom-call(s32[32]{0:T(128)} %refs_0_.1, f32[16,32]{1,0:T(8,128)} %bitcast.17, s32[3,1,1,256]{3,2,1,0:T(1,128)} %refs_2_.1, ...), custom_call_target="tpu_custom_call" | custom-call | tf_op jit(solution)/shard_map/pallas_call | solution.py:702
  1.8 0.5 %collective-permute-start = (f32[4,96,128]{2,1,0:T(8,128)S(1)}, f32[4,96,128]{2,1,0:T(8,128)S(1)}, u32[]{:S(2)}, u32[]{:S(2)}) collective-permute-start(f32[4,96,128]{2,1,0:T(8,128)S(1)} %get-tuple-element.51), channel_id=1, source_target_pairs={{0,4},{4,0},{8,12},{12,8},{16,20},{20,16},{24,28},{28,24},{1,5},{5... | collective-permute-start | bytes 589832 | tf_op jit(solution)/shard_map/ppermute | solution.py:728
  2.4 0.6 %shard_map.114 = (f32[96,128]{1,0:T(8,128)S(1)}, f32[96,128]{1,0:T(8,128)S(1)}, f32[96,128]{1,0:T(8,128)S(1)}, f32[96,128]{1,0:T(8,128)S(1)}) custom-call(f32[8,128]{1,0:T(8,128)S(1)} %get-tuple-element.52.misc, f32[128,128]{1,0:T(8,128)S(1)} %get-tuple-element.53.by_channel, s32[32]{0:T(128)S(1)} %get-tuple-element.50.number, ...), custom_call_target="tpu_custom_call" | custom-call | tf_op jit(solution)/shard_map/pallas_call | solution.py:702
  3.0 0.4 %collective-permute-done.got = f32[4,96,128]{2,1,0:T(8,128)S(1)} collective-permute-done((f32[4,96,128]{2,1,0:T(8,128)S(1)}, f32[4,96,128]{2,1,0:T(8,128)S(1)}, u32[]{:S(2)}, u32[]{:S(2)}) %collective-permute-start) | collective-permute-done | bytes 196640 | tf_op jit(solution)/shard_map/ppermute | solution.py:728
  3.5 0.0 copy-start
  3.5 3.9 %collective-permute-start.1 = (f32[2,96,128]{2,1,0:T(8,128)S(1)}, f32[2,96,128]{2,1,0:T(8,128)S(1)}, u32[]{:S(2)}, u32[]{:S(2)}) collective-permute-start(f32[2,96,128]{2,1,0:T(8,128)S(1)} %get-tuple-element.62), channel_id=1, source_target_pairs={{0,24},{4,28},{8,16},{12,20},{16,8},{20,12},{24,0},{28,4},{1,25},{... | collective-permute-start | bytes 294920 | tf_op jit(solution)/shard_map/ppermute | solution.py:728
  7.3 0.5 %collective-permute-start.2 = (f32[2,96,128]{2,1,0:T(8,128)S(1)}, f32[2,96,128]{2,1,0:T(8,128)S(1)}, u32[]{:S(2)}, u32[]{:S(2)}) collective-permute-start(f32[2,96,128]{2,1,0:T(8,128)S(1)} %get-tuple-element.63), channel_id=1, source_target_pairs={{0,16},{4,20},{8,24},{12,28},{16,0},{20,4},{24,8},{28,12},{1,17},{... | collective-permute-start | bytes 294920 | tf_op jit(solution)/shard_map/ppermute | solution.py:728
  7.9 0.1 collective-permute-start.3
  8.0 2.6 %collective-permute-done.1.refs_1_ = f32[2,96,128]{2,1,0:T(8,128)S(1)} collective-permute-done((f32[2,96,128]{2,1,0:T(8,128)S(1)}, f32[2,96,128]{2,1,0:T(8,128)S(1)}, u32[]{:S(2)}, u32[]{:S(2)}) %collective-permute-start.1) | collective-permute-done | bytes 98336 | tf_op jit(solution)/shard_map/ppermute | solution.py:728
  10.6 2.0 %collective-permute-done.2.refs_2_ = f32[2,96,128]{2,1,0:T(8,128)S(1)} collective-permute-done((f32[2,96,128]{2,1,0:T(8,128)S(1)}, f32[2,96,128]{2,1,0:T(8,128)S(1)}, u32[]{:S(2)}, u32[]{:S(2)}) %collective-permute-start.2) | collective-permute-done | bytes 98336 | tf_op jit(solution)/shard_map/ppermute | solution.py:728
  12.6 0.2 collective-permute-done.3.refs_3_
  12.8 0.7 %shard_map.116 = (f32[8,96,128]{2,1,0:T(8,128)S(1)}, f32[4,4,32,128]{3,2,1,0:T(8,128)S(1)}, f32[2,4,32,128]{3,2,1,0:T(8,128)S(1)}, f32[2,4,32,128]{3,2,1,0:T(8,1...) custom-call(f32[2,96,128]{2,1,0:T(8,128)S(1)} %get-tuple-element.61.refs_0_, ...), custom_call_target="tpu_custom_call" | custom-call | tf_op jit(solution)/shard_map/pallas_call | solution.py:702
  13.5 1.6 %collective-permute-start.4 = (f32[2,4,32,128]{3,2,1,0:T(8,128)S(1)}, f32[2,4,32,128]{3,2,1,0:T(8,128)S(1)}, u32[]{:S(2)}, u32[]{:S(2)}) collective-permute-start(f32[2,4,32,128]{3,2,1,0:T(8,128)S(1)} %get-tuple-element.68), channel_id=1, source_target_pairs={{0,1},{1,0},{2,3},{3,2},{4,5},{5,4},{6,7},{7,6},{8,9},{9,8},{10,11... | collective-permute-start | bytes 393224 | tf_op jit(solution)/shard_map/ppermute | solution.py:681
  15.2 0.0 collective-permute-start.5
  15.2 0.0 copy-done
  15.2 2.2 %shard_map.117 = (f32[4,4,32,128]{3,2,1,0:T(8,128)S(1)}, f32[4,4,32,128]{3,2,1,0:T(8,128)S(1)}, f32[4,32,128]{2,1,0:T(8,128)S(1)}, f32[4,32,128]{2,1,0:T(8,128)S(1)}, f32[400,128]{1,0:T(8,128)S(1)}) custom-call(f32[8,96,128]{2,1,0:T(8,128)S(1)} %get-tuple-element.65.chunks.refs_0_, f32[4,4,32,128]{3,2,1,0:T(8,128)S(1)} %get-tuple-element.66.smoothed, ...), custom_call_target="tpu_custom_call" | custom-call | tf_op jit(solution)/shard_map/pallas_call | solution.py:702
  17.4 1.2 %collective-permute-done.4.even_in = f32[2,4,32,128]{3,2,1,0:T(8,128)S(1)} collective-permute-done((f32[2,4,32,128]{3,2,1,0:T(8,128)S(1)}, f32[2,4,32,128]{3,2,1,0:T(8,128)S(1)}, u32[]{:S(2)}, u32[]{:S(2)}) %collective-permute-start.4) | collective-permute-done | bytes 131104 | tf_op jit(solution)/shard_map/ppermute | solution.py:681
  18.6 0.4 %shard_map.118.partial = f32[4,4,32,128]{3,2,1,0:T(8,128)S(1)} custom-call(f32[4,4,32,128]{3,2,1,0:T(8,128)S(1)} %get-tuple-element.67.partial, f32[2,4,32,128]{3,2,1,0:T(8,128)S(1)} %collective-permute-done.4.even_in, f32[400,128]{1,0:T(8,128)S(1)} %get-tuple-element.69.table.refs_3_), custom_call_target="tpu_custom_call" | custom-call | tf_op jit(solution)/shard_map/pallas_call | solution.py:702
  19.0 0.0 collective-permute-done.5.odd_in
  19.0 0.7 %shard_map.119 = (f32[4,4,32,128]{3,2,1,0:T(8,128)S(1)}, f32[4,4,32,128]{3,2,1,0:T(8,128)S(1)}, f32[2,4,32,128]{3,2,1,0:T(8,128)S(1)}, f32[2,4,32,128]{3,2,1,0:T(8,128)S(1)}) custom-call(f32[4,4,32,128]{3,2,1,0:T(8,128)S(1)} %shard_map.118.partial, f32[2,4,32,128]{3,2,1,0:T(8,128)S(1)} %collective-permute-done.5.odd_in, ...), custom_call_target="tpu_custom_call" | custom-call | tf_op jit(solution)/shard_map/pallas_call | solution.py:702
  19.8 2.8 %collective-permute-start.6 = (f32[2,4,32,128]{3,2,1,0:T(8,128)S(1)}, f32[2,4,32,128]{3,2,1,0:T(8,128)S(1)}, u32[]{:S(2)}, u32[]{:S(2)}) collective-permute-start(f32[2,4,32,128]{3,2,1,0:T(8,128)S(1)} %get-tuple-element.77), channel_id=1, source_target_pairs={{0,1},{1,0},{2,3},{3,2},{4,5},{5,4},{6,7},{7,6},{8,9},{9,8},{10,11... | collective-permute-start | bytes 393224 | tf_op jit(solution)/shard_map/ppermute | solution.py:681
  22.6 0.0 collective-permute-start.7
  22.6 1.7 %shard_map.120 = (f32[4,4,32,128]{3,2,1,0:T(8,128)S(1)}, f32[8,64,128]{2,1,0:T(8,128)S(1)}) custom-call(f32[4,4,32,128]{3,2,1,0:T(8,128)S(1)} %get-tuple-element.74.forcing, f32[400,128]{1,0:T(8,128)S(1)} %get-tuple-element.69.table.refs_3_, f32[4,4,32,128]{3,2,1,0:T(8,128)S(1)} %get-tuple-element.75.potential), custom_call_target="tpu_custom_call" | custom-call | tf_op jit(solution)/shard_map/pallas_call | solution.py:702
  24.3 1.2 %collective-permute-done.6.even_in = f32[2,4,32,128]{3,2,1,0:T(8,128)S(1)} collective-permute-done((f32[2,4,32,128]{3,2,1,0:T(8,128)S(1)}, f32[2,4,32,128]{3,2,1,0:T(8,128)S(1)}, u32[]{:S(2)}, u32[]{:S(2)}) %collective-permute-start.6) | collective-permute-done | bytes 131104 | tf_op jit(solution)/shard_map/ppermute | solution.py:681
  25.6 0.4 %shard_map.121.refs_1_ = f32[4,4,32,128]{3,2,1,0:T(8,128)S(1)} custom-call(f32[4,4,32,128]{3,2,1,0:T(8,128)S(1)} %get-tuple-element.76.partial, f32[2,4,32,128]{3,2,1,0:T(8,128)S(1)} %collective-permute-done.6.even_in, f32[400,128]{1,0:T(8,128)S(1)} %get-tuple-element.69.table.refs_3_), custom_call_target="tpu_custom_call" | custom-call | tf_op jit(solution)/shard_map/pallas_call | solution.py:702
  26.0 0.0 collective-permute-done.7.refs_2_
  26.0 0.4 shard_map.122
  26.4 0.1 collective-permute-start.8
  26.4 1.5 %collective-permute-done.8.got = f32[4,128,128]{2,1,0:T(8,128)S(1)} collective-permute-done((f32[4,128,128]{2,1,0:T(8,128)S(1)}, f32[4,128,128]{2,1,0:T(8,128)S(1)}, u32[]{:S(2)}, u32[]{:S(2)}) %collective-permute-start.8) | collective-permute-done | bytes 262176 | tf_op jit(solution)/shard_map/ppermute | solution.py:728
  28.0 1.5 %collective-permute-start.11 = (f32[2,128,128]{2,1,0:T(8,128)S(1)}, f32[2,128,128]{2,1,0:T(8,128)S(1)}, u32[]{:S(2)}, u32[]{:S(2)}) collective-permute-start(f32[2,128,128]{2,1,0:T(8,128)S(1)} %get-tuple-element.90), channel_id=1, source_target_pairs={{0,24},{4,28},{8,16},{12,20},{16,8},{20,12},{24,0},{28,4},{1,25},{... | collective-permute-start | bytes 393224 | tf_op jit(solution)/shard_map/ppermute | solution.py:728
  29.5 1.7 %collective-permute-start.9 = (f32[2,128,128]{2,1,0:T(8,128)S(1)}, f32[2,128,128]{2,1,0:T(8,128)S(1)}, u32[]{:S(2)}, u32[]{:S(2)}) collective-permute-start(f32[2,128,128]{2,1,0:T(8,128)S(1)} %get-tuple-element.88), channel_id=1, source_target_pairs={{0,16},{4,20},{8,24},{12,28},{16,0},{20,4},{24,8},{28,12},{1,17},{... | collective-permute-start | bytes 393224 | tf_op jit(solution)/shard_map/ppermute | solution.py:728
  31.2 0.4 collective-permute-start.10
  31.6 0.8 %shard_map.124 = (f32[32,16,128]{2,1,0:T(8,128)}, f32[32,16,128]{2,1,0:T(8,128)}) custom-call(s32[32]{0:T(128)S(1)} %get-tuple-element.50.number, f32[2,128,128]{2,1,0:T(8,128)S(1)} %get-tuple-element.91.refs_0_), custom_call_target="tpu_custom_call" | custom-call | tf_op jit(solution)/shard_map/pallas_call | solution.py:702
  32.4 3.0 %collective-permute-done.11.refs_0_ = f32[2,128,128]{2,1,0:T(8,128)S(1)} collective-permute-done((f32[2,128,128]{2,1,0:T(8,128)S(1)}, f32[2,128,128]{2,1,0:T(8,128)S(1)}, u32[]{:S(2)}, u32[]{:S(2)}) %collective-permute-start.11) | collective-permute-done | bytes 131104 | tf_op jit(solution)/shard_map/ppermute | solution.py:728
  35.3 0.8 %shard_map.125 = (f32[32,16,128]{2,1,0:T(8,128)}, f32[32,16,128]{2,1,0:T(8,128)}) custom-call(s32[32]{0:T(128)S(1)} %get-tuple-element.50.number, f32[2,128,128]{2,1,0:T(8,128)S(1)} %collective-permute-done.11.refs_0_, f32[32,16,128]{2,1,0:T(8,128)} %get-tuple-element.92.refs_1_, ...), custom_call_target="tpu_custom_call", output_to_operand_aliasing={{0}: (2, {}), {1}: (3, {})} | custom-call | tf_op jit(solution)/shard_map/pallas_call | solution.py:702
  36.1 1.2 %collective-permute-done.9.refs_0_ = f32[2,128,128]{2,1,0:T(8,128)S(1)} collective-permute-done((f32[2,128,128]{2,1,0:T(8,128)S(1)}, f32[2,128,128]{2,1,0:T(8,128)S(1)}, u32[]{:S(2)}, u32[]{:S(2)}) %collective-permute-start.9) | collective-permute-done | bytes 131104 | tf_op jit(solution)/shard_map/ppermute | solution.py:728
  37.3 0.3 collective-permute-done.10.refs_1_
  37.6 0.9 %shard_map.126 = (f32[32,16,128]{2,1,0:T(8,128)}, f32[32,16,128]{2,1,0:T(8,128)}) custom-call(s32[32]{0:T(128)S(1)} %get-tuple-element.50.number, f32[2,128,128]{2,1,0:T(8,128)S(1)} %collective-permute-done.9.refs_0_, f32[2,128,128]{2,1,0:T(8,128)S(1)} %collective-permute-done.10.refs_1_, ...), custom_call_target="tpu_custom_call", output_to_operand_aliasing={{0}: (3, {}), {1}: (4, {})} | custom-call | tf_op jit(solution)/shard_map/pallas_call | solution.py:702
  (2 shorter events, 0.1 us)
Async XLA Ops:
  1.8 1.6 %collective-permute-start = (f32[4,96,128]{2,1,0:T(8,128)S(1)}, f32[4,96,128]{2,1,0:T(8,128)S(1)}, u32[]{:S(2)}, u32[]{:S(2)}) collective-permute-start(f32[4,96,128]{2,1,0:T(8,128)S(1)} %get-tuple-element.51), channel_id=1, source_target_pairs={{0,4},{4,0},{8,12},{12,8},{16,20},{20,16},{24,28},{28,24},{1,5},{5... | collective-permute-start | bytes 589832 | tf_op jit(solution)/shard_map/ppermute | solution.py:728
  3.5 11.7 %copy-start = (f32[8,4,4,5,5]{0,2,4,3,1:T(4,128)S(1)}, f32[8,4,4,5,5]{0,2,4,3,1:T(4,128)}, u32[]{:S(2)}) copy-start(f32[8,4,4,5,5]{0,2,4,3,1:T(4,128)} %param.12) | copy-start | bytes 38404
  3.5 7.1 %collective-permute-start.1 = (f32[2,96,128]{2,1,0:T(8,128)S(1)}, f32[2,96,128]{2,1,0:T(8,128)S(1)}, u32[]{:S(2)}, u32[]{:S(2)}) collective-permute-start(f32[2,96,128]{2,1,0:T(8,128)S(1)} %get-tuple-element.62), channel_id=1, source_target_pairs={{0,24},{4,28},{8,16},{12,20},{16,8},{20,12},{24,0},{28,4},{1,25},{... | collective-permute-start | bytes 294920 | tf_op jit(solution)/shard_map/ppermute | solution.py:728
  7.3 5.2 %collective-permute-start.2 = (f32[2,96,128]{2,1,0:T(8,128)S(1)}, f32[2,96,128]{2,1,0:T(8,128)S(1)}, u32[]{:S(2)}, u32[]{:S(2)}) collective-permute-start(f32[2,96,128]{2,1,0:T(8,128)S(1)} %get-tuple-element.63), channel_id=1, source_target_pairs={{0,16},{4,20},{8,24},{12,28},{16,0},{20,4},{24,8},{28,12},{1,17},{... | collective-permute-start | bytes 294920 | tf_op jit(solution)/shard_map/ppermute | solution.py:728
  7.9 4.9 %collective-permute-start.3 = (f32[2,96,128]{2,1,0:T(8,128)S(1)}, f32[2,96,128]{2,1,0:T(8,128)S(1)}, u32[]{:S(2)}, u32[]{:S(2)}) collective-permute-start(f32[2,96,128]{2,1,0:T(8,128)S(1)} %get-tuple-element.64), channel_id=1, source_target_pairs={{0,8},{4,12},{8,0},{12,4},{16,24},{20,28},{24,16},{28,20},{1,9},{5... | collective-permute-start | bytes 294920 | tf_op jit(solution)/shard_map/ppermute | solution.py:728
  13.5 5.1 %collective-permute-start.4 = (f32[2,4,32,128]{3,2,1,0:T(8,128)S(1)}, f32[2,4,32,128]{3,2,1,0:T(8,128)S(1)}, u32[]{:S(2)}, u32[]{:S(2)}) collective-permute-start(f32[2,4,32,128]{3,2,1,0:T(8,128)S(1)} %get-tuple-element.68), channel_id=1, source_target_pairs={{0,1},{1,0},{2,3},{3,2},{4,5},{5,4},{6,7},{7,6},{8,9},{9,8},{10,11... | collective-permute-start | bytes 393224 | tf_op jit(solution)/shard_map/ppermute | solution.py:681
  15.2 3.9 %collective-permute-start.5 = (f32[2,4,32,128]{3,2,1,0:T(8,128)S(1)}, f32[2,4,32,128]{3,2,1,0:T(8,128)S(1)}, u32[]{:S(2)}, u32[]{:S(2)}) collective-permute-start(f32[2,4,32,128]{3,2,1,0:T(8,128)S(1)} %get-tuple-element.70), channel_id=1, source_target_pairs={{0,4},{1,2},{2,1},{3,7},{4,0},{5,6},{6,5},{7,3},{8,12},{9,10},{10,... | collective-permute-start | bytes 393224 | tf_op jit(solution)/shard_map/ppermute | solution.py:681
  19.8 5.8 %collective-permute-start.6 = (f32[2,4,32,128]{3,2,1,0:T(8,128)S(1)}, f32[2,4,32,128]{3,2,1,0:T(8,128)S(1)}, u32[]{:S(2)}, u32[]{:S(2)}) collective-permute-start(f32[2,4,32,128]{3,2,1,0:T(8,128)S(1)} %get-tuple-element.77), channel_id=1, source_target_pairs={{0,1},{1,0},{2,3},{3,2},{4,5},{5,4},{6,7},{7,6},{8,9},{9,8},{10,11... | collective-permute-start | bytes 393224 | tf_op jit(solution)/shard_map/ppermute | solution.py:681
  22.6 3.4 %collective-permute-start.7 = (f32[2,4,32,128]{3,2,1,0:T(8,128)S(1)}, f32[2,4,32,128]{3,2,1,0:T(8,128)S(1)}, u32[]{:S(2)}, u32[]{:S(2)}) collective-permute-start(f32[2,4,32,128]{3,2,1,0:T(8,128)S(1)} %get-tuple-element.78), channel_id=1, source_target_pairs={{0,4},{1,2},{2,1},{3,7},{4,0},{5,6},{6,5},{7,3},{8,12},{9,10},{10,... | collective-permute-start | bytes 393224 | tf_op jit(solution)/shard_map/ppermute | solution.py:681
  26.4 1.6 %collective-permute-start.8 = (f32[4,128,128]{2,1,0:T(8,128)S(1)}, f32[4,128,128]{2,1,0:T(8,128)S(1)}, u32[]{:S(2)}, u32[]{:S(2)}) collective-permute-start(f32[4,128,128]{2,1,0:T(8,128)S(1)} %get-tuple-element.83), channel_id=1, source_target_pairs={{0,4},{4,0},{8,12},{12,8},{16,20},{20,16},{24,28},{28,24},{1,5},{5... | collective-permute-start | bytes 786440 | tf_op jit(solution)/shard_map/ppermute | solution.py:728
  28.0 7.3 %collective-permute-start.11 = (f32[2,128,128]{2,1,0:T(8,128)S(1)}, f32[2,128,128]{2,1,0:T(8,128)S(1)}, u32[]{:S(2)}, u32[]{:S(2)}) collective-permute-start(f32[2,128,128]{2,1,0:T(8,128)S(1)} %get-tuple-element.90), channel_id=1, source_target_pairs={{0,24},{4,28},{8,16},{12,20},{16,8},{20,12},{24,0},{28,4},{1,25},{... | collective-permute-start | bytes 393224 | tf_op jit(solution)/shard_map/ppermute | solution.py:728
  29.5 7.8 %collective-permute-start.9 = (f32[2,128,128]{2,1,0:T(8,128)S(1)}, f32[2,128,128]{2,1,0:T(8,128)S(1)}, u32[]{:S(2)}, u32[]{:S(2)}) collective-permute-start(f32[2,128,128]{2,1,0:T(8,128)S(1)} %get-tuple-element.88), channel_id=1, source_target_pairs={{0,16},{4,20},{8,24},{12,28},{16,0},{20,4},{24,8},{28,12},{1,17},{... | collective-permute-start | bytes 393224 | tf_op jit(solution)/shard_map/ppermute | solution.py:728
  31.2 6.4 %collective-permute-start.10 = (f32[2,128,128]{2,1,0:T(8,128)S(1)}, f32[2,128,128]{2,1,0:T(8,128)S(1)}, u32[]{:S(2)}, u32[]{:S(2)}) collective-permute-start(f32[2,128,128]{2,1,0:T(8,128)S(1)} %get-tuple-element.89), channel_id=1, source_target_pairs={{0,8},{4,12},{8,0},{12,4},{16,24},{20,28},{24,16},{28,20},{1,9},{5... | collective-permute-start | bytes 393224 | tf_op jit(solution)/shard_map/ppermute | solution.py:728
